TPU v7x, 32 devices: a whole 2x2x4 slice. The times are simulated.
32 devices in a mesh: dp: 2 (over y), seq: 16 (over z, x, core).
Axes of the slice: x: 2, y: 2, z: 4, core: 2. Of those that a mesh axis runs over, the one named last changes fastest.
Arguments:
- tokens: bfloat16 [2, 4096, 1024], P('dp', 'seq'), may hold values from -6 to 6
- segment_ids: int32 [2, 4096], P('dp', 'seq'), may hold values from 0 to 7, never falling along the last dimension, each value on 1 to 2048 neighbouring positions
- second_doc: int32 [2, 8], P('dp'), may hold values from 0 to 7, as said below
- memory_index: int32 [2, 32, 8, 128], P('dp', 'seq'), may hold values from 0 to 511
- cache_keys: bfloat16 [2, 8, 256, 1024], P('dp'), may hold values from -6 to 6
- cache_values: bfloat16 [2, 8, 256, 1024], P('dp'), may hold values from -6 to 6
- first_gain: bfloat16 [1024], P(('dp', 'seq')), may hold values from 0.099609375 to 1.8984375
- query_weight: bfloat16 [1024, 1024], P(('dp', 'seq')), may hold values from -0.1875 to 0.1875
- key_weight: bfloat16 [1024, 1024], P(('dp', 'seq')), may hold values from -0.1875 to 0.1875
- value_weight: bfloat16 [1024, 1024], P(('dp', 'seq')), may hold values from -0.1875 to 0.1875
- out_weight: bfloat16 [1024, 1024], P(('dp', 'seq')), may hold values from -1.5 to 1.5
- second_gain: bfloat16 [1024], P(('dp', 'seq')), may hold values from 0.099609375 to 1.8984375
- gate_weight: bfloat16 [1024, 2816], P(('dp', 'seq')), may hold values from -0.1875 to 0.1875
- up_weight: bfloat16 [1024, 2816], P(('dp', 'seq')), may hold values from -0.1875 to 0.1875
- down_weight: bfloat16 [2816, 1024], P(('dp', 'seq')), may hold values from -0.109375 to 0.109375
- cotangent: bfloat16 [2, 4096, 1024], P('dp', 'seq'), may hold values from -6 to 6
Outputs:
- output: bfloat16 [2, 4096, 1024], P('dp', 'seq')
- input_grad: float32 [2, 4096, 1024], P('dp', 'seq')
- first_gain_grad: float32 [1024], P(('dp', 'seq'))
- query_weight_grad: float32 [1024, 1024], P(('dp', 'seq'))
- key_weight_grad: float32 [1024, 1024], P(('dp', 'seq'))
- value_weight_grad: float32 [1024, 1024], P(('dp', 'seq'))
- out_weight_grad: float32 [1024, 1024], P(('dp', 'seq'))
- second_gain_grad: float32 [1024], P(('dp', 'seq'))
- gate_weight_grad: float32 [1024, 2816], P(('dp', 'seq'))
- up_weight_grad: float32 [1024, 2816], P(('dp', 'seq'))
- down_weight_grad: float32 [2816, 1024], P(('dp', 'seq'))
Inputs may be any that keep to these rules, and one draw needn't show every extreme that they name: `segment_ids`: within each sequence the numbers never fall; every document spans at most 2048 positions and one spans exactly 2048. `second_doc`: never the document's own number.
All inputs are finite; a program needn't handle non-finite values.
Results may differ from a plain program's by a relative error of at most 0.018.
Values may be sent and summed in bfloat16 or wider, within the bound.
No kernel may reach another device: no remote copies, remote signals or barrier semaphores. Data moves between devices by JAX's collectives and lax.ppermute only.
A program may use at most 320 MiB of HBM per device.

v0:
```python
import functools
import math

import jax
import jax.numpy as jnp
from jax import lax
from jax.experimental import pallas as pl
from jax.experimental.pallas import tpu as pltpu
from jax.sharding import Mesh
from jax.sharding import PartitionSpec as P

D = 1024
FF = 2816
HEADS = 8
HEAD_DIM = 128
QUERY_BLOCK = 128
MEM_ROWS = 256
EPSILON = 1e-05
NEGATIVE = -1e30
SCALE = 1.0 / math.sqrt(HEAD_DIM)
LOG2 = SCALE * math.log2(math.e)
LOW = jnp.bfloat16
WIDE = jnp.float32

RING = [2 * i for i in range(HEADS // 2)] + [2 * i + 1 for i in reversed(range(HEADS // 2))]
PLACE = [RING.index(i) for i in range(HEADS)]


def dot_nn(a, b):
    return lax.dot_general(a, b, (((1,), (0,)), ((), ())), preferred_element_type=WIDE)


def dot_nt(a, b):
    return lax.dot_general(a, b, (((1,), (1,)), ((), ())), preferred_element_type=WIDE)


def dot_tn(a, b):
    return lax.dot_general(a, b, (((0,), (0,)), ((), ())), preferred_element_type=WIDE)


def swap(block, axis):
    return lax.ppermute(block, axis, [(0, 1), (1, 0)])


def turn(block, distance):
    route = [(RING[i], RING[(i + distance) % HEADS]) for i in range(HEADS)]
    return lax.ppermute(block, "h", route)


def at_place(place):
    place = lax.rem(place + 2 * HEADS, HEADS)
    return jnp.where(place < HEADS // 2, 2 * place, 2 * (HEADS - 1 - place) + 1)


def exchange(blocks):
    return lax.all_to_all(blocks, "h", 0, 0)


def pick(flag, first, second):
    return jnp.where(flag == 0, first, second)


def smem():
    return pl.BlockSpec(memory_space=pltpu.SMEM)


def vmem():
    return pl.BlockSpec(memory_space=pltpu.VMEM)


def qkv_kernel(parts, tab, *refs):
    xs, (gain_ref, w_ref, cos_ref, sin_ref) = refs[: sum(parts)], refs[sum(parts) : sum(parts) + 4]
    q_ref, kv_ref, n_ref, x_ref = refs[-4:]
    i = pl.program_id(0)
    first = 0
    for step, number in enumerate(parts):

        @pl.when(i == step)
        def _(blocks=xs[first : first + number]):
            row = 0
            for block in blocks:
                size = block.shape[0]
                x_ref[row : row + size, :] = block[...]
                row += size

        first += number
    x = x_ref[...].astype(WIDE)
    r = lax.rsqrt(jnp.mean(x * x, axis=-1, keepdims=True) + EPSILON)
    normed = (x * r * gain_ref[...].astype(WIDE)).astype(LOW)
    n_ref[0] = normed
    out = dot_nn(normed, w_ref[...])
    c, s = cos_ref[0], sin_ref[0]

    def rot(v):
        return v * c + pltpu.roll(v, HEAD_DIM // 2, 1) * s

    q_ref[0] = rot(out[:, :HEAD_DIM]).astype(LOW)
    kv_ref[0, 0] = rot(out[:, HEAD_DIM : 2 * HEAD_DIM]).astype(LOW)
    kv_ref[1, 0] = out[:, 2 * HEAD_DIM :].astype(LOW)


def qkv_blocks(chips, xs, gain, w, cos, sin, held):
    count = cos.shape[1]
    flat = [piece for block in xs for piece, _ in block]
    read = [size for block in xs for _, size in block]

    def whole(shape):
        return pl.BlockSpec(shape, lambda i, t: (0, 0))

    def block(*shape):
        return pl.BlockSpec((1, *shape), lambda i, t: (t[i], 0, 0))

    spec = pltpu.PrefetchScalarGridSpec(
        num_scalar_prefetch=1,
        grid=(len(xs),),
        in_specs=[whole((size, D)) for size in read]
        + [whole((1, D)), whole((D, 3 * HEAD_DIM)), block(count, HEAD_DIM), block(count, HEAD_DIM)]
        + [pl.BlockSpec(memory_space=pl.ANY)] * len(held),
        out_specs=[
            block(count, HEAD_DIM),
            pl.BlockSpec((2, 1, count, HEAD_DIM), lambda i, t: (0, t[i], 0, 0)),
            block(count, D),
        ],
        scratch_shapes=[pltpu.VMEM((count, D), LOW)],
    )
    return pl.pallas_call(
        functools.partial(qkv_kernel, [len(block) for block in xs]),
        grid_spec=spec,
        out_shape=[
            jax.ShapeDtypeStruct((HEADS, count, HEAD_DIM), LOW),
            jax.ShapeDtypeStruct((2, HEADS, count, HEAD_DIM), LOW),
            jax.ShapeDtypeStruct((HEADS, count, D), LOW),
        ],
        input_output_aliases={len(flat) + 5 + i: i for i in range(len(held))},
        cost_estimate=pl.CostEstimate(
            flops=2 * len(xs) * count * D * 3 * HEAD_DIM,
            bytes_accessed=5 * len(xs) * count * D,
            transcendentals=0,
        ),
        name=f"qkv{len(xs)}",
    )(chips, *flat, gain, w, cos, sin, *held)


def causal(count):
    rows = lax.broadcasted_iota(jnp.int32, (count, count), 0)
    return lax.broadcasted_iota(jnp.int32, (count, count), 1) <= rows


def attend_kernel(
    tab, q_ref, own_ref, oth_ref, segq_ref, sego_ref, segt_ref, idx_ref, ck_ref, cv_ref,
    o_ref, low_ref, lse_ref, mem_ref,
):
    i = pl.program_id(0)
    parity = tab[40]
    count = q_ref.shape[1]
    q = q_ref[0]
    segq = segq_ref[0]

    s1 = dot_nt(q, own_ref[0, i]) * LOG2
    s2 = dot_nt(q, oth_ref[0, i]) * LOG2
    s1 = jnp.where((sego_ref[i] == segq) & causal(count), s1, NEGATIVE)
    s2 = jnp.where(segt_ref[i] == segq + 64 * (1 - parity), s2, NEGATIVE)
    memory = []
    for b in range(count // QUERY_BLOCK):
        rows = slice(b * QUERY_BLOCK, (b + 1) * QUERY_BLOCK)
        doc = tab[2 * i + b]
        mate = tab[16 + 2 * i + b]
        idx = idx_ref[0, rows, :]
        lane = lax.broadcasted_iota(jnp.int32, (QUERY_BLOCK, MEM_ROWS), 1)
        first = jnp.where(idx == lane, 1.0, 0.0).astype(LOW)
        second = jnp.where(idx == lane + MEM_ROWS, 1.0, 0.0).astype(LOW)
        here = pl.ds(pl.multiple_of(doc * MEM_ROWS, MEM_ROWS), MEM_ROWS)
        there = pl.ds(pl.multiple_of(mate * MEM_ROWS, MEM_ROWS), MEM_ROWS)
        mk = (dot_nn(first, ck_ref[here, :]) + dot_nn(second, ck_ref[there, :])).astype(LOW)
        mv = (dot_nn(first, cv_ref[here, :]) + dot_nn(second, cv_ref[there, :])).astype(LOW)
        mem_ref[0, 0, rows, :] = mk
        mem_ref[1, 0, rows, :] = mv
        s = jnp.where(segq[rows] == doc, dot_nt(q[rows], mk) * LOG2, NEGATIVE)
        memory.append((s, mv))
    sm = jnp.concatenate([s for s, _ in memory], axis=0)
    top = jnp.maximum(
        jnp.max(jnp.maximum(s1, s2), axis=-1, keepdims=True), jnp.max(sm, axis=-1, keepdims=True)
    )
    p1 = jnp.exp2(s1 - top)
    p2 = jnp.exp2(s2 - top)
    pm = jnp.exp2(sm - top)
    total = jnp.sum(p1 + p2, axis=-1, keepdims=True) + jnp.sum(pm, axis=-1, keepdims=True)
    pm = pm.astype(LOW)
    acc = jnp.concatenate(
        [
            dot_nn(pm[b * QUERY_BLOCK : (b + 1) * QUERY_BLOCK], mv)
            for b, (_, mv) in enumerate(memory)
        ],
        axis=0,
    )
    acc = acc + dot_nn(p1.astype(LOW), own_ref[1, i]) + dot_nn(p2.astype(LOW), oth_ref[1, i])

    def body(j, state):
        top, total, acc = state
        s1 = dot_nt(q, own_ref[0, j]) * LOG2
        s2 = dot_nt(q, oth_ref[0, j]) * LOG2
        s1 = jnp.where(sego_ref[j] == segq, s1, NEGATIVE)
        s2 = jnp.where(segt_ref[j] == segq, s2, NEGATIVE)
        fresh = jnp.maximum(top, jnp.max(jnp.maximum(s1, s2), axis=-1, keepdims=True))
        p1 = jnp.exp2(s1 - fresh)
        p2 = jnp.exp2(s2 - fresh)
        decay = jnp.exp2(top - fresh)
        total = total * decay + jnp.sum(p1 + p2, axis=-1, keepdims=True)
        acc = (
            acc * decay
            + dot_nn(p1.astype(LOW), own_ref[1, j])
            + dot_nn(p2.astype(LOW), oth_ref[1, j])
        )
        return fresh, total, acc

    top, total, acc = lax.fori_loop(tab[32 + i], i, body, (top, total, acc))
    out = acc / total
    o_ref[0] = out
    low_ref[0] = out.astype(LOW)
    lse_ref[0] = top + jnp.log2(total)


def attend(tab, q, own, oth, segq, sego, segt, idx, ck, cv):
    count = q.shape[1]
    block = pl.BlockSpec((1, count, HEAD_DIM), lambda i, t: (i, 0, 0))
    thin = pl.BlockSpec((1, count, 1), lambda i, t: (i, 0, 0))
    whole = pl.BlockSpec((2, HEADS, count, HEAD_DIM), lambda i, t: (0, 0, 0, 0))
    segs = pl.BlockSpec((HEADS, 1, count), lambda i, t: (0, 0, 0))
    cache = pl.BlockSpec((ck.shape[0], HEAD_DIM), lambda i, t: (0, t[41]))
    mem = pl.BlockSpec((2, 1, count, HEAD_DIM), lambda i, t: (0, i, 0, 0))
    return pl.pallas_call(
        attend_kernel,
        grid_spec=pltpu.PrefetchScalarGridSpec(
            num_scalar_prefetch=1,
            grid=(HEADS,),
            in_specs=[block, whole, whole, thin, segs, segs, thin, cache, cache],
            out_specs=[block, block, thin, mem],
        ),
        out_shape=[
            jax.ShapeDtypeStruct((HEADS, count, HEAD_DIM), WIDE),
            jax.ShapeDtypeStruct((HEADS, count, HEAD_DIM), LOW),
            jax.ShapeDtypeStruct((HEADS, count, 1), WIDE),
            jax.ShapeDtypeStruct((2, HEADS, count, HEAD_DIM), LOW),
        ],
        cost_estimate=pl.CostEstimate(
            flops=25 * 10**9, bytes_accessed=6 * 2**20, transcendentals=3 * 10**6
        ),
        name="attend",
    )(tab, q, own, oth, segq, sego, segt, idx, ck, cv)


def attend_back_kernel(
    tab, q_ref, up_ref, o_ref, lse_ref, own_ref, oth_ref, mem_ref, segq_ref, sego_ref, segt_ref,
    dq_ref, down_ref, doth_ref, sum_ref,
):
    i = pl.program_id(0)

    @pl.when(i == 0)
    def _():
        sum_ref[...] = jnp.zeros_like(sum_ref)

    parity = tab[40]
    count = q_ref.shape[1]
    q = q_ref[0]
    up = up_ref[0]
    lse = lse_ref[0]
    segq = segq_ref[0]
    delta = jnp.sum(up.astype(WIDE) * o_ref[0], axis=-1, keepdims=True)
    partial = []
    for b in range(count // QUERY_BLOCK):
        rows = slice(b * QUERY_BLOCK, (b + 1) * QUERY_BLOCK)
        mk = mem_ref[0, 0, rows, :]
        mv = mem_ref[1, 0, rows, :]
        ok = segq[rows] == tab[2 * i + b]
        p = jnp.exp2(jnp.where(ok, dot_nt(q[rows], mk) * LOG2 - lse[rows], NEGATIVE))
        ds = (p * (dot_nt(up[rows], mv) - delta[rows])).astype(LOW)
        partial.append(dot_nn(ds, mk))

    def tile(side, ref, j, ok, dq):
        k = ref[0, j]
        v = ref[1, j]
        p = jnp.exp2(jnp.where(ok, dot_nt(q, k) * LOG2 - lse, NEGATIVE))
        ds = (p * (dot_nt(up, v) - delta)).astype(LOW)
        sum_ref[side, 0, j] += dot_tn(ds, q)
        sum_ref[side, 1, j] += dot_tn(p.astype(LOW), up)
        return dq + dot_nn(ds, k)

    dq = jnp.concatenate(partial, axis=0)
    dq = tile(0, own_ref, i, (sego_ref[i] == segq) & causal(count), dq)
    dq = tile(1, oth_ref, i, segt_ref[i] == segq + 64 * (1 - parity), dq)

    def body(j, dq):
        dq = tile(0, own_ref, j, sego_ref[j] == segq, dq)
        return tile(1, oth_ref, j, segt_ref[j] == segq, dq)

    dq_ref[0] = lax.fori_loop(tab[32 + i], i, body, dq)

    @pl.when(i == HEADS - 1)
    def _():
        down_ref[...] = sum_ref[0]
        doth_ref[...] = sum_ref[1].astype(LOW)


def attend_back(tab, q, up, o, lse, own, oth, mem, segq, sego, segt):
    count = q.shape[1]
    block = pl.BlockSpec((1, count, HEAD_DIM), lambda i, t: (i, 0, 0))
    thin = pl.BlockSpec((1, count, 1), lambda i, t: (i, 0, 0))
    whole = pl.BlockSpec((2, HEADS, count, HEAD_DIM), lambda i, t: (0, 0, 0, 0))
    segs = pl.BlockSpec((HEADS, 1, count), lambda i, t: (0, 0, 0))
    memory = pl.BlockSpec((2, 1, count, HEAD_DIM), lambda i, t: (0, i, 0, 0))
    return pl.pallas_call(
        attend_back_kernel,
        grid_spec=pltpu.PrefetchScalarGridSpec(
            num_scalar_prefetch=1,
            grid=(HEADS,),
            in_specs=[block, block, block, thin, whole, whole, memory, thin, segs, segs],
            out_specs=[block, whole, whole],
            scratch_shapes=[pltpu.VMEM((2, 2, HEADS, count, HEAD_DIM), WIDE)],
        ),
        out_shape=[
            jax.ShapeDtypeStruct((HEADS, count, HEAD_DIM), WIDE),
            jax.ShapeDtypeStruct((2, HEADS, count, HEAD_DIM), WIDE),
            jax.ShapeDtypeStruct((2, HEADS, count, HEAD_DIM), LOW),
        ],
        cost_estimate=pl.CostEstimate(
            flops=30 * 10**9, bytes_accessed=10 * 2**20, transcendentals=3 * 10**6
        ),
        name="attend_back",
    )(tab, q, up, o, lse, own, oth, mem, segq, sego, segt)


def place_rows(tab, sources, w_ref):
    rows = sources[0].shape[1]
    for k, source in enumerate(sources):
        pair = tab[8] if k < 2 else 1 - tab[8]
        core = tab[9] if k % 2 == 0 else 1 - tab[9]
        for slot in range(HEADS):
            start = ((pair * HEADS + tab[slot]) * 2 + core) * rows
            w_ref[pl.ds(pl.multiple_of(start, rows), rows), :] = source[slot]


def out_kernel(tab, heads_ref, *refs):
    sources, (x_ref, gain_ref, att_ref, mid_ref, n_ref, w_ref) = refs[:-6], refs[-6:]
    if len(sources) == 1:
        w_ref[...] = sources[0][...]
    else:
        place_rows(tab, sources, w_ref)
    for h in range(HEADS):
        att_ref[:, h * HEAD_DIM : (h + 1) * HEAD_DIM] = heads_ref[h]
    mid = x_ref[...].astype(WIDE) + dot_nn(att_ref[...], w_ref[...])
    mid_ref[...] = mid
    r = lax.rsqrt(jnp.mean(mid * mid, axis=-1, keepdims=True) + EPSILON)
    n_ref[...] = (mid * r * gain_ref[...].astype(WIDE)).astype(LOW)


def out_block(tab, heads, sources, x, gain):
    count = x.shape[0]
    return pl.pallas_call(
        out_kernel,
        in_specs=[smem()] + [vmem()] * (3 + len(sources)),
        out_specs=[vmem()] * 4,
        out_shape=[
            jax.ShapeDtypeStruct((count, D), LOW),
            jax.ShapeDtypeStruct((count, D), WIDE),
            jax.ShapeDtypeStruct((count, D), LOW),
            jax.ShapeDtypeStruct((D, D), LOW),
        ],
        cost_estimate=pl.CostEstimate(
            flops=2 * count * D * D, bytes_accessed=6 * 2**20, transcendentals=0
        ),
        name="out_block",
    )(tab, heads, *sources, x, gain)


def weights_kernel(tab, *refs):
    blocks, (gate_ref, up_ref, down_ref, acc_ref) = refs[:-4], refs[-4:]
    units = gate_ref.shape[1]
    half = blocks[0].shape[1] // 2
    held = [(b, b) for b in blocks[: HEADS // 2]]
    held += [(blocks[HEADS // 2], blocks[HEADS // 2 + 1])]
    held += [(b, b) for b in blocks[HEADS // 2 + 2 :]]
    for slot, (upper, lower) in enumerate(held):
        chip = tab[slot]
        first = blocks[HEADS // 2].shape[0]
        rows = first // 2
        share = down_ref.shape[0] // HEADS
        for pair in range(2):
            here = pl.ds(pl.multiple_of((pair * HEADS + chip) * rows, rows), rows)
            gate_ref[here, :] = upper[pair * rows : (pair + 1) * rows, :units]
            up_ref[here, :] = upper[pair * rows : (pair + 1) * rows, half : half + units]
        start = 0 if lower is not upper else first
        here = pl.ds(pl.multiple_of(chip * share, 8), share)
        acc_ref[here, :] = lower[start : start + share, :D].astype(WIDE)
    down_ref[...] = acc_ref[...].astype(LOW)


def weights(chips, blocks, units):
    return pl.pallas_call(
        weights_kernel,
        in_specs=[smem()] + [vmem()] * len(blocks),
        out_specs=[vmem()] * 3,
        out_shape=[
            jax.ShapeDtypeStruct((D, units), LOW),
            jax.ShapeDtypeStruct((D, units), LOW),
            jax.ShapeDtypeStruct((units, D), LOW),
        ],
        scratch_shapes=[pltpu.VMEM((units, D), WIDE)],
        cost_estimate=pl.CostEstimate(
            flops=0, bytes_accessed=12 * D * units, transcendentals=0
        ),
        name="weights",
    )(chips, *blocks)


def ffn_kernel(na, nb, ga, gb, g_ref, u_ref, d_ref, hid_ref, gg_ref, ug_ref, dn_ref):
    for t, (n_ref, c_ref) in enumerate(((na, ga), (nb, gb))):
        n = n_ref[...]
        gate = dot_nn(n, g_ref[...])
        upper = dot_nn(n, u_ref[...])
        sigma = jax.nn.sigmoid(gate)
        silu = gate * sigma
        hid_ref[t] = (silu * upper).astype(LOW)
        hg = dot_nt(c_ref[...], d_ref[...])
        gg = (hg * upper * sigma * (1.0 + gate * (1.0 - sigma))).astype(LOW)
        ug = (hg * silu).astype(LOW)
        gg_ref[t] = gg
        ug_ref[t] = ug
        dn_ref[t] = (dot_nt(gg, g_ref[...]) + dot_nt(ug, u_ref[...])).astype(LOW)


def ffn(na, nb, ga, gb, g, u, d):
    count = na.shape[0]
    units = g.shape[1]
    return pl.pallas_call(
        ffn_kernel,
        in_specs=[vmem()] * 7,
        out_specs=[vmem()] * 4,
        out_shape=[jax.ShapeDtypeStruct((2, count, units), LOW)] * 3
        + [jax.ShapeDtypeStruct((2, count, D), LOW)],
        cost_estimate=pl.CostEstimate(
            flops=20 * count * D * units,
            bytes_accessed=6 * D * units + 16 * count * D,
            transcendentals=2 * count * units,
        ),
        name="ffn",
    )(na, nb, ga, gb, g, u, d)


def grads_kernel(tab, *refs):
    ns, ups, (hid_l, gg_l, ug_l, hid_r, gg_r, ug_r, parts_ref) = (
        refs[:4], refs[4:8], refs[8:],
    )
    wide = parts_ref.shape[2]
    half = wide // 2
    units = hid_l.shape[2]
    share = units // HEADS
    rows = ns[0].shape[1] // (2 * HEADS)
    edge = units - units % HEAD_DIM

    def tokens(near, away):
        return jnp.concatenate([near[0], near[1], away[0], away[1]], axis=0)

    n = jnp.concatenate([v[...] for v in ns], axis=0)
    up = jnp.concatenate([v[...] for v in ups], axis=0)
    for near, away, start in ((gg_l, gg_r, 0), (ug_l, ug_r, half)):
        total = dot_tn(n, tokens(near, away)).astype(LOW)
        for h in range(HEADS):
            slot = tab[h]
            for pair in range(2):
                first = (pair * HEADS + h) * rows
                here = slice(pair * rows, (pair + 1) * rows)
                parts_ref[slot, here, start + edge : start + half] = jnp.zeros(
                    (rows, half - edge), LOW
                )
                parts_ref[slot, here, start : start + units] = total[first : first + rows]
    total = dot_tn(tokens(hid_l, hid_r), up)
    strip = wide - D
    for h in range(HEADS):
        slot = tab[h]
        piece = total[h * share : (h + 1) * share].astype(LOW)
        parts_ref[slot, 2 * rows : 2 * rows + share, :D] = piece
        parts_ref[slot, 2 * rows : 2 * rows + share, D:] = jnp.zeros((share, strip), LOW)


def weight_grads(slot_of, ns, ups, near, away, height, wide):
    count = ns[0].shape[0]
    units = near[0].shape[2]
    return pl.pallas_call(
        grads_kernel,
        in_specs=[smem()] + [vmem()] * 14,
        out_specs=vmem(),
        out_shape=jax.ShapeDtypeStruct((HEADS, height, wide), LOW),
        cost_estimate=pl.CostEstimate(
            flops=24 * count * D * units, bytes_accessed=14 * 2**20, transcendentals=0
        ),
        name="weight_grads",
    )(slot_of, *ns, *ups, *near, *away)


def strips_kernel(tab, out_ref, strips_ref):
    rows, strip = out_ref.shape[1], strips_ref.shape[2]
    for slot in range(HEADS):
        for i in range(D // strip):
            strips_ref[slot, i * rows : (i + 1) * rows, :] = out_ref[
                tab[slot], :, i * strip : (i + 1) * strip
            ]


def out_strips(chips, out, strip):
    return pl.pallas_call(
        strips_kernel,
        in_specs=[smem(), vmem()],
        out_specs=vmem(),
        out_shape=jax.ShapeDtypeStruct((HEADS, out.shape[1] * D // strip, strip), LOW),
        cost_estimate=pl.CostEstimate(
            flops=0, bytes_accessed=4 * HEADS * out.shape[1] * D, transcendentals=0
        ),
        name="out_strips",
    )(chips, out)


def mid_kernel(mid_ref, pa, pb, pc, up_ref, gain_ref, w_ref, mg_ref, bg_ref, ag_ref):
    mid = mid_ref[...]
    scaled = (pa[...].astype(WIDE) + pb[...].astype(WIDE) + pc[...].astype(WIDE)) * gain_ref[
        ...
    ].astype(WIDE)
    r = lax.rsqrt(jnp.mean(mid * mid, axis=-1, keepdims=True) + EPSILON)
    inner = jnp.mean(scaled * mid, axis=-1, keepdims=True)
    mid_grad = up_ref[...].astype(WIDE) + r * scaled - mid * (r * r * r * inner)
    mg_ref[...] = mid_grad
    branch = mid_grad.astype(LOW)
    bg_ref[...] = branch
    att = dot_nt(branch, w_ref[...]).astype(LOW)
    for h in range(HEADS):
        ag_ref[h] = att[:, h * HEAD_DIM : (h + 1) * HEAD_DIM]


def mid_block(mid, pa, pb, pc, up, gain, w):
    count = mid.shape[0]
    return pl.pallas_call(
        mid_kernel,
        in_specs=[vmem()] * 7,
        out_specs=[vmem()] * 3,
        out_shape=[
            jax.ShapeDtypeStruct((count, D), WIDE),
            jax.ShapeDtypeStruct((count, D), LOW),
            jax.ShapeDtypeStruct((HEADS, count, HEAD_DIM), LOW),
        ],
        cost_estimate=pl.CostEstimate(
            flops=2 * count * D * D, bytes_accessed=6 * 2**20, transcendentals=0
        ),
        name="mid_block",
    )(mid, pa, pb, pc, up, gain, w)


def qkv_back_kernel(tab, dq_ref, own_ref, got_ref, cos_ref, sin_ref, w_ref, dx_ref, g_ref):
    c, s = cos_ref[0], sin_ref[0]

    def rot(v):
        return v * c - pltpu.roll(v, HEAD_DIM // 2, 1) * s

    dq = rot(dq_ref[0] * SCALE).astype(LOW)
    dk = rot((own_ref[0, 0] + got_ref[0, 0].astype(WIDE)) * SCALE).astype(LOW)
    dv = (own_ref[1, 0] + got_ref[1, 0].astype(WIDE)).astype(LOW)
    grads = jnp.concatenate([dq, dk, dv], axis=1)
    g_ref[0] = grads
    dx_ref[0] = dot_nt(grads, w_ref[...]).astype(LOW)


def qkv_back(chips, dq, own, got, cos, sin, w):
    count = dq.shape[1]
    block = pl.BlockSpec((1, count, HEAD_DIM), lambda i, t: (t[i], 0, 0))
    pair = pl.BlockSpec((2, 1, count, HEAD_DIM), lambda i, t: (0, t[i], 0, 0))
    return pl.pallas_call(
        qkv_back_kernel,
        grid_spec=pltpu.PrefetchScalarGridSpec(
            num_scalar_prefetch=1,
            grid=(HEADS,),
            in_specs=[
                block, pair, pair, block, block,
                pl.BlockSpec((D, 3 * HEAD_DIM), lambda i, t: (0, 0)),
            ],
            out_specs=[
                pl.BlockSpec((1, count, D), lambda i, t: (i, 0, 0)),
                pl.BlockSpec((1, count, 3 * HEAD_DIM), lambda i, t: (t[i], 0, 0)),
            ],
        ),
        out_shape=[
            jax.ShapeDtypeStruct((HEADS, count, D), LOW),
            jax.ShapeDtypeStruct((HEADS, count, 3 * HEAD_DIM), LOW),
        ],
        cost_estimate=pl.CostEstimate(
            flops=2 * HEADS * count * D * 3 * HEAD_DIM,
            bytes_accessed=4 * HEADS * count * D,
            transcendentals=0,
        ),
        name="qkv_back",
    )(chips, dq, own, got, cos, sin, w)


def local(
    far,
    tokens,
    segment_ids,
    second_doc,
    memory_index,
    cache_keys,
    cache_values,
    first_gain,
    query_weight,
    key_weight,
    value_weight,
    out_weight,
    second_gain,
    gate_weight,
    up_weight,
    down_weight,
    cotangent,
):
    x = tokens[0]
    upstream = cotangent[0]
    count = x.shape[0]
    blocks = count // QUERY_BLOCK
    rows = query_weight.shape[0]
    share = down_weight.shape[0]
    units = far * HEADS * share
    chip, core, pair = lax.axis_index("h"), lax.axis_index("c"), lax.axis_index("dl")
    mine = jnp.where(chip % 2 == 0, chip // 2, HEADS - 1 - chip // 2)
    slots = jnp.arange(HEADS, dtype=jnp.int32)
    chips = at_place(mine - slots)

    def by_head(w):
        return w.reshape(rows, HEADS, HEAD_DIM).transpose(1, 0, 2)

    picked = memory_index[0].transpose(1, 0, 2)
    seg_rows = jnp.broadcast_to(
        segment_ids[0].astype(LOW).reshape(1, blocks, QUERY_BLOCK), (HEADS, blocks, QUERY_BLOCK)
    )
    gains = jnp.concatenate([first_gain, second_gain])
    gain_rows = jnp.broadcast_to(
        jnp.pad(gains, (0, HEAD_DIM - 2 * rows)).reshape(1, 1, HEAD_DIM), (HEADS, 1, HEAD_DIM)
    )
    pack = jnp.concatenate(
        [
            by_head(query_weight),
            by_head(key_weight),
            by_head(value_weight),
            seg_rows,
            (picked // MEM_ROWS).astype(LOW),
            (picked % MEM_ROWS).astype(LOW),
            gain_rows,
        ],
        axis=1,
    )
    height = pack.shape[1]
    pack = jnp.pad(pack, ((0, 0), (0, -height % 16), (0, 0)))

    block = jnp.concatenate([x, out_weight], axis=0)
    split = count // 2
    forth, back = [block, turn(block, 1)], [block, turn(block, -1)]
    pack, forth[1], back[1], gate_late, up_late = lax.optimization_barrier(
        (pack, forth[1], back[1], gate_weight, up_weight)
    )
    got = exchange(pack)
    for step in range(HEADS // 2 - 2):
        forth.append(turn(forth[-1], 1))
        back.append(turn(back[-1], -1))
        if step == 0:
            got, forth[-1], back[-1], parity = lax.optimization_barrier(
                (got, forth[-1], back[-1], core)
            )
    far_first, far_last = turn(forth[-1][:split], 1), turn(back[-1][split:], -1)
    x_slots = [((v, count),) for v in forth] + [((far_first, split), (far_last, count - split))]
    x_slots += [((v, count),) for v in back[:0:-1]]
    outs = [v[count:] for v in forth] + [far_last[count - split :]]
    outs = jnp.stack(outs + [v[count:] for v in back[:0:-1]])
    got_c = swap(got, "c")
    got_y = swap(got, "dl")
    got_yc = swap(got_y, "c")
    near = pick(core, jnp.stack([got, got_c]), jnp.stack([got_c, got]))
    away = pick(core, jnp.stack([got_y, got_yc]), jnp.stack([got_yc, got_y]))
    every = pick(pair, jnp.stack([near, away]), jnp.stack([away, near]))
    every = every.transpose(2, 0, 1, 3, 4)
    if far > 1:
        every = lax.all_gather(every, "dh", axis=0)
    else:
        every = every[None]
    every = every.transpose(0, 2, 1, 3, 4, 5)
    w_qkv = jnp.concatenate(
        [every[..., i * rows : (i + 1) * rows, :].reshape(D, HEAD_DIM) for i in range(3)], axis=1
    )
    gain_all = every[..., 3 * rows + 3 * blocks, : 2 * rows].reshape(-1, 2, rows)
    gain_one = gain_all[:, 0].reshape(1, D)
    gain_two = gain_all[:, 1].reshape(1, D)

    def seg_of(blocks_of):
        return (
            blocks_of[:, 3 * rows : 3 * rows + blocks]
            .astype(WIDE)
            .astype(jnp.int32)
            .reshape(HEADS, count)
        )

    seg_own = seg_of(got)
    seg_oth = seg_of(got_c)
    idx = (
        got[:, 3 * rows + blocks : 3 * rows + 2 * blocks].astype(WIDE) * MEM_ROWS
        + got[:, 3 * rows + 2 * blocks : 3 * rows + 3 * blocks].astype(WIDE)
    ).astype(jnp.int32)
    idx = idx.reshape(HEADS, count, 1)

    block_docs = seg_own[:, ::QUERY_BLOCK]
    docs = second_doc.shape[1]
    doc_ids = jnp.arange(docs, dtype=jnp.int32)
    mates = jnp.sum(
        jnp.where(block_docs[:, :, None] == doc_ids, second_doc[0][None, None, :], 0), axis=-1
    )
    seg_all = jnp.concatenate([seg_own, seg_oth], axis=0)
    before = jnp.sum(
        (seg_all.reshape(1, -1) < block_docs[:, :1]).astype(jnp.int32), axis=1
    )
    tab = jnp.concatenate(
        [
            block_docs.reshape(-1),
            mates.reshape(-1),
            before // (2 * count),
            jnp.stack([core, chip]),
        ]
    ).astype(jnp.int32)

    half = HEAD_DIM // 2
    freqs = 10000.0 ** (-jnp.arange(half, dtype=WIDE) * 2.0 / (2 * half))
    positions = ((2 * slots + parity) * count)[:, None] + jnp.arange(count, dtype=jnp.int32)[None]
    turned = positions.astype(WIDE)[:, :, None] * freqs
    cosine, sine = jnp.cos(turned), jnp.sin(turned)
    cosine = jnp.concatenate([cosine, cosine], axis=-1)
    sine = jnp.concatenate([-sine, sine], axis=-1)

    half = units + -units % HEAD_DIM
    wide = 2 * half

    def by_owner(w):
        w = w.reshape(rows, far, 2, HEADS, 2, share).transpose(2, 4, 0, 1, 3, 5)
        return jnp.pad(w.reshape(2, 2, rows, units), ((0, 0),) * 3 + ((0, half - units),))

    gu = jnp.concatenate([by_owner(gate_late), by_owner(up_late)], axis=-1)
    kept = pick(core, gu[:, 0], gu[:, 1])
    came = swap(pick(core, gu[:, 1], gu[:, 0]), "c")
    gu = pick(core, jnp.stack([kept, came], 1), jnp.stack([came, kept], 1))
    kept = pick(pair, gu[0], gu[1])
    came = swap(pick(pair, gu[1], gu[0]), "dl")
    gu = pick(pair, jnp.stack([kept, came]), jnp.stack([came, kept])).reshape(4 * rows, wide)
    bundle = jnp.concatenate([gu, jnp.pad(down_weight, ((0, 0), (0, wide - D)))], axis=0)
    height = 4 * rows + share
    if far > 1:
        bundle = lax.all_gather(bundle, "dh", axis=0, tiled=True)
    upper = bundle.shape[0] * 4 * rows // height if far == 1 else bundle.shape[0] // 2
    bundle, *_ = lax.optimization_barrier((bundle, far_first, far_last))
    forth, back = [bundle], [bundle]
    for step in range(HEADS // 2 - 1):
        forth.append(turn(forth[-1], 1))
        back.append(turn(back[-1], -1))
    w_slots = forth + [turn(forth[-1][:upper], 1), turn(back[-1][upper:], -1)] + back[:0:-1]

    held = ()
    for order in ([0, 1, 7, 2, 6], [3, 5, 4]):
        held = qkv_blocks(
            at_place(mine - jnp.asarray(order, jnp.int32)).astype(jnp.int32),
            [x_slots[i] for i in order],
            gain_one,
            w_qkv,
            cosine,
            sine,
            held,
        )
    queries, own, normed_one = held
    outs_c = swap(outs, "c")
    outs_y = swap(outs, "dl")
    outs_yc = swap(outs_y, "c")
    other = swap(own, "c")
    up_late, _ = lax.optimization_barrier((upstream, own))
    up_c = swap(up_late, "c")
    up_y = swap(up_late, "dl")
    up_yc = swap(up_y, "c")

    seg_thin = seg_own.reshape(HEADS, count, 1)
    seg_own_row = seg_own.reshape(HEADS, 1, count)
    seg_oth_row = seg_oth.reshape(HEADS, 1, count)
    attention, attention_low, lse, memory = attend(
        tab,
        queries,
        own,
        other,
        seg_thin,
        seg_own_row,
        seg_oth_row,
        idx,
        cache_keys[0].reshape(-1, D),
        cache_values[0].reshape(-1, D),
    )

    heads = exchange(attention_low)
    heads, up_c, up_y, up_yc = lax.optimization_barrier((heads, up_c, up_y, up_yc))
    slot_of = lax.rem(mine - jnp.asarray(PLACE, jnp.int32) + HEADS, HEADS).astype(jnp.int32)
    if far == 1:
        sources = [outs, outs_c, outs_y, outs_yc]
    else:
        near = pick(core, jnp.stack([outs, outs_c], 1), jnp.stack([outs_c, outs], 1))
        away = pick(core, jnp.stack([outs_y, outs_yc], 1), jnp.stack([outs_yc, outs_y], 1))
        sources = pick(pair, jnp.stack([near, away]), jnp.stack([away, near]))
        sources = lax.all_gather(jnp.take(sources, slot_of, axis=1), "dh", axis=0)
        sources = [sources.reshape(D, D)]
    where = jnp.concatenate([chips, jnp.stack([pair, core])]).astype(jnp.int32)
    attended, mid, normed_two, out_w = out_block(where, heads, sources, x, gain_two)

    if far == 1:
        gate_w, up_w, down_w = weights(where, w_slots, units)
    else:
        middle = jnp.concatenate(w_slots[HEADS // 2 : HEADS // 2 + 2], axis=0)
        every = jnp.stack(w_slots[: HEADS // 2] + [middle] + w_slots[HEADS // 2 + 2 :])
        every = jnp.take(every, slot_of, axis=0).reshape(HEADS, far, height, wide)
        gu = every[:, :, : 4 * rows].reshape(HEADS, far, 2, 2 * rows, wide)
        gu = gu.transpose(1, 2, 0, 3, 4).reshape(D, wide)
        gate_w, up_w = gu[:, :units], gu[:, half : half + units]
        down_w = every[:, :, 4 * rows :, :D].transpose(1, 0, 2, 3).reshape(units, D)

    n_c = swap(normed_two, "c")
    n_y = swap(normed_two, "dl")
    n_yc = swap(n_y, "c")
    hid_l, gg_l, ug_l, dn_l = ffn(normed_two, n_c, upstream, up_c, gate_w, up_w, down_w)
    hid_r, gg_r, ug_r, dn_r = ffn(n_y, n_yc, up_y, up_yc, gate_w, up_w, down_w)

    def to_away(away):
        return (away[0].astype(WIDE) + swap(away[1], "c").astype(WIDE)).astype(LOW)

    there = to_away(dn_r)
    there, hid_l, gg_l, ug_l, hid_r, gg_r, ug_r = lax.optimization_barrier(
        (there, hid_l, gg_l, ug_l, hid_r, gg_r, ug_r)
    )
    n_all, u_all = [normed_two, n_c, n_y, n_yc], [upstream, up_c, up_y, up_yc]
    near, away = (hid_l, gg_l, ug_l), (hid_r, gg_r, ug_r)
    if far == 1:
        parts = weight_grads(slot_of, n_all, u_all, near, away, height, wide)
    else:

        def over_tokens(left, right):
            return jnp.einsum(
                "gtd,gtf->df", left, right, preferred_element_type=WIDE
            ).astype(LOW)

        def by_rows(w):
            w = jnp.pad(w, ((0, 0), (0, half - units)))
            return w.reshape(far, 2, HEADS, 2 * rows, half).transpose(2, 0, 1, 3, 4)

        n_all, u_all = jnp.stack(n_all), jnp.stack(u_all)
        hid, gg, ug = (jnp.concatenate(pieces, axis=0) for pieces in zip(near, away))
        gu = jnp.concatenate(
            [by_rows(over_tokens(n_all, gg)), by_rows(over_tokens(n_all, ug))], axis=-1
        ).reshape(HEADS, far, 4 * rows, wide)
        down = over_tokens(hid, u_all).reshape(far, HEADS, share, D).transpose(1, 0, 2, 3)
        down = jnp.pad(down, ((0, 0), (0, 0), (0, 0), (0, wide - D)))
        parts = jnp.concatenate([gu, down], axis=2)
        parts = jnp.take(parts.reshape(HEADS, far * height, wide), chips, axis=0)

    sums = [dn_l[0], swap(dn_l[1], "c"), swap(there, "dl")]
    sums[2], parts = lax.optimization_barrier((sums[2], parts))
    mid_grad, branch, att_grad = mid_block(mid, *sums, upstream, gain_two, out_w)
    ups = exchange(att_grad)

    def plus(block, arrived, start):
        size = arrived.shape[0]
        total = block[start : start + size].astype(WIDE) + arrived.astype(WIDE)
        pieces = [block[:start], total, block[start + size :]]
        pieces = [piece.astype(LOW) for piece in pieces if piece.shape[0]]
        return jnp.concatenate(pieces, axis=0)

    def ring_first(blocks, split):
        middle = blocks[HEADS // 2]
        return (
            plus(blocks[HEADS // 2 + 1], turn(middle[:split].astype(LOW), 1), 0),
            plus(blocks[HEADS // 2 - 1], turn(middle[split:].astype(LOW), -1), split),
        )

    def ring_next(blocks, forth, back, step):
        return (
            plus(blocks[HEADS // 2 + step], turn(forth, 1), 0),
            plus(blocks[HEADS // 2 - step], turn(back, -1), 0),
        )

    def ring_rest(blocks, forth, back, first=2):
        for step in range(first, HEADS // 2):
            forth, back = ring_next(blocks, forth, back, step)
        forth, back = turn(forth, 1), turn(back, -1)
        return blocks[0].astype(WIDE) + forth.astype(WIDE) + back.astype(WIDE)

    def over_owner(w, width):
        w = w.reshape(far, 2, HEADS, 2, rows, width)
        kept = pick(core, w[:, :, :, 0], w[:, :, :, 1])
        came = swap(pick(core, w[:, :, :, 1], w[:, :, :, 0]), "c")
        w = kept.astype(WIDE) + came.astype(WIDE)
        kept = pick(pair, w[:, 0], w[:, 1])
        came = swap(pick(pair, w[:, 1], w[:, 0]).astype(LOW), "dl")
        w = (kept + came.astype(WIDE)).astype(LOW)
        if far > 1:
            w = lax.psum_scatter(w, "dh", scatter_dimension=0, tiled=True)
        return w[0]

    out_part = over_owner(
        jnp.einsum("td,te->de", attended, branch, preferred_element_type=WIDE).astype(LOW), D
    )
    strip = wide - D
    blocks = [parts[slot].astype(WIDE) for slot in range(HEADS)]
    if far == 1:
        strips = out_strips(where, out_part, strip)
        below = share - strips.shape[1]
        for slot in range(HEADS):
            if slot != HEADS // 2:
                blocks[slot] = blocks[slot] + jnp.pad(
                    strips[slot].astype(WIDE), ((4 * rows, below), (D, 0))
                )
        out_far = turn(strips[HEADS // 2], HEADS // 2)
    forth, back = ring_first(blocks, upper)
    ups, forth, back = lax.optimization_barrier((ups, forth, back))
    forth, back = ring_next(blocks, forth, back, 2)

    dq, d_own, d_oth = attend_back(
        tab, queries, ups, attention, lse, own, other, memory, seg_thin, seg_own_row, seg_oth_row
    )
    d_got = swap(d_oth, "c")
    dq, forth, back = lax.optimization_barrier((dq, forth, back))
    dx, grads = qkv_back(chips.astype(jnp.int32), dq, d_own, d_got, cosine, sine, w_qkv)
    dx_forth, dx_back = ring_first(dx, split)
    grads, hid_l, hid_r, _, _ = lax.optimization_barrier((grads, hid_l, hid_r, dx_forth, dx_back))
    normed_one_grad = ring_rest(dx, dx_forth, dx_back)

    summed = ring_rest(blocks, forth, back, 3).astype(LOW)
    if far > 1:
        summed = lax.psum_scatter(summed, "dh", scatter_dimension=0, tiled=True)
    down_w_grad = summed[4 * rows : 4 * rows + share, :D].astype(WIDE)
    if far == 1:
        out_w_grad = summed[4 * rows : 4 * rows + strips.shape[1], D:].astype(WIDE)
        out_w_grad = out_w_grad + out_far.astype(WIDE)
        out_w_grad = out_w_grad.reshape(D // strip, rows, strip).transpose(1, 0, 2).reshape(rows, D)
    else:
        out_w_grad = jnp.sum(exchange(out_part).astype(WIDE), axis=0)
    gu = summed[: 4 * rows].reshape(2, 2, rows, wide)
    kept = pick(core, gu[:, 0], gu[:, 1])
    came = swap(pick(core, gu[:, 1], gu[:, 0]), "c")
    gu = pick(core, jnp.stack([kept, came], 1), jnp.stack([came, kept], 1))
    kept = pick(pair, gu[0], gu[1])
    came = swap(pick(pair, gu[1], gu[0]), "dl")
    gu = pick(pair, jnp.stack([kept, came]), jnp.stack([came, kept]))
    gu = jnp.stack([gu[..., :units], gu[..., half : half + units]])
    gu = (
        gu.reshape(2, 2, 2, rows, far, HEADS, share)
        .transpose(0, 3, 4, 1, 5, 2, 6)
        .reshape(2, rows, FF)
        .astype(WIDE)
    )
    gate_w_grad, up_w_grad = gu[0], gu[1]

    out_l = jnp.einsum("gtf,fd->gtd", hid_l, down_w, preferred_element_type=WIDE).astype(LOW)
    out_r = jnp.einsum("gtf,fd->gtd", hid_r, down_w, preferred_element_type=WIDE).astype(LOW)
    output = mid
    for part in (out_l[0], swap(out_l[1], "c"), swap(to_away(out_r), "dl")):
        output = output + part.astype(WIDE)
    output = output.astype(LOW)

    dw = jnp.einsum("std,stg->dg", normed_one, grads, preferred_element_type=WIDE).astype(LOW)
    qkv_grads = exchange(over_owner(dw, 3 * HEAD_DIM)).astype(WIDE)

    wide_x = x.astype(WIDE)
    r = lax.rsqrt(jnp.mean(wide_x * wide_x, axis=-1, keepdims=True) + EPSILON)
    scaled = normed_one_grad * gain_one.astype(WIDE)
    inner = jnp.mean(scaled * wide_x, axis=-1, keepdims=True)
    input_grad = mid_grad + r * scaled - wide_x * (r * r * r * inner)

    q_w_grad, k_w_grad, v_w_grad = (
        qkv_grads[:, :, i * HEAD_DIM : (i + 1) * HEAD_DIM].transpose(1, 0, 2).reshape(rows, D)
        for i in range(3)
    )

    def gain_grad(gain, pairs):
        total = 0.0
        for grad, weight in pairs:
            total = total + jnp.sum(grad * weight.astype(WIDE), axis=1)
        return total / gain.astype(WIDE)

    first_gain_grad = gain_grad(
        first_gain,
        ((q_w_grad, query_weight), (k_w_grad, key_weight), (v_w_grad, value_weight)),
    )
    second_gain_grad = gain_grad(
        second_gain, ((gate_w_grad, gate_weight), (up_w_grad, up_weight))
    )
    return (
        output[None],
        input_grad[None],
        first_gain_grad,
        q_w_grad,
        k_w_grad,
        v_w_grad,
        out_w_grad,
        second_gain_grad,
        gate_w_grad,
        up_w_grad,
        down_w_grad,
    )


def solution(mesh):
    far = mesh.shape["dp"] // 2
    cores = mesh.shape["seq"] // HEADS
    fine = Mesh(mesh.devices.reshape(far, 2, HEADS, cores), ("dh", "dl", "h", "c"))
    dp, seq, every = ("dh", "dl"), ("h", "c"), ("dh", "dl", "h", "c")
    rows = P(every, None)
    return jax.shard_map(
        functools.partial(local, far),
        mesh=fine,
        in_specs=(
            P(dp, seq, None),
            P(dp, seq),
            P(dp, None),
            P(dp, seq, None, None),
            P(dp, None, None, None),
            P(dp, None, None, None),
            P(every),
            rows,
            rows,
            rows,
            rows,
            P(every),
            rows,
            rows,
            rows,
            P(dp, seq, None),
        ),
        out_specs=(
            P(dp, seq, None),
            P(dp, seq, None),
            P(every),
            rows,
            rows,
            rows,
            rows,
            P(every),
            rows,
            rows,
            rows,
        ),
        check_vma=False,
    )
```

profile of v0, /device:TPU:0, one launch (start us, length us, event | category | flops | bytes accessed | tf_op | source)
XLA Modules:
  0.0 410.7 jit_solution(17881469406884663636)
XLA Ops:
  1.9 3.0 collective-permute-start.1
  8.9 9.4 %collective-permute-done.1.refs_2_ = bf16[288,1024]{1,0:T(8,128)(2,1)S(1)} collective-permute-done((bf16[288,1024]{1,0:T(8,128)(2,1)S(1)}, bf16[288,1024]{1,0:T(8,128)(2,1)S(1)}, u32[]{:S(2)}, u32[]{:S(2)}) %collective-permute-start.1) | collective-permute-done | bytes 589856 | tf_op jit(solution)/shard_map/ppermute | solution.py:47
  22.1 1.6 collective-permute-start.3
  26.1 5.0 %all-to-all-start = ((bf16[8,112,128]{2,1,0:T(8,128)(2,1)}), bf16[8,112,128]{2,1,0:T(8,128)(2,1)S(1)}, u32[]{:S(2)}, u32[]{:S(2)}) async-start(bf16[8,112,128]{2,1,0:T(8,128)(2,1)} %copy.280), calls=%async_computation | async-start | bytes 458752 | tf_op jit(solution)/shard_map/all_to_all | solution.py:56
  31.3 12.6 %all-to-all-done = bf16[8,112,128]{2,1,0:T(8,128)(2,1)S(1)} async-done(((bf16[8,112,128]{2,1,0:T(8,128)(2,1)}), bf16[8,112,128]{2,1,0:T(8,128)(2,1)S(1)}, u32[]{:S(2)}, u32[]{:S(2)}) %all-to-all-start) | async-done | bytes 229408 | tf_op jit(solution)/shard_map/all_to_all | solution.py:56
  46.2 3.7 fusion.45
  49.9 1.9 pad_maximum_fusion
  52.7 1.9 collective-permute-start.6
  60.6 7.6 %collective-permute-done.5.refs_0_ = bf16[288,1024]{1,0:T(8,128)(2,1)S(1)} collective-permute-done((bf16[288,1024]{1,0:T(8,128)(2,1)}, bf16[288,1024]{1,0:T(8,128)(2,1)S(1)}, u32[]{:S(2)}, u32[]{:S(2)}) %collective-permute-start.5) | collective-permute-done | bytes 589856 | tf_op jit(solution)/shard_map/ppermute | solution.py:47
  70.1 1.7 collective-permute-start.8
  73.7 8.2 %qkv5.1 = (bf16[8,256,128]{2,1,0:T(8,128)(2,1)}, bf16[2,8,256,128]{3,2,1,0:T(8,128)(2,1)}, bf16[8,256,1024]{2,1,0:T(8,128)(2,1)}) custom-call(s32[5]{0:T(128)} %compare_select_fusion.8.tab, bf16[288,1024]{1,0:T(8,128)(2,1)} %copy-done.4, bf16[288,1024]{1,0:T(8,128)(2,1)} %copy-done.16, bf16[288,1024]{1,0:T(8,128)(2,1)} %copy-done.15, ...), custom_call_target="tpu_custom_call" | custom-call | flops 1006632960 | bytes 6553600 | tf_op jit(solution)/shard_map/qkv5/pallas_call | solution.py:126
  81.9 6.0 %qkv3.1 = (bf16[8,256,128]{2,1,0:T(8,128)(2,1)}, bf16[2,8,256,128]{3,2,1,0:T(8,128)(2,1)}, bf16[8,256,1024]{2,1,0:T(8,128)(2,1)}) custom-call(s32[3]{0:T(128)} %compare_select_fusion.9.tab, bf16[288,1024]{1,0:T(8,128)(2,1)} %copy-done.10, bf16[288,1024]{1,0:T(8,128)(2,1)} %copy-done.7, ...), custom_call_target="tpu_custom_call", output_to_operand_aliasing={{0}: (9, {}), {1}: (10, {}), {2}: (11, {})} | custom-call | flops 603979776 | bytes 3932160 | tf_op jit(solution)/shard_map/qkv3/pallas_call | solution.py:126
  89.9 11.8 %collective-permute-start.21 = (bf16[216,1536]{1,0:T(8,128)(2,1)S(1)}, bf16[216,1536]{1,0:T(8,128)(2,1)S(1)}, u32[]{:S(2)}, u32[]{:S(2)}) collective-permute-start(bf16[216,1536]{1,0:T(8,128)(2,1)S(1)} %fusion.34.refs_0_), channel_id=1, source_target_pairs={{0,4},{4,8},{8,12},{12,14},{14,10},{10,6},{6,2},{2,0},{1,5},{5,9},... | collective-permute-start | bytes 1990664 | tf_op jit(solution)/shard_map/ppermute | solution.py:47
  107.2 18.4 %attend.1 = (f32[8,256,128]{2,1,0:T(8,128)}, bf16[8,256,128]{2,1,0:T(8,128)(2,1)}, f32[8,256,1]{2,1,0:T(8,128)}, bf16[2,8,256,128]{3,2,1,0:T(8,128)(2,1)}) custom-call(s32[42]{0:T(128)} %concatenate.79.tab, bf16[8,256,128]{2,1,0:T(8,128)(2,1)} %get-tuple-element.87.q_ref, bf16[2,8,256,128]{3,2,1,0:T(8,128)(2,1)} %get-tuple-element.88.own_ref, ...), custom_call_target="tpu_custom_call" | custom-call | flops 24999999488 | bytes 6291456 | tf_op jit(solution)/shard_map/attend/pallas_call | solution.py:231
  125.6 4.5 %all-to-all-start.1 = ((bf16[8,256,128]{2,1,0:T(8,128)(2,1)}), bf16[8,256,128]{2,1,0:T(8,128)(2,1)S(1)}, u32[]{:S(2)}, u32[]{:S(2)}) async-start(bf16[8,256,128]{2,1,0:T(8,128)(2,1)} %get-tuple-element.89), calls=%async_computation.1 | async-start | bytes 1048576 | tf_op jit(solution)/shard_map/all_to_all | solution.py:56
  130.0 2.1 collective-permute-start.22
  134.1 16.2 %collective-permute-done.22.refs_2_ = bf16[216,1536]{1,0:T(8,128)(2,1)} collective-permute-done((bf16[216,1536]{1,0:T(8,128)(2,1)S(1)}, bf16[216,1536]{1,0:T(8,128)(2,1)}, u32[]{:S(2)}, u32[]{:S(2)}) %collective-permute-start.22) | collective-permute-done | bytes 663584 | tf_op jit(solution)/shard_map/ppermute | solution.py:47
  150.3 4.2 %collective-permute-start.23 = (bf16[216,1536]{1,0:T(8,128)(2,1)}, bf16[216,1536]{1,0:T(8,128)(2,1)S(1)}, u32[]{:S(2)}, u32[]{:S(2)}) collective-permute-start(bf16[216,1536]{1,0:T(8,128)(2,1)} %collective-permute-done.22.refs_2_), channel_id=1, source_target_pairs={{0,4},{4,8},{8,12},{12,14},{14,10},{10,6},{6,2},{2,0},{1,5},{5,9},... | collective-permute-start | bytes 1990664 | tf_op jit(solution)/shard_map/ppermute | solution.py:47
  155.3 4.1 out_block.1
  159.4 3.5 collective-permute-start.30
  162.9 11.9 %collective-permute-done.30.na.refs_2_ = bf16[256,1024]{1,0:T(8,128)(2,1)} collective-permute-done((bf16[256,1024]{1,0:T(8,128)(2,1)}, bf16[256,1024]{1,0:T(8,128)(2,1)}, u32[]{:S(2)}, u32[]{:S(2)}) %collective-permute-start.30) | collective-permute-done | bytes 524320 | tf_op jit(solution)/shard_map/ppermute | solution.py:42
  174.9 2.6 collective-permute-start.24
  177.5 2.5 collective-permute-done.27.refs_6_
  180.2 7.0 %collective-permute-done.28.refs_5_ = bf16[88,1536]{1,0:T(8,128)(2,1)S(1)} collective-permute-done((bf16[88,1536]{1,0:T(8,128)(2,1)S(1)}, bf16[88,1536]{1,0:T(8,128)(2,1)S(1)}, u32[]{:S(2)}, u32[]{:S(2)}) %collective-permute-start.28) | collective-permute-done | bytes 270368 | tf_op jit(solution)/shard_map/ppermute | solution.py:47
  188.0 4.8 %weights.1 = (bf16[1024,704]{1,0:T(8,128)(2,1)}, bf16[1024,704]{1,0:T(8,128)(2,1)}, bf16[704,1024]{1,0:T(8,128)(2,1)}) custom-call(s32[10]{0:T(128)} %pad_add_fusion.tab, bf16[216,1536]{1,0:T(8,128)(2,1)} %copy-done.3, bf16[216,1536]{1,0:T(8,128)(2,1)} %copy-done.25, bf16[216,1536]{1,0:T(8,128)(2,1)} %collective-permute-done.22.refs_2_, ...), custom_call_target="tpu_custom_call" | custom-call | bytes 8650752 | tf_op jit(solution)/shard_map/weights/pallas_call | solution.py:398
  192.8 9.1 %ffn.3 = (bf16[2,256,704]{2,1,0:T(8,128)(2,1)}, bf16[2,256,704]{2,1,0:T(8,128)(2,1)}, bf16[2,256,704]{2,1,0:T(8,128)(2,1)}, bf16[2,256,1024]{2,1,0:T(8,128)(2,1)}) custom-call(bf16[256,1024]{1,0:T(8,128)(2,1)} %collective-permute-done.30.na.refs_2_, bf16[256,1024]{1,0:T(8,128)(2,1)} %collective-permute-done.31.nb.refs_3_, ...), custom_call_target="tpu_custom_call" | custom-call | flops 3690987520 | bytes 8519680 | tf_op jit(solution)/shard_map/ffn/pallas_call | solution.py:434
  203.0 9.1 %ffn.2 = (bf16[2,256,704]{2,1,0:T(8,128)(2,1)}, bf16[2,256,704]{2,1,0:T(8,128)(2,1)}, bf16[2,256,704]{2,1,0:T(8,128)(2,1)}, bf16[2,256,1024]{2,1,0:T(8,128)(2,1)}) custom-call(bf16[256,1024]{1,0:T(8,128)(2,1)} %get-tuple-element.93.na.refs_0_, bf16[256,1024]{1,0:T(8,128)(2,1)} %collective-permute-done.18.nb.refs_1_, ...), custom_call_target="tpu_custom_call" | custom-call | flops 3690987520 | bytes 8519680 | tf_op jit(solution)/shard_map/ffn/pallas_call | solution.py:434
  212.1 2.2 slice_bitcast_fusion.7
  216.3 11.4 %weight_grads.1 = bf16[8,216,1536]{2,1,0:T(8,128)(2,1)} custom-call(s32[8]{0:T(128)} %compare_select_fusion.tab, bf16[256,1024]{1,0:T(8,128)(2,1)} %get-tuple-element.93.na.refs_0_, bf16[256,1024]{1,0:T(8,128)(2,1)} %collective-permute-done.18.nb.refs_1_, bf16[256,1024]{1,0:T(8,128)(2,1)} %collective-permute-done.30.na.refs_2_, ...), custom_call_target="tpu_custom_call" | custom-call | flops 4429185024 | bytes 14680064 | tf_op jit(solution)/shard_map/weight_grads/pallas_call | solution.py:488
  229.9 4.6 %mid_block.1 = (f32[256,1024]{1,0:T(8,128)}, bf16[256,1024]{1,0:T(8,128)(2,1)}, bf16[8,256,128]{2,1,0:T(8,128)(2,1)}) custom-call(f32[256,1024]{1,0:T(8,128)} %get-tuple-element.92.mid_ref, bf16[256,1024]{1,0:T(8,128)(2,1)} %get-tuple-element.170.pa, bf16[256,1024]{1,0:T(8,128)(2,1)} %copy-done.26, bf16[256,1024]{1,0:T(8,128)(2,1)} %copy-done.27, ...), custom_call_target="tpu_custom_call" | custom-call | flops 536870912 | bytes 6291456 | tf_op jit(solution)/shard_map/mid_block/pallas_call | solution.py:540
  234.5 1.8 convolution_convert_fusion
  236.5 4.2 %all-to-all-start.2 = ((bf16[8,256,128]{2,1,0:T(8,128)(2,1)}), bf16[8,256,128]{2,1,0:T(8,128)(2,1)}, u32[]{:S(2)}, u32[]{:S(2)}) async-start(bf16[8,256,128]{2,1,0:T(8,128)(2,1)} %get-tuple-element.120), calls=%async_computation.2 | async-start | bytes 1048576 | tf_op jit(solution)/shard_map/all_to_all | solution.py:56
  240.7 1.8 convert_add_fusion
  245.1 2.1 collective-permute-start.37
  248.2 8.7 %collective-permute-done.35 = bf16[1,8,32,1024]{3,2,1,0:T(8,128)(2,1)S(1)} collective-permute-done((bf16[1,8,32,1024]{3,2,1,0:T(8,128)(2,1)S(1)}, bf16[1,8,32,1024]{3,2,1,0:T(8,128)(2,1)S(1)}, u32[]{:S(2)}, u32[]{:S(2)}) %collective-permute-start.35) | collective-permute-done | bytes 524320 | tf_op jit(solution)/shard_map/ppermute | solution.py:42
  258.1 1.9 out_strips.1
  260.0 1.8 slice_bitcast_fusion.21
  261.8 1.6 convert_add_fusion.6
  263.8 1.7 collective-permute-start.38
  265.9 27.1 %attend_back.1 = (f32[8,256,128]{2,1,0:T(8,128)}, f32[2,8,256,128]{3,2,1,0:T(8,128)}, bf16[2,8,256,128]{3,2,1,0:T(8,128)(2,1)}) custom-call(s32[42]{0:T(128)} %concatenate.79.tab, bf16[8,256,128]{2,1,0:T(8,128)(2,1)} %get-tuple-element.87.q_ref, bf16[8,256,128]{2,1,0:T(8,128)(2,1)} %all-to-all-done.2.up_ref, f32[8,256,128]{2,1,0:T(8,128)} %get-tuple-element.125.o_ref, ...), custom_call_target="tpu_custom_call" | custom-call | flops 30000001024 | bytes 10485760 | tf_op jit(solution)/shard_map/attend_back/pallas_call | solution.py:311
  294.0 2.0 fusion.10
  297.0 9.8 %qkv_back.1 = (bf16[8,256,1024]{2,1,0:T(8,128)(2,1)}, bf16[8,256,384]{2,1,0:T(8,128)(2,1)}) custom-call(s32[8]{0:T(128)} %copy-done.39, f32[8,256,128]{2,1,0:T(8,128)} %get-tuple-element.131.dq_ref, f32[2,8,256,128]{3,2,1,0:T(8,128)} %get-tuple-element.132.own_ref, bf16[2,8,256,128]{3,2,1,0:T(8,128)(2,1)} %copy-done.13, ...), custom_call_target="tpu_custom_call" | custom-call | flops 1610612736 | bytes 8388608 | tf_op jit(solution)/shard_map/qkv_back/pallas_call | solution.py:574
  308.0 1.6 collective-permute-start.42
  310.2 4.3 %collective-permute-start.58 = (bf16[64,512]{1,0:T(8,128)(2,1)}, bf16[64,512]{1,0:T(8,128)(2,1)}, u32[]{:S(2)}, u32[]{:S(2)}) collective-permute-start(bf16[64,512]{1,0:T(8,128)(2,1)} %get-tuple-element.175), channel_id=1, source_target_pairs={{0,14},{4,10},{8,6},{12,2},{14,0},{10,4},{6,8},{2,12},{1,15},{5,11... | collective-permute-start | bytes 196616 | tf_op jit(solution)/shard_map/ppermute | solution.py:47
  314.6 2.0 collective-permute-start.56
  316.8 2.1 collective-permute-done.41
  325.9 2.4 bitcast_convert_fusion
  330.2 4.3 %collective-permute-done.54 = bf16[216,1536]{1,0:T(8,128)(2,1)S(1)} collective-permute-done((bf16[216,1536]{1,0:T(8,128)(2,1)S(1)}, bf16[216,1536]{1,0:T(8,128)(2,1)S(1)}, u32[]{:S(2)}, u32[]{:S(2)}) %collective-permute-start.54) | collective-permute-done | bytes 663584 | tf_op jit(solution)/shard_map/ppermute | solution.py:47
  335.0 1.6 fusion.5
  339.9 5.8 %collective-permute-done.46 = bf16[256,1024]{1,0:T(8,128)(2,1)S(1)} collective-permute-done((bf16[256,1024]{1,0:T(8,128)(2,1)S(1)}, bf16[256,1024]{1,0:T(8,128)(2,1)S(1)}, u32[]{:S(2)}, u32[]{:S(2)}) %collective-permute-start.46) | collective-permute-done | bytes 524320 | tf_op jit(solution)/shard_map/ppermute | solution.py:47
  347.0 2.1 fusion.20
  349.1 2.3 collective-permute-done.53
  352.1 5.1 %all-to-all-start.3 = ((bf16[8,32,384]{2,1,0:T(8,128)(2,1)}), bf16[8,32,384]{2,1,0:T(8,128)(2,1)S(1)}, u32[]{:S(2)}, u32[]{:S(2)}) async-start(bf16[8,32,384]{2,1,0:T(8,128)(2,1)} %fusion.48), calls=%async_computation.3 | async-start | bytes 393216 | tf_op jit(solution)/shard_map/all_to_all | solution.py:56
  357.2 2.1 collective-permute-done.55
  360.6 2.7 collective-permute-start.47
  363.3 1.7 fusion.8
  371.9 2.9 collective-permute-done.47
  374.8 2.9 fusion.21
  378.6 1.9 collective-permute-start.50
  380.5 2.2 fusion.38
  384.7 7.4 %collective-permute-done.50 = bf16[256,1024]{1,0:T(8,128)(2,1)S(1)} collective-permute-done((bf16[256,1024]{1,0:T(8,128)(2,1)}, bf16[256,1024]{1,0:T(8,128)(2,1)S(1)}, u32[]{:S(2)}, u32[]{:S(2)}) %collective-permute-start.50) | collective-permute-done | bytes 524320 | tf_op jit(solution)/shard_map/ppermute | solution.py:47
  392.2 2.0 fusion.19
  398.2 8.4 %collective-permute-done.51 = bf16[256,1024]{1,0:T(8,128)(2,1)S(1)} collective-permute-done((bf16[256,1024]{1,0:T(8,128)(2,1)}, bf16[256,1024]{1,0:T(8,128)(2,1)S(1)}, u32[]{:S(2)}, u32[]{:S(2)}) %collective-permute-start.51) | collective-permute-done | bytes 524320 | tf_op jit(solution)/shard_map/ppermute | solution.py:47
  408.0 2.4 fusion.17
  (334 shorter events, 81.2 us)
Async XLA Ops:
  1.9 16.4 %collective-permute-start.1 = (bf16[288,1024]{1,0:T(8,128)(2,1)S(1)}, bf16[288,1024]{1,0:T(8,128)(2,1)S(1)}, u32[]{:S(2)}, u32[]{:S(2)}) collective-permute-start(bf16[288,1024]{1,0:T(8,128)(2,1)S(1)} %pad_maximum_fusion.5.refs_0_), channel_id=1, source_target_pairs={{0,2},{4,0},{8,4},{12,8},{14,12},{10,14},{6,10},{2,6},{1,3},{5,1},... | collective-permute-start | bytes 1769480 | tf_op jit(solution)/shard_map/ppermute | solution.py:47
  4.9 14.8 %collective-permute-start = (bf16[288,1024]{1,0:T(8,128)(2,1)S(1)}, bf16[288,1024]{1,0:T(8,128)(2,1)S(1)}, u32[]{:S(2)}, u32[]{:S(2)}) collective-permute-start(bf16[288,1024]{1,0:T(8,128)(2,1)S(1)} %pad_maximum_fusion.5.refs_0_), channel_id=1, source_target_pairs={{0,4},{4,8},{8,12},{12,14},{14,10},{10,6},{6,2},{2,0},{1,5},{5,9},... | collective-permute-start | bytes 1769480 | tf_op jit(solution)/shard_map/ppermute | solution.py:47
  21.5 2.2 collective-permute-start.19
  21.6 22.2 %collective-permute-start.2 = (bf16[288,1024]{1,0:T(8,128)(2,1)S(1)}, bf16[288,1024]{1,0:T(8,128)(2,1)}, u32[]{:S(2)}, u32[]{:S(2)}) collective-permute-start(bf16[288,1024]{1,0:T(8,128)(2,1)S(1)} %collective-permute-done.refs_1_), channel_id=1, source_target_pairs={{0,4},{4,8},{8,12},{12,14},{14,10},{10,6},{6,2},{2,0},{1,5},{5,9},... | collective-permute-start | bytes 1769480 | tf_op jit(solution)/shard_map/ppermute | solution.py:47
  22.1 21.7 %collective-permute-start.3 = (bf16[288,1024]{1,0:T(8,128)(2,1)S(1)}, bf16[288,1024]{1,0:T(8,128)(2,1)}, u32[]{:S(2)}, u32[]{:S(2)}) collective-permute-start(bf16[288,1024]{1,0:T(8,128)(2,1)S(1)} %collective-permute-done.1.refs_2_), channel_id=1, source_target_pairs={{0,2},{4,0},{8,4},{12,8},{14,12},{10,14},{6,10},{2,6},{1,3},{5,1},... | collective-permute-start | bytes 1769480 | tf_op jit(solution)/shard_map/ppermute | solution.py:47
  23.8 7.3 %collective-permute-start.20 = (bf16[2,32,1536]{2,1,0:T(8,128)(2,1)S(1)}, bf16[2,32,1536]{2,1,0:T(8,128)(2,1)S(1)}, u32[]{:S(2)}, u32[]{:S(2)}) collective-permute-start(bf16[2,32,1536]{2,1,0:T(8,128)(2,1)S(1)} %get-tuple-element.188), channel_id=1, source_target_pairs={{0,16},{16,0},{1,17},{17,1},{2,18},{18,2},{3,19},{19,3},{4,20},{20... | collective-permute-start | bytes 589832 | tf_op jit(solution)/shard_map/ppermute | solution.py:42
  26.1 17.7 %all-to-all-start = ((bf16[8,112,128]{2,1,0:T(8,128)(2,1)}), bf16[8,112,128]{2,1,0:T(8,128)(2,1)S(1)}, u32[]{:S(2)}, u32[]{:S(2)}) async-start(bf16[8,112,128]{2,1,0:T(8,128)(2,1)} %copy.280), calls=%async_computation | async-start | bytes 458752 | tf_op jit(solution)/shard_map/all_to_all | solution.py:56
  44.3 14.1 %collective-permute-start.4 = (bf16[8,112,128]{2,0,1:T(8,128)(2,1)S(1)}, bf16[8,112,128]{2,0,1:T(8,128)(2,1)S(1)}, u32[]{:S(2)}, u32[]{:S(2)}) collective-permute-start(bf16[8,112,128]{2,0,1:T(8,128)(2,1)S(1)} %copy.351), channel_id=1, source_target_pairs={{0,1},{1,0},{2,3},{3,2},{4,5},{5,4},{6,7},{7,6},{8,9},{9,8},{10,11... | collective-permute-start | bytes 688136 | tf_op jit(solution)/shard_map/ppermute | solution.py:42
  44.3 14.3 %collective-permute-start.9 = (bf16[8,112,128]{2,0,1:T(8,128)(2,1)S(1)}, bf16[8,112,128]{2,0,1:T(8,128)(2,1)S(1)}, u32[]{:S(2)}, u32[]{:S(2)}) collective-permute-start(bf16[8,112,128]{2,0,1:T(8,128)(2,1)S(1)} %copy.351), channel_id=1, source_target_pairs={{0,16},{16,0},{1,17},{17,1},{2,18},{18,2},{3,19},{19,3},{4,20},{20... | collective-permute-start | bytes 688136 | tf_op jit(solution)/shard_map/ppermute | solution.py:42
  52.6 15.6 %collective-permute-start.5 = (bf16[288,1024]{1,0:T(8,128)(2,1)}, bf16[288,1024]{1,0:T(8,128)(2,1)S(1)}, u32[]{:S(2)}, u32[]{:S(2)}) collective-permute-start(bf16[288,1024]{1,0:T(8,128)(2,1)} %collective-permute-done.2.refs_3_), channel_id=1, source_target_pairs={{0,4},{4,8},{8,12},{12,14},{14,10},{10,6},{6,2},{2,0},{1,5},{5,9},... | collective-permute-start | bytes 1769480 | tf_op jit(solution)/shard_map/ppermute | solution.py:47
  52.7 16.6 %collective-permute-start.6 = (bf16[288,1024]{1,0:T(8,128)(2,1)}, bf16[288,1024]{1,0:T(8,128)(2,1)S(1)}, u32[]{:S(2)}, u32[]{:S(2)}) collective-permute-start(bf16[288,1024]{1,0:T(8,128)(2,1)} %collective-permute-done.3.refs_4_), channel_id=1, source_target_pairs={{0,2},{4,0},{8,4},{12,8},{14,12},{10,14},{6,10},{2,6},{1,3},{5,1},... | collective-permute-start | bytes 1769480 | tf_op jit(solution)/shard_map/ppermute | solution.py:47
  58.6 1.6 collective-permute-start.10
  69.0 12.9 %collective-permute-start.7 = (bf16[128,1024]{1,0:T(8,128)(2,1)}, bf16[128,1024]{1,0:T(8,128)(2,1)}, u32[]{:S(2)}, u32[]{:S(2)}) collective-permute-start(bf16[128,1024]{1,0:T(8,128)(2,1)} %slice.412), channel_id=1, source_target_pairs={{0,4},{4,8},{8,12},{12,14},{14,10},{10,6},{6,2},{2,0},{1,5},{5,9},... | collective-permute-start | bytes 786440 | tf_op jit(solution)/shard_map/ppermute | solution.py:47
  70.1 11.8 %collective-permute-start.8 = (bf16[160,1024]{1,0:T(8,128)(2,1)}, bf16[160,1024]{1,0:T(8,128)(2,1)}, u32[]{:S(2)}, u32[]{:S(2)}) collective-permute-start(bf16[160,1024]{1,0:T(8,128)(2,1)} %slice.413), channel_id=1, source_target_pairs={{0,2},{4,0},{8,4},{12,8},{14,12},{10,14},{6,10},{2,6},{1,3},{5,1},... | collective-permute-start | bytes 983048 | tf_op jit(solution)/shard_map/ppermute | solution.py:47
  88.0 17.7 %collective-permute-start.11 = (bf16[2,8,256,128]{3,2,1,0:T(8,128)(2,1)}, bf16[2,8,256,128]{3,2,1,0:T(8,128)(2,1)}, u32[]{:S(2)}, u32[]{:S(2)}) collective-permute-start(bf16[2,8,256,128]{3,2,1,0:T(8,128)(2,1)} %get-tuple-element.88.own_ref), channel_id=1, source_target_pairs={{0,1},{1,0},{2,3},{3,2},{4,5},{5,4},{6,7},{7,6},{8,9},{9,8},{10,11... | collective-permute-start | bytes 3145736 | tf_op jit(solution)/shard_map/ppermute | solution.py:42
  88.8 43.9 %collective-permute-start.25 = (bf16[216,1536]{1,0:T(8,128)(2,1)S(1)}, bf16[216,1536]{1,0:T(8,128)(2,1)S(1)}, u32[]{:S(2)}, u32[]{:S(2)}) collective-permute-start(bf16[216,1536]{1,0:T(8,128)(2,1)S(1)} %fusion.34.refs_0_), channel_id=1, source_target_pairs={{0,2},{4,0},{8,4},{12,8},{14,12},{10,14},{6,10},{2,6},{1,3},{5,1},... | collective-permute-start | bytes 1990664 | tf_op jit(solution)/shard_map/ppermute | solution.py:47
  89.9 40.1 %collective-permute-start.21 = (bf16[216,1536]{1,0:T(8,128)(2,1)S(1)}, bf16[216,1536]{1,0:T(8,128)(2,1)S(1)}, u32[]{:S(2)}, u32[]{:S(2)}) collective-permute-start(bf16[216,1536]{1,0:T(8,128)(2,1)S(1)} %fusion.34.refs_0_), channel_id=1, source_target_pairs={{0,4},{4,8},{8,12},{12,14},{14,10},{10,6},{6,2},{2,0},{1,5},{5,9},... | collective-permute-start | bytes 1990664 | tf_op jit(solution)/shard_map/ppermute | solution.py:47
  101.7 30.4 %collective-permute-start.13 = (bf16[256,1024]{1,0:T(8,128)(2,1)}, bf16[256,1024]{1,0:T(8,128)(2,1)}, u32[]{:S(2)}, u32[]{:S(2)}) collective-permute-start(bf16[256,1024]{1,0:T(8,128)(2,1)} %bitcast.31.ga.refs_4_.up_ref), channel_id=1, source_target_pairs={{0,16},{16,0},{1,17},{17,1},{2,18},{18,2},{3,19},{19,3},{4,20},{20... | collective-permute-start | bytes 1572872 | tf_op jit(solution)/shard_map/ppermute | solution.py:42
  102.2 30.4 %collective-permute-start.12 = (bf16[256,1024]{1,0:T(8,128)(2,1)}, bf16[256,1024]{1,0:T(8,128)(2,1)}, u32[]{:S(2)}, u32[]{:S(2)}) collective-permute-start(bf16[256,1024]{1,0:T(8,128)(2,1)} %bitcast.31.ga.refs_4_.up_ref), channel_id=1, source_target_pairs={{0,1},{1,0},{2,3},{3,2},{4,5},{5,4},{6,7},{7,6},{8,9},{9,8},{10,11... | collective-permute-start | bytes 1572872 | tf_op jit(solution)/shard_map/ppermute | solution.py:42
  105.6 26.5 %collective-permute-start.16 = (bf16[8,32,1024]{2,1,0:T(8,128)(2,1)S(1)}, bf16[8,32,1024]{2,1,0:T(8,128)(2,1)}, u32[]{:S(2)}, u32[]{:S(2)}) collective-permute-start(bf16[8,32,1024]{2,1,0:T(8,128)(2,1)S(1)} %bitcast_dynamic-update-slice_fusion.refs_0_), channel_id=1, source_target_pairs={{0,16},{16,0},{1,17},{17,1},{2,18},{18,2},{3,19},{19,3},{4,20},{20... | collective-permute-start | bytes 1572872 | tf_op jit(solution)/shard_map/ppermute | solution.py:42
  125.6 29.0 %all-to-all-start.1 = ((bf16[8,256,128]{2,1,0:T(8,128)(2,1)}), bf16[8,256,128]{2,1,0:T(8,128)(2,1)S(1)}, u32[]{:S(2)}, u32[]{:S(2)}) async-start(bf16[8,256,128]{2,1,0:T(8,128)(2,1)} %get-tuple-element.89), calls=%async_computation.1 | async-start | bytes 1048576 | tf_op jit(solution)/shard_map/all_to_all | solution.py:56
  130.0 20.3 %collective-permute-start.22 = (bf16[216,1536]{1,0:T(8,128)(2,1)S(1)}, bf16[216,1536]{1,0:T(8,128)(2,1)}, u32[]{:S(2)}, u32[]{:S(2)}) collective-permute-start(bf16[216,1536]{1,0:T(8,128)(2,1)S(1)} %collective-permute-done.21.refs_1_), channel_id=1, source_target_pairs={{0,4},{4,8},{8,12},{12,14},{14,10},{10,6},{6,2},{2,0},{1,5},{5,9},... | collective-permute-start | bytes 1990664 | tf_op jit(solution)/shard_map/ppermute | solution.py:47
  132.1 22.4 %collective-permute-start.14 = (bf16[256,1024]{1,0:T(8,128)(2,1)}, bf16[256,1024]{1,0:T(8,128)(2,1)}, u32[]{:S(2)}, u32[]{:S(2)}) collective-permute-start(bf16[256,1024]{1,0:T(8,128)(2,1)} %collective-permute-done.13.ga.refs_6_), channel_id=1, source_target_pairs={{0,1},{1,0},{2,3},{3,2},{4,5},{5,4},{6,7},{7,6},{8,9},{9,8},{10,11... | collective-permute-start | bytes 1572872 | tf_op jit(solution)/shard_map/ppermute | solution.py:42
  132.1 22.4 %collective-permute-start.15 = (bf16[8,32,1024]{2,1,0:T(8,128)(2,1)S(1)}, bf16[8,32,1024]{2,1,0:T(8,128)(2,1)}, u32[]{:S(2)}, u32[]{:S(2)}) collective-permute-start(bf16[8,32,1024]{2,1,0:T(8,128)(2,1)S(1)} %bitcast_dynamic-update-slice_fusion.refs_0_), channel_id=1, source_target_pairs={{0,1},{1,0},{2,3},{3,2},{4,5},{5,4},{6,7},{7,6},{8,9},{9,8},{10,11... | collective-permute-start | bytes 1572872 | tf_op jit(solution)/shard_map/ppermute | solution.py:42
  132.6 21.9 %collective-permute-start.17 = (bf16[8,32,1024]{2,1,0:T(8,128)(2,1)}, bf16[8,32,1024]{2,1,0:T(8,128)(2,1)}, u32[]{:S(2)}, u32[]{:S(2)}) collective-permute-start(bf16[8,32,1024]{2,1,0:T(8,128)(2,1)} %collective-permute-done.16.refs_2_), channel_id=1, source_target_pairs={{0,1},{1,0},{2,3},{3,2},{4,5},{5,4},{6,7},{7,6},{8,9},{9,8},{10,11... | collective-permute-start | bytes 1572872 | tf_op jit(solution)/shard_map/ppermute | solution.py:42
  132.7 30.2 %collective-permute-start.26 = (bf16[216,1536]{1,0:T(8,128)(2,1)S(1)}, bf16[216,1536]{1,0:T(8,128)(2,1)}, u32[]{:S(2)}, u32[]{:S(2)}) collective-permute-start(bf16[216,1536]{1,0:T(8,128)(2,1)S(1)} %collective-permute-done.25.refs_8_), channel_id=1, source_target_pairs={{0,2},{4,0},{8,4},{12,8},{14,12},{10,14},{6,10},{2,6},{1,3},{5,1},... | collective-permute-start | bytes 1990664 | tf_op jit(solution)/shard_map/ppermute | solution.py:47
  150.3 24.6 %collective-permute-start.23 = (bf16[216,1536]{1,0:T(8,128)(2,1)}, bf16[216,1536]{1,0:T(8,128)(2,1)S(1)}, u32[]{:S(2)}, u32[]{:S(2)}) collective-permute-start(bf16[216,1536]{1,0:T(8,128)(2,1)} %collective-permute-done.22.refs_2_), channel_id=1, source_target_pairs={{0,4},{4,8},{8,12},{12,14},{14,10},{10,6},{6,2},{2,0},{1,5},{5,9},... | collective-permute-start | bytes 1990664 | tf_op jit(solution)/shard_map/ppermute | solution.py:47
  159.4 15.4 %collective-permute-start.30 = (bf16[256,1024]{1,0:T(8,128)(2,1)}, bf16[256,1024]{1,0:T(8,128)(2,1)}, u32[]{:S(2)}, u32[]{:S(2)}) collective-permute-start(bf16[256,1024]{1,0:T(8,128)(2,1)} %get-tuple-element.93.na.refs_0_), channel_id=1, source_target_pairs={{0,16},{16,0},{1,17},{17,1},{2,18},{18,2},{3,19},{19,3},{4,20},{20... | collective-permute-start | bytes 1572872 | tf_op jit(solution)/shard_map/ppermute | solution.py:42
  162.9 17.1 %collective-permute-start.27 = (bf16[216,1536]{1,0:T(8,128)(2,1)}, bf16[216,1536]{1,0:T(8,128)(2,1)S(1)}, u32[]{:S(2)}, u32[]{:S(2)}) collective-permute-start(bf16[216,1536]{1,0:T(8,128)(2,1)} %collective-permute-done.26.refs_7_), channel_id=1, source_target_pairs={{0,2},{4,0},{8,4},{12,8},{14,12},{10,14},{6,10},{2,6},{1,3},{5,1},... | collective-permute-start | bytes 1990664 | tf_op jit(solution)/shard_map/ppermute | solution.py:47
  174.8 17.9 %collective-permute-start.31 = (bf16[256,1024]{1,0:T(8,128)(2,1)}, bf16[256,1024]{1,0:T(8,128)(2,1)}, u32[]{:S(2)}, u32[]{:S(2)}) collective-permute-start(bf16[256,1024]{1,0:T(8,128)(2,1)} %collective-permute-done.30.na.refs_2_), channel_id=1, source_target_pairs={{0,1},{1,0},{2,3},{3,2},{4,5},{5,4},{6,7},{7,6},{8,9},{9,8},{10,11... | collective-permute-start | bytes 1572872 | tf_op jit(solution)/shard_map/ppermute | solution.py:42
  174.9 12.4 %collective-permute-start.24 = (bf16[128,1536]{1,0:T(8,128)(2,1)S(1)}, bf16[128,1536]{1,0:T(8,128)(2,1)}, u32[]{:S(2)}, u32[]{:S(2)}) collective-permute-start(bf16[128,1536]{1,0:T(8,128)(2,1)S(1)} %slice.429), channel_id=1, source_target_pairs={{0,4},{4,8},{8,12},{12,14},{14,10},{10,6},{6,2},{2,0},{1,5},{5,9},... | collective-permute-start | bytes 1179656 | tf_op jit(solution)/shard_map/ppermute | solution.py:47
  180.1 7.2 %collective-permute-start.28 = (bf16[88,1536]{1,0:T(8,128)(2,1)S(1)}, bf16[88,1536]{1,0:T(8,128)(2,1)S(1)}, u32[]{:S(2)}, u32[]{:S(2)}) collective-permute-start(bf16[88,1536]{1,0:T(8,128)(2,1)S(1)} %slice.430), channel_id=1, source_target_pairs={{0,2},{4,0},{8,4},{12,8},{14,12},{10,14},{6,10},{2,6},{1,3},{5,1},... | collective-permute-start | bytes 811016 | tf_op jit(solution)/shard_map/ppermute | solution.py:47
  180.2 22.8 %collective-permute-start.18 = (bf16[256,1024]{1,0:T(8,128)(2,1)}, bf16[256,1024]{1,0:T(8,128)(2,1)}, u32[]{:S(2)}, u32[]{:S(2)}) collective-permute-start(bf16[256,1024]{1,0:T(8,128)(2,1)} %get-tuple-element.93.na.refs_0_), channel_id=1, source_target_pairs={{0,1},{1,0},{2,3},{3,2},{4,5},{5,4},{6,7},{7,6},{8,9},{9,8},{10,11... | collective-permute-start | bytes 1572872 | tf_op jit(solution)/shard_map/ppermute | solution.py:42
  202.9 11.9 %collective-permute-start.32 = (bf16[256,1024]{1,0:T(8,128)(2,1)S(1)}, bf16[256,1024]{1,0:T(8,128)(2,1)S(1)}, u32[]{:S(2)}, u32[]{:S(2)}) collective-permute-start(bf16[256,1024]{1,0:T(8,128)(2,1)S(1)} %slice_bitcast_fusion.6), channel_id=1, source_target_pairs={{0,1},{1,0},{2,3},{3,2},{4,5},{5,4},{6,7},{7,6},{8,9},{9,8},{10,11... | collective-permute-start | bytes 1572872 | tf_op jit(solution)/shard_map/ppermute | solution.py:42
  214.3 14.6 %collective-permute-start.29 = (bf16[256,1024]{1,0:T(8,128)(2,1)S(1)}, bf16[256,1024]{1,0:T(8,128)(2,1)S(1)}, u32[]{:S(2)}, u32[]{:S(2)}) collective-permute-start(bf16[256,1024]{1,0:T(8,128)(2,1)S(1)} %get-tuple-element.169), channel_id=1, source_target_pairs={{0,1},{1,0},{2,3},{3,2},{4,5},{5,4},{6,7},{7,6},{8,9},{9,8},{10,11... | collective-permute-start | bytes 1572872 | tf_op jit(solution)/shard_map/ppermute | solution.py:42
  215.0 13.9 %collective-permute-start.33 = (bf16[256,1024]{1,0:T(8,128)(2,1)S(1)}, bf16[256,1024]{1,0:T(8,128)(2,1)S(1)}, u32[]{:S(2)}, u32[]{:S(2)}) collective-permute-start(bf16[256,1024]{1,0:T(8,128)(2,1)S(1)} %fusion.28), channel_id=1, source_target_pairs={{0,16},{16,0},{1,17},{17,1},{2,18},{18,2},{3,19},{19,3},{4,20},{20... | collective-permute-start | bytes 1572872 | tf_op jit(solution)/shard_map/ppermute | solution.py:42
  236.4 4.3 %collective-permute-start.34 = (bf16[1,2,8,32,1024]{4,3,2,1,0:T(8,128)(2,1)S(1)}, bf16[1,2,8,32,1024]{4,3,2,1,0:T(8,128)(2,1)}, u32[]{:S(2)}, u32[]{:S(2)}) collective-permute-start(bf16[1,2,8,32,1024]{4,3,2,1,0:T(8,128)(2,1)S(1)} %select_bitcast_fusion), channel_id=1, source_target_pairs={{0,1},{1,0},{2,3},{3,2},{4,5},{5,4},{6,7},{7,6},{8,9},{9,8},{10,11... | collective-permute-start | bytes 3145736 | tf_op jit(solution)/shard_map/ppermute | solution.py:42
  236.5 27.3 %all-to-all-start.2 = ((bf16[8,256,128]{2,1,0:T(8,128)(2,1)}), bf16[8,256,128]{2,1,0:T(8,128)(2,1)}, u32[]{:S(2)}, u32[]{:S(2)}) async-start(bf16[8,256,128]{2,1,0:T(8,128)(2,1)} %get-tuple-element.120), calls=%async_computation.2 | async-start | bytes 1048576 | tf_op jit(solution)/shard_map/all_to_all | solution.py:56
  242.6 14.4 %collective-permute-start.35 = (bf16[1,8,32,1024]{3,2,1,0:T(8,128)(2,1)S(1)}, bf16[1,8,32,1024]{3,2,1,0:T(8,128)(2,1)S(1)}, u32[]{:S(2)}, u32[]{:S(2)}) collective-permute-start(bf16[1,8,32,1024]{3,2,1,0:T(8,128)(2,1)S(1)} %fusion.36), channel_id=1, source_target_pairs={{0,16},{16,0},{1,17},{17,1},{2,18},{18,2},{3,19},{19,3},{4,20},{20... | collective-permute-start | bytes 1572872 | tf_op jit(solution)/shard_map/ppermute | solution.py:42
  245.1 18.3 %collective-permute-start.37 = (bf16[88,1536]{1,0:T(8,128)(2,1)S(1)}, bf16[88,1536]{1,0:T(8,128)(2,1)S(1)}, u32[]{:S(2)}, u32[]{:S(2)}) collective-permute-start(bf16[88,1536]{1,0:T(8,128)(2,1)S(1)} %slice_bitcast_fusion.10), channel_id=1, source_target_pairs={{0,2},{4,0},{8,4},{12,8},{14,12},{10,14},{6,10},{2,6},{1,3},{5,1},... | collective-permute-start | bytes 811016 | tf_op jit(solution)/shard_map/ppermute | solution.py:47
  248.2 15.4 %collective-permute-start.36 = (bf16[128,1536]{1,0:T(8,128)(2,1)S(1)}, bf16[128,1536]{1,0:T(8,128)(2,1)S(1)}, u32[]{:S(2)}, u32[]{:S(2)}) collective-permute-start(bf16[128,1536]{1,0:T(8,128)(2,1)S(1)} %slice_bitcast_fusion.9), channel_id=1, source_target_pairs={{0,4},{4,8},{8,12},{12,14},{14,10},{10,6},{6,2},{2,0},{1,5},{5,9},... | collective-permute-start | bytes 1179656 | tf_op jit(solution)/shard_map/ppermute | solution.py:47
  263.8 29.3 %collective-permute-start.38 = (bf16[216,1536]{1,0:T(8,128)(2,1)S(1)}, bf16[216,1536]{1,0:T(8,128)(2,1)}, u32[]{:S(2)}, u32[]{:S(2)}) collective-permute-start(bf16[216,1536]{1,0:T(8,128)(2,1)S(1)} %pad_maximum_fusion.3), channel_id=1, source_target_pairs={{0,4},{4,8},{8,12},{12,14},{14,10},{10,6},{6,2},{2,0},{1,5},{5,9},... | collective-permute-start | bytes 1990664 | tf_op jit(solution)/shard_map/ppermute | solution.py:47
  265.4 27.6 %collective-permute-start.39 = (bf16[216,1536]{1,0:T(8,128)(2,1)S(1)}, bf16[216,1536]{1,0:T(8,128)(2,1)S(1)}, u32[]{:S(2)}, u32[]{:S(2)}) collective-permute-start(bf16[216,1536]{1,0:T(8,128)(2,1)S(1)} %pad_maximum_fusion.4), channel_id=1, source_target_pairs={{0,2},{4,0},{8,4},{12,8},{14,12},{10,14},{6,10},{2,6},{1,3},{5,1},... | collective-permute-start | bytes 1990664 | tf_op jit(solution)/shard_map/ppermute | solution.py:47
  293.0 3.0 collective-permute-start.40
  308.0 8.7 %collective-permute-start.42 = (bf16[128,1024]{1,0:T(8,128)(2,1)S(1)}, bf16[128,1024]{1,0:T(8,128)(2,1)S(1)}, u32[]{:S(2)}, u32[]{:S(2)}) collective-permute-start(bf16[128,1024]{1,0:T(8,128)(2,1)S(1)} %get-tuple-element.162), channel_id=1, source_target_pairs={{0,2},{4,0},{8,4},{12,8},{14,12},{10,14},{6,10},{2,6},{1,3},{5,1},... | collective-permute-start | bytes 786440 | tf_op jit(solution)/shard_map/ppermute | solution.py:47
  309.7 9.2 %collective-permute-start.41 = (bf16[128,1024]{1,0:T(8,128)(2,1)S(1)}, bf16[128,1024]{1,0:T(8,128)(2,1)S(1)}, u32[]{:S(2)}, u32[]{:S(2)}) collective-permute-start(bf16[128,1024]{1,0:T(8,128)(2,1)S(1)} %get-tuple-element.164), channel_id=1, source_target_pairs={{0,4},{4,8},{8,12},{12,14},{14,10},{10,6},{6,2},{2,0},{1,5},{5,9},... | collective-permute-start | bytes 786440 | tf_op jit(solution)/shard_map/ppermute | solution.py:47
  310.2 54.9 %collective-permute-start.58 = (bf16[64,512]{1,0:T(8,128)(2,1)}, bf16[64,512]{1,0:T(8,128)(2,1)}, u32[]{:S(2)}, u32[]{:S(2)}) collective-permute-start(bf16[64,512]{1,0:T(8,128)(2,1)} %get-tuple-element.175), channel_id=1, source_target_pairs={{0,14},{4,10},{8,6},{12,2},{14,0},{10,4},{6,8},{2,12},{1,15},{5,11... | collective-permute-start | bytes 196616 | tf_op jit(solution)/shard_map/ppermute | solution.py:47
  314.6 19.9 %collective-permute-start.54 = (bf16[216,1536]{1,0:T(8,128)(2,1)S(1)}, bf16[216,1536]{1,0:T(8,128)(2,1)S(1)}, u32[]{:S(2)}, u32[]{:S(2)}) collective-permute-start(bf16[216,1536]{1,0:T(8,128)(2,1)S(1)} %get-tuple-element.141), channel_id=1, source_target_pairs={{0,4},{4,8},{8,12},{12,14},{14,10},{10,6},{6,2},{2,0},{1,5},{5,9},... | collective-permute-start | bytes 1990664 | tf_op jit(solution)/shard_map/ppermute | solution.py:47
  314.6 19.9 %collective-permute-start.56 = (bf16[216,1536]{1,0:T(8,128)(2,1)S(1)}, bf16[216,1536]{1,0:T(8,128)(2,1)S(1)}, u32[]{:S(2)}, u32[]{:S(2)}) collective-permute-start(bf16[216,1536]{1,0:T(8,128)(2,1)S(1)} %get-tuple-element.142), channel_id=1, source_target_pairs={{0,2},{4,0},{8,4},{12,8},{14,12},{10,14},{6,10},{2,6},{1,3},{5,1},... | collective-permute-start | bytes 1990664 | tf_op jit(solution)/shard_map/ppermute | solution.py:47
  320.2 25.5 %collective-permute-start.46 = (bf16[256,1024]{1,0:T(8,128)(2,1)S(1)}, bf16[256,1024]{1,0:T(8,128)(2,1)S(1)}, u32[]{:S(2)}, u32[]{:S(2)}) collective-permute-start(bf16[256,1024]{1,0:T(8,128)(2,1)S(1)} %pad_maximum_fusion.6), channel_id=1, source_target_pairs={{0,4},{4,8},{8,12},{12,14},{14,10},{10,6},{6,2},{2,0},{1,5},{5,9},... | collective-permute-start | bytes 1572872 | tf_op jit(solution)/shard_map/ppermute | solution.py:47
  321.7 50.2 %collective-permute-start.49 = (bf16[256,1024]{1,0:T(8,128)(2,1)}, bf16[256,1024]{1,0:T(8,128)(2,1)}, u32[]{:S(2)}, u32[]{:S(2)}) collective-permute-start(bf16[256,1024]{1,0:T(8,128)(2,1)} %pad_maximum_fusion.7), channel_id=1, source_target_pairs={{0,2},{4,0},{8,4},{12,8},{14,12},{10,14},{6,10},{2,6},{1,3},{5,1},... | collective-permute-start | bytes 1572872 | tf_op jit(solution)/shard_map/ppermute | solution.py:47
  334.5 2.1 collective-permute-start.52
  334.5 3.3 collective-permute-start.44
  336.6 22.6 %collective-permute-start.55 = (bf16[216,1536]{1,0:T(8,128)(2,1)S(1)}, bf16[216,1536]{1,0:T(8,128)(2,1)}, u32[]{:S(2)}, u32[]{:S(2)}) collective-permute-start(bf16[216,1536]{1,0:T(8,128)(2,1)S(1)} %get-tuple-element.153), channel_id=1, source_target_pairs={{0,4},{4,8},{8,12},{12,14},{14,10},{10,6},{6,2},{2,0},{1,5},{5,9},... | collective-permute-start | bytes 1990664 | tf_op jit(solution)/shard_map/ppermute | solution.py:47
  337.8 22.8 %collective-permute-start.57 = (bf16[216,1536]{1,0:T(8,128)(2,1)S(1)}, bf16[216,1536]{1,0:T(8,128)(2,1)}, u32[]{:S(2)}, u32[]{:S(2)}) collective-permute-start(bf16[216,1536]{1,0:T(8,128)(2,1)S(1)} %get-tuple-element.154), channel_id=1, source_target_pairs={{0,2},{4,0},{8,4},{12,8},{14,12},{10,14},{6,10},{2,6},{1,3},{5,1},... | collective-permute-start | bytes 1990664 | tf_op jit(solution)/shard_map/ppermute | solution.py:47
  345.7 5.7 %collective-permute-start.53 = (bf16[1,8,32,384]{3,2,1,0:T(8,128)(2,1)S(1)}, bf16[1,8,32,384]{3,2,1,0:T(8,128)(2,1)S(1)}, u32[]{:S(2)}, u32[]{:S(2)}) collective-permute-start(bf16[1,8,32,384]{3,2,1,0:T(8,128)(2,1)S(1)} %fusion.47), channel_id=1, source_target_pairs={{0,16},{16,0},{1,17},{17,1},{2,18},{18,2},{3,19},{19,3},{4,20},{20... | collective-permute-start | bytes 589832 | tf_op jit(solution)/shard_map/ppermute | solution.py:42
  351.4 29.1 %collective-permute-start.43 = (bf16[256,1024]{1,0:T(8,128)(2,1)}, bf16[256,1024]{1,0:T(8,128)(2,1)}, u32[]{:S(2)}, u32[]{:S(2)}) collective-permute-start(bf16[256,1024]{1,0:T(8,128)(2,1)} %slice_bitcast_fusion.4), channel_id=1, source_target_pairs={{0,1},{1,0},{2,3},{3,2},{4,5},{5,4},{6,7},{7,6},{8,9},{9,8},{10,11... | collective-permute-start | bytes 1572872 | tf_op jit(solution)/shard_map/ppermute | solution.py:42
  352.1 16.7 %all-to-all-start.3 = ((bf16[8,32,384]{2,1,0:T(8,128)(2,1)}), bf16[8,32,384]{2,1,0:T(8,128)(2,1)S(1)}, u32[]{:S(2)}, u32[]{:S(2)}) async-start(bf16[8,32,384]{2,1,0:T(8,128)(2,1)} %fusion.48), calls=%async_computation.3 | async-start | bytes 393216 | tf_op jit(solution)/shard_map/all_to_all | solution.py:56
  359.3 21.2 %collective-permute-start.45 = (bf16[256,1024]{1,0:T(8,128)(2,1)}, bf16[256,1024]{1,0:T(8,128)(2,1)S(1)}, u32[]{:S(2)}, u32[]{:S(2)}) collective-permute-start(bf16[256,1024]{1,0:T(8,128)(2,1)} %fusion.24), channel_id=1, source_target_pairs={{0,16},{16,0},{1,17},{17,1},{2,18},{18,2},{3,19},{19,3},{4,20},{20... | collective-permute-start | bytes 1572872 | tf_op jit(solution)/shard_map/ppermute | solution.py:42
  360.6 14.2 %collective-permute-start.47 = (bf16[256,1024]{1,0:T(8,128)(2,1)}, bf16[256,1024]{1,0:T(8,128)(2,1)}, u32[]{:S(2)}, u32[]{:S(2)}) collective-permute-start(bf16[256,1024]{1,0:T(8,128)(2,1)} %fusion.20), channel_id=1, source_target_pairs={{0,4},{4,8},{8,12},{12,14},{14,10},{10,6},{6,2},{2,0},{1,5},{5,9},... | collective-permute-start | bytes 1572872 | tf_op jit(solution)/shard_map/ppermute | solution.py:47
  368.2 14.5 %collective-permute-start.60 = (bf16[2,32,1536]{2,1,0:T(8,128)(2,1)S(1)}, bf16[2,32,1536]{2,1,0:T(8,128)(2,1)S(1)}, u32[]{:S(2)}, u32[]{:S(2)}) collective-permute-start(bf16[2,32,1536]{2,1,0:T(8,128)(2,1)S(1)} %fusion.46), channel_id=1, source_target_pairs={{0,16},{16,0},{1,17},{17,1},{2,18},{18,2},{3,19},{19,3},{4,20},{20... | collective-permute-start | bytes 589832 | tf_op jit(solution)/shard_map/ppermute | solution.py:42
  377.7 20.5 %collective-permute-start.48 = (bf16[256,1024]{1,0:T(8,128)(2,1)}, bf16[256,1024]{1,0:T(8,128)(2,1)S(1)}, u32[]{:S(2)}, u32[]{:S(2)}) collective-permute-start(bf16[256,1024]{1,0:T(8,128)(2,1)} %get-tuple-element.159), channel_id=1, source_target_pairs={{0,4},{4,8},{8,12},{12,14},{14,10},{10,6},{6,2},{2,0},{1,5},{5,9},... | collective-permute-start | bytes 1572872 | tf_op jit(solution)/shard_map/ppermute | solution.py:47
  378.6 13.6 %collective-permute-start.50 = (bf16[256,1024]{1,0:T(8,128)(2,1)}, bf16[256,1024]{1,0:T(8,128)(2,1)S(1)}, u32[]{:S(2)}, u32[]{:S(2)}) collective-permute-start(bf16[256,1024]{1,0:T(8,128)(2,1)} %get-tuple-element.160), channel_id=1, source_target_pairs={{0,2},{4,0},{8,4},{12,8},{14,12},{10,14},{6,10},{2,6},{1,3},{5,1},... | collective-permute-start | bytes 1572872 | tf_op jit(solution)/shard_map/ppermute | solution.py:47
  394.2 12.3 %collective-permute-start.51 = (bf16[256,1024]{1,0:T(8,128)(2,1)}, bf16[256,1024]{1,0:T(8,128)(2,1)S(1)}, u32[]{:S(2)}, u32[]{:S(2)}) collective-permute-start(bf16[256,1024]{1,0:T(8,128)(2,1)} %fusion.19), channel_id=1, source_target_pairs={{0,2},{4,0},{8,4},{12,8},{14,12},{10,14},{6,10},{2,6},{1,3},{5,1},... | collective-permute-start | bytes 1572872 | tf_op jit(solution)/shard_map/ppermute | solution.py:47
  (51 other events, 544.6 us)
where the time goes:
time: 416 us; the launch traced here: 411 us
  waiting for transfers between devices  115 us (28%)
  Pallas kernels  114 us (27%)
  starting transfers between devices  90.4 us (22%)
  other arithmetic  46 us (11%)
  local copies, waits for them, and re-layouts  36.7 us (9%)
  matrix products  6.13 us (1%)
    ppermute x33, waiting for transfers between devices, turn(): return lax.ppermute(block, 'h', route)  77.3 us
    ppermute x33, starting transfers between devices, turn(): return lax.ppermute(block, 'h', route)  55.5 us
    pallas_call x1, Pallas kernels, attend_back(): pl.pallas_call(attend_back_kernel, grid_spec=pltpu.PrefetchScalarGridSpec...  27.1 us
    ppermute x28, waiting for transfers between devices, swap(): return lax.ppermute(block, axis, [(0, 1), (1, 0)])  25 us
    all_to_all x4, starting transfers between devices, exchange(): return lax.all_to_all(blocks, 'h', 0, 0)  18.7 us
    pallas_call x1, Pallas kernels, attend(): pl.pallas_call(attend_kernel, grid_spec=pltpu.PrefetchScalarGridSpec(num_...  18.4 us
    pallas_call x2, Pallas kernels, ffn(): pl.pallas_call(ffn_kernel, in_specs=[vmem()] * 7, out_specs=[vmem()] * 4,...  18.1 us
    ppermute x28, starting transfers between devices, swap(): return lax.ppermute(block, axis, [(0, 1), (1, 0)])  16.2 us
  transfers between devices with their start and end apart: 65, of which 21 were waited for; matrix products, arithmetic and copies ran while one was open for 18% of the time, Pallas kernels for 23%

commit v1 on v0

--- a/solution.py
+++ b/solution.py
@@ -372,25 +372,53 @@
     )(tab, heads, *sources, x, gain)
 
 
+def fold(block, deep):
+    half, rest = D // 2, block.shape[0] - deep
+    middle = jnp.concatenate([block[deep:, :half], block[: deep - rest, half:]], axis=0)
+    last = block[deep - rest :, half:]
+    last = jnp.concatenate([last, jnp.zeros((deep - last.shape[0], half), last.dtype)], axis=0)
+    return block[:deep, :half], middle, last
+
+
+def unfolded(block, share):
+    deep, half = block.shape[0], D // 2
+    rest = share - deep
+    return [
+        (0, deep, 0, block[:, :half]),
+        (deep, rest, 0, block[:rest, half:D]),
+        (0, deep - rest, half, block[rest:, half:D]),
+        (deep - rest, share - deep + rest, half, block[: share - deep + rest, D:]),
+    ]
+
+
 def weights_kernel(tab, *refs):
     blocks, (gate_ref, up_ref, down_ref, acc_ref) = refs[:-4], refs[-4:]
     units = gate_ref.shape[1]
-    half = blocks[0].shape[1] // 2
-    held = [(b, b) for b in blocks[: HEADS // 2]]
-    held += [(blocks[HEADS // 2], blocks[HEADS // 2 + 1])]
-    held += [(b, b) for b in blocks[HEADS // 2 + 2 :]]
-    for slot, (upper, lower) in enumerate(held):
+    height, wide = blocks[0].shape
+    half = wide // 2
+    share = units // HEADS
+    rows = D // (2 * HEADS)
+    middle = blocks[HEADS // 2].shape[0]
+    for slot in range(HEADS):
         chip = tab[slot]
-        first = blocks[HEADS // 2].shape[0]
-        rows = first // 2
-        share = down_ref.shape[0] // HEADS
-        for pair in range(2):
-            here = pl.ds(pl.multiple_of((pair * HEADS + chip) * rows, rows), rows)
-            gate_ref[here, :] = upper[pair * rows : (pair + 1) * rows, :units]
-            up_ref[here, :] = upper[pair * rows : (pair + 1) * rows, half : half + units]
-        start = 0 if lower is not upper else first
-        here = pl.ds(pl.multiple_of(chip * share, 8), share)
-        acc_ref[here, :] = lower[start : start + share, :D].astype(WIDE)
+        if slot == HEADS // 2:
+            pieces = [(0, blocks[slot]), (middle, blocks[slot + 1])]
+        else:
+            pieces = [(0, blocks[slot if slot < HEADS // 2 else slot + 1])]
+        for start, ref in pieces:
+            stop = start + ref.shape[0]
+            for pair in range(2):
+                first, last = max(start, pair * rows), min(stop, (pair + 1) * rows)
+                if first < last:
+                    size = last - first
+                    here = (pair * HEADS + chip) * rows + first - pair * rows
+                    here = pl.ds(pl.multiple_of(here, math.gcd(rows, first)), size)
+                    gate_ref[here, :] = ref[first - start : last - start, :units]
+                    up_ref[here, :] = ref[first - start : last - start, half : half + units]
+        lower = ref[2 * rows - start :, :].astype(WIDE)
+        for row, size, column, piece in unfolded(lower, share):
+            here = pl.ds(pl.multiple_of(chip * share + row, 8), size)
+            acc_ref[here, column : column + D // 2] = piece
     down_ref[...] = acc_ref[...].astype(LOW)
 
 
@@ -474,12 +502,11 @@
                 )
                 parts_ref[slot, here, start : start + units] = total[first : first + rows]
     total = dot_tn(tokens(hid_l, hid_r), up)
-    strip = wide - D
+    deep = parts_ref.shape[1] - 2 * rows
     for h in range(HEADS):
-        slot = tab[h]
-        piece = total[h * share : (h + 1) * share].astype(LOW)
-        parts_ref[slot, 2 * rows : 2 * rows + share, :D] = piece
-        parts_ref[slot, 2 * rows : 2 * rows + share, D:] = jnp.zeros((share, strip), LOW)
+        for i, piece in enumerate(fold(total[h * share : (h + 1) * share], deep)):
+            columns = slice(i * D // 2, (i + 1) * D // 2)
+            parts_ref[tab[h], 2 * rows :, columns] = piece.astype(LOW)
 
 
 def weight_grads(slot_of, ns, ups, near, away, height, wide):
@@ -495,28 +522,6 @@
         ),
         name="weight_grads",
     )(slot_of, *ns, *ups, *near, *away)
-
-
-def strips_kernel(tab, out_ref, strips_ref):
-    rows, strip = out_ref.shape[1], strips_ref.shape[2]
-    for slot in range(HEADS):
-        for i in range(D // strip):
-            strips_ref[slot, i * rows : (i + 1) * rows, :] = out_ref[
-                tab[slot], :, i * strip : (i + 1) * strip
-            ]
-
-
-def out_strips(chips, out, strip):
-    return pl.pallas_call(
-        strips_kernel,
-        in_specs=[smem(), vmem()],
-        out_specs=vmem(),
-        out_shape=jax.ShapeDtypeStruct((HEADS, out.shape[1] * D // strip, strip), LOW),
-        cost_estimate=pl.CostEstimate(
-            flops=0, bytes_accessed=4 * HEADS * out.shape[1] * D, transcendentals=0
-        ),
-        name="out_strips",
-    )(chips, out)
 
 
 def mid_kernel(mid_ref, pa, pb, pc, up_ref, gain_ref, w_ref, mg_ref, bg_ref, ag_ref):
@@ -665,7 +670,7 @@
     for step in range(HEADS // 2 - 2):
         forth.append(turn(forth[-1], 1))
         back.append(turn(back[-1], -1))
-        if step == 0:
+        if step == 1:
             got, forth[-1], back[-1], parity = lax.optimization_barrier(
                 (got, forth[-1], back[-1], core)
             )
@@ -750,11 +755,17 @@
     kept = pick(pair, gu[0], gu[1])
     came = swap(pick(pair, gu[1], gu[0]), "dl")
     gu = pick(pair, jnp.stack([kept, came]), jnp.stack([came, kept])).reshape(4 * rows, wide)
-    bundle = jnp.concatenate([gu, jnp.pad(down_weight, ((0, 0), (0, wide - D)))], axis=0)
-    height = 4 * rows + share
+    if far == 1:
+        deep = 2 * rows
+        lower = jnp.concatenate(fold(down_weight, deep), axis=1)
+    else:
+        deep = share
+        lower = jnp.pad(down_weight, ((0, 0), (0, wide - D)))
+    bundle = jnp.concatenate([gu, lower], axis=0)
+    height = 4 * rows + deep
     if far > 1:
         bundle = lax.all_gather(bundle, "dh", axis=0, tiled=True)
-    upper = bundle.shape[0] * 4 * rows // height if far == 1 else bundle.shape[0] // 2
+    upper = bundle.shape[0] // 2
     bundle, *_ = lax.optimization_barrier((bundle, far_first, far_last))
     forth, back = [bundle], [bundle]
     for step in range(HEADS // 2 - 1):
@@ -887,10 +898,7 @@
             plus(blocks[HEADS // 2 - step], turn(back, -1), 0),
         )
 
-    def ring_rest(blocks, forth, back, first=2):
-        for step in range(first, HEADS // 2):
-            forth, back = ring_next(blocks, forth, back, step)
-        forth, back = turn(forth, 1), turn(back, -1)
+    def ring_last(blocks, forth, back):
         return blocks[0].astype(WIDE) + forth.astype(WIDE) + back.astype(WIDE)
 
     def over_owner(w, width):
@@ -905,23 +913,15 @@
             w = lax.psum_scatter(w, "dh", scatter_dimension=0, tiled=True)
         return w[0]
 
+    blocks = [parts[slot] for slot in range(HEADS)]
+    forth, back = ring_first(blocks, upper)
+    branch, forth, back = lax.optimization_barrier((branch, forth, back))
     out_part = over_owner(
         jnp.einsum("td,te->de", attended, branch, preferred_element_type=WIDE).astype(LOW), D
     )
-    strip = wide - D
-    blocks = [parts[slot].astype(WIDE) for slot in range(HEADS)]
-    if far == 1:
-        strips = out_strips(where, out_part, strip)
-        below = share - strips.shape[1]
-        for slot in range(HEADS):
-            if slot != HEADS // 2:
-                blocks[slot] = blocks[slot] + jnp.pad(
-                    strips[slot].astype(WIDE), ((4 * rows, below), (D, 0))
-                )
-        out_far = turn(strips[HEADS // 2], HEADS // 2)
-    forth, back = ring_first(blocks, upper)
-    ups, forth, back = lax.optimization_barrier((ups, forth, back))
     forth, back = ring_next(blocks, forth, back, 2)
+    ups, out_part, forth, back = lax.optimization_barrier((ups, out_part, forth, back))
+    forth, back = ring_next(blocks, forth, back, 3)
 
     dq, d_own, d_oth = attend_back(
         tab, queries, ups, attention, lse, own, other, memory, seg_thin, seg_own_row, seg_oth_row
@@ -929,20 +929,37 @@
     d_got = swap(d_oth, "c")
     dq, forth, back = lax.optimization_barrier((dq, forth, back))
     dx, grads = qkv_back(chips.astype(jnp.int32), dq, d_own, d_got, cosine, sine, w_qkv)
+    out_part = exchange(out_part)
+    forth, back = turn(forth, 1), turn(back, -1)
+    dx, forth, back = lax.optimization_barrier((dx, forth, back))
     dx_forth, dx_back = ring_first(dx, split)
-    grads, hid_l, hid_r, _, _ = lax.optimization_barrier((grads, hid_l, hid_r, dx_forth, dx_back))
-    normed_one_grad = ring_rest(dx, dx_forth, dx_back)
-
-    summed = ring_rest(blocks, forth, back, 3).astype(LOW)
+    grads, out_part, dx_forth, dx_back = lax.optimization_barrier(
+        (grads, out_part, dx_forth, dx_back)
+    )
+    out_w_grad = jnp.sum(out_part.astype(WIDE), axis=0)
+
+    dw = jnp.einsum("std,stg->dg", normed_one, grads, preferred_element_type=WIDE).astype(LOW)
+    dw = over_owner(dw, 3 * HEAD_DIM)
+    dx_forth, dx_back = ring_next(dx, dx_forth, dx_back, 2)
+    dw, hid_l, hid_r, dx_forth, dx_back, forth, back = lax.optimization_barrier(
+        (dw, hid_l, hid_r, dx_forth, dx_back, forth, back)
+    )
+    qkv_grads = exchange(dw).astype(WIDE)
+    dx_forth, dx_back = ring_next(dx, dx_forth, dx_back, 3)
+    normed_one_grad = ring_last(dx, turn(dx_forth, 1), turn(dx_back, -1))
+
+    summed = ring_last(blocks, forth, back).astype(LOW)
     if far > 1:
         summed = lax.psum_scatter(summed, "dh", scatter_dimension=0, tiled=True)
-    down_w_grad = summed[4 * rows : 4 * rows + share, :D].astype(WIDE)
+    lower = summed[4 * rows :].astype(WIDE)
     if far == 1:
-        out_w_grad = summed[4 * rows : 4 * rows + strips.shape[1], D:].astype(WIDE)
-        out_w_grad = out_w_grad + out_far.astype(WIDE)
-        out_w_grad = out_w_grad.reshape(D // strip, rows, strip).transpose(1, 0, 2).reshape(rows, D)
+        half_d = D // 2
+        rest = share - deep
+        left = jnp.concatenate([lower[:, :half_d], lower[:rest, half_d:D]], axis=0)
+        right = jnp.concatenate([lower[rest:, half_d:D], lower[: 2 * rest, D:]], axis=0)
+        down_w_grad = jnp.concatenate([left, right], axis=1)
     else:
-        out_w_grad = jnp.sum(exchange(out_part).astype(WIDE), axis=0)
+        down_w_grad = lower[:, :D]
     gu = summed[: 4 * rows].reshape(2, 2, rows, wide)
     kept = pick(core, gu[:, 0], gu[:, 1])
     came = swap(pick(core, gu[:, 1], gu[:, 0]), "c")
@@ -965,9 +982,6 @@
     for part in (out_l[0], swap(out_l[1], "c"), swap(to_away(out_r), "dl")):
         output = output + part.astype(WIDE)
     output = output.astype(LOW)
-
-    dw = jnp.einsum("std,stg->dg", normed_one, grads, preferred_element_type=WIDE).astype(LOW)
-    qkv_grads = exchange(over_owner(dw, 3 * HEAD_DIM)).astype(WIDE)
 
     wide_x = x.astype(WIDE)
     r = lax.rsqrt(jnp.mean(wide_x * wide_x, axis=-1, keepdims=True) + EPSILON)

time: 416 us -> 426 us (1.024)
  waiting for transfers between devices: 115 us -> 126 us
  starting transfers between devices: 90.4 us -> 83.5 us
    ppermute x33 -> x32, waiting for transfers between devices: 77.3 us -> 109 us  [turn(): return lax.ppermute(block, 'h', route)]
    ppermute x28, waiting for transfers between devices: 25 us -> 9.26 us  [swap(): return lax.ppermute(block, axis, [(0, 1), (1, 0)])]
    ppermute x28, starting transfers between devices: 16.2 us -> 10 us  [swap(): return lax.ppermute(block, axis, [(0, 1), (1, 0)])]
    all_to_all x4 -> x5, waiting for transfers between devices: 12.6 us -> 7.22 us  [exchange(): return lax.all_to_all(blocks, 'h', 0, 0)]
    ppermute x33 -> x32, starting transfers between devices: 55.5 us -> 50.8 us  [turn(): return lax.ppermute(block, 'h', route)]
    unnamed x116 -> x122, local copies, waits for them, and re-layouts: 12.2 us -> 16.6 us
    all_to_all x4 -> x5, starting transfers between devices: 18.7 us -> 22.7 us  [exchange(): return lax.all_to_all(blocks, 'h', 0, 0)]
    convert_element_type x8 -> x6, other arithmetic: 12.1 us -> 10.9 us  [plus(): pieces = [piece.astype(LOW) for piece in pieces if piece.shape[0]]]
  transfers between devices with their start and end apart: 65 -> 65, of which waited for: 21 -> 28; matrix products, arithmetic and copies ran while one was open for 18% -> 17% of each run, Pallas kernels for 23% -> 25%
where the time goes in v1:
time: 426 us; the launch traced here: 420 us
  waiting for transfers between devices  126 us (30%)
  Pallas kernels  112 us (26%)
  starting transfers between devices  83.5 us (20%)
  other arithmetic  48.3 us (11%)
  local copies, waits for them, and re-layouts  38.6 us (9%)
  matrix products  9.25 us (2%)
    ppermute x32, waiting for transfers between devices, turn(): return lax.ppermute(block, 'h', route)  109 us
    ppermute x32, starting transfers between devices, turn(): return lax.ppermute(block, 'h', route)  50.8 us
    pallas_call x1, Pallas kernels, attend_back(): pl.pallas_call(attend_back_kernel, grid_spec=pltpu.PrefetchScalarGridSpec...  27 us
    all_to_all x5, starting transfers between devices, exchange(): return lax.all_to_all(blocks, 'h', 0, 0)  22.7 us
    pallas_call x1, Pallas kernels, attend(): pl.pallas_call(attend_kernel, grid_spec=pltpu.PrefetchScalarGridSpec(num_...  18.5 us
    pallas_call x2, Pallas kernels, ffn(): pl.pallas_call(ffn_kernel, in_specs=[vmem()] * 7, out_specs=[vmem()] * 4,...  18.2 us
    unnamed x122, local copies, waits for them, and re-layouts  16.6 us
    pallas_call x2, Pallas kernels, qkv_blocks(): pl.pallas_call(functools.partial(qkv_kernel, [len(block) for block in xs]...  14.2 us
  transfers between devices with their start and end apart: 65, of which 28 were waited for; matrix products, arithmetic and copies ran while one was open for 17% of the time, Pallas kernels for 25%

profile of v1, /device:TPU:0, one launch (start us, length us, event | category | flops | bytes accessed | tf_op | source)
XLA Modules:
  0.0 419.8 jit_solution(12216542707586276018)
XLA Ops:
  1.9 3.0 collective-permute-start.1
  11.0 7.3 %collective-permute-done.1.refs_2_ = bf16[288,1024]{1,0:T(8,128)(2,1)S(1)} collective-permute-done((bf16[288,1024]{1,0:T(8,128)(2,1)S(1)}, bf16[288,1024]{1,0:T(8,128)(2,1)S(1)}, u32[]{:S(2)}, u32[]{:S(2)}) %collective-permute-start.1) | collective-permute-done | bytes 589856 | tf_op jit(solution)/shard_map/ppermute | solution.py:47
  22.4 4.9 %all-to-all-start = ((bf16[8,112,128]{2,1,0:T(8,128)(2,1)}), bf16[8,112,128]{2,1,0:T(8,128)(2,1)S(1)}, u32[]{:S(2)}, u32[]{:S(2)}) async-start(bf16[8,112,128]{2,1,0:T(8,128)(2,1)} %copy.288), calls=%async_computation | async-start | bytes 458752 | tf_op jit(solution)/shard_map/all_to_all | solution.py:56
  27.3 2.0 collective-permute-start.2
  29.4 1.6 collective-permute-start.20
  31.7 13.8 %collective-permute-done.2.refs_3_ = bf16[288,1024]{1,0:T(8,128)(2,1)} collective-permute-done((bf16[288,1024]{1,0:T(8,128)(2,1)S(1)}, bf16[288,1024]{1,0:T(8,128)(2,1)}, u32[]{:S(2)}, u32[]{:S(2)}) %collective-permute-start.2) | collective-permute-done | bytes 589856 | tf_op jit(solution)/shard_map/ppermute | solution.py:47
  45.5 1.6 collective-permute-start.3
  48.3 1.6 fusion.52
  49.9 11.4 %collective-permute-done.3.refs_0_ = bf16[288,1024]{1,0:T(8,128)(2,1)S(1)} collective-permute-done((bf16[288,1024]{1,0:T(8,128)(2,1)}, bf16[288,1024]{1,0:T(8,128)(2,1)S(1)}, u32[]{:S(2)}, u32[]{:S(2)}) %collective-permute-start.3) | collective-permute-done | bytes 589856 | tf_op jit(solution)/shard_map/ppermute | solution.py:47
  61.2 1.7 collective-permute-done.5.refs_1_
  63.1 1.6 collective-permute-start.9
  65.1 3.7 fusion.45
  68.8 2.0 pad_maximum_fusion
  71.8 1.8 collective-permute-start.7
  83.8 8.2 %qkv5.1 = (bf16[8,256,128]{2,1,0:T(8,128)(2,1)}, bf16[2,8,256,128]{3,2,1,0:T(8,128)(2,1)}, bf16[8,256,1024]{2,1,0:T(8,128)(2,1)}) custom-call(s32[5]{0:T(128)} %compare_select_fusion.8.tab, bf16[288,1024]{1,0:T(8,128)(2,1)} %copy-done.3, bf16[288,1024]{1,0:T(8,128)(2,1)} %copy-done.16, bf16[288,1024]{1,0:T(8,128)(2,1)} %copy-done.15, ...), custom_call_target="tpu_custom_call" | custom-call | flops 1006632960 | bytes 6553600 | tf_op jit(solution)/shard_map/qkv5/pallas_call | solution.py:126
  92.8 6.0 %qkv3.1 = (bf16[8,256,128]{2,1,0:T(8,128)(2,1)}, bf16[2,8,256,128]{3,2,1,0:T(8,128)(2,1)}, bf16[8,256,1024]{2,1,0:T(8,128)(2,1)}) custom-call(s32[3]{0:T(128)} %compare_select_fusion.9.tab, bf16[288,1024]{1,0:T(8,128)(2,1)} %copy-done.8, bf16[288,1024]{1,0:T(8,128)(2,1)} %copy-done.5, ...), custom_call_target="tpu_custom_call", output_to_operand_aliasing={{0}: (9, {}), {1}: (10, {}), {2}: (11, {})} | custom-call | flops 603979776 | bytes 3932160 | tf_op jit(solution)/shard_map/qkv3/pallas_call | solution.py:126
  100.5 11.9 %collective-permute-start.21 = (bf16[192,1536]{1,0:T(8,128)(2,1)S(1)}, bf16[192,1536]{1,0:T(8,128)(2,1)S(1)}, u32[]{:S(2)}, u32[]{:S(2)}) collective-permute-start(bf16[192,1536]{1,0:T(8,128)(2,1)S(1)} %fusion.33.refs_0_), channel_id=1, source_target_pairs={{0,4},{4,8},{8,12},{12,14},{14,10},{10,6},{6,2},{2,0},{1,5},{5,9},... | collective-permute-start | bytes 1769480 | tf_op jit(solution)/shard_map/ppermute | solution.py:47
  116.8 1.5 bitcast_dynamic-update-slice_fusion.refs_0_
  118.8 1.5 collective-permute-start.13
  120.3 18.5 %attend.1 = (f32[8,256,128]{2,1,0:T(8,128)}, bf16[8,256,128]{2,1,0:T(8,128)(2,1)}, f32[8,256,1]{2,1,0:T(8,128)}, bf16[2,8,256,128]{3,2,1,0:T(8,128)(2,1)}) custom-call(s32[42]{0:T(128)} %concatenate.97.tab, bf16[8,256,128]{2,1,0:T(8,128)(2,1)} %get-tuple-element.102.q_ref, bf16[2,8,256,128]{3,2,1,0:T(8,128)(2,1)} %get-tuple-element.103.own_ref, ...), custom_call_target="tpu_custom_call" | custom-call | flops 24999999488 | bytes 6291456 | tf_op jit(solution)/shard_map/attend/pallas_call | solution.py:231
  138.8 4.7 %all-to-all-start.1 = ((bf16[8,256,128]{2,1,0:T(8,128)(2,1)}), bf16[8,256,128]{2,1,0:T(8,128)(2,1)S(1)}, u32[]{:S(2)}, u32[]{:S(2)}) async-start(bf16[8,256,128]{2,1,0:T(8,128)(2,1)} %get-tuple-element.104), calls=%async_computation.1 | async-start | bytes 1048576 | tf_op jit(solution)/shard_map/all_to_all | solution.py:56
  144.6 2.0 collective-permute-start.26
  149.5 7.2 %all-to-all-done.1.heads_ref = bf16[8,256,128]{2,1,0:T(8,128)(2,1)S(1)} async-done(((bf16[8,256,128]{2,1,0:T(8,128)(2,1)}), bf16[8,256,128]{2,1,0:T(8,128)(2,1)S(1)}, u32[]{:S(2)}, u32[]{:S(2)}) %all-to-all-start.1) | async-done | bytes 524320 | tf_op jit(solution)/shard_map/all_to_all | solution.py:56
  157.6 4.0 out_block.1
  161.7 2.8 collective-permute-done.26.refs_7_
  164.6 3.2 collective-permute-start.23
  167.8 3.3 collective-permute-done.30.na.refs_2_
  171.1 8.0 %collective-permute-done.27.refs_6_ = bf16[192,1536]{1,0:T(8,128)(2,1)S(1)} collective-permute-done((bf16[192,1536]{1,0:T(8,128)(2,1)S(1)}, bf16[192,1536]{1,0:T(8,128)(2,1)S(1)}, u32[]{:S(2)}, u32[]{:S(2)}) %collective-permute-start.27) | collective-permute-done | bytes 589856 | tf_op jit(solution)/shard_map/ppermute | solution.py:47
  179.8 1.5 collective-permute-start.24
  181.3 4.7 %collective-permute-done.28.refs_5_ = bf16[96,1536]{1,0:T(8,128)(2,1)} collective-permute-done((bf16[96,1536]{1,0:T(8,128)(2,1)S(1)}, bf16[96,1536]{1,0:T(8,128)(2,1)}, u32[]{:S(2)}, u32[]{:S(2)}) %collective-permute-start.28) | collective-permute-done | bytes 294944 | tf_op jit(solution)/shard_map/ppermute | solution.py:47
  187.3 4.6 %weights.1 = (bf16[1024,704]{1,0:T(8,128)(2,1)}, bf16[1024,704]{1,0:T(8,128)(2,1)}, bf16[704,1024]{1,0:T(8,128)(2,1)}) custom-call(s32[10]{0:T(128)} %pad_add_fusion.tab, bf16[192,1536]{1,0:T(8,128)(2,1)} %copy-done.2, bf16[192,1536]{1,0:T(8,128)(2,1)} %copy-done.21, bf16[192,1536]{1,0:T(8,128)(2,1)} %copy-done.23, bf16[192,1536]{1,0:T(8,128)(2,1)} %copy-done.10, ...), custom_call_target="tpu_custom_call" | custom-call | bytes 8650752 | tf_op jit(solution)/shard_map/weights/pallas_call | solution.py:426
  191.9 9.1 %ffn.3 = (bf16[2,256,704]{2,1,0:T(8,128)(2,1)}, bf16[2,256,704]{2,1,0:T(8,128)(2,1)}, bf16[2,256,704]{2,1,0:T(8,128)(2,1)}, bf16[2,256,1024]{2,1,0:T(8,128)(2,1)}) custom-call(bf16[256,1024]{1,0:T(8,128)(2,1)} %collective-permute-done.30.na.refs_2_, bf16[256,1024]{1,0:T(8,128)(2,1)} %collective-permute-done.31.nb.refs_3_, ...), custom_call_target="tpu_custom_call" | custom-call | flops 3690987520 | bytes 8519680 | tf_op jit(solution)/shard_map/ffn/pallas_call | solution.py:462
  203.9 9.1 %ffn.2 = (bf16[2,256,704]{2,1,0:T(8,128)(2,1)}, bf16[2,256,704]{2,1,0:T(8,128)(2,1)}, bf16[2,256,704]{2,1,0:T(8,128)(2,1)}, bf16[2,256,1024]{2,1,0:T(8,128)(2,1)}) custom-call(bf16[256,1024]{1,0:T(8,128)(2,1)} %get-tuple-element.109.na.refs_0_, bf16[256,1024]{1,0:T(8,128)(2,1)} %copy-done.47, bf16[256,1024]{1,0:T(8,128)(2,1)} %bitcast.364, ...), custom_call_target="tpu_custom_call" | custom-call | flops 3690987520 | bytes 8519680 | tf_op jit(solution)/shard_map/ffn/pallas_call | solution.py:462
  215.1 11.3 %weight_grads.1 = bf16[8,192,1536]{2,1,0:T(8,128)(2,1)} custom-call(s32[8]{0:T(128)} %compare_select_fusion.tab, bf16[256,1024]{1,0:T(8,128)(2,1)} %get-tuple-element.109.na.refs_0_, bf16[256,1024]{1,0:T(8,128)(2,1)} %copy-done.47, bf16[256,1024]{1,0:T(8,128)(2,1)} %collective-permute-done.30.na.refs_2_, ...), custom_call_target="tpu_custom_call" | custom-call | flops 4429185024 | bytes 14680064 | tf_op jit(solution)/shard_map/weight_grads/pallas_call | solution.py:515
  227.1 1.5 slice_bitcast_fusion.8
  231.5 4.7 %mid_block.1 = (f32[256,1024]{1,0:T(8,128)}, bf16[256,1024]{1,0:T(8,128)(2,1)}, bf16[8,256,128]{2,1,0:T(8,128)(2,1)}) custom-call(f32[256,1024]{1,0:T(8,128)} %get-tuple-element.107.mid_ref, bf16[256,1024]{1,0:T(8,128)(2,1)} %get-tuple-element.206.pa, bf16[256,1024]{1,0:T(8,128)(2,1)} %copy-done.26, bf16[256,1024]{1,0:T(8,128)(2,1)} %copy-done.25, ...), custom_call_target="tpu_custom_call" | custom-call | flops 536870912 | bytes 6291456 | tf_op jit(solution)/shard_map/mid_block/pallas_call | solution.py:545
  242.6 4.2 %all-to-all-start.2 = ((bf16[8,256,128]{2,1,0:T(8,128)(2,1)}), bf16[8,256,128]{2,1,0:T(8,128)(2,1)}, u32[]{:S(2)}, u32[]{:S(2)}) async-start(bf16[8,256,128]{2,1,0:T(8,128)(2,1)} %get-tuple-element.136), calls=%async_computation.2 | async-start | bytes 1048576 | tf_op jit(solution)/shard_map/all_to_all | solution.py:56
  246.8 2.0 collective-permute-start.38
  248.9 1.8 convert_add_fusion
  251.9 17.2 %collective-permute-done.38 = bf16[192,1536]{1,0:T(8,128)(2,1)S(1)} collective-permute-done((bf16[192,1536]{1,0:T(8,128)(2,1)}, bf16[192,1536]{1,0:T(8,128)(2,1)S(1)}, u32[]{:S(2)}, u32[]{:S(2)}) %collective-permute-start.38) | collective-permute-done | bytes 589856 | tf_op jit(solution)/shard_map/ppermute | solution.py:47
  269.1 1.9 collective-permute-done.39
  271.0 1.5 fusion.8
  273.6 4.3 %collective-permute-start.40 = (bf16[192,1536]{1,0:T(8,128)(2,1)S(1)}, bf16[192,1536]{1,0:T(8,128)(2,1)S(1)}, u32[]{:S(2)}, u32[]{:S(2)}) collective-permute-start(bf16[192,1536]{1,0:T(8,128)(2,1)S(1)} %get-tuple-element.148), channel_id=1, source_target_pairs={{0,4},{4,8},{8,12},{12,14},{14,10},{10,6},{6,2},{2,0},{1,5},{5,9},... | collective-permute-start | bytes 1769480 | tf_op jit(solution)/shard_map/ppermute | solution.py:47
  277.9 27.0 %attend_back.1 = (f32[8,256,128]{2,1,0:T(8,128)}, f32[2,8,256,128]{3,2,1,0:T(8,128)}, bf16[2,8,256,128]{3,2,1,0:T(8,128)(2,1)}) custom-call(s32[42]{0:T(128)} %concatenate.97.tab, bf16[8,256,128]{2,1,0:T(8,128)(2,1)} %get-tuple-element.102.q_ref, bf16[8,256,128]{2,1,0:T(8,128)(2,1)} %all-to-all-done.2.up_ref, f32[8,256,128]{2,1,0:T(8,128)} %get-tuple-element.144.o_ref, ...), custom_call_target="tpu_custom_call" | custom-call | flops 30000001024 | bytes 10485760 | tf_op jit(solution)/shard_map/attend_back/pallas_call | solution.py:311
  305.1 2.4 fusion.6
  307.4 2.0 collective-permute-start.43
  309.5 4.2 %all-to-all-start.3 = ((bf16[8,32,1024]{2,1,0:T(8,128)(2,1)}), bf16[8,32,1024]{2,1,0:T(8,128)(2,1)S(1)}, u32[]{:S(2)}, u32[]{:S(2)}) async-start(bf16[8,32,1024]{2,1,0:T(8,128)(2,1)} %fusion.37), calls=%async_computation.3 | async-start | bytes 1048576 | tf_op jit(solution)/shard_map/all_to_all | solution.py:56
  314.7 9.8 %qkv_back.1 = (bf16[8,256,1024]{2,1,0:T(8,128)(2,1)}, bf16[8,256,384]{2,1,0:T(8,128)(2,1)}) custom-call(s32[8]{0:T(128)} %copy-done.39, f32[8,256,128]{2,1,0:T(8,128)} %get-tuple-element.150.dq_ref, f32[2,8,256,128]{3,2,1,0:T(8,128)} %get-tuple-element.151.own_ref, bf16[2,8,256,128]{3,2,1,0:T(8,128)(2,1)} %copy-done.12, ...), custom_call_target="tpu_custom_call" | custom-call | flops 1610612736 | bytes 8388608 | tf_op jit(solution)/shard_map/qkv_back/pallas_call | solution.py:579
  329.2 9.7 %collective-permute-done.46 = bf16[128,1024]{1,0:T(8,128)(2,1)S(1)} collective-permute-done((bf16[128,1024]{1,0:T(8,128)(2,1)S(1)}, bf16[128,1024]{1,0:T(8,128)(2,1)S(1)}, u32[]{:S(2)}, u32[]{:S(2)}) %collective-permute-start.46) | collective-permute-done | bytes 262176 | tf_op jit(solution)/shard_map/ppermute | solution.py:47
  340.3 5.0 %bitcast_convert_fusion = bf16[1024,384]{1,0:T(8,128)(2,1)S(1)} fusion(bf16[8,256,1024]{2,1,0:T(8,128)(2,1)} %get-tuple-element.108, bf16[8,256,384]{2,1,0:T(8,128)(2,1)} %get-tuple-element.159), kind=kOutput, calls=%fused_computation.3 | convolution fusion | flops 1611005952 | bytes 6553600 | tf_op jit(solution)/shard_map/std,stg->dg/dot_general | solution.py:941
  347.5 3.3 collective-permute-start.49
  353.1 9.7 %collective-permute-done.49 = bf16[256,1024]{1,0:T(8,128)(2,1)S(1)} collective-permute-done((bf16[256,1024]{1,0:T(8,128)(2,1)S(1)}, bf16[256,1024]{1,0:T(8,128)(2,1)S(1)}, u32[]{:S(2)}, u32[]{:S(2)}) %collective-permute-start.49) | collective-permute-done | bytes 524320 | tf_op jit(solution)/shard_map/ppermute | solution.py:47
  362.7 2.4 collective-permute-done.50
  365.1 2.6 fusion.25
  369.9 4.7 %all-to-all-start.4 = ((bf16[8,32,384]{2,1,0:T(8,128)(2,1)}), bf16[8,32,384]{2,1,0:T(8,128)(2,1)S(1)}, u32[]{:S(2)}, u32[]{:S(2)}) async-start(bf16[8,32,384]{2,1,0:T(8,128)(2,1)} %fusion.48), calls=%async_computation.4 | async-start | bytes 393216 | tf_op jit(solution)/shard_map/all_to_all | solution.py:56
  374.6 2.5 convolution_convert_fusion.2
  380.5 2.0 collective-permute-start.54
  387.0 3.4 collective-permute-done.59
  396.8 1.9 fusion.18
  398.8 1.5 collective-permute-start.55
  403.0 9.0 %collective-permute-done.55 = bf16[256,1024]{1,0:T(8,128)(2,1)S(1)} collective-permute-done((bf16[256,1024]{1,0:T(8,128)(2,1)S(1)}, bf16[256,1024]{1,0:T(8,128)(2,1)S(1)}, u32[]{:S(2)}, u32[]{:S(2)}) %collective-permute-start.55) | collective-permute-done | bytes 524320 | tf_op jit(solution)/shard_map/ppermute | solution.py:47
  413.1 1.5 fusion.11
  415.0 2.2 fusion.38
  417.2 2.4 fusion.14
  (340 shorter events, 88.3 us)
Async XLA Ops:
  1.9 16.4 %collective-permute-start.1 = (bf16[288,1024]{1,0:T(8,128)(2,1)S(1)}, bf16[288,1024]{1,0:T(8,128)(2,1)S(1)}, u32[]{:S(2)}, u32[]{:S(2)}) collective-permute-start(bf16[288,1024]{1,0:T(8,128)(2,1)S(1)} %pad_maximum_fusion.3.refs_0_), channel_id=1, source_target_pairs={{0,2},{4,0},{8,4},{12,8},{14,12},{10,14},{6,10},{2,6},{1,3},{5,1},... | collective-permute-start | bytes 1769480 | tf_op jit(solution)/shard_map/ppermute | solution.py:47
  5.0 14.8 %collective-permute-start = (bf16[288,1024]{1,0:T(8,128)(2,1)S(1)}, bf16[288,1024]{1,0:T(8,128)(2,1)S(1)}, u32[]{:S(2)}, u32[]{:S(2)}) collective-permute-start(bf16[288,1024]{1,0:T(8,128)(2,1)S(1)} %pad_maximum_fusion.3.refs_0_), channel_id=1, source_target_pairs={{0,4},{4,8},{8,12},{12,14},{14,10},{10,6},{6,2},{2,0},{1,5},{5,9},... | collective-permute-start | bytes 1769480 | tf_op jit(solution)/shard_map/ppermute | solution.py:47
  21.5 7.8 %collective-permute-start.19 = (bf16[2,32,1536]{2,1,0:T(8,128)(2,1)S(1)}, bf16[2,32,1536]{2,1,0:T(8,128)(2,1)S(1)}, u32[]{:S(2)}, u32[]{:S(2)}) collective-permute-start(bf16[2,32,1536]{2,1,0:T(8,128)(2,1)S(1)} %select_bitcast_fusion.1), channel_id=1, source_target_pairs={{0,1},{1,0},{2,3},{3,2},{4,5},{5,4},{6,7},{7,6},{8,9},{9,8},{10,11... | collective-permute-start | bytes 589832 | tf_op jit(solution)/shard_map/ppermute | solution.py:42
  22.4 27.5 %all-to-all-start = ((bf16[8,112,128]{2,1,0:T(8,128)(2,1)}), bf16[8,112,128]{2,1,0:T(8,128)(2,1)S(1)}, u32[]{:S(2)}, u32[]{:S(2)}) async-start(bf16[8,112,128]{2,1,0:T(8,128)(2,1)} %copy.288), calls=%async_computation | async-start | bytes 458752 | tf_op jit(solution)/shard_map/all_to_all | solution.py:56
  27.3 18.2 %collective-permute-start.2 = (bf16[288,1024]{1,0:T(8,128)(2,1)S(1)}, bf16[288,1024]{1,0:T(8,128)(2,1)}, u32[]{:S(2)}, u32[]{:S(2)}) collective-permute-start(bf16[288,1024]{1,0:T(8,128)(2,1)S(1)} %collective-permute-done.refs_1_), channel_id=1, source_target_pairs={{0,4},{4,8},{8,12},{12,14},{14,10},{10,6},{6,2},{2,0},{1,5},{5,9},... | collective-permute-start | bytes 1769480 | tf_op jit(solution)/shard_map/ppermute | solution.py:47
  29.3 17.8 %collective-permute-start.4 = (bf16[288,1024]{1,0:T(8,128)(2,1)S(1)}, bf16[288,1024]{1,0:T(8,128)(2,1)}, u32[]{:S(2)}, u32[]{:S(2)}) collective-permute-start(bf16[288,1024]{1,0:T(8,128)(2,1)S(1)} %collective-permute-done.1.refs_2_), channel_id=1, source_target_pairs={{0,2},{4,0},{8,4},{12,8},{14,12},{10,14},{6,10},{2,6},{1,3},{5,1},... | collective-permute-start | bytes 1769480 | tf_op jit(solution)/shard_map/ppermute | solution.py:47
  29.4 18.7 %collective-permute-start.20 = (bf16[2,32,1536]{2,1,0:T(8,128)(2,1)S(1)}, bf16[2,32,1536]{2,1,0:T(8,128)(2,1)S(1)}, u32[]{:S(2)}, u32[]{:S(2)}) collective-permute-start(bf16[2,32,1536]{2,1,0:T(8,128)(2,1)S(1)} %get-tuple-element.216), channel_id=1, source_target_pairs={{0,16},{16,0},{1,17},{17,1},{2,18},{18,2},{3,19},{19,3},{4,20},{20... | collective-permute-start | bytes 589832 | tf_op jit(solution)/shard_map/ppermute | solution.py:42
  45.5 15.7 %collective-permute-start.3 = (bf16[288,1024]{1,0:T(8,128)(2,1)}, bf16[288,1024]{1,0:T(8,128)(2,1)S(1)}, u32[]{:S(2)}, u32[]{:S(2)}) collective-permute-start(bf16[288,1024]{1,0:T(8,128)(2,1)} %collective-permute-done.2.refs_3_), channel_id=1, source_target_pairs={{0,4},{4,8},{8,12},{12,14},{14,10},{10,6},{6,2},{2,0},{1,5},{5,9},... | collective-permute-start | bytes 1769480 | tf_op jit(solution)/shard_map/ppermute | solution.py:47
  47.1 15.8 %collective-permute-start.5 = (bf16[288,1024]{1,0:T(8,128)(2,1)}, bf16[288,1024]{1,0:T(8,128)(2,1)S(1)}, u32[]{:S(2)}, u32[]{:S(2)}) collective-permute-start(bf16[288,1024]{1,0:T(8,128)(2,1)} %collective-permute-done.4.refs_4_), channel_id=1, source_target_pairs={{0,2},{4,0},{8,4},{12,8},{14,12},{10,14},{6,10},{2,6},{1,3},{5,1},... | collective-permute-start | bytes 1769480 | tf_op jit(solution)/shard_map/ppermute | solution.py:47
  63.0 14.4 %collective-permute-start.6 = (bf16[8,112,128]{2,0,1:T(8,128)(2,1)S(1)}, bf16[8,112,128]{2,0,1:T(8,128)(2,1)S(1)}, u32[]{:S(2)}, u32[]{:S(2)}) collective-permute-start(bf16[8,112,128]{2,0,1:T(8,128)(2,1)S(1)} %copy.358), channel_id=1, source_target_pairs={{0,1},{1,0},{2,3},{3,2},{4,5},{5,4},{6,7},{7,6},{8,9},{9,8},{10,11... | collective-permute-start | bytes 688136 | tf_op jit(solution)/shard_map/ppermute | solution.py:42
  63.1 15.0 %collective-permute-start.9 = (bf16[8,112,128]{2,0,1:T(8,128)(2,1)S(1)}, bf16[8,112,128]{2,0,1:T(8,128)(2,1)}, u32[]{:S(2)}, u32[]{:S(2)}) collective-permute-start(bf16[8,112,128]{2,0,1:T(8,128)(2,1)S(1)} %copy.358), channel_id=1, source_target_pairs={{0,16},{16,0},{1,17},{17,1},{2,18},{18,2},{3,19},{19,3},{4,20},{20... | collective-permute-start | bytes 688136 | tf_op jit(solution)/shard_map/ppermute | solution.py:42
  71.8 20.1 %collective-permute-start.7 = (bf16[128,1024]{1,0:T(8,128)(2,1)S(1)}, bf16[128,1024]{1,0:T(8,128)(2,1)S(1)}, u32[]{:S(2)}, u32[]{:S(2)}) collective-permute-start(bf16[128,1024]{1,0:T(8,128)(2,1)S(1)} %slice.326), channel_id=1, source_target_pairs={{0,4},{4,8},{8,12},{12,14},{14,10},{10,6},{6,2},{2,0},{1,5},{5,9},... | collective-permute-start | bytes 786440 | tf_op jit(solution)/shard_map/ppermute | solution.py:47
  73.6 18.3 %collective-permute-start.8 = (bf16[160,1024]{1,0:T(8,128)(2,1)S(1)}, bf16[160,1024]{1,0:T(8,128)(2,1)S(1)}, u32[]{:S(2)}, u32[]{:S(2)}) collective-permute-start(bf16[160,1024]{1,0:T(8,128)(2,1)S(1)} %slice.327), channel_id=1, source_target_pairs={{0,2},{4,0},{8,4},{12,8},{14,12},{10,14},{6,10},{2,6},{1,3},{5,1},... | collective-permute-start | bytes 983048 | tf_op jit(solution)/shard_map/ppermute | solution.py:47
  98.8 21.5 %collective-permute-start.11 = (bf16[2,8,256,128]{3,2,1,0:T(8,128)(2,1)}, bf16[2,8,256,128]{3,2,1,0:T(8,128)(2,1)}, u32[]{:S(2)}, u32[]{:S(2)}) collective-permute-start(bf16[2,8,256,128]{3,2,1,0:T(8,128)(2,1)} %get-tuple-element.103.own_ref), channel_id=1, source_target_pairs={{0,1},{1,0},{2,3},{3,2},{4,5},{5,4},{6,7},{7,6},{8,9},{9,8},{10,11... | collective-permute-start | bytes 3145736 | tf_op jit(solution)/shard_map/ppermute | solution.py:42
  99.5 44.6 %collective-permute-start.25 = (bf16[192,1536]{1,0:T(8,128)(2,1)S(1)}, bf16[192,1536]{1,0:T(8,128)(2,1)S(1)}, u32[]{:S(2)}, u32[]{:S(2)}) collective-permute-start(bf16[192,1536]{1,0:T(8,128)(2,1)S(1)} %fusion.33.refs_0_), channel_id=1, source_target_pairs={{0,2},{4,0},{8,4},{12,8},{14,12},{10,14},{6,10},{2,6},{1,3},{5,1},... | collective-permute-start | bytes 1769480 | tf_op jit(solution)/shard_map/ppermute | solution.py:47
  100.5 44.0 %collective-permute-start.21 = (bf16[192,1536]{1,0:T(8,128)(2,1)S(1)}, bf16[192,1536]{1,0:T(8,128)(2,1)S(1)}, u32[]{:S(2)}, u32[]{:S(2)}) collective-permute-start(bf16[192,1536]{1,0:T(8,128)(2,1)S(1)} %fusion.33.refs_0_), channel_id=1, source_target_pairs={{0,4},{4,8},{8,12},{12,14},{14,10},{10,6},{6,2},{2,0},{1,5},{5,9},... | collective-permute-start | bytes 1769480 | tf_op jit(solution)/shard_map/ppermute | solution.py:47
  118.3 25.7 %collective-permute-start.16 = (bf16[8,32,1024]{2,1,0:T(8,128)(2,1)}, bf16[8,32,1024]{2,1,0:T(8,128)(2,1)}, u32[]{:S(2)}, u32[]{:S(2)}) collective-permute-start(bf16[8,32,1024]{2,1,0:T(8,128)(2,1)} %bitcast_dynamic-update-slice_fusion.refs_0_), channel_id=1, source_target_pairs={{0,16},{16,0},{1,17},{17,1},{2,18},{18,2},{3,19},{19,3},{4,20},{20... | collective-permute-start | bytes 1572872 | tf_op jit(solution)/shard_map/ppermute | solution.py:42
  118.8 24.7 %collective-permute-start.13 = (bf16[256,1024]{1,0:T(8,128)(2,1)S(1)}, bf16[256,1024]{1,0:T(8,128)(2,1)}, u32[]{:S(2)}, u32[]{:S(2)}) collective-permute-start(bf16[256,1024]{1,0:T(8,128)(2,1)S(1)} %bitcast.367), channel_id=1, source_target_pairs={{0,16},{16,0},{1,17},{17,1},{2,18},{18,2},{3,19},{19,3},{4,20},{20... | collective-permute-start | bytes 1572872 | tf_op jit(solution)/shard_map/ppermute | solution.py:42
  138.8 17.9 %all-to-all-start.1 = ((bf16[8,256,128]{2,1,0:T(8,128)(2,1)}), bf16[8,256,128]{2,1,0:T(8,128)(2,1)S(1)}, u32[]{:S(2)}, u32[]{:S(2)}) async-start(bf16[8,256,128]{2,1,0:T(8,128)(2,1)} %get-tuple-element.104), calls=%async_computation.1 | async-start | bytes 1048576 | tf_op jit(solution)/shard_map/all_to_all | solution.py:56
  143.5 3.1 collective-permute-start.12
  143.5 6.0 %collective-permute-start.14 = (bf16[256,1024]{1,0:T(8,128)(2,1)}, bf16[256,1024]{1,0:T(8,128)(2,1)}, u32[]{:S(2)}, u32[]{:S(2)}) collective-permute-start(bf16[256,1024]{1,0:T(8,128)(2,1)} %collective-permute-done.13.ga.refs_6_), channel_id=1, source_target_pairs={{0,1},{1,0},{2,3},{3,2},{4,5},{5,4},{6,7},{7,6},{8,9},{9,8},{10,11... | collective-permute-start | bytes 1572872 | tf_op jit(solution)/shard_map/ppermute | solution.py:42
  144.0 12.7 %collective-permute-start.15 = (bf16[8,32,1024]{2,1,0:T(8,128)(2,1)}, bf16[8,32,1024]{2,1,0:T(8,128)(2,1)}, u32[]{:S(2)}, u32[]{:S(2)}) collective-permute-start(bf16[8,32,1024]{2,1,0:T(8,128)(2,1)} %bitcast_dynamic-update-slice_fusion.refs_0_), channel_id=1, source_target_pairs={{0,1},{1,0},{2,3},{3,2},{4,5},{5,4},{6,7},{7,6},{8,9},{9,8},{10,11... | collective-permute-start | bytes 1572872 | tf_op jit(solution)/shard_map/ppermute | solution.py:42
  144.1 12.6 %collective-permute-start.17 = (bf16[8,32,1024]{2,1,0:T(8,128)(2,1)}, bf16[8,32,1024]{2,1,0:T(8,128)(2,1)}, u32[]{:S(2)}, u32[]{:S(2)}) collective-permute-start(bf16[8,32,1024]{2,1,0:T(8,128)(2,1)} %collective-permute-done.16.refs_2_), channel_id=1, source_target_pairs={{0,1},{1,0},{2,3},{3,2},{4,5},{5,4},{6,7},{7,6},{8,9},{9,8},{10,11... | collective-permute-start | bytes 1572872 | tf_op jit(solution)/shard_map/ppermute | solution.py:42
  144.6 20.0 %collective-permute-start.26 = (bf16[192,1536]{1,0:T(8,128)(2,1)S(1)}, bf16[192,1536]{1,0:T(8,128)(2,1)S(1)}, u32[]{:S(2)}, u32[]{:S(2)}) collective-permute-start(bf16[192,1536]{1,0:T(8,128)(2,1)S(1)} %collective-permute-done.25.refs_8_), channel_id=1, source_target_pairs={{0,2},{4,0},{8,4},{12,8},{14,12},{10,14},{6,10},{2,6},{1,3},{5,1},... | collective-permute-start | bytes 1769480 | tf_op jit(solution)/shard_map/ppermute | solution.py:47
  147.4 17.2 %collective-permute-start.22 = (bf16[192,1536]{1,0:T(8,128)(2,1)S(1)}, bf16[192,1536]{1,0:T(8,128)(2,1)S(1)}, u32[]{:S(2)}, u32[]{:S(2)}) collective-permute-start(bf16[192,1536]{1,0:T(8,128)(2,1)S(1)} %collective-permute-done.21.refs_1_), channel_id=1, source_target_pairs={{0,4},{4,8},{8,12},{12,14},{14,10},{10,6},{6,2},{2,0},{1,5},{5,9},... | collective-permute-start | bytes 1769480 | tf_op jit(solution)/shard_map/ppermute | solution.py:47
  161.6 9.5 %collective-permute-start.30 = (bf16[256,1024]{1,0:T(8,128)(2,1)}, bf16[256,1024]{1,0:T(8,128)(2,1)}, u32[]{:S(2)}, u32[]{:S(2)}) collective-permute-start(bf16[256,1024]{1,0:T(8,128)(2,1)} %get-tuple-element.109.na.refs_0_), channel_id=1, source_target_pairs={{0,16},{16,0},{1,17},{17,1},{2,18},{18,2},{3,19},{19,3},{4,20},{20... | collective-permute-start | bytes 1572872 | tf_op jit(solution)/shard_map/ppermute | solution.py:42
  164.5 14.5 %collective-permute-start.27 = (bf16[192,1536]{1,0:T(8,128)(2,1)S(1)}, bf16[192,1536]{1,0:T(8,128)(2,1)S(1)}, u32[]{:S(2)}, u32[]{:S(2)}) collective-permute-start(bf16[192,1536]{1,0:T(8,128)(2,1)S(1)} %collective-permute-done.26.refs_7_), channel_id=1, source_target_pairs={{0,2},{4,0},{8,4},{12,8},{14,12},{10,14},{6,10},{2,6},{1,3},{5,1},... | collective-permute-start | bytes 1769480 | tf_op jit(solution)/shard_map/ppermute | solution.py:47
  164.6 15.2 %collective-permute-start.23 = (bf16[192,1536]{1,0:T(8,128)(2,1)S(1)}, bf16[192,1536]{1,0:T(8,128)(2,1)S(1)}, u32[]{:S(2)}, u32[]{:S(2)}) collective-permute-start(bf16[192,1536]{1,0:T(8,128)(2,1)S(1)} %collective-permute-done.22.refs_2_), channel_id=1, source_target_pairs={{0,4},{4,8},{8,12},{12,14},{14,10},{10,6},{6,2},{2,0},{1,5},{5,9},... | collective-permute-start | bytes 1769480 | tf_op jit(solution)/shard_map/ppermute | solution.py:47
  171.1 20.8 %collective-permute-start.31 = (bf16[256,1024]{1,0:T(8,128)(2,1)}, bf16[256,1024]{1,0:T(8,128)(2,1)}, u32[]{:S(2)}, u32[]{:S(2)}) collective-permute-start(bf16[256,1024]{1,0:T(8,128)(2,1)} %collective-permute-done.30.na.refs_2_), channel_id=1, source_target_pairs={{0,1},{1,0},{2,3},{3,2},{4,5},{5,4},{6,7},{7,6},{8,9},{9,8},{10,11... | collective-permute-start | bytes 1572872 | tf_op jit(solution)/shard_map/ppermute | solution.py:42
  179.1 6.9 %collective-permute-start.28 = (bf16[96,1536]{1,0:T(8,128)(2,1)S(1)}, bf16[96,1536]{1,0:T(8,128)(2,1)}, u32[]{:S(2)}, u32[]{:S(2)}) collective-permute-start(bf16[96,1536]{1,0:T(8,128)(2,1)S(1)} %slice.434), channel_id=1, source_target_pairs={{0,2},{4,0},{8,4},{12,8},{14,12},{10,14},{6,10},{2,6},{1,3},{5,1},... | collective-permute-start | bytes 884744 | tf_op jit(solution)/shard_map/ppermute | solution.py:47
  179.8 7.4 %collective-permute-start.24 = (bf16[96,1536]{1,0:T(8,128)(2,1)S(1)}, bf16[96,1536]{1,0:T(8,128)(2,1)}, u32[]{:S(2)}, u32[]{:S(2)}) collective-permute-start(bf16[96,1536]{1,0:T(8,128)(2,1)S(1)} %slice.433), channel_id=1, source_target_pairs={{0,4},{4,8},{8,12},{12,14},{14,10},{10,6},{6,2},{2,0},{1,5},{5,9},... | collective-permute-start | bytes 884744 | tf_op jit(solution)/shard_map/ppermute | solution.py:47
  191.8 11.3 %collective-permute-start.18 = (bf16[256,1024]{1,0:T(8,128)(2,1)}, bf16[256,1024]{1,0:T(8,128)(2,1)S(1)}, u32[]{:S(2)}, u32[]{:S(2)}) collective-permute-start(bf16[256,1024]{1,0:T(8,128)(2,1)} %get-tuple-element.109.na.refs_0_), channel_id=1, source_target_pairs={{0,1},{1,0},{2,3},{3,2},{4,5},{5,4},{6,7},{7,6},{8,9},{9,8},{10,11... | collective-permute-start | bytes 1572872 | tf_op jit(solution)/shard_map/ppermute | solution.py:42
  202.0 11.0 %collective-permute-start.32 = (bf16[256,1024]{1,0:T(8,128)(2,1)S(1)}, bf16[256,1024]{1,0:T(8,128)(2,1)S(1)}, u32[]{:S(2)}, u32[]{:S(2)}) collective-permute-start(bf16[256,1024]{1,0:T(8,128)(2,1)S(1)} %slice_bitcast_fusion.4), channel_id=1, source_target_pairs={{0,1},{1,0},{2,3},{3,2},{4,5},{5,4},{6,7},{7,6},{8,9},{9,8},{10,11... | collective-permute-start | bytes 1572872 | tf_op jit(solution)/shard_map/ppermute | solution.py:42
  213.2 13.9 %collective-permute-start.33 = (bf16[256,1024]{1,0:T(8,128)(2,1)S(1)}, bf16[256,1024]{1,0:T(8,128)(2,1)S(1)}, u32[]{:S(2)}, u32[]{:S(2)}) collective-permute-start(bf16[256,1024]{1,0:T(8,128)(2,1)S(1)} %fusion.27), channel_id=1, source_target_pairs={{0,16},{16,0},{1,17},{17,1},{2,18},{18,2},{3,19},{19,3},{4,20},{20... | collective-permute-start | bytes 1572872 | tf_op jit(solution)/shard_map/ppermute | solution.py:42
  215.1 15.6 %collective-permute-start.29 = (bf16[256,1024]{1,0:T(8,128)(2,1)S(1)}, bf16[256,1024]{1,0:T(8,128)(2,1)S(1)}, u32[]{:S(2)}, u32[]{:S(2)}) collective-permute-start(bf16[256,1024]{1,0:T(8,128)(2,1)S(1)} %get-tuple-element.205), channel_id=1, source_target_pairs={{0,1},{1,0},{2,3},{3,2},{4,5},{5,4},{6,7},{7,6},{8,9},{9,8},{10,11... | collective-permute-start | bytes 1572872 | tf_op jit(solution)/shard_map/ppermute | solution.py:42
  228.6 8.7 %collective-permute-start.35 = (bf16[96,1536]{1,0:T(8,128)(2,1)S(1)}, bf16[96,1536]{1,0:T(8,128)(2,1)S(1)}, u32[]{:S(2)}, u32[]{:S(2)}) collective-permute-start(bf16[96,1536]{1,0:T(8,128)(2,1)S(1)} %get-tuple-element.188), channel_id=1, source_target_pairs={{0,2},{4,0},{8,4},{12,8},{14,12},{10,14},{6,10},{2,6},{1,3},{5,1},... | collective-permute-start | bytes 884744 | tf_op jit(solution)/shard_map/ppermute | solution.py:47
  229.9 8.7 %collective-permute-start.34 = (bf16[96,1536]{1,0:T(8,128)(2,1)S(1)}, bf16[96,1536]{1,0:T(8,128)(2,1)}, u32[]{:S(2)}, u32[]{:S(2)}) collective-permute-start(bf16[96,1536]{1,0:T(8,128)(2,1)S(1)} %get-tuple-element.190), channel_id=1, source_target_pairs={{0,4},{4,8},{8,12},{12,14},{14,10},{10,6},{6,2},{2,0},{1,5},{5,9},... | collective-permute-start | bytes 884744 | tf_op jit(solution)/shard_map/ppermute | solution.py:47
  242.5 6.3 %collective-permute-start.36 = (bf16[1,2,8,32,1024]{4,3,2,1,0:T(8,128)(2,1)S(1)}, bf16[1,2,8,32,1024]{4,3,2,1,0:T(8,128)(2,1)}, u32[]{:S(2)}, u32[]{:S(2)}) collective-permute-start(bf16[1,2,8,32,1024]{4,3,2,1,0:T(8,128)(2,1)S(1)} %fusion.15), channel_id=1, source_target_pairs={{0,1},{1,0},{2,3},{3,2},{4,5},{5,4},{6,7},{7,6},{8,9},{9,8},{10,11... | collective-permute-start | bytes 3145736 | tf_op jit(solution)/shard_map/ppermute | solution.py:42
  242.6 31.0 %all-to-all-start.2 = ((bf16[8,256,128]{2,1,0:T(8,128)(2,1)}), bf16[8,256,128]{2,1,0:T(8,128)(2,1)}, u32[]{:S(2)}, u32[]{:S(2)}) async-start(bf16[8,256,128]{2,1,0:T(8,128)(2,1)} %get-tuple-element.136), calls=%async_computation.2 | async-start | bytes 1048576 | tf_op jit(solution)/shard_map/all_to_all | solution.py:56
  246.8 22.3 %collective-permute-start.38 = (bf16[192,1536]{1,0:T(8,128)(2,1)}, bf16[192,1536]{1,0:T(8,128)(2,1)S(1)}, u32[]{:S(2)}, u32[]{:S(2)}) collective-permute-start(bf16[192,1536]{1,0:T(8,128)(2,1)} %pad_maximum_fusion.4), channel_id=1, source_target_pairs={{0,4},{4,8},{8,12},{12,14},{14,10},{10,6},{6,2},{2,0},{1,5},{5,9},... | collective-permute-start | bytes 1769480 | tf_op jit(solution)/shard_map/ppermute | solution.py:47
  248.8 22.2 %collective-permute-start.39 = (bf16[192,1536]{1,0:T(8,128)(2,1)}, bf16[192,1536]{1,0:T(8,128)(2,1)S(1)}, u32[]{:S(2)}, u32[]{:S(2)}) collective-permute-start(bf16[192,1536]{1,0:T(8,128)(2,1)} %pad_maximum_fusion.5), channel_id=1, source_target_pairs={{0,2},{4,0},{8,4},{12,8},{14,12},{10,14},{6,10},{2,6},{1,3},{5,1},... | collective-permute-start | bytes 1769480 | tf_op jit(solution)/shard_map/ppermute | solution.py:47
  250.8 21.8 %collective-permute-start.37 = (bf16[1,8,32,1024]{3,2,1,0:T(8,128)(2,1)S(1)}, bf16[1,8,32,1024]{3,2,1,0:T(8,128)(2,1)S(1)}, u32[]{:S(2)}, u32[]{:S(2)}) collective-permute-start(bf16[1,8,32,1024]{3,2,1,0:T(8,128)(2,1)S(1)} %fusion.36), channel_id=1, source_target_pairs={{0,16},{16,0},{1,17},{17,1},{2,18},{18,2},{3,19},{19,3},{4,20},{20... | collective-permute-start | bytes 1572872 | tf_op jit(solution)/shard_map/ppermute | solution.py:42
  273.6 31.4 %collective-permute-start.40 = (bf16[192,1536]{1,0:T(8,128)(2,1)S(1)}, bf16[192,1536]{1,0:T(8,128)(2,1)S(1)}, u32[]{:S(2)}, u32[]{:S(2)}) collective-permute-start(bf16[192,1536]{1,0:T(8,128)(2,1)S(1)} %get-tuple-element.148), channel_id=1, source_target_pairs={{0,4},{4,8},{8,12},{12,14},{14,10},{10,6},{6,2},{2,0},{1,5},{5,9},... | collective-permute-start | bytes 1769480 | tf_op jit(solution)/shard_map/ppermute | solution.py:47
  277.9 27.1 %collective-permute-start.41 = (bf16[192,1536]{1,0:T(8,128)(2,1)S(1)}, bf16[192,1536]{1,0:T(8,128)(2,1)S(1)}, u32[]{:S(2)}, u32[]{:S(2)}) collective-permute-start(bf16[192,1536]{1,0:T(8,128)(2,1)S(1)} %get-tuple-element.149), channel_id=1, source_target_pairs={{0,2},{4,0},{8,4},{12,8},{14,12},{10,14},{6,10},{2,6},{1,3},{5,1},... | collective-permute-start | bytes 1769480 | tf_op jit(solution)/shard_map/ppermute | solution.py:47
  305.0 8.7 %collective-permute-start.42 = (bf16[2,8,256,128]{3,2,1,0:T(8,128)(2,1)}, bf16[2,8,256,128]{3,2,1,0:T(8,128)(2,1)S(1)}, u32[]{:S(2)}, u32[]{:S(2)}) collective-permute-start(bf16[2,8,256,128]{3,2,1,0:T(8,128)(2,1)} %get-tuple-element.152), channel_id=1, source_target_pairs={{0,1},{1,0},{2,3},{3,2},{4,5},{5,4},{6,7},{7,6},{8,9},{9,8},{10,11... | collective-permute-start | bytes 3145736 | tf_op jit(solution)/shard_map/ppermute | solution.py:42
  307.4 17.1 %collective-permute-start.43 = (bf16[192,1536]{1,0:T(8,128)(2,1)}, bf16[192,1536]{1,0:T(8,128)(2,1)S(1)}, u32[]{:S(2)}, u32[]{:S(2)}) collective-permute-start(bf16[192,1536]{1,0:T(8,128)(2,1)} %get-tuple-element.156), channel_id=1, source_target_pairs={{0,4},{4,8},{8,12},{12,14},{14,10},{10,6},{6,2},{2,0},{1,5},{5,9},... | collective-permute-start | bytes 1769480 | tf_op jit(solution)/shard_map/ppermute | solution.py:47
  309.5 16.4 %collective-permute-start.44 = (bf16[192,1536]{1,0:T(8,128)(2,1)S(1)}, bf16[192,1536]{1,0:T(8,128)(2,1)S(1)}, u32[]{:S(2)}, u32[]{:S(2)}) collective-permute-start(bf16[192,1536]{1,0:T(8,128)(2,1)S(1)} %get-tuple-element.157), channel_id=1, source_target_pairs={{0,2},{4,0},{8,4},{12,8},{14,12},{10,14},{6,10},{2,6},{1,3},{5,1},... | collective-permute-start | bytes 1769480 | tf_op jit(solution)/shard_map/ppermute | solution.py:47
  309.5 30.8 %all-to-all-start.3 = ((bf16[8,32,1024]{2,1,0:T(8,128)(2,1)}), bf16[8,32,1024]{2,1,0:T(8,128)(2,1)S(1)}, u32[]{:S(2)}, u32[]{:S(2)}) async-start(bf16[8,32,1024]{2,1,0:T(8,128)(2,1)} %fusion.37), calls=%async_computation.3 | async-start | bytes 1048576 | tf_op jit(solution)/shard_map/all_to_all | solution.py:56
  327.1 11.8 %collective-permute-start.46 = (bf16[128,1024]{1,0:T(8,128)(2,1)S(1)}, bf16[128,1024]{1,0:T(8,128)(2,1)S(1)}, u32[]{:S(2)}, u32[]{:S(2)}) collective-permute-start(bf16[128,1024]{1,0:T(8,128)(2,1)S(1)} %get-tuple-element.198), channel_id=1, source_target_pairs={{0,2},{4,0},{8,4},{12,8},{14,12},{10,14},{6,10},{2,6},{1,3},{5,1},... | collective-permute-start | bytes 786440 | tf_op jit(solution)/shard_map/ppermute | solution.py:47
  327.8 11.1 %collective-permute-start.45 = (bf16[128,1024]{1,0:T(8,128)(2,1)S(1)}, bf16[128,1024]{1,0:T(8,128)(2,1)S(1)}, u32[]{:S(2)}, u32[]{:S(2)}) collective-permute-start(bf16[128,1024]{1,0:T(8,128)(2,1)S(1)} %get-tuple-element.200), channel_id=1, source_target_pairs={{0,4},{4,8},{8,12},{12,14},{14,10},{10,6},{6,2},{2,0},{1,5},{5,9},... | collective-permute-start | bytes 786440 | tf_op jit(solution)/shard_map/ppermute | solution.py:47
  346.1 5.7 %collective-permute-start.47 = (bf16[1,2,8,32,384]{4,3,2,1,0:T(8,128)(2,1)}, bf16[1,2,8,32,384]{4,3,2,1,0:T(8,128)(2,1)}, u32[]{:S(2)}, u32[]{:S(2)}) collective-permute-start(bf16[1,2,8,32,384]{4,3,2,1,0:T(8,128)(2,1)} %fusion.41), channel_id=1, source_target_pairs={{0,1},{1,0},{2,3},{3,2},{4,5},{5,4},{6,7},{7,6},{8,9},{9,8},{10,11... | collective-permute-start | bytes 1179656 | tf_op jit(solution)/shard_map/ppermute | solution.py:42
  347.5 15.2 %collective-permute-start.49 = (bf16[256,1024]{1,0:T(8,128)(2,1)S(1)}, bf16[256,1024]{1,0:T(8,128)(2,1)S(1)}, u32[]{:S(2)}, u32[]{:S(2)}) collective-permute-start(bf16[256,1024]{1,0:T(8,128)(2,1)S(1)} %pad_maximum_fusion.6), channel_id=1, source_target_pairs={{0,4},{4,8},{8,12},{12,14},{14,10},{10,6},{6,2},{2,0},{1,5},{5,9},... | collective-permute-start | bytes 1572872 | tf_op jit(solution)/shard_map/ppermute | solution.py:47
  350.9 14.2 %collective-permute-start.50 = (bf16[256,1024]{1,0:T(8,128)(2,1)S(1)}, bf16[256,1024]{1,0:T(8,128)(2,1)S(1)}, u32[]{:S(2)}, u32[]{:S(2)}) collective-permute-start(bf16[256,1024]{1,0:T(8,128)(2,1)S(1)} %pad_maximum_fusion.7), channel_id=1, source_target_pairs={{0,2},{4,0},{8,4},{12,8},{14,12},{10,14},{6,10},{2,6},{1,3},{5,1},... | collective-permute-start | bytes 1572872 | tf_op jit(solution)/shard_map/ppermute | solution.py:47
  353.0 14.7 %collective-permute-start.48 = (bf16[1,8,32,384]{3,2,1,0:T(8,128)(2,1)S(1)}, bf16[1,8,32,384]{3,2,1,0:T(8,128)(2,1)S(1)}, u32[]{:S(2)}, u32[]{:S(2)}) collective-permute-start(bf16[1,8,32,384]{3,2,1,0:T(8,128)(2,1)S(1)} %fusion.47), channel_id=1, source_target_pairs={{0,16},{16,0},{1,17},{17,1},{2,18},{18,2},{3,19},{19,3},{4,20},{20... | collective-permute-start | bytes 589832 | tf_op jit(solution)/shard_map/ppermute | solution.py:42
  369.9 13.7 %all-to-all-start.4 = ((bf16[8,32,384]{2,1,0:T(8,128)(2,1)}), bf16[8,32,384]{2,1,0:T(8,128)(2,1)S(1)}, u32[]{:S(2)}, u32[]{:S(2)}) async-start(bf16[8,32,384]{2,1,0:T(8,128)(2,1)} %fusion.48), calls=%async_computation.4 | async-start | bytes 393216 | tf_op jit(solution)/shard_map/all_to_all | solution.py:56
  378.1 5.2 %collective-permute-start.58 = (bf16[2,32,1536]{2,1,0:T(8,128)(2,1)S(1)}, bf16[2,32,1536]{2,1,0:T(8,128)(2,1)S(1)}, u32[]{:S(2)}, u32[]{:S(2)}) collective-permute-start(bf16[2,32,1536]{2,1,0:T(8,128)(2,1)S(1)} %fusion.49), channel_id=1, source_target_pairs={{0,1},{1,0},{2,3},{3,2},{4,5},{5,4},{6,7},{7,6},{8,9},{9,8},{10,11... | collective-permute-start | bytes 589832 | tf_op jit(solution)/shard_map/ppermute | solution.py:42
  379.9 34.8 %collective-permute-start.51 = (bf16[256,1024]{1,0:T(8,128)(2,1)}, bf16[256,1024]{1,0:T(8,128)(2,1)}, u32[]{:S(2)}, u32[]{:S(2)}) collective-permute-start(bf16[256,1024]{1,0:T(8,128)(2,1)} %slice_bitcast_fusion.2), channel_id=1, source_target_pairs={{0,1},{1,0},{2,3},{3,2},{4,5},{5,4},{6,7},{7,6},{8,9},{9,8},{10,11... | collective-permute-start | bytes 1572872 | tf_op jit(solution)/shard_map/ppermute | solution.py:42
  380.5 20.6 %collective-permute-start.52 = (bf16[256,1024]{1,0:T(8,128)(2,1)}, bf16[256,1024]{1,0:T(8,128)(2,1)}, u32[]{:S(2)}, u32[]{:S(2)}) collective-permute-start(bf16[256,1024]{1,0:T(8,128)(2,1)} %slice_bitcast_fusion), channel_id=1, source_target_pairs={{0,1},{1,0},{2,3},{3,2},{4,5},{5,4},{6,7},{7,6},{8,9},{9,8},{10,11... | collective-permute-start | bytes 1572872 | tf_op jit(solution)/shard_map/ppermute | solution.py:42
  380.5 14.8 %collective-permute-start.54 = (bf16[256,1024]{1,0:T(8,128)(2,1)}, bf16[256,1024]{1,0:T(8,128)(2,1)}, u32[]{:S(2)}, u32[]{:S(2)}) collective-permute-start(bf16[256,1024]{1,0:T(8,128)(2,1)} %get-tuple-element.167), channel_id=1, source_target_pairs={{0,4},{4,8},{8,12},{12,14},{14,10},{10,6},{6,2},{2,0},{1,5},{5,9},... | collective-permute-start | bytes 1572872 | tf_op jit(solution)/shard_map/ppermute | solution.py:47
  382.5 14.3 %collective-permute-start.56 = (bf16[256,1024]{1,0:T(8,128)(2,1)}, bf16[256,1024]{1,0:T(8,128)(2,1)}, u32[]{:S(2)}, u32[]{:S(2)}) collective-permute-start(bf16[256,1024]{1,0:T(8,128)(2,1)} %get-tuple-element.168), channel_id=1, source_target_pairs={{0,2},{4,0},{8,4},{12,8},{14,12},{10,14},{6,10},{2,6},{1,3},{5,1},... | collective-permute-start | bytes 1572872 | tf_op jit(solution)/shard_map/ppermute | solution.py:47
  383.5 7.0 %collective-permute-start.59 = (bf16[2,32,1536]{2,1,0:T(8,128)(2,1)S(1)}, bf16[2,32,1536]{2,1,0:T(8,128)(2,1)S(1)}, u32[]{:S(2)}, u32[]{:S(2)}) collective-permute-start(bf16[2,32,1536]{2,1,0:T(8,128)(2,1)S(1)} %fusion.46), channel_id=1, source_target_pairs={{0,16},{16,0},{1,17},{17,1},{2,18},{18,2},{3,19},{19,3},{4,20},{20... | collective-permute-start | bytes 589832 | tf_op jit(solution)/shard_map/ppermute | solution.py:42
  398.8 13.2 %collective-permute-start.55 = (bf16[256,1024]{1,0:T(8,128)(2,1)S(1)}, bf16[256,1024]{1,0:T(8,128)(2,1)S(1)}, u32[]{:S(2)}, u32[]{:S(2)}) collective-permute-start(bf16[256,1024]{1,0:T(8,128)(2,1)S(1)} %get-tuple-element.193), channel_id=1, source_target_pairs={{0,4},{4,8},{8,12},{12,14},{14,10},{10,6},{6,2},{2,0},{1,5},{5,9},... | collective-permute-start | bytes 1572872 | tf_op jit(solution)/shard_map/ppermute | solution.py:47
  400.3 12.8 %collective-permute-start.57 = (bf16[256,1024]{1,0:T(8,128)(2,1)S(1)}, bf16[256,1024]{1,0:T(8,128)(2,1)S(1)}, u32[]{:S(2)}, u32[]{:S(2)}) collective-permute-start(bf16[256,1024]{1,0:T(8,128)(2,1)S(1)} %get-tuple-element.194), channel_id=1, source_target_pairs={{0,2},{4,0},{8,4},{12,8},{14,12},{10,14},{6,10},{2,6},{1,3},{5,1},... | collective-permute-start | bytes 1572872 | tf_op jit(solution)/shard_map/ppermute | solution.py:47
  402.4 12.6 %collective-permute-start.53 = (bf16[256,1024]{1,0:T(8,128)(2,1)S(1)}, bf16[256,1024]{1,0:T(8,128)(2,1)S(1)}, u32[]{:S(2)}, u32[]{:S(2)}) collective-permute-start(bf16[256,1024]{1,0:T(8,128)(2,1)S(1)} %fusion.21), channel_id=1, source_target_pairs={{0,16},{16,0},{1,17},{17,1},{2,18},{18,2},{3,19},{19,3},{4,20},{20... | collective-permute-start | bytes 1572872 | tf_op jit(solution)/shard_map/ppermute | solution.py:42
  (54 other events, 589.2 us)

commit v2 on v1

--- a/solution.py
+++ b/solution.py
@@ -147,10 +147,11 @@
 
 
 def attend_kernel(
-    tab, q_ref, own_ref, oth_ref, segq_ref, sego_ref, segt_ref, idx_ref, ck_ref, cv_ref,
-    o_ref, low_ref, lse_ref, mem_ref,
+    begin, tab, q_ref, own_ref, oth_ref, segq_ref, sego_ref, segt_ref, idx_ref, ck_ref, cv_ref,
+    *rest,
 ):
-    i = pl.program_id(0)
+    o_ref, low_ref, lse_ref, mem_ref = rest[-4:]
+    i = pl.program_id(0) + begin
     parity = tab[40]
     count = q_ref.shape[1]
     q = q_ref[0]
@@ -220,20 +221,21 @@
     lse_ref[0] = top + jnp.log2(total)
 
 
-def attend(tab, q, own, oth, segq, sego, segt, idx, ck, cv):
+def attend(tab, q, own, oth, segq, sego, segt, idx, ck, cv, begin, held):
     count = q.shape[1]
-    block = pl.BlockSpec((1, count, HEAD_DIM), lambda i, t: (i, 0, 0))
-    thin = pl.BlockSpec((1, count, 1), lambda i, t: (i, 0, 0))
+    block = pl.BlockSpec((1, count, HEAD_DIM), lambda i, t: (i + begin, 0, 0))
+    thin = pl.BlockSpec((1, count, 1), lambda i, t: (i + begin, 0, 0))
     whole = pl.BlockSpec((2, HEADS, count, HEAD_DIM), lambda i, t: (0, 0, 0, 0))
     segs = pl.BlockSpec((HEADS, 1, count), lambda i, t: (0, 0, 0))
     cache = pl.BlockSpec((ck.shape[0], HEAD_DIM), lambda i, t: (0, t[41]))
-    mem = pl.BlockSpec((2, 1, count, HEAD_DIM), lambda i, t: (0, i, 0, 0))
+    mem = pl.BlockSpec((2, 1, count, HEAD_DIM), lambda i, t: (0, i + begin, 0, 0))
     return pl.pallas_call(
-        attend_kernel,
+        functools.partial(attend_kernel, begin),
         grid_spec=pltpu.PrefetchScalarGridSpec(
             num_scalar_prefetch=1,
-            grid=(HEADS,),
-            in_specs=[block, whole, whole, thin, segs, segs, thin, cache, cache],
+            grid=(HEADS // 2,),
+            in_specs=[block, whole, whole, thin, segs, segs, thin, cache, cache]
+            + [pl.BlockSpec(memory_space=pl.ANY)] * len(held),
             out_specs=[block, block, thin, mem],
         ),
         out_shape=[
@@ -242,11 +244,12 @@
             jax.ShapeDtypeStruct((HEADS, count, 1), WIDE),
             jax.ShapeDtypeStruct((2, HEADS, count, HEAD_DIM), LOW),
         ],
+        input_output_aliases={10 + i: i for i in range(len(held))},
         cost_estimate=pl.CostEstimate(
-            flops=25 * 10**9, bytes_accessed=6 * 2**20, transcendentals=3 * 10**6
-        ),
-        name="attend",
-    )(tab, q, own, oth, segq, sego, segt, idx, ck, cv)
+            flops=12 * 10**9, bytes_accessed=4 * 2**20, transcendentals=2 * 10**6
+        ),
+        name=f"attend{begin}",
+    )(tab, q, own, oth, segq, sego, segt, idx, ck, cv, *held)
 
 
 def attend_back_kernel(
@@ -440,14 +443,16 @@
     )(chips, *blocks)
 
 
-def ffn_kernel(na, nb, ga, gb, g_ref, u_ref, d_ref, hid_ref, gg_ref, ug_ref, dn_ref):
+def ffn_kernel(na, nb, ga, gb, g_ref, u_ref, d_ref, hid_ref, gg_ref, ug_ref, dn_ref, out_ref):
     for t, (n_ref, c_ref) in enumerate(((na, ga), (nb, gb))):
         n = n_ref[...]
         gate = dot_nn(n, g_ref[...])
         upper = dot_nn(n, u_ref[...])
         sigma = jax.nn.sigmoid(gate)
         silu = gate * sigma
-        hid_ref[t] = (silu * upper).astype(LOW)
+        hid = (silu * upper).astype(LOW)
+        hid_ref[t] = hid
+        out_ref[t] = dot_nn(hid, d_ref[...]).astype(LOW)
         hg = dot_nt(c_ref[...], d_ref[...])
         gg = (hg * upper * sigma * (1.0 + gate * (1.0 - sigma))).astype(LOW)
         ug = (hg * silu).astype(LOW)
@@ -462,11 +467,11 @@
     return pl.pallas_call(
         ffn_kernel,
         in_specs=[vmem()] * 7,
-        out_specs=[vmem()] * 4,
+        out_specs=[vmem()] * 5,
         out_shape=[jax.ShapeDtypeStruct((2, count, units), LOW)] * 3
-        + [jax.ShapeDtypeStruct((2, count, D), LOW)],
+        + [jax.ShapeDtypeStruct((2, count, D), LOW)] * 2,
         cost_estimate=pl.CostEstimate(
-            flops=20 * count * D * units,
+            flops=24 * count * D * units,
             bytes_accessed=6 * D * units + 16 * count * D,
             transcendentals=2 * count * units,
         ),
@@ -502,11 +507,12 @@
                 )
                 parts_ref[slot, here, start : start + units] = total[first : first + rows]
     total = dot_tn(tokens(hid_l, hid_r), up)
-    deep = parts_ref.shape[1] - 2 * rows
+    strip = wide - D
     for h in range(HEADS):
-        for i, piece in enumerate(fold(total[h * share : (h + 1) * share], deep)):
-            columns = slice(i * D // 2, (i + 1) * D // 2)
-            parts_ref[tab[h], 2 * rows :, columns] = piece.astype(LOW)
+        slot = tab[h]
+        piece = total[h * share : (h + 1) * share].astype(LOW)
+        parts_ref[slot, 2 * rows : 2 * rows + share, :D] = piece
+        parts_ref[slot, 2 * rows : 2 * rows + share, D:] = jnp.zeros((share, strip), LOW)
 
 
 def weight_grads(slot_of, ns, ups, near, away, height, wide):
@@ -522,6 +528,28 @@
         ),
         name="weight_grads",
     )(slot_of, *ns, *ups, *near, *away)
+
+
+def strips_kernel(tab, out_ref, strips_ref):
+    rows, strip = out_ref.shape[1], strips_ref.shape[2]
+    for slot in range(HEADS):
+        for i in range(D // strip):
+            strips_ref[slot, i * rows : (i + 1) * rows, :] = out_ref[
+                tab[slot], :, i * strip : (i + 1) * strip
+            ]
+
+
+def out_strips(chips, out, strip):
+    return pl.pallas_call(
+        strips_kernel,
+        in_specs=[smem(), vmem()],
+        out_specs=vmem(),
+        out_shape=jax.ShapeDtypeStruct((HEADS, out.shape[1] * D // strip, strip), LOW),
+        cost_estimate=pl.CostEstimate(
+            flops=0, bytes_accessed=4 * HEADS * out.shape[1] * D, transcendentals=0
+        ),
+        name="out_strips",
+    )(chips, out)
 
 
 def mid_kernel(mid_ref, pa, pb, pc, up_ref, gain_ref, w_ref, mg_ref, bg_ref, ag_ref):
@@ -558,7 +586,8 @@
     )(mid, pa, pb, pc, up, gain, w)
 
 
-def qkv_back_kernel(tab, dq_ref, own_ref, got_ref, cos_ref, sin_ref, w_ref, dx_ref, g_ref):
+def qkv_back_kernel(tab, dq_ref, own_ref, got_ref, cos_ref, sin_ref, n_ref, w_ref, dx_ref, dw_ref, sum_ref):
+    i = pl.program_id(0)
     c, s = cos_ref[0], sin_ref[0]
 
     def rot(v):
@@ -568,14 +597,27 @@
     dk = rot((own_ref[0, 0] + got_ref[0, 0].astype(WIDE)) * SCALE).astype(LOW)
     dv = (own_ref[1, 0] + got_ref[1, 0].astype(WIDE)).astype(LOW)
     grads = jnp.concatenate([dq, dk, dv], axis=1)
-    g_ref[0] = grads
     dx_ref[0] = dot_nt(grads, w_ref[...]).astype(LOW)
-
-
-def qkv_back(chips, dq, own, got, cos, sin, w):
+    part = dot_tn(n_ref[0], grads)
+
+    @pl.when(i == 0)
+    def _():
+        sum_ref[...] = part
+
+    @pl.when(i > 0)
+    def _():
+        sum_ref[...] += part
+
+    @pl.when(i == HEADS - 1)
+    def _():
+        dw_ref[...] = sum_ref[...].astype(LOW)
+
+
+def qkv_back(chips, dq, own, got, cos, sin, normed, w):
     count = dq.shape[1]
     block = pl.BlockSpec((1, count, HEAD_DIM), lambda i, t: (t[i], 0, 0))
     pair = pl.BlockSpec((2, 1, count, HEAD_DIM), lambda i, t: (0, t[i], 0, 0))
+    weight = pl.BlockSpec((D, 3 * HEAD_DIM), lambda i, t: (0, 0))
     return pl.pallas_call(
         qkv_back_kernel,
         grid_spec=pltpu.PrefetchScalarGridSpec(
@@ -583,24 +625,23 @@
             grid=(HEADS,),
             in_specs=[
                 block, pair, pair, block, block,
-                pl.BlockSpec((D, 3 * HEAD_DIM), lambda i, t: (0, 0)),
+                pl.BlockSpec((1, count, D), lambda i, t: (t[i], 0, 0)),
+                weight,
             ],
-            out_specs=[
-                pl.BlockSpec((1, count, D), lambda i, t: (i, 0, 0)),
-                pl.BlockSpec((1, count, 3 * HEAD_DIM), lambda i, t: (t[i], 0, 0)),
-            ],
+            out_specs=[pl.BlockSpec((1, count, D), lambda i, t: (i, 0, 0)), weight],
+            scratch_shapes=[pltpu.VMEM((D, 3 * HEAD_DIM), WIDE)],
         ),
         out_shape=[
             jax.ShapeDtypeStruct((HEADS, count, D), LOW),
-            jax.ShapeDtypeStruct((HEADS, count, 3 * HEAD_DIM), LOW),
+            jax.ShapeDtypeStruct((D, 3 * HEAD_DIM), LOW),
         ],
         cost_estimate=pl.CostEstimate(
-            flops=2 * HEADS * count * D * 3 * HEAD_DIM,
-            bytes_accessed=4 * HEADS * count * D,
+            flops=4 * HEADS * count * D * 3 * HEAD_DIM,
+            bytes_accessed=6 * HEADS * count * D,
             transcendentals=0,
         ),
         name="qkv_back",
-    )(chips, dq, own, got, cos, sin, w)
+    )(chips, dq, own, got, cos, sin, normed, w)
 
 
 def local(
@@ -671,14 +712,14 @@
         forth.append(turn(forth[-1], 1))
         back.append(turn(back[-1], -1))
         if step == 1:
-            got, forth[-1], back[-1], parity = lax.optimization_barrier(
+            _, forth[-1], back[-1], parity = lax.optimization_barrier(
                 (got, forth[-1], back[-1], core)
             )
     far_first, far_last = turn(forth[-1][:split], 1), turn(back[-1][split:], -1)
     x_slots = [((v, count),) for v in forth] + [((far_first, split), (far_last, count - split))]
     x_slots += [((v, count),) for v in back[:0:-1]]
     outs = [v[count:] for v in forth] + [far_last[count - split :]]
-    outs = jnp.stack(outs + [v[count:] for v in back[:0:-1]])
+    outs += [v[count:] for v in back[:0:-1]]
     got_c = swap(got, "c")
     got_y = swap(got, "dl")
     got_yc = swap(got_y, "c")
@@ -762,16 +803,12 @@
         deep = share
         lower = jnp.pad(down_weight, ((0, 0), (0, wide - D)))
     bundle = jnp.concatenate([gu, lower], axis=0)
-    height = 4 * rows + deep
+    height = 4 * rows + share
     if far > 1:
         bundle = lax.all_gather(bundle, "dh", axis=0, tiled=True)
     upper = bundle.shape[0] // 2
     bundle, *_ = lax.optimization_barrier((bundle, far_first, far_last))
-    forth, back = [bundle], [bundle]
-    for step in range(HEADS // 2 - 1):
-        forth.append(turn(forth[-1], 1))
-        back.append(turn(back[-1], -1))
-    w_slots = forth + [turn(forth[-1][:upper], 1), turn(back[-1][upper:], -1)] + back[:0:-1]
+    forth, back = [bundle, turn(bundle, 1)], [bundle, turn(bundle, -1)]
 
     held = ()
     for order in ([0, 1, 7, 2, 6], [3, 5, 4]):
@@ -785,18 +822,17 @@
             held,
         )
     queries, own, normed_one = held
-    outs_c = swap(outs, "c")
-    outs_y = swap(outs, "dl")
-    outs_yc = swap(outs_y, "c")
     other = swap(own, "c")
-    up_late, _ = lax.optimization_barrier((upstream, own))
-    up_c = swap(up_late, "c")
-    up_y = swap(up_late, "dl")
-    up_yc = swap(up_y, "c")
-
     seg_thin = seg_own.reshape(HEADS, count, 1)
     seg_own_row = seg_own.reshape(HEADS, 1, count)
     seg_oth_row = seg_oth.reshape(HEADS, 1, count)
+    cached = [cache[0].reshape(-1, D) for cache in (cache_keys, cache_values)]
+    half_attended = attend(
+        tab, queries, own, other, seg_thin, seg_own_row, seg_oth_row, idx, *cached, 0, ()
+    )
+    first_lse, forth[1], back[1] = lax.optimization_barrier(
+        (half_attended[2], forth[1], back[1])
+    )
     attention, attention_low, lse, memory = attend(
         tab,
         queries,
@@ -806,12 +842,31 @@
         seg_own_row,
         seg_oth_row,
         idx,
-        cache_keys[0].reshape(-1, D),
-        cache_values[0].reshape(-1, D),
-    )
-
+        *cached,
+        HEADS // 2,
+        (*half_attended[:2], first_lse, half_attended[3]),
+    )
+    w_forth, w_back = turn(forth[1], 1), turn(back[1], -1)
+    attention_low, w_forth, w_back = lax.optimization_barrier((attention_low, w_forth, w_back))
+    forth.append(w_forth)
+    back.append(w_back)
+
+    *outs, up_late, _ = lax.optimization_barrier((*outs, upstream, attention_low))
+    up_c = swap(up_late, "c")
+    up_y = swap(up_late, "dl")
+    up_yc = swap(up_y, "c")
+    outs = jnp.stack(outs)
+    outs_c = swap(outs, "c")
+    outs_y = swap(outs, "dl")
+    outs_yc = swap(outs_y, "c")
     heads = exchange(attention_low)
-    heads, up_c, up_y, up_yc = lax.optimization_barrier((heads, up_c, up_y, up_yc))
+    w_forth, w_back = turn(w_forth, 1), turn(w_back, -1)
+    heads, w_forth, w_back, up_c, up_y, up_yc = lax.optimization_barrier(
+        (heads, w_forth, w_back, up_c, up_y, up_yc)
+    )
+    forth.append(w_forth)
+    back.append(w_back)
+    w_first, w_last = turn(w_forth[:upper], 1), turn(w_back[upper:], -1)
     slot_of = lax.rem(mine - jnp.asarray(PLACE, jnp.int32) + HEADS, HEADS).astype(jnp.int32)
     if far == 1:
         sources = [outs, outs_c, outs_y, outs_yc]
@@ -823,6 +878,8 @@
         sources = [sources.reshape(D, D)]
     where = jnp.concatenate([chips, jnp.stack([pair, core])]).astype(jnp.int32)
     attended, mid, normed_two, out_w = out_block(where, heads, sources, x, gain_two)
+    normed_two, w_first, w_last = lax.optimization_barrier((normed_two, w_first, w_last))
+    w_slots = forth + [w_first, w_last] + back[:0:-1]
 
     if far == 1:
         gate_w, up_w, down_w = weights(where, w_slots, units)
@@ -838,8 +895,9 @@
     n_c = swap(normed_two, "c")
     n_y = swap(normed_two, "dl")
     n_yc = swap(n_y, "c")
-    hid_l, gg_l, ug_l, dn_l = ffn(normed_two, n_c, upstream, up_c, gate_w, up_w, down_w)
-    hid_r, gg_r, ug_r, dn_r = ffn(n_y, n_yc, up_y, up_yc, gate_w, up_w, down_w)
+    hid_l, gg_l, ug_l, dn_l, out_l = ffn(normed_two, n_c, upstream, up_c, gate_w, up_w, down_w)
+    n_y, n_yc, dn_l = lax.optimization_barrier((n_y, n_yc, dn_l))
+    hid_r, gg_r, ug_r, dn_r, out_r = ffn(n_y, n_yc, up_y, up_yc, gate_w, up_w, down_w)
 
     def to_away(away):
         return (away[0].astype(WIDE) + swap(away[1], "c").astype(WIDE)).astype(LOW)
@@ -872,6 +930,12 @@
         down = jnp.pad(down, ((0, 0), (0, 0), (0, 0), (0, wide - D)))
         parts = jnp.concatenate([gu, down], axis=2)
         parts = jnp.take(parts.reshape(HEADS, far * height, wide), chips, axis=0)
+
+    out_l, out_r, _ = lax.optimization_barrier((out_l, out_r, parts))
+    output = mid
+    for part in (out_l[0], swap(out_l[1], "c"), swap(to_away(out_r), "dl")):
+        output = output + part.astype(WIDE)
+    output = output.astype(LOW)
 
     sums = [dn_l[0], swap(dn_l[1], "c"), swap(there, "dl")]
     sums[2], parts = lax.optimization_barrier((sums[2], parts))
@@ -913,53 +977,61 @@
             w = lax.psum_scatter(w, "dh", scatter_dimension=0, tiled=True)
         return w[0]
 
-    blocks = [parts[slot] for slot in range(HEADS)]
-    forth, back = ring_first(blocks, upper)
-    branch, forth, back = lax.optimization_barrier((branch, forth, back))
     out_part = over_owner(
         jnp.einsum("td,te->de", attended, branch, preferred_element_type=WIDE).astype(LOW), D
     )
+    strip = wide - D
+    upper = 4 * rows if far == 1 else parts.shape[1] // 2
+    blocks = [parts[slot].astype(WIDE) for slot in range(HEADS)]
+    if far == 1:
+        strips = out_strips(where, out_part, strip)
+        below = share - strips.shape[1]
+        for slot in range(HEADS):
+            if slot != HEADS // 2:
+                blocks[slot] = blocks[slot] + jnp.pad(
+                    strips[slot].astype(WIDE), ((4 * rows, below), (D, 0))
+                )
+        out_far = turn(strips[HEADS // 2], HEADS // 2)
+    else:
+        out_far = exchange(out_part)
+    forth, back = ring_first(blocks, upper)
+    ups, forth, back = lax.optimization_barrier((ups, forth, back))
     forth, back = ring_next(blocks, forth, back, 2)
-    ups, out_part, forth, back = lax.optimization_barrier((ups, out_part, forth, back))
-    forth, back = ring_next(blocks, forth, back, 3)
 
     dq, d_own, d_oth = attend_back(
         tab, queries, ups, attention, lse, own, other, memory, seg_thin, seg_own_row, seg_oth_row
     )
     d_got = swap(d_oth, "c")
-    dq, forth, back = lax.optimization_barrier((dq, forth, back))
-    dx, grads = qkv_back(chips.astype(jnp.int32), dq, d_own, d_got, cosine, sine, w_qkv)
-    out_part = exchange(out_part)
-    forth, back = turn(forth, 1), turn(back, -1)
-    dx, forth, back = lax.optimization_barrier((dx, forth, back))
+    dq, out_far, forth, back = lax.optimization_barrier((dq, out_far, forth, back))
+    dx, dw = qkv_back(
+        chips.astype(jnp.int32), dq, d_own, d_got, cosine, sine, normed_one, w_qkv
+    )
+    arrived_forth, arrived_back = turn(forth, 1), turn(back, -1)
+    dx, arrived_forth, arrived_back = lax.optimization_barrier((dx, arrived_forth, arrived_back))
     dx_forth, dx_back = ring_first(dx, split)
-    grads, out_part, dx_forth, dx_back = lax.optimization_barrier(
-        (grads, out_part, dx_forth, dx_back)
-    )
-    out_w_grad = jnp.sum(out_part.astype(WIDE), axis=0)
-
-    dw = jnp.einsum("std,stg->dg", normed_one, grads, preferred_element_type=WIDE).astype(LOW)
+    dx_forth, dx_back, arrived_forth, arrived_back = lax.optimization_barrier(
+        (dx_forth, dx_back, arrived_forth, arrived_back)
+    )
+    forth = plus(blocks[HEADS - 1], arrived_forth, 0)
+    back = plus(blocks[1], arrived_back, 0)
+
     dw = over_owner(dw, 3 * HEAD_DIM)
     dx_forth, dx_back = ring_next(dx, dx_forth, dx_back, 2)
-    dw, hid_l, hid_r, dx_forth, dx_back, forth, back = lax.optimization_barrier(
-        (dw, hid_l, hid_r, dx_forth, dx_back, forth, back)
-    )
+    dw, dx_forth, dx_back = lax.optimization_barrier((dw, dx_forth, dx_back))
     qkv_grads = exchange(dw).astype(WIDE)
     dx_forth, dx_back = ring_next(dx, dx_forth, dx_back, 3)
     normed_one_grad = ring_last(dx, turn(dx_forth, 1), turn(dx_back, -1))
 
-    summed = ring_last(blocks, forth, back).astype(LOW)
+    summed = ring_last(blocks, turn(forth, 1), turn(back, -1)).astype(LOW)
     if far > 1:
         summed = lax.psum_scatter(summed, "dh", scatter_dimension=0, tiled=True)
-    lower = summed[4 * rows :].astype(WIDE)
+    down_w_grad = summed[4 * rows : 4 * rows + share, :D].astype(WIDE)
     if far == 1:
-        half_d = D // 2
-        rest = share - deep
-        left = jnp.concatenate([lower[:, :half_d], lower[:rest, half_d:D]], axis=0)
-        right = jnp.concatenate([lower[rest:, half_d:D], lower[: 2 * rest, D:]], axis=0)
-        down_w_grad = jnp.concatenate([left, right], axis=1)
+        out_w_grad = summed[4 * rows : 4 * rows + strips.shape[1], D:].astype(WIDE)
+        out_w_grad = out_w_grad + out_far.astype(WIDE)
+        out_w_grad = out_w_grad.reshape(D // strip, rows, strip).transpose(1, 0, 2).reshape(rows, D)
     else:
-        down_w_grad = lower[:, :D]
+        out_w_grad = jnp.sum(out_far.astype(WIDE), axis=0)
     gu = summed[: 4 * rows].reshape(2, 2, rows, wide)
     kept = pick(core, gu[:, 0], gu[:, 1])
     came = swap(pick(core, gu[:, 1], gu[:, 0]), "c")
@@ -975,13 +1047,6 @@
         .astype(WIDE)
     )
     gate_w_grad, up_w_grad = gu[0], gu[1]
-
-    out_l = jnp.einsum("gtf,fd->gtd", hid_l, down_w, preferred_element_type=WIDE).astype(LOW)
-    out_r = jnp.einsum("gtf,fd->gtd", hid_r, down_w, preferred_element_type=WIDE).astype(LOW)
-    output = mid
-    for part in (out_l[0], swap(out_l[1], "c"), swap(to_away(out_r), "dl")):
-        output = output + part.astype(WIDE)
-    output = output.astype(LOW)
 
     wide_x = x.astype(WIDE)
     r = lax.rsqrt(jnp.mean(wide_x * wide_x, axis=-1, keepdims=True) + EPSILON)

time: 426 us -> 417 us (0.979)
  Pallas kernels: 112 us -> 123 us
  waiting for transfers between devices: 126 us -> 115 us
  matrix products: 9.25 us -> 1.78 us
    ppermute x32 -> x33, waiting for transfers between devices: 109 us -> 65.5 us  [turn(): return lax.ppermute(block, 'h', route)]
    ppermute x28, waiting for transfers between devices: 9.26 us -> 45.8 us  [swap(): return lax.ppermute(block, axis, [(0, 1), (1, 0)])]
    dot_general x3 -> x0, matrix products: 8.51 us -> none  [the longest x1 5.03 us: local(): jnp.einsum('std,stg->dg', normed_one, grads, preferred_element_type=WIDE)]
    pallas_call x3 -> x5, Pallas kernels: 36.7 us -> 44.5 us  [the longest x2 22 us: attend(): pl.pallas_call(functools.partial(attend_kernel, begin), grid_spec=pltpu.P...]
    unnamed x122 -> x168, local copies, waits for them, and re-layouts: 16.6 us -> 9.35 us
    slice x6 -> x12, local copies, waits for them, and re-layouts: 0.07 us -> 5.76 us  [the longest x6 2.12 us: local(): outs = [v[count:] for v in forth] + [far_last[count - split:]]]
    all_to_all x5 -> x4, starting transfers between devices: 22.7 us -> 17.8 us  [exchange(): return lax.all_to_all(blocks, 'h', 0, 0)]
    ppermute x28, starting transfers between devices: 10 us -> 14.7 us  [swap(): return lax.ppermute(block, axis, [(0, 1), (1, 0)])]
  transfers between devices with their start and end apart: 65 -> 65, of which waited for: 28 -> 34; matrix products, arithmetic and copies ran while one was open for 17% -> 18% of each run, Pallas kernels for 25% -> 25%
where the time goes in v2:
time: 417 us; the launch traced here: 412 us
  Pallas kernels  123 us (29%)
  waiting for transfers between devices  115 us (28%)
  starting transfers between devices  80.6 us (19%)
  other arithmetic  51.9 us (12%)
  local copies, waits for them, and re-layouts  37.5 us (9%)
    ppermute x33, waiting for transfers between devices, turn(): return lax.ppermute(block, 'h', route)  65.5 us
    ppermute x33, starting transfers between devices, turn(): return lax.ppermute(block, 'h', route)  48.1 us
    ppermute x28, waiting for transfers between devices, swap(): return lax.ppermute(block, axis, [(0, 1), (1, 0)])  45.8 us
    pallas_call x1, Pallas kernels, attend_back(): pl.pallas_call(attend_back_kernel, grid_spec=pltpu.PrefetchScalarGridSpec...  27.2 us
    pallas_call x2, Pallas kernels, attend(): pl.pallas_call(functools.partial(attend_kernel, begin), grid_spec=pltpu.P...  22 us
    pallas_call x2, Pallas kernels, ffn(): pl.pallas_call(ffn_kernel, in_specs=[vmem()] * 7, out_specs=[vmem()] * 5,...  20.6 us
    all_to_all x4, starting transfers between devices, exchange(): return lax.all_to_all(blocks, 'h', 0, 0)  17.8 us
    ppermute x28, starting transfers between devices, swap(): return lax.ppermute(block, axis, [(0, 1), (1, 0)])  14.7 us
  transfers between devices with their start and end apart: 65, of which 34 were waited for; matrix products, arithmetic and copies ran while one was open for 18% of the time, Pallas kernels for 25%

profile of v2, /device:TPU:0, one launch (start us, length us, event | category | flops | bytes accessed | tf_op | source)
XLA Modules:
  0.0 411.8 jit_solution(6420287405809296156)
XLA Ops:
  1.9 3.0 collective-permute-start.1
  7.6 10.8 %collective-permute-done.1.refs_2_ = bf16[288,1024]{1,0:T(8,128)(2,1)S(1)} collective-permute-done((bf16[288,1024]{1,0:T(8,128)(2,1)S(1)}, bf16[288,1024]{1,0:T(8,128)(2,1)S(1)}, u32[]{:S(2)}, u32[]{:S(2)}) %collective-permute-start.1) | collective-permute-done | bytes 589856 | tf_op jit(solution)/shard_map/ppermute | solution.py:47
  22.4 4.9 %all-to-all-start = ((bf16[8,112,128]{2,1,0:T(8,128)(2,1)}), bf16[8,112,128]{2,1,0:T(8,128)(2,1)S(1)}, u32[]{:S(2)}, u32[]{:S(2)}) async-start(bf16[8,112,128]{2,1,0:T(8,128)(2,1)} %copy.276), calls=%async_computation | async-start | bytes 458752 | tf_op jit(solution)/shard_map/all_to_all | solution.py:56
  27.3 1.6 collective-permute-start.13
  30.7 2.0 collective-permute-start.3
  34.5 2.0 all-to-all-done
  36.6 1.9 collective-permute-start.9
  38.6 6.1 %collective-permute-done.9 = bf16[8,112,128]{2,0,1:T(8,128)(2,1)S(1)} collective-permute-done((bf16[8,112,128]{2,0,1:T(8,128)(2,1)S(1)}, bf16[8,112,128]{2,0,1:T(8,128)(2,1)S(1)}, u32[]{:S(2)}, u32[]{:S(2)}) %collective-permute-start.9) | collective-permute-done | bytes 229408 | tf_op jit(solution)/shard_map/ppermute | solution.py:42
  53.2 9.1 %collective-permute-done.4.refs_0_ = bf16[288,1024]{1,0:T(8,128)(2,1)S(1)} collective-permute-done((bf16[288,1024]{1,0:T(8,128)(2,1)}, bf16[288,1024]{1,0:T(8,128)(2,1)S(1)}, u32[]{:S(2)}, u32[]{:S(2)}) %collective-permute-start.4) | collective-permute-done | bytes 589856 | tf_op jit(solution)/shard_map/ppermute | solution.py:47
  64.9 3.7 fusion.46
  68.7 1.9 pad_maximum_fusion
  70.6 8.1 %qkv5.1 = (bf16[8,256,128]{2,1,0:T(8,128)(2,1)}, bf16[2,8,256,128]{3,2,1,0:T(8,128)(2,1)}, bf16[8,256,1024]{2,1,0:T(8,128)(2,1)}) custom-call(s32[5]{0:T(128)} %compare_select_fusion.8.tab, bf16[288,1024]{1,0:T(8,128)(2,1)} %copy-done.5, bf16[288,1024]{1,0:T(8,128)(2,1)} %copy-done.19, bf16[288,1024]{1,0:T(8,128)(2,1)} %copy-done.18, ...), custom_call_target="tpu_custom_call" | custom-call | flops 1006632960 | bytes 6553600 | tf_op jit(solution)/shard_map/qkv5/pallas_call | solution.py:126
  79.6 6.1 %qkv3.1 = (bf16[8,256,128]{2,1,0:T(8,128)(2,1)}, bf16[2,8,256,128]{3,2,1,0:T(8,128)(2,1)}, bf16[8,256,1024]{2,1,0:T(8,128)(2,1)}) custom-call(s32[3]{0:T(128)} %compare_select_fusion.9.tab, bf16[288,1024]{1,0:T(8,128)(2,1)} %copy-done.10, bf16[288,1024]{1,0:T(8,128)(2,1)} %copy-done.7, ...), custom_call_target="tpu_custom_call", output_to_operand_aliasing={{0}: (9, {}), {1}: (10, {}), {2}: (11, {})} | custom-call | flops 603979776 | bytes 3932160 | tf_op jit(solution)/shard_map/qkv3/pallas_call | solution.py:126
  96.2 11.8 %collective-permute-start.14 = (bf16[192,1536]{1,0:T(8,128)(2,1)S(1)}, bf16[192,1536]{1,0:T(8,128)(2,1)S(1)}, u32[]{:S(2)}, u32[]{:S(2)}) collective-permute-start(bf16[192,1536]{1,0:T(8,128)(2,1)S(1)} %fusion.35.refs_0_), channel_id=1, source_target_pairs={{0,4},{4,8},{8,12},{12,14},{14,10},{10,6},{6,2},{2,0},{1,5},{5,9},... | collective-permute-start | bytes 1769480 | tf_op jit(solution)/shard_map/ppermute | solution.py:47
  108.0 9.7 %attend0.1 = (f32[8,256,128]{2,1,0:T(8,128)}, bf16[8,256,128]{2,1,0:T(8,128)(2,1)}, f32[8,256,1]{2,1,0:T(8,128)}, bf16[2,8,256,128]{3,2,1,0:T(8,128)(2,1)}) custom-call(s32[42]{0:T(128)} %concatenate.88.tab, bf16[8,256,128]{2,1,0:T(8,128)(2,1)} %get-tuple-element.123.q_ref, bf16[2,8,256,128]{3,2,1,0:T(8,128)(2,1)} %get-tuple-element.124.own_ref, ...), custom_call_target="tpu_custom_call" | custom-call | flops 12000000000 | bytes 4194304 | tf_op jit(solution)/shard_map/attend0/pallas_call | solution.py:232
  117.7 5.0 %collective-permute-done.14.refs_1_ = bf16[192,1536]{1,0:T(8,128)(2,1)S(1)} collective-permute-done((bf16[192,1536]{1,0:T(8,128)(2,1)S(1)}, bf16[192,1536]{1,0:T(8,128)(2,1)S(1)}, u32[]{:S(2)}, u32[]{:S(2)}) %collective-permute-start.14) | collective-permute-done | bytes 589856 | tf_op jit(solution)/shard_map/ppermute | solution.py:47
  124.8 12.3 %attend4.1 = (f32[8,256,128]{2,1,0:T(8,128)}, bf16[8,256,128]{2,1,0:T(8,128)(2,1)}, f32[8,256,1]{2,1,0:T(8,128)}, bf16[2,8,256,128]{3,2,1,0:T(8,128)(2,1)}) custom-call(s32[42]{0:T(128)} %concatenate.88.tab, bf16[8,256,128]{2,1,0:T(8,128)(2,1)} %get-tuple-element.123.q_ref, ...), custom_call_target="tpu_custom_call", output_to_operand_aliasing={{0}: (10, {}), {1}: (11, {}), {2}: (12, {}), {3}: (13, {})} | custom-call | flops 12000000000 | bytes 4194304 | tf_op jit(solution)/shard_map/attend4/pallas_call | solution.py:232
  137.8 5.0 %all-to-all-start.1 = ((bf16[8,256,128]{2,1,0:T(8,128)(2,1)}), bf16[8,256,128]{2,1,0:T(8,128)(2,1)S(1)}, u32[]{:S(2)}, u32[]{:S(2)}) async-start(bf16[8,256,128]{2,1,0:T(8,128)(2,1)} %get-tuple-element.136), calls=%async_computation.1 | async-start | bytes 1048576 | tf_op jit(solution)/shard_map/all_to_all | solution.py:56
  146.7 2.0 collective-permute-start.18
  148.7 9.8 %collective-permute-done.21.ga.refs_6_ = bf16[256,1024]{1,0:T(8,128)(2,1)} collective-permute-done((bf16[256,1024]{1,0:T(8,128)(2,1)S(1)}, bf16[256,1024]{1,0:T(8,128)(2,1)}, u32[]{:S(2)}, u32[]{:S(2)}) %collective-permute-start.21) | collective-permute-done | bytes 524320 | tf_op jit(solution)/shard_map/ppermute | solution.py:42
  158.5 8.1 %collective-permute-done.24.refs_2_ = bf16[8,32,1024]{2,1,0:T(8,128)(2,1)S(1)} collective-permute-done((bf16[8,32,1024]{2,1,0:T(8,128)(2,1)S(1)}, bf16[8,32,1024]{2,1,0:T(8,128)(2,1)S(1)}, u32[]{:S(2)}, u32[]{:S(2)}) %collective-permute-start.24) | collective-permute-done | bytes 524320 | tf_op jit(solution)/shard_map/ppermute | solution.py:42
  169.0 1.7 collective-permute-start.27
  173.2 4.0 out_block.1
  177.2 1.5 collective-permute-done.27.refs_5_
  181.6 12.0 %collective-permute-done.29.na.refs_2_ = bf16[256,1024]{1,0:T(8,128)(2,1)S(1)} collective-permute-done((bf16[256,1024]{1,0:T(8,128)(2,1)}, bf16[256,1024]{1,0:T(8,128)(2,1)S(1)}, u32[]{:S(2)}, u32[]{:S(2)}) %collective-permute-start.29) | collective-permute-done | bytes 524320 | tf_op jit(solution)/shard_map/ppermute | solution.py:42
  193.6 4.8 %weights.1 = (bf16[1024,704]{1,0:T(8,128)(2,1)}, bf16[1024,704]{1,0:T(8,128)(2,1)}, bf16[704,1024]{1,0:T(8,128)(2,1)}) custom-call(s32[10]{0:T(128)} %pad_add_fusion.tab, bf16[192,1536]{1,0:T(8,128)(2,1)} %copy-done.4, bf16[192,1536]{1,0:T(8,128)(2,1)} %copy-done.25, bf16[192,1536]{1,0:T(8,128)(2,1)} %copy-done.26, bf16[192,1536]{1,0:T(8,128)(2,1)} %copy-done.11, ...), custom_call_target="tpu_custom_call" | custom-call | bytes 8650752 | tf_op jit(solution)/shard_map/weights/pallas_call | solution.py:429
  199.2 10.3 %ffn.2 = (bf16[2,256,704]{2,1,0:T(8,128)(2,1)}, bf16[2,256,704]{2,1,0:T(8,128)(2,1)}, bf16[2,256,704]{2,1,0:T(8,128)(2,1)}, bf16[2,256,1024]{2,1,0:T(8,128)(2,1)}, bf16[2,256,1024]{2,1,0:T(8,128)(2,1)}) custom-call(bf16[256,1024]{1,0:T(8,128)(2,1)} %get-tuple-element.153.na.refs_0_, bf16[256,1024]{1,0:T(8,128)(2,1)} %copy-done.71, ...), custom_call_target="tpu_custom_call" | custom-call | flops 4429185024 | bytes 8519680 | tf_op jit(solution)/shard_map/ffn/pallas_call | solution.py:467
  210.3 10.3 %ffn.3 = (bf16[2,256,704]{2,1,0:T(8,128)(2,1)}, bf16[2,256,704]{2,1,0:T(8,128)(2,1)}, bf16[2,256,704]{2,1,0:T(8,128)(2,1)}, bf16[2,256,1024]{2,1,0:T(8,128)(2,1)}, bf16[2,256,1024]{2,1,0:T(8,128)(2,1)}) custom-call(bf16[256,1024]{1,0:T(8,128)(2,1)} %copy-done.70, bf16[256,1024]{1,0:T(8,128)(2,1)} %copy-done.72, ...), custom_call_target="tpu_custom_call" | custom-call | flops 4429185024 | bytes 8519680 | tf_op jit(solution)/shard_map/ffn/pallas_call | solution.py:467
  226.0 11.0 %weight_grads.1 = bf16[8,216,1536]{2,1,0:T(8,128)(2,1)} custom-call(s32[8]{0:T(128)} %compare_select_fusion.tab, bf16[256,1024]{1,0:T(8,128)(2,1)} %get-tuple-element.153.na.refs_0_, bf16[256,1024]{1,0:T(8,128)(2,1)} %copy-done.71, bf16[256,1024]{1,0:T(8,128)(2,1)} %copy-done.70, bf16[256,1024]{1,0:T(8,128)(2,1)} %copy-done.72, bf16[256,1024]{1,0:T(8,128)(2,1)} %bitcast.357, ...), custom_call_target="tpu_custom_call" | custom-call | flops 4429185024 | bytes 14680064 | tf_op jit(solution)/shard_map/weight_grads/pallas_call | solution.py:521
  239.3 4.7 %mid_block.1 = (f32[256,1024]{1,0:T(8,128)}, bf16[256,1024]{1,0:T(8,128)(2,1)}, bf16[8,256,128]{2,1,0:T(8,128)(2,1)}) custom-call(f32[256,1024]{1,0:T(8,128)} %get-tuple-element.149.mid_ref, bf16[256,1024]{1,0:T(8,128)(2,1)} %get-tuple-element.246.pa, bf16[256,1024]{1,0:T(8,128)(2,1)} %copy-done.28, bf16[256,1024]{1,0:T(8,128)(2,1)} %copy-done.29, ...), custom_call_target="tpu_custom_call" | custom-call | flops 536870912 | bytes 6291456 | tf_op jit(solution)/shard_map/mid_block/pallas_call | solution.py:573
  243.9 1.8 convolution_convert_fusion
  246.1 2.6 collective-permute-done.37
  248.7 1.8 convert_add_fusion
  253.0 1.5 collective-permute-start.40
  256.2 4.5 %all-to-all-start.2 = ((bf16[8,256,128]{2,1,0:T(8,128)(2,1)}), bf16[8,256,128]{2,1,0:T(8,128)(2,1)S(1)}, u32[]{:S(2)}, u32[]{:S(2)}) async-start(bf16[8,256,128]{2,1,0:T(8,128)(2,1)} %get-tuple-element.187), calls=%async_computation.2 | async-start | bytes 1048576 | tf_op jit(solution)/shard_map/all_to_all | solution.py:56
  260.7 3.9 collective-permute-done.38
  264.7 2.6 fusion.38.out_ref
  267.3 1.9 out_strips.1
  269.2 1.8 slice_bitcast_fusion.18
  270.9 1.6 convert_add_fusion.6
  275.8 3.3 collective-permute-start.42
  280.4 27.2 %attend_back.1 = (f32[8,256,128]{2,1,0:T(8,128)}, f32[2,8,256,128]{3,2,1,0:T(8,128)}, bf16[2,8,256,128]{3,2,1,0:T(8,128)(2,1)}) custom-call(s32[42]{0:T(128)} %concatenate.88.tab, bf16[8,256,128]{2,1,0:T(8,128)(2,1)} %get-tuple-element.123.q_ref, bf16[8,256,128]{2,1,0:T(8,128)(2,1)} %copy-done.30, f32[8,256,128]{2,1,0:T(8,128)} %get-tuple-element.192.o_ref, ...), custom_call_target="tpu_custom_call" | custom-call | flops 30000001024 | bytes 10485760 | tf_op jit(solution)/shard_map/attend_back/pallas_call | solution.py:314
  310.5 2.9 fusion.8
  313.4 3.5 collective-permute-done.41
  317.5 2.2 collective-permute-start.46
  319.7 12.8 %qkv_back.1 = (bf16[8,256,1024]{2,1,0:T(8,128)(2,1)}, bf16[1024,384]{1,0:T(8,128)(2,1)}) custom-call(s32[8]{0:T(128)} %copy-done.67, f32[8,256,128]{2,1,0:T(8,128)} %get-tuple-element.198.dq_ref, f32[2,8,256,128]{3,2,1,0:T(8,128)} %get-tuple-element.199.own_ref, bf16[2,8,256,128]{3,2,1,0:T(8,128)(2,1)} %collective-permute-done.44.got_ref, ...), custom_call_target="tpu_custom_call" | custom-call | flops 3221225472 | bytes 12582912 | tf_op jit(solution)/shard_map/qkv_back/pallas_call | solution.py:621
  335.0 1.6 collective-permute-start.34
  337.9 2.0 collective-permute-start.50
  340.7 5.6 %collective-permute-done.50 = bf16[128,1024]{1,0:T(8,128)(2,1)S(1)} collective-permute-done((bf16[128,1024]{1,0:T(8,128)(2,1)S(1)}, bf16[128,1024]{1,0:T(8,128)(2,1)S(1)}, u32[]{:S(2)}, u32[]{:S(2)}) %collective-permute-start.50) | collective-permute-done | bytes 262176 | tf_op jit(solution)/shard_map/ppermute | solution.py:47
  346.4 1.6 collective-permute-done.49
  349.7 1.7 collective-permute-start.52
  351.4 2.8 fusion.3
  354.5 1.7 collective-permute-start.58
  356.2 2.2 fusion.39
  359.2 5.0 %collective-permute-done.51 = bf16[256,1024]{1,0:T(8,128)(2,1)S(1)} collective-permute-done((bf16[256,1024]{1,0:T(8,128)(2,1)S(1)}, bf16[256,1024]{1,0:T(8,128)(2,1)S(1)}, u32[]{:S(2)}, u32[]{:S(2)}) %collective-permute-start.51) | collective-permute-done | bytes 524320 | tf_op jit(solution)/shard_map/ppermute | solution.py:47
  364.5 2.4 fusion.19
  366.8 3.4 all-to-all-start.3
  370.2 1.9 collective-permute-start.53
  372.3 6.9 %collective-permute-done.57 = bf16[216,1536]{1,0:T(8,128)(2,1)S(1)} collective-permute-done((bf16[216,1536]{1,0:T(8,128)(2,1)}, bf16[216,1536]{1,0:T(8,128)(2,1)S(1)}, u32[]{:S(2)}, u32[]{:S(2)}) %collective-permute-start.57) | collective-permute-done | bytes 663584 | tf_op jit(solution)/shard_map/ppermute | solution.py:47
  380.4 1.5 fusion.6
  391.2 2.9 fusion.21
  400.6 5.7 %collective-permute-done.54 = bf16[256,1024]{1,0:T(8,128)(2,1)S(1)} collective-permute-done((bf16[256,1024]{1,0:T(8,128)(2,1)}, bf16[256,1024]{1,0:T(8,128)(2,1)S(1)}, u32[]{:S(2)}, u32[]{:S(2)}) %collective-permute-start.54) | collective-permute-done | bytes 524320 | tf_op jit(solution)/shard_map/ppermute | solution.py:47
  407.7 1.5 fusion.14
  409.2 2.4 fusion.17
  (397 shorter events, 95.2 us)
Async XLA Ops:
  1.9 16.4 %collective-permute-start.1 = (bf16[288,1024]{1,0:T(8,128)(2,1)S(1)}, bf16[288,1024]{1,0:T(8,128)(2,1)S(1)}, u32[]{:S(2)}, u32[]{:S(2)}) collective-permute-start(bf16[288,1024]{1,0:T(8,128)(2,1)S(1)} %pad_maximum_fusion.5.refs_0_), channel_id=1, source_target_pairs={{0,2},{4,0},{8,4},{12,8},{14,12},{10,14},{6,10},{2,6},{1,3},{5,1},... | collective-permute-start | bytes 1769480 | tf_op jit(solution)/shard_map/ppermute | solution.py:47
  4.9 14.8 %collective-permute-start = (bf16[288,1024]{1,0:T(8,128)(2,1)S(1)}, bf16[288,1024]{1,0:T(8,128)(2,1)S(1)}, u32[]{:S(2)}, u32[]{:S(2)}) collective-permute-start(bf16[288,1024]{1,0:T(8,128)(2,1)S(1)} %pad_maximum_fusion.5.refs_0_), channel_id=1, source_target_pairs={{0,4},{4,8},{8,12},{12,14},{14,10},{10,6},{6,2},{2,0},{1,5},{5,9},... | collective-permute-start | bytes 1769480 | tf_op jit(solution)/shard_map/ppermute | solution.py:47
  21.5 5.7 %collective-permute-start.12 = (bf16[2,32,1536]{2,1,0:T(8,128)(2,1)S(1)}, bf16[2,32,1536]{2,1,0:T(8,128)(2,1)S(1)}, u32[]{:S(2)}, u32[]{:S(2)}) collective-permute-start(bf16[2,32,1536]{2,1,0:T(8,128)(2,1)S(1)} %select_bitcast_fusion.2), channel_id=1, source_target_pairs={{0,1},{1,0},{2,3},{3,2},{4,5},{5,4},{6,7},{7,6},{8,9},{9,8},{10,11... | collective-permute-start | bytes 589832 | tf_op jit(solution)/shard_map/ppermute | solution.py:42
  22.4 14.1 %all-to-all-start = ((bf16[8,112,128]{2,1,0:T(8,128)(2,1)}), bf16[8,112,128]{2,1,0:T(8,128)(2,1)S(1)}, u32[]{:S(2)}, u32[]{:S(2)}) async-start(bf16[8,112,128]{2,1,0:T(8,128)(2,1)} %copy.276), calls=%async_computation | async-start | bytes 458752 | tf_op jit(solution)/shard_map/all_to_all | solution.py:56
  27.3 7.1 %collective-permute-start.13 = (bf16[2,32,1536]{2,1,0:T(8,128)(2,1)S(1)}, bf16[2,32,1536]{2,1,0:T(8,128)(2,1)S(1)}, u32[]{:S(2)}, u32[]{:S(2)}) collective-permute-start(bf16[2,32,1536]{2,1,0:T(8,128)(2,1)S(1)} %get-tuple-element.264), channel_id=1, source_target_pairs={{0,16},{16,0},{1,17},{17,1},{2,18},{18,2},{3,19},{19,3},{4,20},{20... | collective-permute-start | bytes 589832 | tf_op jit(solution)/shard_map/ppermute | solution.py:42
  30.7 16.1 %collective-permute-start.3 = (bf16[288,1024]{1,0:T(8,128)(2,1)S(1)}, bf16[288,1024]{1,0:T(8,128)(2,1)}, u32[]{:S(2)}, u32[]{:S(2)}) collective-permute-start(bf16[288,1024]{1,0:T(8,128)(2,1)S(1)} %collective-permute-done.refs_1_), channel_id=1, source_target_pairs={{0,4},{4,8},{8,12},{12,14},{14,10},{10,6},{6,2},{2,0},{1,5},{5,9},... | collective-permute-start | bytes 1769480 | tf_op jit(solution)/shard_map/ppermute | solution.py:47
  33.4 15.0 %collective-permute-start.5 = (bf16[288,1024]{1,0:T(8,128)(2,1)S(1)}, bf16[288,1024]{1,0:T(8,128)(2,1)}, u32[]{:S(2)}, u32[]{:S(2)}) collective-permute-start(bf16[288,1024]{1,0:T(8,128)(2,1)S(1)} %collective-permute-done.1.refs_2_), channel_id=1, source_target_pairs={{0,2},{4,0},{8,4},{12,8},{14,12},{10,14},{6,10},{2,6},{1,3},{5,1},... | collective-permute-start | bytes 1769480 | tf_op jit(solution)/shard_map/ppermute | solution.py:47
  36.5 12.6 %collective-permute-start.2 = (bf16[8,112,128]{2,0,1:T(8,128)(2,1)S(1)}, bf16[8,112,128]{2,0,1:T(8,128)(2,1)S(1)}, u32[]{:S(2)}, u32[]{:S(2)}) collective-permute-start(bf16[8,112,128]{2,0,1:T(8,128)(2,1)S(1)} %copy.343), channel_id=1, source_target_pairs={{0,1},{1,0},{2,3},{3,2},{4,5},{5,4},{6,7},{7,6},{8,9},{9,8},{10,11... | collective-permute-start | bytes 688136 | tf_op jit(solution)/shard_map/ppermute | solution.py:42
  36.6 8.1 %collective-permute-start.9 = (bf16[8,112,128]{2,0,1:T(8,128)(2,1)S(1)}, bf16[8,112,128]{2,0,1:T(8,128)(2,1)S(1)}, u32[]{:S(2)}, u32[]{:S(2)}) collective-permute-start(bf16[8,112,128]{2,0,1:T(8,128)(2,1)S(1)} %copy.343), channel_id=1, source_target_pairs={{0,16},{16,0},{1,17},{17,1},{2,18},{18,2},{3,19},{19,3},{4,20},{20... | collective-permute-start | bytes 688136 | tf_op jit(solution)/shard_map/ppermute | solution.py:42
  44.7 4.4 %collective-permute-start.10 = (bf16[8,112,128]{2,0,1:T(8,128)(2,1)S(1)}, bf16[8,112,128]{2,0,1:T(8,128)(2,1)}, u32[]{:S(2)}, u32[]{:S(2)}) collective-permute-start(bf16[8,112,128]{2,0,1:T(8,128)(2,1)S(1)} %collective-permute-done.9), channel_id=1, source_target_pairs={{0,1},{1,0},{2,3},{3,2},{4,5},{5,4},{6,7},{7,6},{8,9},{9,8},{10,11... | collective-permute-start | bytes 688136 | tf_op jit(solution)/shard_map/ppermute | solution.py:42
  46.8 15.5 %collective-permute-start.4 = (bf16[288,1024]{1,0:T(8,128)(2,1)}, bf16[288,1024]{1,0:T(8,128)(2,1)S(1)}, u32[]{:S(2)}, u32[]{:S(2)}) collective-permute-start(bf16[288,1024]{1,0:T(8,128)(2,1)} %collective-permute-done.3.refs_3_), channel_id=1, source_target_pairs={{0,4},{4,8},{8,12},{12,14},{14,10},{10,6},{6,2},{2,0},{1,5},{5,9},... | collective-permute-start | bytes 1769480 | tf_op jit(solution)/shard_map/ppermute | solution.py:47
  48.4 14.3 %collective-permute-start.6 = (bf16[288,1024]{1,0:T(8,128)(2,1)}, bf16[288,1024]{1,0:T(8,128)(2,1)S(1)}, u32[]{:S(2)}, u32[]{:S(2)}) collective-permute-start(bf16[288,1024]{1,0:T(8,128)(2,1)} %collective-permute-done.5.refs_4_), channel_id=1, source_target_pairs={{0,2},{4,0},{8,4},{12,8},{14,12},{10,14},{6,10},{2,6},{1,3},{5,1},... | collective-permute-start | bytes 1769480 | tf_op jit(solution)/shard_map/ppermute | solution.py:47
  62.8 16.0 %collective-permute-start.7 = (bf16[128,1024]{1,0:T(8,128)(2,1)S(1)}, bf16[128,1024]{1,0:T(8,128)(2,1)S(1)}, u32[]{:S(2)}, u32[]{:S(2)}) collective-permute-start(bf16[128,1024]{1,0:T(8,128)(2,1)S(1)} %slice.333), channel_id=1, source_target_pairs={{0,4},{4,8},{8,12},{12,14},{14,10},{10,6},{6,2},{2,0},{1,5},{5,9},... | collective-permute-start | bytes 786440 | tf_op jit(solution)/shard_map/ppermute | solution.py:47
  64.3 14.5 %collective-permute-start.8 = (bf16[160,1024]{1,0:T(8,128)(2,1)S(1)}, bf16[160,1024]{1,0:T(8,128)(2,1)S(1)}, u32[]{:S(2)}, u32[]{:S(2)}) collective-permute-start(bf16[160,1024]{1,0:T(8,128)(2,1)S(1)} %slice.334), channel_id=1, source_target_pairs={{0,2},{4,0},{8,4},{12,8},{14,12},{10,14},{6,10},{2,6},{1,3},{5,1},... | collective-permute-start | bytes 983048 | tf_op jit(solution)/shard_map/ppermute | solution.py:47
  85.7 22.3 %collective-permute-start.11 = (bf16[2,8,256,128]{3,2,1,0:T(8,128)(2,1)}, bf16[2,8,256,128]{3,2,1,0:T(8,128)(2,1)}, u32[]{:S(2)}, u32[]{:S(2)}) collective-permute-start(bf16[2,8,256,128]{3,2,1,0:T(8,128)(2,1)} %get-tuple-element.124.own_ref), channel_id=1, source_target_pairs={{0,1},{1,0},{2,3},{3,2},{4,5},{5,4},{6,7},{7,6},{8,9},{9,8},{10,11... | collective-permute-start | bytes 3145736 | tf_op jit(solution)/shard_map/ppermute | solution.py:42
  94.8 22.8 %collective-permute-start.15 = (bf16[192,1536]{1,0:T(8,128)(2,1)S(1)}, bf16[192,1536]{1,0:T(8,128)(2,1)S(1)}, u32[]{:S(2)}, u32[]{:S(2)}) collective-permute-start(bf16[192,1536]{1,0:T(8,128)(2,1)S(1)} %fusion.35.refs_0_), channel_id=1, source_target_pairs={{0,2},{4,0},{8,4},{12,8},{14,12},{10,14},{6,10},{2,6},{1,3},{5,1},... | collective-permute-start | bytes 1769480 | tf_op jit(solution)/shard_map/ppermute | solution.py:47
  96.2 26.5 %collective-permute-start.14 = (bf16[192,1536]{1,0:T(8,128)(2,1)S(1)}, bf16[192,1536]{1,0:T(8,128)(2,1)S(1)}, u32[]{:S(2)}, u32[]{:S(2)}) collective-permute-start(bf16[192,1536]{1,0:T(8,128)(2,1)S(1)} %fusion.35.refs_0_), channel_id=1, source_target_pairs={{0,4},{4,8},{8,12},{12,14},{14,10},{10,6},{6,2},{2,0},{1,5},{5,9},... | collective-permute-start | bytes 1769480 | tf_op jit(solution)/shard_map/ppermute | solution.py:47
  122.7 14.6 %collective-permute-start.16 = (bf16[192,1536]{1,0:T(8,128)(2,1)S(1)}, bf16[192,1536]{1,0:T(8,128)(2,1)S(1)}, u32[]{:S(2)}, u32[]{:S(2)}) collective-permute-start(bf16[192,1536]{1,0:T(8,128)(2,1)S(1)} %collective-permute-done.14.refs_1_), channel_id=1, source_target_pairs={{0,4},{4,8},{8,12},{12,14},{14,10},{10,6},{6,2},{2,0},{1,5},{5,9},... | collective-permute-start | bytes 1769480 | tf_op jit(solution)/shard_map/ppermute | solution.py:47
  123.4 14.4 %collective-permute-start.17 = (bf16[192,1536]{1,0:T(8,128)(2,1)S(1)}, bf16[192,1536]{1,0:T(8,128)(2,1)}, u32[]{:S(2)}, u32[]{:S(2)}) collective-permute-start(bf16[192,1536]{1,0:T(8,128)(2,1)S(1)} %collective-permute-done.15.refs_8_), channel_id=1, source_target_pairs={{0,2},{4,0},{8,4},{12,8},{14,12},{10,14},{6,10},{2,6},{1,3},{5,1},... | collective-permute-start | bytes 1769480 | tf_op jit(solution)/shard_map/ppermute | solution.py:47
  137.8 29.7 %all-to-all-start.1 = ((bf16[8,256,128]{2,1,0:T(8,128)(2,1)}), bf16[8,256,128]{2,1,0:T(8,128)(2,1)S(1)}, u32[]{:S(2)}, u32[]{:S(2)}) async-start(bf16[8,256,128]{2,1,0:T(8,128)(2,1)} %get-tuple-element.136), calls=%async_computation.1 | async-start | bytes 1048576 | tf_op jit(solution)/shard_map/all_to_all | solution.py:56
  143.6 14.9 %collective-permute-start.21 = (bf16[256,1024]{1,0:T(8,128)(2,1)S(1)}, bf16[256,1024]{1,0:T(8,128)(2,1)}, u32[]{:S(2)}, u32[]{:S(2)}) collective-permute-start(bf16[256,1024]{1,0:T(8,128)(2,1)S(1)} %bitcast.359), channel_id=1, source_target_pairs={{0,16},{16,0},{1,17},{17,1},{2,18},{18,2},{3,19},{19,3},{4,20},{20... | collective-permute-start | bytes 1572872 | tf_op jit(solution)/shard_map/ppermute | solution.py:42
  146.0 20.6 %collective-permute-start.24 = (bf16[8,32,1024]{2,1,0:T(8,128)(2,1)S(1)}, bf16[8,32,1024]{2,1,0:T(8,128)(2,1)S(1)}, u32[]{:S(2)}, u32[]{:S(2)}) collective-permute-start(bf16[8,32,1024]{2,1,0:T(8,128)(2,1)S(1)} %bitcast_dynamic-update-slice_fusion.refs_0_), channel_id=1, source_target_pairs={{0,16},{16,0},{1,17},{17,1},{2,18},{18,2},{3,19},{19,3},{4,20},{20... | collective-permute-start | bytes 1572872 | tf_op jit(solution)/shard_map/ppermute | solution.py:42
  146.7 19.9 %collective-permute-start.20 = (bf16[256,1024]{1,0:T(8,128)(2,1)S(1)}, bf16[256,1024]{1,0:T(8,128)(2,1)S(1)}, u32[]{:S(2)}, u32[]{:S(2)}) collective-permute-start(bf16[256,1024]{1,0:T(8,128)(2,1)S(1)} %bitcast.360), channel_id=1, source_target_pairs={{0,1},{1,0},{2,3},{3,2},{4,5},{5,4},{6,7},{7,6},{8,9},{9,8},{10,11... | collective-permute-start | bytes 1572872 | tf_op jit(solution)/shard_map/ppermute | solution.py:42
  146.7 20.4 %collective-permute-start.18 = (bf16[192,1536]{1,0:T(8,128)(2,1)}, bf16[192,1536]{1,0:T(8,128)(2,1)S(1)}, u32[]{:S(2)}, u32[]{:S(2)}) collective-permute-start(bf16[192,1536]{1,0:T(8,128)(2,1)} %copy-done.26), channel_id=1, source_target_pairs={{0,4},{4,8},{8,12},{12,14},{14,10},{10,6},{6,2},{2,0},{1,5},{5,9},... | collective-permute-start | bytes 1769480 | tf_op jit(solution)/shard_map/ppermute | solution.py:47
  148.7 18.7 %collective-permute-start.19 = (bf16[192,1536]{1,0:T(8,128)(2,1)}, bf16[192,1536]{1,0:T(8,128)(2,1)S(1)}, u32[]{:S(2)}, u32[]{:S(2)}) collective-permute-start(bf16[192,1536]{1,0:T(8,128)(2,1)} %collective-permute-done.17.refs_7_), channel_id=1, source_target_pairs={{0,2},{4,0},{8,4},{12,8},{14,12},{10,14},{6,10},{2,6},{1,3},{5,1},... | collective-permute-start | bytes 1769480 | tf_op jit(solution)/shard_map/ppermute | solution.py:47
  158.5 8.9 %collective-permute-start.22 = (bf16[256,1024]{1,0:T(8,128)(2,1)}, bf16[256,1024]{1,0:T(8,128)(2,1)}, u32[]{:S(2)}, u32[]{:S(2)}) collective-permute-start(bf16[256,1024]{1,0:T(8,128)(2,1)} %collective-permute-done.21.ga.refs_6_), channel_id=1, source_target_pairs={{0,1},{1,0},{2,3},{3,2},{4,5},{5,4},{6,7},{7,6},{8,9},{9,8},{10,11... | collective-permute-start | bytes 1572872 | tf_op jit(solution)/shard_map/ppermute | solution.py:42
  166.6 5.7 %collective-permute-start.23 = (bf16[8,32,1024]{2,1,0:T(8,128)(2,1)S(1)}, bf16[8,32,1024]{2,1,0:T(8,128)(2,1)}, u32[]{:S(2)}, u32[]{:S(2)}) collective-permute-start(bf16[8,32,1024]{2,1,0:T(8,128)(2,1)S(1)} %bitcast_dynamic-update-slice_fusion.refs_0_), channel_id=1, source_target_pairs={{0,1},{1,0},{2,3},{3,2},{4,5},{5,4},{6,7},{7,6},{8,9},{9,8},{10,11... | collective-permute-start | bytes 1572872 | tf_op jit(solution)/shard_map/ppermute | solution.py:42
  166.7 5.7 %collective-permute-start.25 = (bf16[8,32,1024]{2,1,0:T(8,128)(2,1)S(1)}, bf16[8,32,1024]{2,1,0:T(8,128)(2,1)S(1)}, u32[]{:S(2)}, u32[]{:S(2)}) collective-permute-start(bf16[8,32,1024]{2,1,0:T(8,128)(2,1)S(1)} %collective-permute-done.24.refs_2_), channel_id=1, source_target_pairs={{0,1},{1,0},{2,3},{3,2},{4,5},{5,4},{6,7},{7,6},{8,9},{9,8},{10,11... | collective-permute-start | bytes 1572872 | tf_op jit(solution)/shard_map/ppermute | solution.py:42
  169.0 9.7 %collective-permute-start.27 = (bf16[96,1536]{1,0:T(8,128)(2,1)}, bf16[96,1536]{1,0:T(8,128)(2,1)}, u32[]{:S(2)}, u32[]{:S(2)}) collective-permute-start(bf16[96,1536]{1,0:T(8,128)(2,1)} %slice.359), channel_id=1, source_target_pairs={{0,2},{4,0},{8,4},{12,8},{14,12},{10,14},{6,10},{2,6},{1,3},{5,1},... | collective-permute-start | bytes 884744 | tf_op jit(solution)/shard_map/ppermute | solution.py:47
  170.8 9.4 %collective-permute-start.26 = (bf16[96,1536]{1,0:T(8,128)(2,1)}, bf16[96,1536]{1,0:T(8,128)(2,1)}, u32[]{:S(2)}, u32[]{:S(2)}) collective-permute-start(bf16[96,1536]{1,0:T(8,128)(2,1)} %slice.358), channel_id=1, source_target_pairs={{0,4},{4,8},{8,12},{12,14},{14,10},{10,6},{6,2},{2,0},{1,5},{5,9},... | collective-permute-start | bytes 884744 | tf_op jit(solution)/shard_map/ppermute | solution.py:47
  180.2 13.4 %collective-permute-start.29 = (bf16[256,1024]{1,0:T(8,128)(2,1)}, bf16[256,1024]{1,0:T(8,128)(2,1)S(1)}, u32[]{:S(2)}, u32[]{:S(2)}) collective-permute-start(bf16[256,1024]{1,0:T(8,128)(2,1)} %get-tuple-element.153.na.refs_0_), channel_id=1, source_target_pairs={{0,16},{16,0},{1,17},{17,1},{2,18},{18,2},{3,19},{19,3},{4,20},{20... | collective-permute-start | bytes 1572872 | tf_op jit(solution)/shard_map/ppermute | solution.py:42
  181.6 16.8 %collective-permute-start.28 = (bf16[256,1024]{1,0:T(8,128)(2,1)}, bf16[256,1024]{1,0:T(8,128)(2,1)S(1)}, u32[]{:S(2)}, u32[]{:S(2)}) collective-permute-start(bf16[256,1024]{1,0:T(8,128)(2,1)} %get-tuple-element.153.na.refs_0_), channel_id=1, source_target_pairs={{0,1},{1,0},{2,3},{3,2},{4,5},{5,4},{6,7},{7,6},{8,9},{9,8},{10,11... | collective-permute-start | bytes 1572872 | tf_op jit(solution)/shard_map/ppermute | solution.py:42
  193.6 15.9 %collective-permute-start.30 = (bf16[256,1024]{1,0:T(8,128)(2,1)S(1)}, bf16[256,1024]{1,0:T(8,128)(2,1)S(1)}, u32[]{:S(2)}, u32[]{:S(2)}) collective-permute-start(bf16[256,1024]{1,0:T(8,128)(2,1)S(1)} %collective-permute-done.29.na.refs_2_), channel_id=1, source_target_pairs={{0,1},{1,0},{2,3},{3,2},{4,5},{5,4},{6,7},{7,6},{8,9},{9,8},{10,11... | collective-permute-start | bytes 1572872 | tf_op jit(solution)/shard_map/ppermute | solution.py:42
  221.9 2.0 collective-permute-start.31
  223.5 14.8 %collective-permute-start.35 = (bf16[256,1024]{1,0:T(8,128)(2,1)S(1)}, bf16[256,1024]{1,0:T(8,128)(2,1)S(1)}, u32[]{:S(2)}, u32[]{:S(2)}) collective-permute-start(bf16[256,1024]{1,0:T(8,128)(2,1)S(1)} %get-tuple-element.245), channel_id=1, source_target_pairs={{0,1},{1,0},{2,3},{3,2},{4,5},{5,4},{6,7},{7,6},{8,9},{9,8},{10,11... | collective-permute-start | bytes 1572872 | tf_op jit(solution)/shard_map/ppermute | solution.py:42
  224.1 14.2 %collective-permute-start.36 = (bf16[256,1024]{1,0:T(8,128)(2,1)S(1)}, bf16[256,1024]{1,0:T(8,128)(2,1)S(1)}, u32[]{:S(2)}, u32[]{:S(2)}) collective-permute-start(bf16[256,1024]{1,0:T(8,128)(2,1)S(1)} %fusion.28), channel_id=1, source_target_pairs={{0,16},{16,0},{1,17},{17,1},{2,18},{18,2},{3,19},{19,3},{4,20},{20... | collective-permute-start | bytes 1572872 | tf_op jit(solution)/shard_map/ppermute | solution.py:42
  245.9 2.9 collective-permute-start.37
  250.6 14.0 %collective-permute-start.38 = (bf16[1,8,32,1024]{3,2,1,0:T(8,128)(2,1)S(1)}, bf16[1,8,32,1024]{3,2,1,0:T(8,128)(2,1)S(1)}, u32[]{:S(2)}, u32[]{:S(2)}) collective-permute-start(bf16[1,8,32,1024]{3,2,1,0:T(8,128)(2,1)S(1)} %fusion.37), channel_id=1, source_target_pairs={{0,16},{16,0},{1,17},{17,1},{2,18},{18,2},{3,19},{19,3},{4,20},{20... | collective-permute-start | bytes 1572872 | tf_op jit(solution)/shard_map/ppermute | solution.py:42
  253.0 19.5 %collective-permute-start.40 = (bf16[88,1536]{1,0:T(8,128)(2,1)S(1)}, bf16[88,1536]{1,0:T(8,128)(2,1)S(1)}, u32[]{:S(2)}, u32[]{:S(2)}) collective-permute-start(bf16[88,1536]{1,0:T(8,128)(2,1)S(1)} %slice_bitcast_fusion.8), channel_id=1, source_target_pairs={{0,2},{4,0},{8,4},{12,8},{14,12},{10,14},{6,10},{2,6},{1,3},{5,1},... | collective-permute-start | bytes 811016 | tf_op jit(solution)/shard_map/ppermute | solution.py:47
  255.6 18.0 %collective-permute-start.39 = (bf16[128,1536]{1,0:T(8,128)(2,1)S(1)}, bf16[128,1536]{1,0:T(8,128)(2,1)S(1)}, u32[]{:S(2)}, u32[]{:S(2)}) collective-permute-start(bf16[128,1536]{1,0:T(8,128)(2,1)S(1)} %slice_bitcast_fusion.7), channel_id=1, source_target_pairs={{0,4},{4,8},{8,12},{12,14},{14,10},{10,6},{6,2},{2,0},{1,5},{5,9},... | collective-permute-start | bytes 1179656 | tf_op jit(solution)/shard_map/ppermute | solution.py:47
  256.2 19.6 %all-to-all-start.2 = ((bf16[8,256,128]{2,1,0:T(8,128)(2,1)}), bf16[8,256,128]{2,1,0:T(8,128)(2,1)S(1)}, u32[]{:S(2)}, u32[]{:S(2)}) async-start(bf16[8,256,128]{2,1,0:T(8,128)(2,1)} %get-tuple-element.187), calls=%async_computation.2 | async-start | bytes 1048576 | tf_op jit(solution)/shard_map/all_to_all | solution.py:56
  275.8 33.8 %collective-permute-start.42 = (bf16[216,1536]{1,0:T(8,128)(2,1)}, bf16[216,1536]{1,0:T(8,128)(2,1)S(1)}, u32[]{:S(2)}, u32[]{:S(2)}) collective-permute-start(bf16[216,1536]{1,0:T(8,128)(2,1)} %pad_maximum_fusion.3), channel_id=1, source_target_pairs={{0,4},{4,8},{8,12},{12,14},{14,10},{10,6},{6,2},{2,0},{1,5},{5,9},... | collective-permute-start | bytes 1990664 | tf_op jit(solution)/shard_map/ppermute | solution.py:47
  279.1 31.3 %collective-permute-start.43 = (bf16[216,1536]{1,0:T(8,128)(2,1)}, bf16[216,1536]{1,0:T(8,128)(2,1)}, u32[]{:S(2)}, u32[]{:S(2)}) collective-permute-start(bf16[216,1536]{1,0:T(8,128)(2,1)} %pad_maximum_fusion.4), channel_id=1, source_target_pairs={{0,2},{4,0},{8,4},{12,8},{14,12},{10,14},{6,10},{2,6},{1,3},{5,1},... | collective-permute-start | bytes 1990664 | tf_op jit(solution)/shard_map/ppermute | solution.py:47
  307.7 12.0 %collective-permute-start.44 = (bf16[2,8,256,128]{3,2,1,0:T(8,128)(2,1)}, bf16[2,8,256,128]{3,2,1,0:T(8,128)(2,1)}, u32[]{:S(2)}, u32[]{:S(2)}) collective-permute-start(bf16[2,8,256,128]{3,2,1,0:T(8,128)(2,1)} %get-tuple-element.200), channel_id=1, source_target_pairs={{0,1},{1,0},{2,3},{3,2},{4,5},{5,4},{6,7},{7,6},{8,9},{9,8},{10,11... | collective-permute-start | bytes 3145736 | tf_op jit(solution)/shard_map/ppermute | solution.py:42
  307.8 26.0 %collective-permute-start.33 = (bf16[256,1024]{1,0:T(8,128)(2,1)S(1)}, bf16[256,1024]{1,0:T(8,128)(2,1)}, u32[]{:S(2)}, u32[]{:S(2)}) collective-permute-start(bf16[256,1024]{1,0:T(8,128)(2,1)S(1)} %slice_bitcast_fusion.4), channel_id=1, source_target_pairs={{0,1},{1,0},{2,3},{3,2},{4,5},{5,4},{6,7},{7,6},{8,9},{9,8},{10,11... | collective-permute-start | bytes 1572872 | tf_op jit(solution)/shard_map/ppermute | solution.py:42
  309.7 44.5 %collective-permute-start.32 = (bf16[256,1024]{1,0:T(8,128)(2,1)}, bf16[256,1024]{1,0:T(8,128)(2,1)}, u32[]{:S(2)}, u32[]{:S(2)}) collective-permute-start(bf16[256,1024]{1,0:T(8,128)(2,1)} %slice_bitcast_fusion.5), channel_id=1, source_target_pairs={{0,1},{1,0},{2,3},{3,2},{4,5},{5,4},{6,7},{7,6},{8,9},{9,8},{10,11... | collective-permute-start | bytes 1572872 | tf_op jit(solution)/shard_map/ppermute | solution.py:42
  309.7 7.2 %collective-permute-start.41 = (bf16[64,512]{1,0:T(8,128)(2,1)S(1)}, bf16[64,512]{1,0:T(8,128)(2,1)S(1)}, u32[]{:S(2)}, u32[]{:S(2)}) collective-permute-start(bf16[64,512]{1,0:T(8,128)(2,1)S(1)} %copy-done.50), channel_id=1, source_target_pairs={{0,14},{4,10},{8,6},{12,2},{14,0},{10,4},{6,8},{2,12},{1,15},{5,11... | collective-permute-start | bytes 196616 | tf_op jit(solution)/shard_map/ppermute | solution.py:47
  317.5 19.1 %collective-permute-start.45 = (bf16[216,1536]{1,0:T(8,128)(2,1)}, bf16[216,1536]{1,0:T(8,128)(2,1)S(1)}, u32[]{:S(2)}, u32[]{:S(2)}) collective-permute-start(bf16[216,1536]{1,0:T(8,128)(2,1)} %get-tuple-element.203), channel_id=1, source_target_pairs={{0,4},{4,8},{8,12},{12,14},{14,10},{10,6},{6,2},{2,0},{1,5},{5,9},... | collective-permute-start | bytes 1990664 | tf_op jit(solution)/shard_map/ppermute | solution.py:47
  317.5 19.1 %collective-permute-start.46 = (bf16[216,1536]{1,0:T(8,128)(2,1)}, bf16[216,1536]{1,0:T(8,128)(2,1)}, u32[]{:S(2)}, u32[]{:S(2)}) collective-permute-start(bf16[216,1536]{1,0:T(8,128)(2,1)} %get-tuple-element.204), channel_id=1, source_target_pairs={{0,2},{4,0},{8,4},{12,8},{14,12},{10,14},{6,10},{2,6},{1,3},{5,1},... | collective-permute-start | bytes 1990664 | tf_op jit(solution)/shard_map/ppermute | solution.py:47
  333.7 6.3 %collective-permute-start.47 = (bf16[1,2,8,32,384]{4,3,2,1,0:T(8,128)(2,1)S(1)}, bf16[1,2,8,32,384]{4,3,2,1,0:T(8,128)(2,1)S(1)}, u32[]{:S(2)}, u32[]{:S(2)}) collective-permute-start(bf16[1,2,8,32,384]{4,3,2,1,0:T(8,128)(2,1)S(1)} %fusion.42), channel_id=1, source_target_pairs={{0,1},{1,0},{2,3},{3,2},{4,5},{5,4},{6,7},{7,6},{8,9},{9,8},{10,11... | collective-permute-start | bytes 1179656 | tf_op jit(solution)/shard_map/ppermute | solution.py:42
  335.0 19.4 %collective-permute-start.34 = (bf16[256,1024]{1,0:T(8,128)(2,1)S(1)}, bf16[256,1024]{1,0:T(8,128)(2,1)S(1)}, u32[]{:S(2)}, u32[]{:S(2)}) collective-permute-start(bf16[256,1024]{1,0:T(8,128)(2,1)S(1)} %fusion.24), channel_id=1, source_target_pairs={{0,16},{16,0},{1,17},{17,1},{2,18},{18,2},{3,19},{19,3},{4,20},{20... | collective-permute-start | bytes 1572872 | tf_op jit(solution)/shard_map/ppermute | solution.py:42
  337.9 8.5 %collective-permute-start.50 = (bf16[128,1024]{1,0:T(8,128)(2,1)S(1)}, bf16[128,1024]{1,0:T(8,128)(2,1)S(1)}, u32[]{:S(2)}, u32[]{:S(2)}) collective-permute-start(bf16[128,1024]{1,0:T(8,128)(2,1)S(1)} %get-tuple-element.238), channel_id=1, source_target_pairs={{0,2},{4,0},{8,4},{12,8},{14,12},{10,14},{6,10},{2,6},{1,3},{5,1},... | collective-permute-start | bytes 786440 | tf_op jit(solution)/shard_map/ppermute | solution.py:47
  339.9 8.1 %collective-permute-start.49 = (bf16[128,1024]{1,0:T(8,128)(2,1)S(1)}, bf16[128,1024]{1,0:T(8,128)(2,1)S(1)}, u32[]{:S(2)}, u32[]{:S(2)}) collective-permute-start(bf16[128,1024]{1,0:T(8,128)(2,1)S(1)} %get-tuple-element.240), channel_id=1, source_target_pairs={{0,4},{4,8},{8,12},{12,14},{14,10},{10,6},{6,2},{2,0},{1,5},{5,9},... | collective-permute-start | bytes 786440 | tf_op jit(solution)/shard_map/ppermute | solution.py:47
  340.2 18.2 %collective-permute-start.48 = (bf16[1,8,32,384]{3,2,1,0:T(8,128)(2,1)S(1)}, bf16[1,8,32,384]{3,2,1,0:T(8,128)(2,1)S(1)}, u32[]{:S(2)}, u32[]{:S(2)}) collective-permute-start(bf16[1,8,32,384]{3,2,1,0:T(8,128)(2,1)S(1)} %fusion.48), channel_id=1, source_target_pairs={{0,16},{16,0},{1,17},{17,1},{2,18},{18,2},{3,19},{19,3},{4,20},{20... | collective-permute-start | bytes 589832 | tf_op jit(solution)/shard_map/ppermute | solution.py:42
  349.4 14.8 %collective-permute-start.51 = (bf16[256,1024]{1,0:T(8,128)(2,1)S(1)}, bf16[256,1024]{1,0:T(8,128)(2,1)S(1)}, u32[]{:S(2)}, u32[]{:S(2)}) collective-permute-start(bf16[256,1024]{1,0:T(8,128)(2,1)S(1)} %pad_maximum_fusion.6), channel_id=1, source_target_pairs={{0,4},{4,8},{8,12},{12,14},{14,10},{10,6},{6,2},{2,0},{1,5},{5,9},... | collective-permute-start | bytes 1572872 | tf_op jit(solution)/shard_map/ppermute | solution.py:47
  349.7 14.8 %collective-permute-start.52 = (bf16[256,1024]{1,0:T(8,128)(2,1)S(1)}, bf16[256,1024]{1,0:T(8,128)(2,1)S(1)}, u32[]{:S(2)}, u32[]{:S(2)}) collective-permute-start(bf16[256,1024]{1,0:T(8,128)(2,1)S(1)} %pad_maximum_fusion.7), channel_id=1, source_target_pairs={{0,2},{4,0},{8,4},{12,8},{14,12},{10,14},{6,10},{2,6},{1,3},{5,1},... | collective-permute-start | bytes 1572872 | tf_op jit(solution)/shard_map/ppermute | solution.py:47
  354.2 25.0 %collective-permute-start.57 = (bf16[216,1536]{1,0:T(8,128)(2,1)}, bf16[216,1536]{1,0:T(8,128)(2,1)S(1)}, u32[]{:S(2)}, u32[]{:S(2)}) collective-permute-start(bf16[216,1536]{1,0:T(8,128)(2,1)} %get-tuple-element.227), channel_id=1, source_target_pairs={{0,4},{4,8},{8,12},{12,14},{14,10},{10,6},{6,2},{2,0},{1,5},{5,9},... | collective-permute-start | bytes 1990664 | tf_op jit(solution)/shard_map/ppermute | solution.py:47
  354.5 25.9 %collective-permute-start.58 = (bf16[216,1536]{1,0:T(8,128)(2,1)S(1)}, bf16[216,1536]{1,0:T(8,128)(2,1)}, u32[]{:S(2)}, u32[]{:S(2)}) collective-permute-start(bf16[216,1536]{1,0:T(8,128)(2,1)S(1)} %get-tuple-element.228), channel_id=1, source_target_pairs={{0,2},{4,0},{8,4},{12,8},{14,12},{10,14},{6,10},{2,6},{1,3},{5,1},... | collective-permute-start | bytes 1990664 | tf_op jit(solution)/shard_map/ppermute | solution.py:47
  366.8 18.9 %all-to-all-start.3 = ((bf16[8,32,384]{2,1,0:T(8,128)(2,1)}), bf16[8,32,384]{2,1,0:T(8,128)(2,1)S(1)}, u32[]{:S(2)}, u32[]{:S(2)}) async-start(bf16[8,32,384]{2,1,0:T(8,128)(2,1)} %fusion.49), calls=%async_computation.3 | async-start | bytes 393216 | tf_op jit(solution)/shard_map/all_to_all | solution.py:56
  370.2 19.7 %collective-permute-start.53 = (bf16[256,1024]{1,0:T(8,128)(2,1)}, bf16[256,1024]{1,0:T(8,128)(2,1)}, u32[]{:S(2)}, u32[]{:S(2)}) collective-permute-start(bf16[256,1024]{1,0:T(8,128)(2,1)} %get-tuple-element.211), channel_id=1, source_target_pairs={{0,4},{4,8},{8,12},{12,14},{14,10},{10,6},{6,2},{2,0},{1,5},{5,9},... | collective-permute-start | bytes 1572872 | tf_op jit(solution)/shard_map/ppermute | solution.py:47
  372.2 19.0 %collective-permute-start.55 = (bf16[256,1024]{1,0:T(8,128)(2,1)S(1)}, bf16[256,1024]{1,0:T(8,128)(2,1)}, u32[]{:S(2)}, u32[]{:S(2)}) collective-permute-start(bf16[256,1024]{1,0:T(8,128)(2,1)S(1)} %get-tuple-element.212), channel_id=1, source_target_pairs={{0,2},{4,0},{8,4},{12,8},{14,12},{10,14},{6,10},{2,6},{1,3},{5,1},... | collective-permute-start | bytes 1572872 | tf_op jit(solution)/shard_map/ppermute | solution.py:47
  385.0 11.1 %collective-permute-start.60 = (bf16[2,32,1536]{2,1,0:T(8,128)(2,1)S(1)}, bf16[2,32,1536]{2,1,0:T(8,128)(2,1)S(1)}, u32[]{:S(2)}, u32[]{:S(2)}) collective-permute-start(bf16[2,32,1536]{2,1,0:T(8,128)(2,1)S(1)} %fusion.47), channel_id=1, source_target_pairs={{0,16},{16,0},{1,17},{17,1},{2,18},{18,2},{3,19},{19,3},{4,20},{20... | collective-permute-start | bytes 589832 | tf_op jit(solution)/shard_map/ppermute | solution.py:42
  394.1 12.2 %collective-permute-start.54 = (bf16[256,1024]{1,0:T(8,128)(2,1)}, bf16[256,1024]{1,0:T(8,128)(2,1)S(1)}, u32[]{:S(2)}, u32[]{:S(2)}) collective-permute-start(bf16[256,1024]{1,0:T(8,128)(2,1)} %get-tuple-element.233), channel_id=1, source_target_pairs={{0,4},{4,8},{8,12},{12,14},{14,10},{10,6},{6,2},{2,0},{1,5},{5,9},... | collective-permute-start | bytes 1572872 | tf_op jit(solution)/shard_map/ppermute | solution.py:47
  395.5 12.1 %collective-permute-start.56 = (bf16[256,1024]{1,0:T(8,128)(2,1)}, bf16[256,1024]{1,0:T(8,128)(2,1)S(1)}, u32[]{:S(2)}, u32[]{:S(2)}) collective-permute-start(bf16[256,1024]{1,0:T(8,128)(2,1)} %get-tuple-element.234), channel_id=1, source_target_pairs={{0,2},{4,0},{8,4},{12,8},{14,12},{10,14},{6,10},{2,6},{1,3},{5,1},... | collective-permute-start | bytes 1572872 | tf_op jit(solution)/shard_map/ppermute | solution.py:47
  (80 other events, 639.4 us)

commit v3 on v2

--- a/solution.py
+++ b/solution.py
@@ -147,11 +147,10 @@
 
 
 def attend_kernel(
-    begin, tab, q_ref, own_ref, oth_ref, segq_ref, sego_ref, segt_ref, idx_ref, ck_ref, cv_ref,
-    *rest,
+    tab, q_ref, own_ref, oth_ref, segq_ref, sego_ref, segt_ref, idx_ref, ck_ref, cv_ref,
+    o_ref, low_ref, lse_ref, mem_ref,
 ):
-    o_ref, low_ref, lse_ref, mem_ref = rest[-4:]
-    i = pl.program_id(0) + begin
+    i = pl.program_id(0)
     parity = tab[40]
     count = q_ref.shape[1]
     q = q_ref[0]
@@ -221,21 +220,20 @@
     lse_ref[0] = top + jnp.log2(total)
 
 
-def attend(tab, q, own, oth, segq, sego, segt, idx, ck, cv, begin, held):
+def attend(tab, q, own, oth, segq, sego, segt, idx, ck, cv):
     count = q.shape[1]
-    block = pl.BlockSpec((1, count, HEAD_DIM), lambda i, t: (i + begin, 0, 0))
-    thin = pl.BlockSpec((1, count, 1), lambda i, t: (i + begin, 0, 0))
+    block = pl.BlockSpec((1, count, HEAD_DIM), lambda i, t: (i, 0, 0))
+    thin = pl.BlockSpec((1, count, 1), lambda i, t: (i, 0, 0))
     whole = pl.BlockSpec((2, HEADS, count, HEAD_DIM), lambda i, t: (0, 0, 0, 0))
     segs = pl.BlockSpec((HEADS, 1, count), lambda i, t: (0, 0, 0))
     cache = pl.BlockSpec((ck.shape[0], HEAD_DIM), lambda i, t: (0, t[41]))
-    mem = pl.BlockSpec((2, 1, count, HEAD_DIM), lambda i, t: (0, i + begin, 0, 0))
+    mem = pl.BlockSpec((2, 1, count, HEAD_DIM), lambda i, t: (0, i, 0, 0))
     return pl.pallas_call(
-        functools.partial(attend_kernel, begin),
+        attend_kernel,
         grid_spec=pltpu.PrefetchScalarGridSpec(
             num_scalar_prefetch=1,
-            grid=(HEADS // 2,),
-            in_specs=[block, whole, whole, thin, segs, segs, thin, cache, cache]
-            + [pl.BlockSpec(memory_space=pl.ANY)] * len(held),
+            grid=(HEADS,),
+            in_specs=[block, whole, whole, thin, segs, segs, thin, cache, cache],
             out_specs=[block, block, thin, mem],
         ),
         out_shape=[
@@ -244,12 +242,11 @@
             jax.ShapeDtypeStruct((HEADS, count, 1), WIDE),
             jax.ShapeDtypeStruct((2, HEADS, count, HEAD_DIM), LOW),
         ],
-        input_output_aliases={10 + i: i for i in range(len(held))},
         cost_estimate=pl.CostEstimate(
-            flops=12 * 10**9, bytes_accessed=4 * 2**20, transcendentals=2 * 10**6
-        ),
-        name=f"attend{begin}",
-    )(tab, q, own, oth, segq, sego, segt, idx, ck, cv, *held)
+            flops=25 * 10**9, bytes_accessed=6 * 2**20, transcendentals=3 * 10**6
+        ),
+        name="attend",
+    )(tab, q, own, oth, segq, sego, segt, idx, ck, cv)
 
 
 def attend_back_kernel(
@@ -703,23 +700,14 @@
 
     block = jnp.concatenate([x, out_weight], axis=0)
     split = count // 2
-    forth, back = [block, turn(block, 1)], [block, turn(block, -1)]
-    pack, forth[1], back[1], gate_late, up_late = lax.optimization_barrier(
-        (pack, forth[1], back[1], gate_weight, up_weight)
-    )
     got = exchange(pack)
-    for step in range(HEADS // 2 - 2):
-        forth.append(turn(forth[-1], 1))
-        back.append(turn(back[-1], -1))
-        if step == 1:
-            _, forth[-1], back[-1], parity = lax.optimization_barrier(
-                (got, forth[-1], back[-1], core)
-            )
-    far_first, far_last = turn(forth[-1][:split], 1), turn(back[-1][split:], -1)
-    x_slots = [((v, count),) for v in forth] + [((far_first, split), (far_last, count - split))]
-    x_slots += [((v, count),) for v in back[:0:-1]]
-    outs = [v[count:] for v in forth] + [far_last[count - split :]]
-    outs += [v[count:] for v in back[:0:-1]]
+    up_c = swap(upstream, "c")
+    up_y = swap(upstream, "dl")
+    up_yc = swap(up_y, "c")
+    got, up_c, up_y, up_yc, x_forth, x_back, parity = lax.optimization_barrier(
+        (got, up_c, up_y, up_yc, turn(block, 1), turn(block, -1), core)
+    )
+    forth, back = [block, x_forth, turn(x_forth, 1)], [block, x_back, turn(x_back, -1)]
     got_c = swap(got, "c")
     got_y = swap(got, "dl")
     got_yc = swap(got_y, "c")
@@ -782,6 +770,23 @@
     cosine = jnp.concatenate([cosine, cosine], axis=-1)
     sine = jnp.concatenate([-sine, sine], axis=-1)
 
+    seg_thin = seg_own.reshape(HEADS, count, 1)
+    early = (w_qkv, gain_one, cosine, sine, tab, seg_thin, idx)
+    early, gate_late, up_late, forth[2], back[2] = lax.optimization_barrier(
+        (early, gate_weight, up_weight, forth[2], back[2])
+    )
+    w_qkv, gain_one, cosine, sine, tab, seg_thin, idx = early
+    forth.append(turn(forth[2], 1))
+    back.append(turn(back[2], -1))
+    at_near, at_far = [0, 1, 7, 2, 6], [3, 5, 4]
+
+    def chips_at(order):
+        return at_place(mine - jnp.asarray(order, jnp.int32)).astype(jnp.int32)
+
+    near_slots = [forth[0], forth[1], back[1], forth[2], back[2]]
+    held = qkv_blocks(
+        chips_at(at_near), [((v, count),) for v in near_slots], gain_one, w_qkv, cosine, sine, ()
+    )
     half = units + -units % HEAD_DIM
     wide = 2 * half
 
@@ -807,66 +812,45 @@
     if far > 1:
         bundle = lax.all_gather(bundle, "dh", axis=0, tiled=True)
     upper = bundle.shape[0] // 2
+    *held, bundle, forth[3], back[3] = lax.optimization_barrier(
+        (*held, bundle, forth[3], back[3])
+    )
+    far_first, far_last = turn(forth[3][:split], 1), turn(back[3][split:], -1)
     bundle, *_ = lax.optimization_barrier((bundle, far_first, far_last))
-    forth, back = [bundle, turn(bundle, 1)], [bundle, turn(bundle, -1)]
-
-    held = ()
-    for order in ([0, 1, 7, 2, 6], [3, 5, 4]):
-        held = qkv_blocks(
-            at_place(mine - jnp.asarray(order, jnp.int32)).astype(jnp.int32),
-            [x_slots[i] for i in order],
-            gain_one,
-            w_qkv,
-            cosine,
-            sine,
-            held,
-        )
-    queries, own, normed_one = held
+    w_forth, w_back = [bundle, turn(bundle, 1)], [bundle, turn(bundle, -1)]
+
+    far_slots = [
+        ((forth[3], count),),
+        ((back[3], count),),
+        ((far_first, split), (far_last, count - split)),
+    ]
+    queries, own, normed_one = qkv_blocks(
+        chips_at(at_far), far_slots, gain_one, w_qkv, cosine, sine, tuple(held)
+    )
     other = swap(own, "c")
-    seg_thin = seg_own.reshape(HEADS, count, 1)
     seg_own_row = seg_own.reshape(HEADS, 1, count)
     seg_oth_row = seg_oth.reshape(HEADS, 1, count)
     cached = [cache[0].reshape(-1, D) for cache in (cache_keys, cache_values)]
-    half_attended = attend(
-        tab, queries, own, other, seg_thin, seg_own_row, seg_oth_row, idx, *cached, 0, ()
-    )
-    first_lse, forth[1], back[1] = lax.optimization_barrier(
-        (half_attended[2], forth[1], back[1])
-    )
+    queries, w_forth[1], w_back[1] = lax.optimization_barrier((queries, w_forth[1], w_back[1]))
     attention, attention_low, lse, memory = attend(
-        tab,
-        queries,
-        own,
-        other,
-        seg_thin,
-        seg_own_row,
-        seg_oth_row,
-        idx,
-        *cached,
-        HEADS // 2,
-        (*half_attended[:2], first_lse, half_attended[3]),
-    )
-    w_forth, w_back = turn(forth[1], 1), turn(back[1], -1)
-    attention_low, w_forth, w_back = lax.optimization_barrier((attention_low, w_forth, w_back))
-    forth.append(w_forth)
-    back.append(w_back)
-
-    *outs, up_late, _ = lax.optimization_barrier((*outs, upstream, attention_low))
-    up_c = swap(up_late, "c")
-    up_y = swap(up_late, "dl")
-    up_yc = swap(up_y, "c")
-    outs = jnp.stack(outs)
+        tab, queries, own, other, seg_thin, seg_own_row, seg_oth_row, idx, *cached
+    )
+    w_forth.append(turn(w_forth[1], 1))
+    w_back.append(turn(w_back[1], -1))
+    out_rows = [*forth, far_last, *back[:0:-1]]
+    *out_rows, attention_low, w_forth[2], w_back[2] = lax.optimization_barrier(
+        (*out_rows, attention_low, w_forth[2], w_back[2])
+    )
+
+    heads = exchange(attention_low)
+    w_forth.append(turn(w_forth[2], 1))
+    w_back.append(turn(w_back[2], -1))
+    outs = jnp.stack([v[-rows:] for v in out_rows])
     outs_c = swap(outs, "c")
     outs_y = swap(outs, "dl")
     outs_yc = swap(outs_y, "c")
-    heads = exchange(attention_low)
-    w_forth, w_back = turn(w_forth, 1), turn(w_back, -1)
-    heads, w_forth, w_back, up_c, up_y, up_yc = lax.optimization_barrier(
-        (heads, w_forth, w_back, up_c, up_y, up_yc)
-    )
-    forth.append(w_forth)
-    back.append(w_back)
-    w_first, w_last = turn(w_forth[:upper], 1), turn(w_back[upper:], -1)
+    heads, w_forth[3], w_back[3] = lax.optimization_barrier((heads, w_forth[3], w_back[3]))
+    w_first, w_last = turn(w_forth[3][:upper], 1), turn(w_back[3][upper:], -1)
     slot_of = lax.rem(mine - jnp.asarray(PLACE, jnp.int32) + HEADS, HEADS).astype(jnp.int32)
     if far == 1:
         sources = [outs, outs_c, outs_y, outs_yc]
@@ -879,7 +863,7 @@
     where = jnp.concatenate([chips, jnp.stack([pair, core])]).astype(jnp.int32)
     attended, mid, normed_two, out_w = out_block(where, heads, sources, x, gain_two)
     normed_two, w_first, w_last = lax.optimization_barrier((normed_two, w_first, w_last))
-    w_slots = forth + [w_first, w_last] + back[:0:-1]
+    w_slots = w_forth + [w_first, w_last] + w_back[:0:-1]
 
     if far == 1:
         gate_w, up_w, down_w = weights(where, w_slots, units)
@@ -894,9 +878,9 @@
 
     n_c = swap(normed_two, "c")
     n_y = swap(normed_two, "dl")
+    hid_l, gg_l, ug_l, dn_l, out_l = ffn(normed_two, n_c, upstream, up_c, gate_w, up_w, down_w)
+    n_y, dn_l = lax.optimization_barrier((n_y, dn_l))
     n_yc = swap(n_y, "c")
-    hid_l, gg_l, ug_l, dn_l, out_l = ffn(normed_two, n_c, upstream, up_c, gate_w, up_w, down_w)
-    n_y, n_yc, dn_l = lax.optimization_barrier((n_y, n_yc, dn_l))
     hid_r, gg_r, ug_r, dn_r, out_r = ffn(n_y, n_yc, up_y, up_yc, gate_w, up_w, down_w)
 
     def to_away(away):
@@ -1002,12 +986,14 @@
         tab, queries, ups, attention, lse, own, other, memory, seg_thin, seg_own_row, seg_oth_row
     )
     d_got = swap(d_oth, "c")
-    dq, out_far, forth, back = lax.optimization_barrier((dq, out_far, forth, back))
+    dq, forth, back = lax.optimization_barrier((dq, forth, back))
     dx, dw = qkv_back(
         chips.astype(jnp.int32), dq, d_own, d_got, cosine, sine, normed_one, w_qkv
     )
     arrived_forth, arrived_back = turn(forth, 1), turn(back, -1)
-    dx, arrived_forth, arrived_back = lax.optimization_barrier((dx, arrived_forth, arrived_back))
+    dx, out_far, arrived_forth, arrived_back = lax.optimization_barrier(
+        (dx, out_far, arrived_forth, arrived_back)
+    )
     dx_forth, dx_back = ring_first(dx, split)
     dx_forth, dx_back, arrived_forth, arrived_back = lax.optimization_barrier(
         (dx_forth, dx_back, arrived_forth, arrived_back)

time: 417 us -> 392 us (0.940)
  waiting for transfers between devices: 115 us -> 94.5 us
    ppermute x28, waiting for transfers between devices: 45.8 us -> 28.2 us  [swap(): return lax.ppermute(block, axis, [(0, 1), (1, 0)])]
    ppermute x33, waiting for transfers between devices: 65.5 us -> 57.3 us  [turn(): return lax.ppermute(block, 'h', route)]
    all_to_all x4, waiting for transfers between devices: 3.25 us -> 9.02 us  [exchange(): return lax.all_to_all(blocks, 'h', 0, 0)]
    unnamed x168 -> x145, local copies, waits for them, and re-layouts: 9.35 us -> 14.6 us
    slice x14 -> x4, local copies, waits for them, and re-layouts: 5.8 us -> 1.57 us  [the longest x2 1.53 us: local(): w_first, w_last = (turn(w_forth[3][:upper], 1), turn(w_back[3][upper:], -1))]
    pallas_call x2 -> x1, Pallas kernels: 22 us -> 18.4 us  [attend(): pl.pallas_call(attend_kernel, grid_spec=pltpu.PrefetchScalarGridSpec(num_...]
  transfers between devices with their start and end apart: 65 -> 65, of which waited for: 34 -> 28; matrix products, arithmetic and copies ran while one was open for 18% -> 19% of each run, Pallas kernels for 25% -> 25%
where the time goes in v3:
time: 392 us; the launch traced here: 386 us
  Pallas kernels  119 us (30%)
  waiting for transfers between devices  94.5 us (24%)
  starting transfers between devices  79.8 us (20%)
  other arithmetic  49.3 us (13%)
  local copies, waits for them, and re-layouts  39.6 us (10%)
    ppermute x33, waiting for transfers between devices, turn(): return lax.ppermute(block, 'h', route)  57.3 us
    ppermute x33, starting transfers between devices, turn(): return lax.ppermute(block, 'h', route)  48.1 us
    ppermute x28, waiting for transfers between devices, swap(): return lax.ppermute(block, axis, [(0, 1), (1, 0)])  28.2 us
    pallas_call x1, Pallas kernels, attend_back(): pl.pallas_call(attend_back_kernel, grid_spec=pltpu.PrefetchScalarGridSpec...  27.2 us
    pallas_call x2, Pallas kernels, ffn(): pl.pallas_call(ffn_kernel, in_specs=[vmem()] * 7, out_specs=[vmem()] * 5,...  20.6 us
    pallas_call x1, Pallas kernels, attend(): pl.pallas_call(attend_kernel, grid_spec=pltpu.PrefetchScalarGridSpec(num_...  18.4 us
    all_to_all x4, starting transfers between devices, exchange(): return lax.all_to_all(blocks, 'h', 0, 0)  17 us
    ppermute x28, starting transfers between devices, swap(): return lax.ppermute(block, axis, [(0, 1), (1, 0)])  14.6 us
  transfers between devices with their start and end apart: 65, of which 28 were waited for; matrix products, arithmetic and copies ran while one was open for 19% of the time, Pallas kernels for 25%

profile of v3, /device:TPU:0, one launch (start us, length us, event | category | flops | bytes accessed | tf_op | source)
XLA Modules:
  0.0 386.3 jit_solution(3783420579485874914)
XLA Ops:
  0.7 3.1 collective-permute-start.1
  4.9 1.5 collective-permute-start.4
  8.8 7.1 %collective-permute-done.1.ga.refs_6_ = bf16[256,1024]{1,0:T(8,128)(2,1)S(1)} collective-permute-done((bf16[256,1024]{1,0:T(8,128)(2,1)}, bf16[256,1024]{1,0:T(8,128)(2,1)S(1)}, u32[]{:S(2)}, u32[]{:S(2)}) %collective-permute-start.1) | collective-permute-done | bytes 524320 | tf_op jit(solution)/shard_map/ppermute | solution.py:42
  16.7 6.0 %all-to-all-start = ((bf16[8,112,128]{2,1,0:T(8,128)(2,1)}), bf16[8,112,128]{2,1,0:T(8,128)(2,1)S(1)}, u32[]{:S(2)}, u32[]{:S(2)}) async-start(bf16[8,112,128]{2,1,0:T(8,128)(2,1)} %pad.60.clone), calls=%async_computation | async-start | bytes 458752 | tf_op jit(solution)/shard_map/all_to_all | solution.py:56
  22.8 9.0 %all-to-all-done = bf16[8,112,128]{2,1,0:T(8,128)(2,1)S(1)} async-done(((bf16[8,112,128]{2,1,0:T(8,128)(2,1)}), bf16[8,112,128]{2,1,0:T(8,128)(2,1)S(1)}, u32[]{:S(2)}, u32[]{:S(2)}) %all-to-all-start) | async-done | bytes 229408 | tf_op jit(solution)/shard_map/all_to_all | solution.py:56
  32.7 1.6 collective-permute-start.6
  36.8 3.7 fusion.46
  40.5 2.0 pad_maximum_fusion
  47.6 2.7 collective-permute-done.8.refs_3_
  53.3 1.6 collective-permute-start.13
  56.1 8.2 %qkv5.1 = (bf16[8,256,128]{2,1,0:T(8,128)(2,1)}, bf16[2,8,256,128]{3,2,1,0:T(8,128)(2,1)}, bf16[8,256,1024]{2,1,0:T(8,128)(2,1)}) custom-call(s32[5]{0:T(128)} %compare_select_fusion.9.tab, bf16[288,1024]{1,0:T(8,128)(2,1)} %copy-done.3, bf16[288,1024]{1,0:T(8,128)(2,1)} %copy-done.18, bf16[288,1024]{1,0:T(8,128)(2,1)} %copy-done.17, ...), custom_call_target="tpu_custom_call" | custom-call | flops 1006632960 | bytes 6553600 | tf_op jit(solution)/shard_map/qkv5/pallas_call | solution.py:126
  64.4 4.2 %collective-permute-done.12.refs_0_ = bf16[288,1024]{1,0:T(8,128)(2,1)S(1)} collective-permute-done((bf16[288,1024]{1,0:T(8,128)(2,1)S(1)}, bf16[288,1024]{1,0:T(8,128)(2,1)S(1)}, u32[]{:S(2)}, u32[]{:S(2)}) %collective-permute-start.12) | collective-permute-done | bytes 589856 | tf_op jit(solution)/shard_map/ppermute | solution.py:47
  68.8 1.6 collective-permute-start.14
  71.5 6.3 %collective-permute-done.15.refs_2_ = bf16[128,1024]{1,0:T(8,128)(2,1)S(1)} collective-permute-done((bf16[128,1024]{1,0:T(8,128)(2,1)S(1)}, bf16[128,1024]{1,0:T(8,128)(2,1)S(1)}, u32[]{:S(2)}, u32[]{:S(2)}) %collective-permute-start.15) | collective-permute-done | bytes 262176 | tf_op jit(solution)/shard_map/ppermute | solution.py:47
  79.2 5.9 %qkv3.1 = (bf16[8,256,128]{2,1,0:T(8,128)(2,1)}, bf16[2,8,256,128]{3,2,1,0:T(8,128)(2,1)}, bf16[8,256,1024]{2,1,0:T(8,128)(2,1)}) custom-call(s32[3]{0:T(128)} %compare_select_fusion.8.tab, bf16[288,1024]{1,0:T(8,128)(2,1)} %copy-done.9, bf16[288,1024]{1,0:T(8,128)(2,1)} %copy-done.6, ...), custom_call_target="tpu_custom_call", output_to_operand_aliasing={{0}: (9, {}), {1}: (10, {}), {2}: (11, {})} | custom-call | flops 603979776 | bytes 3932160 | tf_op jit(solution)/shard_map/qkv3/pallas_call | solution.py:126
  86.3 11.2 %collective-permute-start.16 = (bf16[192,1536]{1,0:T(8,128)(2,1)S(1)}, bf16[192,1536]{1,0:T(8,128)(2,1)S(1)}, u32[]{:S(2)}, u32[]{:S(2)}) collective-permute-start(bf16[192,1536]{1,0:T(8,128)(2,1)S(1)} %fusion.35.refs_0_), channel_id=1, source_target_pairs={{0,4},{4,8},{8,12},{12,14},{14,10},{10,6},{6,2},{2,0},{1,5},{5,9},... | collective-permute-start | bytes 1769480 | tf_op jit(solution)/shard_map/ppermute | solution.py:47
  101.4 10.6 %collective-permute-done.16.refs_1_ = bf16[192,1536]{1,0:T(8,128)(2,1)S(1)} collective-permute-done((bf16[192,1536]{1,0:T(8,128)(2,1)S(1)}, bf16[192,1536]{1,0:T(8,128)(2,1)S(1)}, u32[]{:S(2)}, u32[]{:S(2)}) %collective-permute-start.16) | collective-permute-done | bytes 589856 | tf_op jit(solution)/shard_map/ppermute | solution.py:47
  114.1 18.4 %attend.1 = (f32[8,256,128]{2,1,0:T(8,128)}, bf16[8,256,128]{2,1,0:T(8,128)(2,1)}, f32[8,256,1]{2,1,0:T(8,128)}, bf16[2,8,256,128]{3,2,1,0:T(8,128)(2,1)}) custom-call(s32[42]{0:T(128)} %concatenate.91.tab, bf16[8,256,128]{2,1,0:T(8,128)(2,1)} %get-tuple-element.145.q_ref, bf16[2,8,256,128]{3,2,1,0:T(8,128)(2,1)} %get-tuple-element.146.own_ref, ...), custom_call_target="tpu_custom_call" | custom-call | flops 24999999488 | bytes 6291456 | tf_op jit(solution)/shard_map/attend/pallas_call | solution.py:231
  133.4 3.5 all-to-all-start.1
  143.7 2.0 collective-permute-start.21
  145.8 9.0 %collective-permute-done.24.refs_2_ = bf16[8,32,1024]{2,1,0:T(8,128)(2,1)S(1)} collective-permute-done((bf16[8,32,1024]{2,1,0:T(8,128)(2,1)S(1)}, bf16[8,32,1024]{2,1,0:T(8,128)(2,1)S(1)}, u32[]{:S(2)}, u32[]{:S(2)}) %collective-permute-start.24) | collective-permute-done | bytes 524320 | tf_op jit(solution)/shard_map/ppermute | solution.py:42
  154.8 3.4 collective-permute-done.21.refs_3_
  158.2 1.7 collective-permute-done.22.refs_6_
  165.8 3.9 %out_block.1 = (bf16[256,1024]{1,0:T(8,128)(2,1)}, f32[256,1024]{1,0:T(8,128)}, bf16[256,1024]{1,0:T(8,128)(2,1)}, bf16[1024,1024]{1,0:T(8,128)(2,1)}) custom-call(s32[10]{0:T(128)} %pad_add_fusion.tab, bf16[8,256,128]{2,1,0:T(8,128)(2,1)} %copy-done.5, bf16[8,32,1024]{2,1,0:T(8,128)(2,1)} %copy-done.23, bf16[8,32,1024]{2,1,0:T(8,128)(2,1)} %copy-done.33, ...), custom_call_target="tpu_custom_call" | custom-call | flops 536870912 | bytes 6291456 | tf_op jit(solution)/shard_map/out_block/pallas_call | solution.py:358
  170.5 4.6 %weights.1 = (bf16[1024,704]{1,0:T(8,128)(2,1)}, bf16[1024,704]{1,0:T(8,128)(2,1)}, bf16[704,1024]{1,0:T(8,128)(2,1)}) custom-call(s32[10]{0:T(128)} %pad_add_fusion.tab, bf16[192,1536]{1,0:T(8,128)(2,1)} %copy-done.4, bf16[192,1536]{1,0:T(8,128)(2,1)} %copy-done.25, bf16[192,1536]{1,0:T(8,128)(2,1)} %copy-done.26, bf16[192,1536]{1,0:T(8,128)(2,1)} %copy-done.10, ...), custom_call_target="tpu_custom_call" | custom-call | bytes 8650752 | tf_op jit(solution)/shard_map/weights/pallas_call | solution.py:426
  175.9 10.3 %ffn.2 = (bf16[2,256,704]{2,1,0:T(8,128)(2,1)}, bf16[2,256,704]{2,1,0:T(8,128)(2,1)}, bf16[2,256,704]{2,1,0:T(8,128)(2,1)}, bf16[2,256,1024]{2,1,0:T(8,128)(2,1)}, bf16[2,256,1024]{2,1,0:T(8,128)(2,1)}) custom-call(bf16[256,1024]{1,0:T(8,128)(2,1)} %get-tuple-element.168.na.refs_0_, bf16[256,1024]{1,0:T(8,128)(2,1)} %copy-done.58, ...), custom_call_target="tpu_custom_call" | custom-call | flops 4429185024 | bytes 8519680 | tf_op jit(solution)/shard_map/ffn/pallas_call | solution.py:464
  186.5 1.7 collective-permute-done.30.nb.refs_3_
  189.0 10.3 %ffn.3 = (bf16[2,256,704]{2,1,0:T(8,128)(2,1)}, bf16[2,256,704]{2,1,0:T(8,128)(2,1)}, bf16[2,256,704]{2,1,0:T(8,128)(2,1)}, bf16[2,256,1024]{2,1,0:T(8,128)(2,1)}, bf16[2,256,1024]{2,1,0:T(8,128)(2,1)}) custom-call(bf16[256,1024]{1,0:T(8,128)(2,1)} %copy-done.59, bf16[256,1024]{1,0:T(8,128)(2,1)} %copy-done.60, bf16[256,1024]{1,0:T(8,128)(2,1)} %copy-done.56, ...), custom_call_target="tpu_custom_call" | custom-call | flops 4429185024 | bytes 8519680 | tf_op jit(solution)/shard_map/ffn/pallas_call | solution.py:464
  202.7 1.8 collective-permute-start.36
  205.0 11.0 %weight_grads.1 = bf16[8,216,1536]{2,1,0:T(8,128)(2,1)} custom-call(s32[8]{0:T(128)} %compare_select_fusion.tab, bf16[256,1024]{1,0:T(8,128)(2,1)} %get-tuple-element.168.na.refs_0_, bf16[256,1024]{1,0:T(8,128)(2,1)} %copy-done.58, bf16[256,1024]{1,0:T(8,128)(2,1)} %copy-done.59, bf16[256,1024]{1,0:T(8,128)(2,1)} %copy-done.60, bf16[256,1024]{1,0:T(8,128)(2,1)} %bitcast.360, ...), custom_call_target="tpu_custom_call" | custom-call | flops 4429185024 | bytes 14680064 | tf_op jit(solution)/shard_map/weight_grads/pallas_call | solution.py:518
  217.8 4.6 %mid_block.1 = (f32[256,1024]{1,0:T(8,128)}, bf16[256,1024]{1,0:T(8,128)(2,1)}, bf16[8,256,128]{2,1,0:T(8,128)(2,1)}) custom-call(f32[256,1024]{1,0:T(8,128)} %get-tuple-element.164.mid_ref, bf16[256,1024]{1,0:T(8,128)(2,1)} %get-tuple-element.260.pa, bf16[256,1024]{1,0:T(8,128)(2,1)} %copy-done.29, bf16[256,1024]{1,0:T(8,128)(2,1)} %copy-done.30, ...), custom_call_target="tpu_custom_call" | custom-call | flops 536870912 | bytes 6291456 | tf_op jit(solution)/shard_map/mid_block/pallas_call | solution.py:570
  222.4 1.8 convolution_convert_fusion
  224.9 4.1 %all-to-all-start.2 = ((bf16[8,256,128]{2,1,0:T(8,128)(2,1)}), bf16[8,256,128]{2,1,0:T(8,128)(2,1)}, u32[]{:S(2)}, u32[]{:S(2)}) async-start(bf16[8,256,128]{2,1,0:T(8,128)(2,1)} %get-tuple-element.201), calls=%async_computation.2 | async-start | bytes 1048576 | tf_op jit(solution)/shard_map/all_to_all | solution.py:56
  229.1 1.8 convert_add_fusion
  231.0 1.8 collective-permute-start.38
  233.8 2.0 collective-permute-start.40
  236.9 8.0 %collective-permute-done.38 = bf16[1,8,32,1024]{3,2,1,0:T(8,128)(2,1)S(1)} collective-permute-done((bf16[1,8,32,1024]{3,2,1,0:T(8,128)(2,1)S(1)}, bf16[1,8,32,1024]{3,2,1,0:T(8,128)(2,1)S(1)}, u32[]{:S(2)}, u32[]{:S(2)}) %collective-permute-start.38) | collective-permute-done | bytes 524320 | tf_op jit(solution)/shard_map/ppermute | solution.py:42
  246.0 1.9 out_strips.1
  247.9 1.8 slice_bitcast_fusion.18
  249.7 1.6 convert_add_fusion.6
  253.4 1.6 collective-permute-start.41
  255.4 27.2 %attend_back.1 = (f32[8,256,128]{2,1,0:T(8,128)}, f32[2,8,256,128]{3,2,1,0:T(8,128)}, bf16[2,8,256,128]{3,2,1,0:T(8,128)(2,1)}) custom-call(s32[42]{0:T(128)} %concatenate.91.tab, bf16[8,256,128]{2,1,0:T(8,128)(2,1)} %get-tuple-element.145.q_ref, bf16[8,256,128]{2,1,0:T(8,128)(2,1)} %all-to-all-done.2.up_ref, f32[8,256,128]{2,1,0:T(8,128)} %get-tuple-element.206.o_ref, ...), custom_call_target="tpu_custom_call" | custom-call | flops 30000001024 | bytes 10485760 | tf_op jit(solution)/shard_map/attend_back/pallas_call | solution.py:311
  284.9 4.3 %collective-permute-start.44 = (bf16[64,512]{1,0:T(8,128)(2,1)}, bf16[64,512]{1,0:T(8,128)(2,1)}, u32[]{:S(2)}, u32[]{:S(2)}) collective-permute-start(bf16[64,512]{1,0:T(8,128)(2,1)} %get-tuple-element.267), channel_id=1, source_target_pairs={{0,14},{4,10},{8,6},{12,2},{14,0},{10,4},{6,8},{2,12},{1,15},{5,11... | collective-permute-start | bytes 196616 | tf_op jit(solution)/shard_map/ppermute | solution.py:47
  289.3 3.0 fusion.8
  292.2 2.2 collective-permute-start.46
  294.4 12.8 %qkv_back.1 = (bf16[8,256,1024]{2,1,0:T(8,128)(2,1)}, bf16[1024,384]{1,0:T(8,128)(2,1)}) custom-call(s32[8]{0:T(128)} %copy-done.55, f32[8,256,128]{2,1,0:T(8,128)} %get-tuple-element.212.dq_ref, f32[2,8,256,128]{3,2,1,0:T(8,128)} %get-tuple-element.213.own_ref, bf16[2,8,256,128]{3,2,1,0:T(8,128)(2,1)} %collective-permute-done.43.got_ref, ...), custom_call_target="tpu_custom_call" | custom-call | flops 3221225472 | bytes 12582912 | tf_op jit(solution)/shard_map/qkv_back/pallas_call | solution.py:618
  314.2 2.0 collective-permute-start.48
  316.2 4.5 %collective-permute-done.50 = bf16[128,1024]{1,0:T(8,128)(2,1)S(1)} collective-permute-done((bf16[128,1024]{1,0:T(8,128)(2,1)S(1)}, bf16[128,1024]{1,0:T(8,128)(2,1)S(1)}, u32[]{:S(2)}, u32[]{:S(2)}) %collective-permute-start.50) | collective-permute-done | bytes 262176 | tf_op jit(solution)/shard_map/ppermute | solution.py:47
  322.3 1.5 collective-permute-start.51
  324.4 2.8 fusion.3
  329.2 2.2 fusion.39
  332.2 5.0 %collective-permute-done.51 = bf16[256,1024]{1,0:T(8,128)(2,1)S(1)} collective-permute-done((bf16[256,1024]{1,0:T(8,128)(2,1)S(1)}, bf16[256,1024]{1,0:T(8,128)(2,1)S(1)}, u32[]{:S(2)}, u32[]{:S(2)}) %collective-permute-start.51) | collective-permute-done | bytes 524320 | tf_op jit(solution)/shard_map/ppermute | solution.py:47
  338.7 2.6 fusion.19
  341.2 3.4 all-to-all-start.3
  344.6 1.9 collective-permute-start.53
  346.7 5.5 %collective-permute-done.57 = bf16[216,1536]{1,0:T(8,128)(2,1)S(1)} collective-permute-done((bf16[216,1536]{1,0:T(8,128)(2,1)}, bf16[216,1536]{1,0:T(8,128)(2,1)S(1)}, u32[]{:S(2)}, u32[]{:S(2)}) %collective-permute-start.57) | collective-permute-done | bytes 663584 | tf_op jit(solution)/shard_map/ppermute | solution.py:47
  352.2 2.2 collective-permute-done.58
  359.0 1.7 collective-permute-start.60
  363.8 1.7 collective-permute-done.55
  365.5 2.9 fusion.21
  368.4 1.6 collective-permute-start.54
  375.9 4.8 %collective-permute-done.54 = bf16[256,1024]{1,0:T(8,128)(2,1)S(1)} collective-permute-done((bf16[256,1024]{1,0:T(8,128)(2,1)}, bf16[256,1024]{1,0:T(8,128)(2,1)S(1)}, u32[]{:S(2)}, u32[]{:S(2)}) %collective-permute-start.54) | collective-permute-done | bytes 524320 | tf_op jit(solution)/shard_map/ppermute | solution.py:47
  382.2 1.5 fusion.14
  383.7 2.4 fusion.17
  (361 shorter events, 85.5 us)
Async XLA Ops:
  0.7 15.2 %collective-permute-start.1 = (bf16[256,1024]{1,0:T(8,128)(2,1)}, bf16[256,1024]{1,0:T(8,128)(2,1)S(1)}, u32[]{:S(2)}, u32[]{:S(2)}) collective-permute-start(bf16[256,1024]{1,0:T(8,128)(2,1)} %bitcast.357), channel_id=1, source_target_pairs={{0,16},{16,0},{1,17},{17,1},{2,18},{18,2},{3,19},{19,3},{4,20},{20... | collective-permute-start | bytes 1572872 | tf_op jit(solution)/shard_map/ppermute | solution.py:42
  3.8 28.0 %collective-permute-start = (bf16[256,1024]{1,0:T(8,128)(2,1)}, bf16[256,1024]{1,0:T(8,128)(2,1)S(1)}, u32[]{:S(2)}, u32[]{:S(2)}) collective-permute-start(bf16[256,1024]{1,0:T(8,128)(2,1)} %bitcast.358), channel_id=1, source_target_pairs={{0,1},{1,0},{2,3},{3,2},{4,5},{5,4},{6,7},{7,6},{8,9},{9,8},{10,11... | collective-permute-start | bytes 1572872 | tf_op jit(solution)/shard_map/ppermute | solution.py:42
  4.9 26.9 %collective-permute-start.4 = (bf16[288,1024]{1,0:T(8,128)(2,1)S(1)}, bf16[288,1024]{1,0:T(8,128)(2,1)S(1)}, u32[]{:S(2)}, u32[]{:S(2)}) collective-permute-start(bf16[288,1024]{1,0:T(8,128)(2,1)S(1)} %pad_maximum_fusion.5.refs_0_), channel_id=1, source_target_pairs={{0,2},{4,0},{8,4},{12,8},{14,12},{10,14},{6,10},{2,6},{1,3},{5,1},... | collective-permute-start | bytes 1769480 | tf_op jit(solution)/shard_map/ppermute | solution.py:47
  6.4 25.4 %collective-permute-start.3 = (bf16[288,1024]{1,0:T(8,128)(2,1)S(1)}, bf16[288,1024]{1,0:T(8,128)(2,1)S(1)}, u32[]{:S(2)}, u32[]{:S(2)}) collective-permute-start(bf16[288,1024]{1,0:T(8,128)(2,1)S(1)} %pad_maximum_fusion.5.refs_0_), channel_id=1, source_target_pairs={{0,4},{4,8},{8,12},{12,14},{14,10},{10,6},{6,2},{2,0},{1,5},{5,9},... | collective-permute-start | bytes 1769480 | tf_op jit(solution)/shard_map/ppermute | solution.py:47
  15.9 15.9 %collective-permute-start.2 = (bf16[256,1024]{1,0:T(8,128)(2,1)S(1)}, bf16[256,1024]{1,0:T(8,128)(2,1)}, u32[]{:S(2)}, u32[]{:S(2)}) collective-permute-start(bf16[256,1024]{1,0:T(8,128)(2,1)S(1)} %collective-permute-done.1.ga.refs_6_), channel_id=1, source_target_pairs={{0,1},{1,0},{2,3},{3,2},{4,5},{5,4},{6,7},{7,6},{8,9},{9,8},{10,11... | collective-permute-start | bytes 1572872 | tf_op jit(solution)/shard_map/ppermute | solution.py:42
  16.7 15.0 %all-to-all-start = ((bf16[8,112,128]{2,1,0:T(8,128)(2,1)}), bf16[8,112,128]{2,1,0:T(8,128)(2,1)S(1)}, u32[]{:S(2)}, u32[]{:S(2)}) async-start(bf16[8,112,128]{2,1,0:T(8,128)(2,1)} %pad.60.clone), calls=%async_computation | async-start | bytes 458752 | tf_op jit(solution)/shard_map/all_to_all | solution.py:56
  32.7 10.4 %collective-permute-start.6 = (bf16[8,112,128]{2,0,1:T(8,128)(2,1)S(1)}, bf16[8,112,128]{2,0,1:T(8,128)(2,1)S(1)}, u32[]{:S(2)}, u32[]{:S(2)}) collective-permute-start(bf16[8,112,128]{2,0,1:T(8,128)(2,1)S(1)} %copy.328), channel_id=1, source_target_pairs={{0,16},{16,0},{1,17},{17,1},{2,18},{18,2},{3,19},{19,3},{4,20},{20... | collective-permute-start | bytes 688136 | tf_op jit(solution)/shard_map/ppermute | solution.py:42
  34.3 8.6 %collective-permute-start.5 = (bf16[8,112,128]{2,0,1:T(8,128)(2,1)S(1)}, bf16[8,112,128]{2,0,1:T(8,128)(2,1)S(1)}, u32[]{:S(2)}, u32[]{:S(2)}) collective-permute-start(bf16[8,112,128]{2,0,1:T(8,128)(2,1)S(1)} %copy.328), channel_id=1, source_target_pairs={{0,1},{1,0},{2,3},{3,2},{4,5},{5,4},{6,7},{7,6},{8,9},{9,8},{10,11... | collective-permute-start | bytes 688136 | tf_op jit(solution)/shard_map/ppermute | solution.py:42
  34.5 15.7 %collective-permute-start.8 = (bf16[288,1024]{1,0:T(8,128)(2,1)S(1)}, bf16[288,1024]{1,0:T(8,128)(2,1)S(1)}, u32[]{:S(2)}, u32[]{:S(2)}) collective-permute-start(bf16[288,1024]{1,0:T(8,128)(2,1)S(1)} %collective-permute-done.3.refs_1_), channel_id=1, source_target_pairs={{0,4},{4,8},{8,12},{12,14},{14,10},{10,6},{6,2},{2,0},{1,5},{5,9},... | collective-permute-start | bytes 1769480 | tf_op jit(solution)/shard_map/ppermute | solution.py:47
  35.4 15.5 %collective-permute-start.9 = (bf16[288,1024]{1,0:T(8,128)(2,1)S(1)}, bf16[288,1024]{1,0:T(8,128)(2,1)S(1)}, u32[]{:S(2)}, u32[]{:S(2)}) collective-permute-start(bf16[288,1024]{1,0:T(8,128)(2,1)S(1)} %collective-permute-done.4.refs_2_), channel_id=1, source_target_pairs={{0,2},{4,0},{8,4},{12,8},{14,12},{10,14},{6,10},{2,6},{1,3},{5,1},... | collective-permute-start | bytes 1769480 | tf_op jit(solution)/shard_map/ppermute | solution.py:47
  43.1 1.6 collective-permute-start.7
  52.7 2.2 collective-permute-start.10
  52.8 15.8 %collective-permute-start.12 = (bf16[288,1024]{1,0:T(8,128)(2,1)S(1)}, bf16[288,1024]{1,0:T(8,128)(2,1)S(1)}, u32[]{:S(2)}, u32[]{:S(2)}) collective-permute-start(bf16[288,1024]{1,0:T(8,128)(2,1)S(1)} %collective-permute-done.8.refs_3_), channel_id=1, source_target_pairs={{0,4},{4,8},{8,12},{12,14},{14,10},{10,6},{6,2},{2,0},{1,5},{5,9},... | collective-permute-start | bytes 1769480 | tf_op jit(solution)/shard_map/ppermute | solution.py:47
  53.3 15.4 %collective-permute-start.13 = (bf16[288,1024]{1,0:T(8,128)(2,1)S(1)}, bf16[288,1024]{1,0:T(8,128)(2,1)S(1)}, u32[]{:S(2)}, u32[]{:S(2)}) collective-permute-start(bf16[288,1024]{1,0:T(8,128)(2,1)S(1)} %collective-permute-done.9.refs_4_), channel_id=1, source_target_pairs={{0,2},{4,0},{8,4},{12,8},{14,12},{10,14},{6,10},{2,6},{1,3},{5,1},... | collective-permute-start | bytes 1769480 | tf_op jit(solution)/shard_map/ppermute | solution.py:47
  55.0 9.3 %collective-permute-start.11 = (bf16[2,32,1536]{2,1,0:T(8,128)(2,1)S(1)}, bf16[2,32,1536]{2,1,0:T(8,128)(2,1)S(1)}, u32[]{:S(2)}, u32[]{:S(2)}) collective-permute-start(bf16[2,32,1536]{2,1,0:T(8,128)(2,1)S(1)} %get-tuple-element.278), channel_id=1, source_target_pairs={{0,16},{16,0},{1,17},{17,1},{2,18},{18,2},{3,19},{19,3},{4,20},{20... | collective-permute-start | bytes 589832 | tf_op jit(solution)/shard_map/ppermute | solution.py:42
  68.8 9.1 %collective-permute-start.14 = (bf16[160,1024]{1,0:T(8,128)(2,1)S(1)}, bf16[160,1024]{1,0:T(8,128)(2,1)S(1)}, u32[]{:S(2)}, u32[]{:S(2)}) collective-permute-start(bf16[160,1024]{1,0:T(8,128)(2,1)S(1)} %slice.351), channel_id=1, source_target_pairs={{0,2},{4,0},{8,4},{12,8},{14,12},{10,14},{6,10},{2,6},{1,3},{5,1},... | collective-permute-start | bytes 983048 | tf_op jit(solution)/shard_map/ppermute | solution.py:47
  70.4 7.3 %collective-permute-start.15 = (bf16[128,1024]{1,0:T(8,128)(2,1)S(1)}, bf16[128,1024]{1,0:T(8,128)(2,1)S(1)}, u32[]{:S(2)}, u32[]{:S(2)}) collective-permute-start(bf16[128,1024]{1,0:T(8,128)(2,1)S(1)} %slice.352), channel_id=1, source_target_pairs={{0,4},{4,8},{8,12},{12,14},{14,10},{10,6},{6,2},{2,0},{1,5},{5,9},... | collective-permute-start | bytes 786440 | tf_op jit(solution)/shard_map/ppermute | solution.py:47
  85.1 29.0 %collective-permute-start.18 = (bf16[2,8,256,128]{3,2,1,0:T(8,128)(2,1)}, bf16[2,8,256,128]{3,2,1,0:T(8,128)(2,1)}, u32[]{:S(2)}, u32[]{:S(2)}) collective-permute-start(bf16[2,8,256,128]{3,2,1,0:T(8,128)(2,1)} %get-tuple-element.146.own_ref), channel_id=1, source_target_pairs={{0,1},{1,0},{2,3},{3,2},{4,5},{5,4},{6,7},{7,6},{8,9},{9,8},{10,11... | collective-permute-start | bytes 3145736 | tf_op jit(solution)/shard_map/ppermute | solution.py:42
  85.1 16.3 %collective-permute-start.17 = (bf16[192,1536]{1,0:T(8,128)(2,1)S(1)}, bf16[192,1536]{1,0:T(8,128)(2,1)S(1)}, u32[]{:S(2)}, u32[]{:S(2)}) collective-permute-start(bf16[192,1536]{1,0:T(8,128)(2,1)S(1)} %fusion.35.refs_0_), channel_id=1, source_target_pairs={{0,2},{4,0},{8,4},{12,8},{14,12},{10,14},{6,10},{2,6},{1,3},{5,1},... | collective-permute-start | bytes 1769480 | tf_op jit(solution)/shard_map/ppermute | solution.py:47
  86.3 25.7 %collective-permute-start.16 = (bf16[192,1536]{1,0:T(8,128)(2,1)S(1)}, bf16[192,1536]{1,0:T(8,128)(2,1)S(1)}, u32[]{:S(2)}, u32[]{:S(2)}) collective-permute-start(bf16[192,1536]{1,0:T(8,128)(2,1)S(1)} %fusion.35.refs_0_), channel_id=1, source_target_pairs={{0,4},{4,8},{8,12},{12,14},{14,10},{10,6},{6,2},{2,0},{1,5},{5,9},... | collective-permute-start | bytes 1769480 | tf_op jit(solution)/shard_map/ppermute | solution.py:47
  112.0 20.5 %collective-permute-start.19 = (bf16[192,1536]{1,0:T(8,128)(2,1)S(1)}, bf16[192,1536]{1,0:T(8,128)(2,1)S(1)}, u32[]{:S(2)}, u32[]{:S(2)}) collective-permute-start(bf16[192,1536]{1,0:T(8,128)(2,1)S(1)} %collective-permute-done.16.refs_1_), channel_id=1, source_target_pairs={{0,4},{4,8},{8,12},{12,14},{14,10},{10,6},{6,2},{2,0},{1,5},{5,9},... | collective-permute-start | bytes 1769480 | tf_op jit(solution)/shard_map/ppermute | solution.py:47
  112.9 19.6 %collective-permute-start.20 = (bf16[192,1536]{1,0:T(8,128)(2,1)S(1)}, bf16[192,1536]{1,0:T(8,128)(2,1)S(1)}, u32[]{:S(2)}, u32[]{:S(2)}) collective-permute-start(bf16[192,1536]{1,0:T(8,128)(2,1)S(1)} %collective-permute-done.17.refs_8_), channel_id=1, source_target_pairs={{0,2},{4,0},{8,4},{12,8},{14,12},{10,14},{6,10},{2,6},{1,3},{5,1},... | collective-permute-start | bytes 1769480 | tf_op jit(solution)/shard_map/ppermute | solution.py:47
  133.4 26.5 %all-to-all-start.1 = ((bf16[8,256,128]{2,1,0:T(8,128)(2,1)}), bf16[8,256,128]{2,1,0:T(8,128)(2,1)S(1)}, u32[]{:S(2)}, u32[]{:S(2)}) async-start(bf16[8,256,128]{2,1,0:T(8,128)(2,1)} %get-tuple-element.152), calls=%async_computation.1 | async-start | bytes 1048576 | tf_op jit(solution)/shard_map/all_to_all | solution.py:56
  143.6 11.1 %collective-permute-start.24 = (bf16[8,32,1024]{2,1,0:T(8,128)(2,1)S(1)}, bf16[8,32,1024]{2,1,0:T(8,128)(2,1)S(1)}, u32[]{:S(2)}, u32[]{:S(2)}) collective-permute-start(bf16[8,32,1024]{2,1,0:T(8,128)(2,1)S(1)} %bitcast_dynamic-update-slice_fusion.refs_0_), channel_id=1, source_target_pairs={{0,16},{16,0},{1,17},{17,1},{2,18},{18,2},{3,19},{19,3},{4,20},{20... | collective-permute-start | bytes 1572872 | tf_op jit(solution)/shard_map/ppermute | solution.py:42
  143.7 14.4 %collective-permute-start.21 = (bf16[192,1536]{1,0:T(8,128)(2,1)}, bf16[192,1536]{1,0:T(8,128)(2,1)S(1)}, u32[]{:S(2)}, u32[]{:S(2)}) collective-permute-start(bf16[192,1536]{1,0:T(8,128)(2,1)} %copy-done.26), channel_id=1, source_target_pairs={{0,4},{4,8},{8,12},{12,14},{14,10},{10,6},{6,2},{2,0},{1,5},{5,9},... | collective-permute-start | bytes 1769480 | tf_op jit(solution)/shard_map/ppermute | solution.py:47
  145.7 14.2 %collective-permute-start.22 = (bf16[192,1536]{1,0:T(8,128)(2,1)}, bf16[192,1536]{1,0:T(8,128)(2,1)S(1)}, u32[]{:S(2)}, u32[]{:S(2)}) collective-permute-start(bf16[192,1536]{1,0:T(8,128)(2,1)} %copy-done.27), channel_id=1, source_target_pairs={{0,2},{4,0},{8,4},{12,8},{14,12},{10,14},{6,10},{2,6},{1,3},{5,1},... | collective-permute-start | bytes 1769480 | tf_op jit(solution)/shard_map/ppermute | solution.py:47
  145.8 19.2 %collective-permute-start.23 = (bf16[8,32,1024]{2,1,0:T(8,128)(2,1)S(1)}, bf16[8,32,1024]{2,1,0:T(8,128)(2,1)S(1)}, u32[]{:S(2)}, u32[]{:S(2)}) collective-permute-start(bf16[8,32,1024]{2,1,0:T(8,128)(2,1)S(1)} %bitcast_dynamic-update-slice_fusion.refs_0_), channel_id=1, source_target_pairs={{0,1},{1,0},{2,3},{3,2},{4,5},{5,4},{6,7},{7,6},{8,9},{9,8},{10,11... | collective-permute-start | bytes 1572872 | tf_op jit(solution)/shard_map/ppermute | solution.py:42
  154.8 10.2 %collective-permute-start.25 = (bf16[8,32,1024]{2,1,0:T(8,128)(2,1)S(1)}, bf16[8,32,1024]{2,1,0:T(8,128)(2,1)}, u32[]{:S(2)}, u32[]{:S(2)}) collective-permute-start(bf16[8,32,1024]{2,1,0:T(8,128)(2,1)S(1)} %collective-permute-done.24.refs_2_), channel_id=1, source_target_pairs={{0,1},{1,0},{2,3},{3,2},{4,5},{5,4},{6,7},{7,6},{8,9},{9,8},{10,11... | collective-permute-start | bytes 1572872 | tf_op jit(solution)/shard_map/ppermute | solution.py:42
  161.4 8.4 %collective-permute-start.27 = (bf16[96,1536]{1,0:T(8,128)(2,1)}, bf16[96,1536]{1,0:T(8,128)(2,1)}, u32[]{:S(2)}, u32[]{:S(2)}) collective-permute-start(bf16[96,1536]{1,0:T(8,128)(2,1)} %slice.363), channel_id=1, source_target_pairs={{0,2},{4,0},{8,4},{12,8},{14,12},{10,14},{6,10},{2,6},{1,3},{5,1},... | collective-permute-start | bytes 884744 | tf_op jit(solution)/shard_map/ppermute | solution.py:47
  162.5 7.7 %collective-permute-start.26 = (bf16[96,1536]{1,0:T(8,128)(2,1)}, bf16[96,1536]{1,0:T(8,128)(2,1)}, u32[]{:S(2)}, u32[]{:S(2)}) collective-permute-start(bf16[96,1536]{1,0:T(8,128)(2,1)} %slice.362), channel_id=1, source_target_pairs={{0,4},{4,8},{8,12},{12,14},{14,10},{10,6},{6,2},{2,0},{1,5},{5,9},... | collective-permute-start | bytes 884744 | tf_op jit(solution)/shard_map/ppermute | solution.py:47
  170.2 4.9 %collective-permute-start.28 = (bf16[256,1024]{1,0:T(8,128)(2,1)}, bf16[256,1024]{1,0:T(8,128)(2,1)S(1)}, u32[]{:S(2)}, u32[]{:S(2)}) collective-permute-start(bf16[256,1024]{1,0:T(8,128)(2,1)} %get-tuple-element.168.na.refs_0_), channel_id=1, source_target_pairs={{0,1},{1,0},{2,3},{3,2},{4,5},{5,4},{6,7},{7,6},{8,9},{9,8},{10,11... | collective-permute-start | bytes 1572872 | tf_op jit(solution)/shard_map/ppermute | solution.py:42
  170.2 16.0 %collective-permute-start.29 = (bf16[256,1024]{1,0:T(8,128)(2,1)}, bf16[256,1024]{1,0:T(8,128)(2,1)S(1)}, u32[]{:S(2)}, u32[]{:S(2)}) collective-permute-start(bf16[256,1024]{1,0:T(8,128)(2,1)} %get-tuple-element.168.na.refs_0_), channel_id=1, source_target_pairs={{0,16},{16,0},{1,17},{17,1},{2,18},{18,2},{3,19},{19,3},{4,20},{20... | collective-permute-start | bytes 1572872 | tf_op jit(solution)/shard_map/ppermute | solution.py:42
  186.2 2.0 collective-permute-start.30
  200.5 2.0 collective-permute-start.31
  202.1 14.7 %collective-permute-start.35 = (bf16[256,1024]{1,0:T(8,128)(2,1)S(1)}, bf16[256,1024]{1,0:T(8,128)(2,1)S(1)}, u32[]{:S(2)}, u32[]{:S(2)}) collective-permute-start(bf16[256,1024]{1,0:T(8,128)(2,1)S(1)} %get-tuple-element.259), channel_id=1, source_target_pairs={{0,1},{1,0},{2,3},{3,2},{4,5},{5,4},{6,7},{7,6},{8,9},{9,8},{10,11... | collective-permute-start | bytes 1572872 | tf_op jit(solution)/shard_map/ppermute | solution.py:42
  202.7 14.1 %collective-permute-start.36 = (bf16[256,1024]{1,0:T(8,128)(2,1)S(1)}, bf16[256,1024]{1,0:T(8,128)(2,1)S(1)}, u32[]{:S(2)}, u32[]{:S(2)}) collective-permute-start(bf16[256,1024]{1,0:T(8,128)(2,1)S(1)} %fusion.28), channel_id=1, source_target_pairs={{0,16},{16,0},{1,17},{17,1},{2,18},{18,2},{3,19},{19,3},{4,20},{20... | collective-permute-start | bytes 1572872 | tf_op jit(solution)/shard_map/ppermute | solution.py:42
  224.4 4.7 %collective-permute-start.37 = (bf16[1,2,8,32,1024]{4,3,2,1,0:T(8,128)(2,1)S(1)}, bf16[1,2,8,32,1024]{4,3,2,1,0:T(8,128)(2,1)}, u32[]{:S(2)}, u32[]{:S(2)}) collective-permute-start(bf16[1,2,8,32,1024]{4,3,2,1,0:T(8,128)(2,1)S(1)} %select_bitcast_fusion), channel_id=1, source_target_pairs={{0,1},{1,0},{2,3},{3,2},{4,5},{5,4},{6,7},{7,6},{8,9},{9,8},{10,11... | collective-permute-start | bytes 3145736 | tf_op jit(solution)/shard_map/ppermute | solution.py:42
  224.9 28.5 %all-to-all-start.2 = ((bf16[8,256,128]{2,1,0:T(8,128)(2,1)}), bf16[8,256,128]{2,1,0:T(8,128)(2,1)}, u32[]{:S(2)}, u32[]{:S(2)}) async-start(bf16[8,256,128]{2,1,0:T(8,128)(2,1)} %get-tuple-element.201), calls=%async_computation.2 | async-start | bytes 1048576 | tf_op jit(solution)/shard_map/all_to_all | solution.py:56
  231.0 13.9 %collective-permute-start.38 = (bf16[1,8,32,1024]{3,2,1,0:T(8,128)(2,1)S(1)}, bf16[1,8,32,1024]{3,2,1,0:T(8,128)(2,1)S(1)}, u32[]{:S(2)}, u32[]{:S(2)}) collective-permute-start(bf16[1,8,32,1024]{3,2,1,0:T(8,128)(2,1)S(1)} %fusion.37), channel_id=1, source_target_pairs={{0,16},{16,0},{1,17},{17,1},{2,18},{18,2},{3,19},{19,3},{4,20},{20... | collective-permute-start | bytes 1572872 | tf_op jit(solution)/shard_map/ppermute | solution.py:42
  233.8 17.5 %collective-permute-start.40 = (bf16[88,1536]{1,0:T(8,128)(2,1)S(1)}, bf16[88,1536]{1,0:T(8,128)(2,1)S(1)}, u32[]{:S(2)}, u32[]{:S(2)}) collective-permute-start(bf16[88,1536]{1,0:T(8,128)(2,1)S(1)} %slice_bitcast_fusion.8), channel_id=1, source_target_pairs={{0,2},{4,0},{8,4},{12,8},{14,12},{10,14},{6,10},{2,6},{1,3},{5,1},... | collective-permute-start | bytes 811016 | tf_op jit(solution)/shard_map/ppermute | solution.py:47
  236.8 15.6 %collective-permute-start.39 = (bf16[128,1536]{1,0:T(8,128)(2,1)S(1)}, bf16[128,1536]{1,0:T(8,128)(2,1)S(1)}, u32[]{:S(2)}, u32[]{:S(2)}) collective-permute-start(bf16[128,1536]{1,0:T(8,128)(2,1)S(1)} %slice_bitcast_fusion.7), channel_id=1, source_target_pairs={{0,4},{4,8},{8,12},{12,14},{14,10},{10,6},{6,2},{2,0},{1,5},{5,9},... | collective-permute-start | bytes 1179656 | tf_op jit(solution)/shard_map/ppermute | solution.py:47
  253.4 31.6 %collective-permute-start.41 = (bf16[216,1536]{1,0:T(8,128)(2,1)}, bf16[216,1536]{1,0:T(8,128)(2,1)S(1)}, u32[]{:S(2)}, u32[]{:S(2)}) collective-permute-start(bf16[216,1536]{1,0:T(8,128)(2,1)} %pad_maximum_fusion.3), channel_id=1, source_target_pairs={{0,4},{4,8},{8,12},{12,14},{14,10},{10,6},{6,2},{2,0},{1,5},{5,9},... | collective-permute-start | bytes 1990664 | tf_op jit(solution)/shard_map/ppermute | solution.py:47
  255.0 34.3 %collective-permute-start.42 = (bf16[216,1536]{1,0:T(8,128)(2,1)}, bf16[216,1536]{1,0:T(8,128)(2,1)}, u32[]{:S(2)}, u32[]{:S(2)}) collective-permute-start(bf16[216,1536]{1,0:T(8,128)(2,1)} %pad_maximum_fusion.4), channel_id=1, source_target_pairs={{0,2},{4,0},{8,4},{12,8},{14,12},{10,14},{6,10},{2,6},{1,3},{5,1},... | collective-permute-start | bytes 1990664 | tf_op jit(solution)/shard_map/ppermute | solution.py:47
  282.6 9.6 %collective-permute-start.43 = (bf16[2,8,256,128]{3,2,1,0:T(8,128)(2,1)}, bf16[2,8,256,128]{3,2,1,0:T(8,128)(2,1)}, u32[]{:S(2)}, u32[]{:S(2)}) collective-permute-start(bf16[2,8,256,128]{3,2,1,0:T(8,128)(2,1)} %get-tuple-element.214), channel_id=1, source_target_pairs={{0,1},{1,0},{2,3},{3,2},{4,5},{5,4},{6,7},{7,6},{8,9},{9,8},{10,11... | collective-permute-start | bytes 3145736 | tf_op jit(solution)/shard_map/ppermute | solution.py:42
  283.6 24.9 %collective-permute-start.33 = (bf16[256,1024]{1,0:T(8,128)(2,1)}, bf16[256,1024]{1,0:T(8,128)(2,1)S(1)}, u32[]{:S(2)}, u32[]{:S(2)}) collective-permute-start(bf16[256,1024]{1,0:T(8,128)(2,1)} %slice_bitcast_fusion.4), channel_id=1, source_target_pairs={{0,1},{1,0},{2,3},{3,2},{4,5},{5,4},{6,7},{7,6},{8,9},{9,8},{10,11... | collective-permute-start | bytes 1572872 | tf_op jit(solution)/shard_map/ppermute | solution.py:42
  284.9 42.3 %collective-permute-start.32 = (bf16[256,1024]{1,0:T(8,128)(2,1)}, bf16[256,1024]{1,0:T(8,128)(2,1)}, u32[]{:S(2)}, u32[]{:S(2)}) collective-permute-start(bf16[256,1024]{1,0:T(8,128)(2,1)} %slice_bitcast_fusion.5), channel_id=1, source_target_pairs={{0,1},{1,0},{2,3},{3,2},{4,5},{5,4},{6,7},{7,6},{8,9},{9,8},{10,11... | collective-permute-start | bytes 1572872 | tf_op jit(solution)/shard_map/ppermute | solution.py:42
  284.9 25.6 %collective-permute-start.44 = (bf16[64,512]{1,0:T(8,128)(2,1)}, bf16[64,512]{1,0:T(8,128)(2,1)}, u32[]{:S(2)}, u32[]{:S(2)}) collective-permute-start(bf16[64,512]{1,0:T(8,128)(2,1)} %get-tuple-element.267), channel_id=1, source_target_pairs={{0,14},{4,10},{8,6},{12,2},{14,0},{10,4},{6,8},{2,12},{1,15},{5,11... | collective-permute-start | bytes 196616 | tf_op jit(solution)/shard_map/ppermute | solution.py:47
  292.2 18.4 %collective-permute-start.45 = (bf16[216,1536]{1,0:T(8,128)(2,1)}, bf16[216,1536]{1,0:T(8,128)(2,1)S(1)}, u32[]{:S(2)}, u32[]{:S(2)}) collective-permute-start(bf16[216,1536]{1,0:T(8,128)(2,1)} %get-tuple-element.217), channel_id=1, source_target_pairs={{0,4},{4,8},{8,12},{12,14},{14,10},{10,6},{6,2},{2,0},{1,5},{5,9},... | collective-permute-start | bytes 1990664 | tf_op jit(solution)/shard_map/ppermute | solution.py:47
  292.2 18.4 %collective-permute-start.46 = (bf16[216,1536]{1,0:T(8,128)(2,1)}, bf16[216,1536]{1,0:T(8,128)(2,1)}, u32[]{:S(2)}, u32[]{:S(2)}) collective-permute-start(bf16[216,1536]{1,0:T(8,128)(2,1)} %get-tuple-element.218), channel_id=1, source_target_pairs={{0,2},{4,0},{8,4},{12,8},{14,12},{10,14},{6,10},{2,6},{1,3},{5,1},... | collective-permute-start | bytes 1990664 | tf_op jit(solution)/shard_map/ppermute | solution.py:47
  309.2 4.8 %collective-permute-start.47 = (bf16[1,2,8,32,384]{4,3,2,1,0:T(8,128)(2,1)S(1)}, bf16[1,2,8,32,384]{4,3,2,1,0:T(8,128)(2,1)S(1)}, u32[]{:S(2)}, u32[]{:S(2)}) collective-permute-start(bf16[1,2,8,32,384]{4,3,2,1,0:T(8,128)(2,1)S(1)} %fusion.42), channel_id=1, source_target_pairs={{0,1},{1,0},{2,3},{3,2},{4,5},{5,4},{6,7},{7,6},{8,9},{9,8},{10,11... | collective-permute-start | bytes 1179656 | tf_op jit(solution)/shard_map/ppermute | solution.py:42
  310.5 18.2 %collective-permute-start.34 = (bf16[256,1024]{1,0:T(8,128)(2,1)S(1)}, bf16[256,1024]{1,0:T(8,128)(2,1)S(1)}, u32[]{:S(2)}, u32[]{:S(2)}) collective-permute-start(bf16[256,1024]{1,0:T(8,128)(2,1)S(1)} %fusion.24), channel_id=1, source_target_pairs={{0,16},{16,0},{1,17},{17,1},{2,18},{18,2},{3,19},{19,3},{4,20},{20... | collective-permute-start | bytes 1572872 | tf_op jit(solution)/shard_map/ppermute | solution.py:42
  312.0 8.8 %collective-permute-start.50 = (bf16[128,1024]{1,0:T(8,128)(2,1)S(1)}, bf16[128,1024]{1,0:T(8,128)(2,1)S(1)}, u32[]{:S(2)}, u32[]{:S(2)}) collective-permute-start(bf16[128,1024]{1,0:T(8,128)(2,1)S(1)} %get-tuple-element.252), channel_id=1, source_target_pairs={{0,2},{4,0},{8,4},{12,8},{14,12},{10,14},{6,10},{2,6},{1,3},{5,1},... | collective-permute-start | bytes 786440 | tf_op jit(solution)/shard_map/ppermute | solution.py:47
  312.8 8.2 %collective-permute-start.49 = (bf16[128,1024]{1,0:T(8,128)(2,1)S(1)}, bf16[128,1024]{1,0:T(8,128)(2,1)S(1)}, u32[]{:S(2)}, u32[]{:S(2)}) collective-permute-start(bf16[128,1024]{1,0:T(8,128)(2,1)S(1)} %get-tuple-element.254), channel_id=1, source_target_pairs={{0,4},{4,8},{8,12},{12,14},{14,10},{10,6},{6,2},{2,0},{1,5},{5,9},... | collective-permute-start | bytes 786440 | tf_op jit(solution)/shard_map/ppermute | solution.py:47
  314.2 17.2 %collective-permute-start.48 = (bf16[1,8,32,384]{3,2,1,0:T(8,128)(2,1)S(1)}, bf16[1,8,32,384]{3,2,1,0:T(8,128)(2,1)S(1)}, u32[]{:S(2)}, u32[]{:S(2)}) collective-permute-start(bf16[1,8,32,384]{3,2,1,0:T(8,128)(2,1)S(1)} %fusion.48), channel_id=1, source_target_pairs={{0,16},{16,0},{1,17},{17,1},{2,18},{18,2},{3,19},{19,3},{4,20},{20... | collective-permute-start | bytes 589832 | tf_op jit(solution)/shard_map/ppermute | solution.py:42
  322.3 14.9 %collective-permute-start.51 = (bf16[256,1024]{1,0:T(8,128)(2,1)S(1)}, bf16[256,1024]{1,0:T(8,128)(2,1)S(1)}, u32[]{:S(2)}, u32[]{:S(2)}) collective-permute-start(bf16[256,1024]{1,0:T(8,128)(2,1)S(1)} %pad_maximum_fusion.6), channel_id=1, source_target_pairs={{0,4},{4,8},{8,12},{12,14},{14,10},{10,6},{6,2},{2,0},{1,5},{5,9},... | collective-permute-start | bytes 1572872 | tf_op jit(solution)/shard_map/ppermute | solution.py:47
  323.9 14.8 %collective-permute-start.52 = (bf16[256,1024]{1,0:T(8,128)(2,1)S(1)}, bf16[256,1024]{1,0:T(8,128)(2,1)S(1)}, u32[]{:S(2)}, u32[]{:S(2)}) collective-permute-start(bf16[256,1024]{1,0:T(8,128)(2,1)S(1)} %pad_maximum_fusion.7), channel_id=1, source_target_pairs={{0,2},{4,0},{8,4},{12,8},{14,12},{10,14},{6,10},{2,6},{1,3},{5,1},... | collective-permute-start | bytes 1572872 | tf_op jit(solution)/shard_map/ppermute | solution.py:47
  327.2 25.0 %collective-permute-start.57 = (bf16[216,1536]{1,0:T(8,128)(2,1)}, bf16[216,1536]{1,0:T(8,128)(2,1)S(1)}, u32[]{:S(2)}, u32[]{:S(2)}) collective-permute-start(bf16[216,1536]{1,0:T(8,128)(2,1)} %get-tuple-element.241), channel_id=1, source_target_pairs={{0,4},{4,8},{8,12},{12,14},{14,10},{10,6},{6,2},{2,0},{1,5},{5,9},... | collective-permute-start | bytes 1990664 | tf_op jit(solution)/shard_map/ppermute | solution.py:47
  328.7 25.8 %collective-permute-start.58 = (bf16[216,1536]{1,0:T(8,128)(2,1)S(1)}, bf16[216,1536]{1,0:T(8,128)(2,1)S(1)}, u32[]{:S(2)}, u32[]{:S(2)}) collective-permute-start(bf16[216,1536]{1,0:T(8,128)(2,1)S(1)} %get-tuple-element.242), channel_id=1, source_target_pairs={{0,2},{4,0},{8,4},{12,8},{14,12},{10,14},{6,10},{2,6},{1,3},{5,1},... | collective-permute-start | bytes 1990664 | tf_op jit(solution)/shard_map/ppermute | solution.py:47
  341.2 19.6 %all-to-all-start.3 = ((bf16[8,32,384]{2,1,0:T(8,128)(2,1)}), bf16[8,32,384]{2,1,0:T(8,128)(2,1)S(1)}, u32[]{:S(2)}, u32[]{:S(2)}) async-start(bf16[8,32,384]{2,1,0:T(8,128)(2,1)} %fusion.49), calls=%async_computation.3 | async-start | bytes 393216 | tf_op jit(solution)/shard_map/all_to_all | solution.py:56
  344.6 19.1 %collective-permute-start.53 = (bf16[256,1024]{1,0:T(8,128)(2,1)}, bf16[256,1024]{1,0:T(8,128)(2,1)}, u32[]{:S(2)}, u32[]{:S(2)}) collective-permute-start(bf16[256,1024]{1,0:T(8,128)(2,1)} %get-tuple-element.225), channel_id=1, source_target_pairs={{0,4},{4,8},{8,12},{12,14},{14,10},{10,6},{6,2},{2,0},{1,5},{5,9},... | collective-permute-start | bytes 1572872 | tf_op jit(solution)/shard_map/ppermute | solution.py:47
  346.6 18.9 %collective-permute-start.55 = (bf16[256,1024]{1,0:T(8,128)(2,1)}, bf16[256,1024]{1,0:T(8,128)(2,1)}, u32[]{:S(2)}, u32[]{:S(2)}) collective-permute-start(bf16[256,1024]{1,0:T(8,128)(2,1)} %get-tuple-element.226), channel_id=1, source_target_pairs={{0,2},{4,0},{8,4},{12,8},{14,12},{10,14},{6,10},{2,6},{1,3},{5,1},... | collective-permute-start | bytes 1572872 | tf_op jit(solution)/shard_map/ppermute | solution.py:47
  359.0 11.4 %collective-permute-start.60 = (bf16[2,32,1536]{2,1,0:T(8,128)(2,1)S(1)}, bf16[2,32,1536]{2,1,0:T(8,128)(2,1)S(1)}, u32[]{:S(2)}, u32[]{:S(2)}) collective-permute-start(bf16[2,32,1536]{2,1,0:T(8,128)(2,1)S(1)} %fusion.47), channel_id=1, source_target_pairs={{0,16},{16,0},{1,17},{17,1},{2,18},{18,2},{3,19},{19,3},{4,20},{20... | collective-permute-start | bytes 589832 | tf_op jit(solution)/shard_map/ppermute | solution.py:42
  368.4 12.3 %collective-permute-start.54 = (bf16[256,1024]{1,0:T(8,128)(2,1)}, bf16[256,1024]{1,0:T(8,128)(2,1)S(1)}, u32[]{:S(2)}, u32[]{:S(2)}) collective-permute-start(bf16[256,1024]{1,0:T(8,128)(2,1)} %get-tuple-element.247), channel_id=1, source_target_pairs={{0,4},{4,8},{8,12},{12,14},{14,10},{10,6},{6,2},{2,0},{1,5},{5,9},... | collective-permute-start | bytes 1572872 | tf_op jit(solution)/shard_map/ppermute | solution.py:47
  370.0 12.2 %collective-permute-start.56 = (bf16[256,1024]{1,0:T(8,128)(2,1)}, bf16[256,1024]{1,0:T(8,128)(2,1)S(1)}, u32[]{:S(2)}, u32[]{:S(2)}) collective-permute-start(bf16[256,1024]{1,0:T(8,128)(2,1)} %get-tuple-element.248), channel_id=1, source_target_pairs={{0,2},{4,0},{8,4},{12,8},{14,12},{10,14},{6,10},{2,6},{1,3},{5,1},... | collective-permute-start | bytes 1572872 | tf_op jit(solution)/shard_map/ppermute | solution.py:47
  (65 other events, 510.4 us)

commit v4 on v3

--- a/solution.py
+++ b/solution.py
@@ -133,9 +133,7 @@
         ],
         input_output_aliases={len(flat) + 5 + i: i for i in range(len(held))},
         cost_estimate=pl.CostEstimate(
-            flops=2 * len(xs) * count * D * 3 * HEAD_DIM,
-            bytes_accessed=5 * len(xs) * count * D,
-            transcendentals=0,
+            flops=len(xs) * count * D, bytes_accessed=len(xs) * count, transcendentals=0
         ),
         name=f"qkv{len(xs)}",
     )(chips, *flat, gain, w, cos, sin, *held)
@@ -704,8 +702,8 @@
     up_c = swap(upstream, "c")
     up_y = swap(upstream, "dl")
     up_yc = swap(up_y, "c")
-    got, up_c, up_y, up_yc, x_forth, x_back, parity = lax.optimization_barrier(
-        (got, up_c, up_y, up_yc, turn(block, 1), turn(block, -1), core)
+    got, x_forth, x_back, parity = lax.optimization_barrier(
+        (got, turn(block, 1), turn(block, -1), core)
     )
     forth, back = [block, x_forth, turn(x_forth, 1)], [block, x_back, turn(x_back, -1)]
     got_c = swap(got, "c")
@@ -771,11 +769,11 @@
     sine = jnp.concatenate([-sine, sine], axis=-1)
 
     seg_thin = seg_own.reshape(HEADS, count, 1)
-    early = (w_qkv, gain_one, cosine, sine, tab, seg_thin, idx)
+    early = (w_qkv, gain_one, cosine, sine, tab, up_c, up_y, up_yc)
     early, gate_late, up_late, forth[2], back[2] = lax.optimization_barrier(
         (early, gate_weight, up_weight, forth[2], back[2])
     )
-    w_qkv, gain_one, cosine, sine, tab, seg_thin, idx = early
+    w_qkv, gain_one, cosine, sine, tab, up_c, up_y, up_yc = early
     forth.append(turn(forth[2], 1))
     back.append(turn(back[2], -1))
     at_near, at_far = [0, 1, 7, 2, 6], [3, 5, 4]
@@ -827,27 +825,28 @@
     queries, own, normed_one = qkv_blocks(
         chips_at(at_far), far_slots, gain_one, w_qkv, cosine, sine, tuple(held)
     )
+    outs = jnp.stack([v[-rows:] for v in (*forth, far_last, *back[:0:-1])])
+    queries, own, outs, w_forth[1], w_back[1] = lax.optimization_barrier(
+        (queries, own, outs, w_forth[1], w_back[1])
+    )
     other = swap(own, "c")
+    outs_c = swap(outs, "c")
+    outs_y = swap(outs, "dl")
     seg_own_row = seg_own.reshape(HEADS, 1, count)
     seg_oth_row = seg_oth.reshape(HEADS, 1, count)
     cached = [cache[0].reshape(-1, D) for cache in (cache_keys, cache_values)]
-    queries, w_forth[1], w_back[1] = lax.optimization_barrier((queries, w_forth[1], w_back[1]))
     attention, attention_low, lse, memory = attend(
         tab, queries, own, other, seg_thin, seg_own_row, seg_oth_row, idx, *cached
     )
     w_forth.append(turn(w_forth[1], 1))
     w_back.append(turn(w_back[1], -1))
-    out_rows = [*forth, far_last, *back[:0:-1]]
-    *out_rows, attention_low, w_forth[2], w_back[2] = lax.optimization_barrier(
-        (*out_rows, attention_low, w_forth[2], w_back[2])
+    attention_low, outs_y, w_forth[2], w_back[2] = lax.optimization_barrier(
+        (attention_low, outs_y, w_forth[2], w_back[2])
     )
 
     heads = exchange(attention_low)
     w_forth.append(turn(w_forth[2], 1))
     w_back.append(turn(w_back[2], -1))
-    outs = jnp.stack([v[-rows:] for v in out_rows])
-    outs_c = swap(outs, "c")
-    outs_y = swap(outs, "dl")
     outs_yc = swap(outs_y, "c")
     heads, w_forth[3], w_back[3] = lax.optimization_barrier((heads, w_forth[3], w_back[3]))
     w_first, w_last = turn(w_forth[3][:upper], 1), turn(w_back[3][upper:], -1)
@@ -991,12 +990,10 @@
         chips.astype(jnp.int32), dq, d_own, d_got, cosine, sine, normed_one, w_qkv
     )
     arrived_forth, arrived_back = turn(forth, 1), turn(back, -1)
-    dx, out_far, arrived_forth, arrived_back = lax.optimization_barrier(
-        (dx, out_far, arrived_forth, arrived_back)
-    )
+    dx, arrived_forth, arrived_back = lax.optimization_barrier((dx, arrived_forth, arrived_back))
     dx_forth, dx_back = ring_first(dx, split)
-    dx_forth, dx_back, arrived_forth, arrived_back = lax.optimization_barrier(
-        (dx_forth, dx_back, arrived_forth, arrived_back)
+    dw, dx_forth, dx_back, arrived_forth, arrived_back = lax.optimization_barrier(
+        (dw, dx_forth, dx_back, arrived_forth, arrived_back)
     )
     forth = plus(blocks[HEADS - 1], arrived_forth, 0)
     back = plus(blocks[1], arrived_back, 0)

time: 392 us -> 392 us (level)
  starting transfers between devices: 79.8 us -> 86.1 us
  Pallas kernels: 119 us -> 114 us
    ppermute x28, waiting for transfers between devices: 28.2 us -> 17.3 us  [swap(): return lax.ppermute(block, axis, [(0, 1), (1, 0)])]
    ppermute x33, waiting for transfers between devices: 57.3 us -> 66.4 us  [turn(): return lax.ppermute(block, 'h', route)]
    unnamed x145 -> x149, local copies, waits for them, and re-layouts: 14.6 us -> 11.9 us
  transfers between devices with their start and end apart: 65 -> 65, of which waited for: 28 -> 28; matrix products, arithmetic and copies ran while one was open for 19% -> 18% of each run, Pallas kernels for 25% -> 26%
where the time goes in v4:
time: 392 us; the launch traced here: 385 us
  Pallas kernels  114 us (29%)
  waiting for transfers between devices  92.8 us (24%)
  starting transfers between devices  86.1 us (22%)
  other arithmetic  48.9 us (12%)
  local copies, waits for them, and re-layouts  39.4 us (10%)
    ppermute x33, waiting for transfers between devices, turn(): return lax.ppermute(block, 'h', route)  66.4 us
    ppermute x33, starting transfers between devices, turn(): return lax.ppermute(block, 'h', route)  51.6 us
    pallas_call x1, Pallas kernels, attend_back(): pl.pallas_call(attend_back_kernel, grid_spec=pltpu.PrefetchScalarGridSpec...  23.4 us
    pallas_call x2, Pallas kernels, ffn(): pl.pallas_call(ffn_kernel, in_specs=[vmem()] * 7, out_specs=[vmem()] * 5,...  20.8 us
    all_to_all x4, starting transfers between devices, exchange(): return lax.all_to_all(blocks, 'h', 0, 0)  19.5 us
    ppermute x28, waiting for transfers between devices, swap(): return lax.ppermute(block, axis, [(0, 1), (1, 0)])  17.3 us
    pallas_call x1, Pallas kernels, attend(): pl.pallas_call(attend_kernel, grid_spec=pltpu.PrefetchScalarGridSpec(num_...  16.4 us
    ppermute x28, starting transfers between devices, swap(): return lax.ppermute(block, axis, [(0, 1), (1, 0)])  14.9 us
  transfers between devices with their start and end apart: 65, of which 28 were waited for; matrix products, arithmetic and copies ran while one was open for 18% of the time, Pallas kernels for 26%

profile of v4, /device:TPU:0, one launch (start us, length us, event | category | flops | bytes accessed | tf_op | source)
XLA Modules:
  0.0 384.9 jit_solution(4921536424684150801)
XLA Ops:
  0.7 3.1 collective-permute-start.6
  4.9 1.5 collective-permute-start.1
  9.6 5.8 %all-to-all-start = ((bf16[8,112,128]{2,1,0:T(8,128)(2,1)}), bf16[8,112,128]{2,1,0:T(8,128)(2,1)S(1)}, u32[]{:S(2)}, u32[]{:S(2)}) async-start(bf16[8,112,128]{2,1,0:T(8,128)(2,1)} %pad.60.clone), calls=%async_computation | async-start | bytes 458752 | tf_op jit(solution)/shard_map/all_to_all | solution.py:56
  19.7 8.7 %all-to-all-done = bf16[8,112,128]{2,1,0:T(8,128)(2,1)S(1)} async-done(((bf16[8,112,128]{2,1,0:T(8,128)(2,1)}), bf16[8,112,128]{2,1,0:T(8,128)(2,1)S(1)}, u32[]{:S(2)}, u32[]{:S(2)}) %all-to-all-start) | async-done | bytes 229408 | tf_op jit(solution)/shard_map/all_to_all | solution.py:56
  29.9 3.7 fusion.46
  33.7 2.0 pad_maximum_fusion
  35.7 1.9 collective-permute-start.9
  42.9 2.6 collective-permute-done.8.refs_3_
  45.5 5.7 %collective-permute-done.9.refs_4_ = bf16[288,1024]{1,0:T(8,128)(2,1)S(1)} collective-permute-done((bf16[288,1024]{1,0:T(8,128)(2,1)S(1)}, bf16[288,1024]{1,0:T(8,128)(2,1)S(1)}, u32[]{:S(2)}, u32[]{:S(2)}) %collective-permute-start.9) | collective-permute-done | bytes 589856 | tf_op jit(solution)/shard_map/ppermute | solution.py:47
  55.4 1.6 collective-permute-start.11
  57.0 8.3 %qkv5.1 = (bf16[8,256,128]{2,1,0:T(8,128)(2,1)}, bf16[2,8,256,128]{3,2,1,0:T(8,128)(2,1)}, bf16[8,256,1024]{2,1,0:T(8,128)(2,1)}) custom-call(s32[5]{0:T(128)} %compare_select_fusion.8.tab, bf16[288,1024]{1,0:T(8,128)(2,1)} %copy-done.4, bf16[288,1024]{1,0:T(8,128)(2,1)} %copy-done.18, bf16[288,1024]{1,0:T(8,128)(2,1)} %copy-done.17, ...), custom_call_target="tpu_custom_call" | custom-call | flops 1310720 | bytes 1280 | tf_op jit(solution)/shard_map/qkv5/pallas_call | solution.py:126
  65.5 3.7 collective-permute-done.12.refs_0_
  72.7 4.6 %collective-permute-done.14.refs_2_ = bf16[128,1024]{1,0:T(8,128)(2,1)S(1)} collective-permute-done((bf16[128,1024]{1,0:T(8,128)(2,1)S(1)}, bf16[128,1024]{1,0:T(8,128)(2,1)S(1)}, u32[]{:S(2)}, u32[]{:S(2)}) %collective-permute-start.14) | collective-permute-done | bytes 262176 | tf_op jit(solution)/shard_map/ppermute | solution.py:47
  78.1 1.5 collective-permute-done.15.refs_3_
  80.6 11.9 %collective-permute-start.16 = (bf16[192,1536]{1,0:T(8,128)(2,1)S(1)}, bf16[192,1536]{1,0:T(8,128)(2,1)}, u32[]{:S(2)}, u32[]{:S(2)}) collective-permute-start(bf16[192,1536]{1,0:T(8,128)(2,1)S(1)} %fusion.35.refs_0_), channel_id=1, source_target_pairs={{0,4},{4,8},{8,12},{12,14},{14,10},{10,6},{6,2},{2,0},{1,5},{5,9},... | collective-permute-start | bytes 1769480 | tf_op jit(solution)/shard_map/ppermute | solution.py:47
  92.5 5.9 %qkv3.1 = (bf16[8,256,128]{2,1,0:T(8,128)(2,1)}, bf16[2,8,256,128]{3,2,1,0:T(8,128)(2,1)}, bf16[8,256,1024]{2,1,0:T(8,128)(2,1)}) custom-call(s32[3]{0:T(128)} %compare_select_fusion.9.tab, bf16[288,1024]{1,0:T(8,128)(2,1)} %copy-done.9, bf16[288,1024]{1,0:T(8,128)(2,1)} %copy-done.6, ...), custom_call_target="tpu_custom_call", output_to_operand_aliasing={{0}: (9, {}), {1}: (10, {}), {2}: (11, {})} | custom-call | flops 786432 | bytes 768 | tf_op jit(solution)/shard_map/qkv3/pallas_call | solution.py:126
  101.0 3.8 collective-permute-done.16.refs_1_
  108.7 1.5 collective-permute-start.19
  112.2 16.4 %attend.1 = (f32[8,256,128]{2,1,0:T(8,128)}, bf16[8,256,128]{2,1,0:T(8,128)(2,1)}, f32[8,256,1]{2,1,0:T(8,128)}, bf16[2,8,256,128]{3,2,1,0:T(8,128)(2,1)}) custom-call(s32[42]{0:T(128)} %concatenate.91.tab, bf16[8,256,128]{2,1,0:T(8,128)(2,1)} %get-tuple-element.139.q_ref, bf16[2,8,256,128]{3,2,1,0:T(8,128)(2,1)} %get-tuple-element.140.own_ref, ...), custom_call_target="tpu_custom_call" | custom-call | flops 24999999488 | bytes 6291456 | tf_op jit(solution)/shard_map/attend/pallas_call | solution.py:229
  129.7 4.2 %all-to-all-start.1 = ((bf16[8,256,128]{2,1,0:T(8,128)(2,1)}), bf16[8,256,128]{2,1,0:T(8,128)(2,1)S(1)}, u32[]{:S(2)}, u32[]{:S(2)}) async-start(bf16[8,256,128]{2,1,0:T(8,128)(2,1)} %get-tuple-element.145), calls=%async_computation.1 | async-start | bytes 1048576 | tf_op jit(solution)/shard_map/all_to_all | solution.py:56
  133.9 2.0 collective-permute-start.22
  136.5 17.6 %collective-permute-done.22.refs_3_ = bf16[192,1536]{1,0:T(8,128)(2,1)S(1)} collective-permute-done((bf16[192,1536]{1,0:T(8,128)(2,1)}, bf16[192,1536]{1,0:T(8,128)(2,1)S(1)}, u32[]{:S(2)}, u32[]{:S(2)}) %collective-permute-start.22) | collective-permute-done | bytes 589856 | tf_op jit(solution)/shard_map/ppermute | solution.py:47
  154.1 2.2 collective-permute-done.23.refs_6_
  159.2 2.8 collective-permute-start.26
  164.2 4.0 %out_block.1 = (bf16[256,1024]{1,0:T(8,128)(2,1)}, f32[256,1024]{1,0:T(8,128)}, bf16[256,1024]{1,0:T(8,128)(2,1)}, bf16[1024,1024]{1,0:T(8,128)(2,1)}) custom-call(s32[10]{0:T(128)} %pad_add_fusion.tab, bf16[8,256,128]{2,1,0:T(8,128)(2,1)} %copy-done.5, bf16[8,32,1024]{2,1,0:T(8,128)(2,1)} %copy-done.24, bf16[8,32,1024]{2,1,0:T(8,128)(2,1)} %copy-done.31, ...), custom_call_target="tpu_custom_call" | custom-call | flops 536870912 | bytes 6291456 | tf_op jit(solution)/shard_map/out_block/pallas_call | solution.py:356
  169.1 4.7 %weights.1 = (bf16[1024,704]{1,0:T(8,128)(2,1)}, bf16[1024,704]{1,0:T(8,128)(2,1)}, bf16[704,1024]{1,0:T(8,128)(2,1)}) custom-call(s32[10]{0:T(128)} %pad_add_fusion.tab, bf16[192,1536]{1,0:T(8,128)(2,1)} %copy-done.3, bf16[192,1536]{1,0:T(8,128)(2,1)} %collective-permute-done.16.refs_1_, bf16[192,1536]{1,0:T(8,128)(2,1)} %collective-permute-done.20.refs_2_, ...), custom_call_target="tpu_custom_call" | custom-call | bytes 8650752 | tf_op jit(solution)/shard_map/weights/pallas_call | solution.py:424
  174.5 10.3 %ffn.2 = (bf16[2,256,704]{2,1,0:T(8,128)(2,1)}, bf16[2,256,704]{2,1,0:T(8,128)(2,1)}, bf16[2,256,704]{2,1,0:T(8,128)(2,1)}, bf16[2,256,1024]{2,1,0:T(8,128)(2,1)}, bf16[2,256,1024]{2,1,0:T(8,128)(2,1)}) custom-call(bf16[256,1024]{1,0:T(8,128)(2,1)} %get-tuple-element.154.na.refs_0_, bf16[256,1024]{1,0:T(8,128)(2,1)} %copy-done.60, ...), custom_call_target="tpu_custom_call" | custom-call | flops 4429185024 | bytes 8519680 | tf_op jit(solution)/shard_map/ffn/pallas_call | solution.py:462
  185.5 1.5 collective-permute-done.30.nb.refs_3_
  187.8 10.4 %ffn.3 = (bf16[2,256,704]{2,1,0:T(8,128)(2,1)}, bf16[2,256,704]{2,1,0:T(8,128)(2,1)}, bf16[2,256,704]{2,1,0:T(8,128)(2,1)}, bf16[2,256,1024]{2,1,0:T(8,128)(2,1)}, bf16[2,256,1024]{2,1,0:T(8,128)(2,1)}) custom-call(bf16[256,1024]{1,0:T(8,128)(2,1)} %copy-done.61, bf16[256,1024]{1,0:T(8,128)(2,1)} %copy-done.62, ...), custom_call_target="tpu_custom_call" | custom-call | flops 4429185024 | bytes 8519680 | tf_op jit(solution)/shard_map/ffn/pallas_call | solution.py:462
  201.7 1.9 collective-permute-start.36
  204.1 11.0 %weight_grads.1 = bf16[8,216,1536]{2,1,0:T(8,128)(2,1)} custom-call(s32[8]{0:T(128)} %compare_select_fusion.tab, bf16[256,1024]{1,0:T(8,128)(2,1)} %get-tuple-element.154.na.refs_0_, bf16[256,1024]{1,0:T(8,128)(2,1)} %copy-done.60, bf16[256,1024]{1,0:T(8,128)(2,1)} %copy-done.61, bf16[256,1024]{1,0:T(8,128)(2,1)} %copy-done.62, bf16[256,1024]{1,0:T(8,128)(2,1)} %bitcast.362, ...), custom_call_target="tpu_custom_call" | custom-call | flops 4429185024 | bytes 14680064 | tf_op jit(solution)/shard_map/weight_grads/pallas_call | solution.py:516
  216.9 4.7 %mid_block.1 = (f32[256,1024]{1,0:T(8,128)}, bf16[256,1024]{1,0:T(8,128)(2,1)}, bf16[8,256,128]{2,1,0:T(8,128)(2,1)}) custom-call(f32[256,1024]{1,0:T(8,128)} %get-tuple-element.150.mid_ref, bf16[256,1024]{1,0:T(8,128)(2,1)} %get-tuple-element.246.pa, bf16[256,1024]{1,0:T(8,128)(2,1)} %copy-done.27, bf16[256,1024]{1,0:T(8,128)(2,1)} %copy-done.28, ...), custom_call_target="tpu_custom_call" | custom-call | flops 536870912 | bytes 6291456 | tf_op jit(solution)/shard_map/mid_block/pallas_call | solution.py:568
  221.6 1.8 convolution_convert_fusion
  225.8 4.1 %all-to-all-start.2 = ((bf16[8,256,128]{2,1,0:T(8,128)(2,1)}), bf16[8,256,128]{2,1,0:T(8,128)(2,1)}, u32[]{:S(2)}, u32[]{:S(2)}) async-start(bf16[8,256,128]{2,1,0:T(8,128)(2,1)} %get-tuple-element.187), calls=%async_computation.2 | async-start | bytes 1048576 | tf_op jit(solution)/shard_map/all_to_all | solution.py:56
  230.0 1.8 convert_add_fusion
  231.9 1.8 collective-permute-start.38
  234.7 1.9 collective-permute-start.40
  237.8 8.5 %collective-permute-done.38 = bf16[1,8,32,1024]{3,2,1,0:T(8,128)(2,1)S(1)} collective-permute-done((bf16[1,8,32,1024]{3,2,1,0:T(8,128)(2,1)S(1)}, bf16[1,8,32,1024]{3,2,1,0:T(8,128)(2,1)S(1)}, u32[]{:S(2)}, u32[]{:S(2)}) %collective-permute-start.38) | collective-permute-done | bytes 524320 | tf_op jit(solution)/shard_map/ppermute | solution.py:42
  247.4 1.9 out_strips.1
  249.3 1.8 slice_bitcast_fusion.19
  251.1 1.6 convert_add_fusion.6
  254.8 1.6 collective-permute-start.41
  256.8 23.4 %attend_back.1 = (f32[8,256,128]{2,1,0:T(8,128)}, f32[2,8,256,128]{3,2,1,0:T(8,128)}, bf16[2,8,256,128]{3,2,1,0:T(8,128)(2,1)}) custom-call(s32[42]{0:T(128)} %concatenate.91.tab, bf16[8,256,128]{2,1,0:T(8,128)(2,1)} %get-tuple-element.139.q_ref, bf16[8,256,128]{2,1,0:T(8,128)(2,1)} %all-to-all-done.2.up_ref, f32[8,256,128]{2,1,0:T(8,128)} %get-tuple-element.192.o_ref, ...), custom_call_target="tpu_custom_call" | custom-call | flops 30000001024 | bytes 10485760 | tf_op jit(solution)/shard_map/attend_back/pallas_call | solution.py:309
  281.2 3.0 fusion.8
  284.1 1.6 collective-permute-start.44
  287.2 2.0 fusion.24
  289.2 1.7 collective-permute-start.34
  290.9 12.8 %qkv_back.1 = (bf16[8,256,1024]{2,1,0:T(8,128)(2,1)}, bf16[1024,384]{1,0:T(8,128)(2,1)}) custom-call(s32[8]{0:T(128)} %copy-done.59, f32[8,256,128]{2,1,0:T(8,128)} %get-tuple-element.198.dq_ref, f32[2,8,256,128]{3,2,1,0:T(8,128)} %get-tuple-element.199.own_ref, bf16[2,8,256,128]{3,2,1,0:T(8,128)(2,1)} %collective-permute-done.43.got_ref, ...), custom_call_target="tpu_custom_call" | custom-call | flops 3221225472 | bytes 12582912 | tf_op jit(solution)/shard_map/qkv_back/pallas_call | solution.py:616
  305.2 1.8 collective-permute-start.47
  307.3 2.2 fusion.39
  309.4 4.3 %collective-permute-start.58 = (bf16[64,512]{1,0:T(8,128)(2,1)S(1)}, bf16[64,512]{1,0:T(8,128)(2,1)}, u32[]{:S(2)}, u32[]{:S(2)}) collective-permute-start(bf16[64,512]{1,0:T(8,128)(2,1)S(1)} %copy-done.50), channel_id=1, source_target_pairs={{0,14},{4,10},{8,6},{12,2},{14,0},{10,4},{6,8},{2,12},{1,15},{5,11... | collective-permute-start | bytes 196616 | tf_op jit(solution)/shard_map/ppermute | solution.py:47
  319.7 1.8 fusion.3
  324.1 8.3 %collective-permute-done.50 = bf16[256,1024]{1,0:T(8,128)(2,1)S(1)} collective-permute-done((bf16[256,1024]{1,0:T(8,128)(2,1)S(1)}, bf16[256,1024]{1,0:T(8,128)(2,1)S(1)}, u32[]{:S(2)}, u32[]{:S(2)}) %collective-permute-start.50) | collective-permute-done | bytes 524320 | tf_op jit(solution)/shard_map/ppermute | solution.py:47
  333.8 2.6 fusion.19
  336.4 1.9 collective-permute-done.49
  339.1 5.4 %all-to-all-start.3 = ((bf16[8,32,384]{2,1,0:T(8,128)(2,1)}), bf16[8,32,384]{2,1,0:T(8,128)(2,1)S(1)}, u32[]{:S(2)}, u32[]{:S(2)}) async-start(bf16[8,32,384]{2,1,0:T(8,128)(2,1)} %fusion.49), calls=%async_computation.3 | async-start | bytes 393216 | tf_op jit(solution)/shard_map/all_to_all | solution.py:56
  344.4 2.0 collective-permute-start.52
  356.6 3.1 collective-permute-done.60
  361.9 2.9 fusion.21
  364.8 2.8 collective-permute-start.53
  370.0 8.6 %collective-permute-done.53 = bf16[256,1024]{1,0:T(8,128)(2,1)S(1)} collective-permute-done((bf16[256,1024]{1,0:T(8,128)(2,1)}, bf16[256,1024]{1,0:T(8,128)(2,1)S(1)}, u32[]{:S(2)}, u32[]{:S(2)}) %collective-permute-start.53) | collective-permute-done | bytes 524320 | tf_op jit(solution)/shard_map/ppermute | solution.py:47
  378.6 2.1 collective-permute-done.55
  380.7 1.5 fusion.14
  382.2 2.4 fusion.17
  (365 shorter events, 86.1 us)
Async XLA Ops:
  0.7 19.0 %collective-permute-start.6 = (bf16[256,1024]{1,0:T(8,128)(2,1)}, bf16[256,1024]{1,0:T(8,128)(2,1)}, u32[]{:S(2)}, u32[]{:S(2)}) collective-permute-start(bf16[256,1024]{1,0:T(8,128)(2,1)} %bitcast.359), channel_id=1, source_target_pairs={{0,16},{16,0},{1,17},{17,1},{2,18},{18,2},{3,19},{19,3},{4,20},{20... | collective-permute-start | bytes 1572872 | tf_op jit(solution)/shard_map/ppermute | solution.py:42
  3.8 39.2 %collective-permute-start.5 = (bf16[256,1024]{1,0:T(8,128)(2,1)}, bf16[256,1024]{1,0:T(8,128)(2,1)}, u32[]{:S(2)}, u32[]{:S(2)}) collective-permute-start(bf16[256,1024]{1,0:T(8,128)(2,1)} %bitcast.360), channel_id=1, source_target_pairs={{0,1},{1,0},{2,3},{3,2},{4,5},{5,4},{6,7},{7,6},{8,9},{9,8},{10,11... | collective-permute-start | bytes 1572872 | tf_op jit(solution)/shard_map/ppermute | solution.py:42
  4.9 23.4 %collective-permute-start.1 = (bf16[288,1024]{1,0:T(8,128)(2,1)S(1)}, bf16[288,1024]{1,0:T(8,128)(2,1)S(1)}, u32[]{:S(2)}, u32[]{:S(2)}) collective-permute-start(bf16[288,1024]{1,0:T(8,128)(2,1)S(1)} %pad_maximum_fusion.5.refs_0_), channel_id=1, source_target_pairs={{0,2},{4,0},{8,4},{12,8},{14,12},{10,14},{6,10},{2,6},{1,3},{5,1},... | collective-permute-start | bytes 1769480 | tf_op jit(solution)/shard_map/ppermute | solution.py:47
  6.5 21.9 %collective-permute-start = (bf16[288,1024]{1,0:T(8,128)(2,1)S(1)}, bf16[288,1024]{1,0:T(8,128)(2,1)S(1)}, u32[]{:S(2)}, u32[]{:S(2)}) collective-permute-start(bf16[288,1024]{1,0:T(8,128)(2,1)S(1)} %pad_maximum_fusion.5.refs_0_), channel_id=1, source_target_pairs={{0,4},{4,8},{8,12},{12,14},{14,10},{10,6},{6,2},{2,0},{1,5},{5,9},... | collective-permute-start | bytes 1769480 | tf_op jit(solution)/shard_map/ppermute | solution.py:47
  9.6 18.8 %all-to-all-start = ((bf16[8,112,128]{2,1,0:T(8,128)(2,1)}), bf16[8,112,128]{2,1,0:T(8,128)(2,1)S(1)}, u32[]{:S(2)}, u32[]{:S(2)}) async-start(bf16[8,112,128]{2,1,0:T(8,128)(2,1)} %pad.60.clone), calls=%async_computation | async-start | bytes 458752 | tf_op jit(solution)/shard_map/all_to_all | solution.py:56
  19.7 23.3 %collective-permute-start.7 = (bf16[256,1024]{1,0:T(8,128)(2,1)}, bf16[256,1024]{1,0:T(8,128)(2,1)}, u32[]{:S(2)}, u32[]{:S(2)}) collective-permute-start(bf16[256,1024]{1,0:T(8,128)(2,1)} %collective-permute-done.6.ga.refs_6_), channel_id=1, source_target_pairs={{0,1},{1,0},{2,3},{3,2},{4,5},{5,4},{6,7},{7,6},{8,9},{9,8},{10,11... | collective-permute-start | bytes 1572872 | tf_op jit(solution)/shard_map/ppermute | solution.py:42
  28.7 9.7 %collective-permute-start.3 = (bf16[8,112,128]{2,0,1:T(8,128)(2,1)S(1)}, bf16[8,112,128]{2,0,1:T(8,128)(2,1)S(1)}, u32[]{:S(2)}, u32[]{:S(2)}) collective-permute-start(bf16[8,112,128]{2,0,1:T(8,128)(2,1)S(1)} %copy.328), channel_id=1, source_target_pairs={{0,16},{16,0},{1,17},{17,1},{2,18},{18,2},{3,19},{19,3},{4,20},{20... | collective-permute-start | bytes 688136 | tf_op jit(solution)/shard_map/ppermute | solution.py:42
  29.2 6.5 %collective-permute-start.2 = (bf16[8,112,128]{2,0,1:T(8,128)(2,1)S(1)}, bf16[8,112,128]{2,0,1:T(8,128)(2,1)S(1)}, u32[]{:S(2)}, u32[]{:S(2)}) collective-permute-start(bf16[8,112,128]{2,0,1:T(8,128)(2,1)S(1)} %copy.328), channel_id=1, source_target_pairs={{0,1},{1,0},{2,3},{3,2},{4,5},{5,4},{6,7},{7,6},{8,9},{9,8},{10,11... | collective-permute-start | bytes 688136 | tf_op jit(solution)/shard_map/ppermute | solution.py:42
  29.7 15.9 %collective-permute-start.8 = (bf16[288,1024]{1,0:T(8,128)(2,1)S(1)}, bf16[288,1024]{1,0:T(8,128)(2,1)}, u32[]{:S(2)}, u32[]{:S(2)}) collective-permute-start(bf16[288,1024]{1,0:T(8,128)(2,1)S(1)} %collective-permute-done.refs_1_), channel_id=1, source_target_pairs={{0,4},{4,8},{8,12},{12,14},{14,10},{10,6},{6,2},{2,0},{1,5},{5,9},... | collective-permute-start | bytes 1769480 | tf_op jit(solution)/shard_map/ppermute | solution.py:47
  35.7 15.6 %collective-permute-start.9 = (bf16[288,1024]{1,0:T(8,128)(2,1)S(1)}, bf16[288,1024]{1,0:T(8,128)(2,1)S(1)}, u32[]{:S(2)}, u32[]{:S(2)}) collective-permute-start(bf16[288,1024]{1,0:T(8,128)(2,1)S(1)} %collective-permute-done.1.refs_2_), channel_id=1, source_target_pairs={{0,2},{4,0},{8,4},{12,8},{14,12},{10,14},{6,10},{2,6},{1,3},{5,1},... | collective-permute-start | bytes 1769480 | tf_op jit(solution)/shard_map/ppermute | solution.py:47
  38.4 1.6 collective-permute-start.4
  53.1 2.2 collective-permute-start.10
  53.2 16.0 %collective-permute-start.12 = (bf16[288,1024]{1,0:T(8,128)(2,1)}, bf16[288,1024]{1,0:T(8,128)(2,1)S(1)}, u32[]{:S(2)}, u32[]{:S(2)}) collective-permute-start(bf16[288,1024]{1,0:T(8,128)(2,1)} %collective-permute-done.8.refs_3_), channel_id=1, source_target_pairs={{0,4},{4,8},{8,12},{12,14},{14,10},{10,6},{6,2},{2,0},{1,5},{5,9},... | collective-permute-start | bytes 1769480 | tf_op jit(solution)/shard_map/ppermute | solution.py:47
  54.1 15.7 %collective-permute-start.13 = (bf16[288,1024]{1,0:T(8,128)(2,1)}, bf16[288,1024]{1,0:T(8,128)(2,1)S(1)}, u32[]{:S(2)}, u32[]{:S(2)}) collective-permute-start(bf16[288,1024]{1,0:T(8,128)(2,1)} %copy-done.19), channel_id=1, source_target_pairs={{0,2},{4,0},{8,4},{12,8},{14,12},{10,14},{6,10},{2,6},{1,3},{5,1},... | collective-permute-start | bytes 1769480 | tf_op jit(solution)/shard_map/ppermute | solution.py:47
  55.4 9.9 %collective-permute-start.11 = (bf16[2,32,1536]{2,1,0:T(8,128)(2,1)S(1)}, bf16[2,32,1536]{2,1,0:T(8,128)(2,1)S(1)}, u32[]{:S(2)}, u32[]{:S(2)}) collective-permute-start(bf16[2,32,1536]{2,1,0:T(8,128)(2,1)S(1)} %get-tuple-element.264), channel_id=1, source_target_pairs={{0,16},{16,0},{1,17},{17,1},{2,18},{18,2},{3,19},{19,3},{4,20},{20... | collective-permute-start | bytes 589832 | tf_op jit(solution)/shard_map/ppermute | solution.py:42
  69.7 7.6 %collective-permute-start.14 = (bf16[128,1024]{1,0:T(8,128)(2,1)S(1)}, bf16[128,1024]{1,0:T(8,128)(2,1)S(1)}, u32[]{:S(2)}, u32[]{:S(2)}) collective-permute-start(bf16[128,1024]{1,0:T(8,128)(2,1)S(1)} %slice.346), channel_id=1, source_target_pairs={{0,4},{4,8},{8,12},{12,14},{14,10},{10,6},{6,2},{2,0},{1,5},{5,9},... | collective-permute-start | bytes 786440 | tf_op jit(solution)/shard_map/ppermute | solution.py:47
  70.8 8.7 %collective-permute-start.15 = (bf16[160,1024]{1,0:T(8,128)(2,1)S(1)}, bf16[160,1024]{1,0:T(8,128)(2,1)S(1)}, u32[]{:S(2)}, u32[]{:S(2)}) collective-permute-start(bf16[160,1024]{1,0:T(8,128)(2,1)S(1)} %slice.347), channel_id=1, source_target_pairs={{0,2},{4,0},{8,4},{12,8},{14,12},{10,14},{6,10},{2,6},{1,3},{5,1},... | collective-permute-start | bytes 983048 | tf_op jit(solution)/shard_map/ppermute | solution.py:47
  79.5 21.4 %collective-permute-start.17 = (bf16[192,1536]{1,0:T(8,128)(2,1)S(1)}, bf16[192,1536]{1,0:T(8,128)(2,1)S(1)}, u32[]{:S(2)}, u32[]{:S(2)}) collective-permute-start(bf16[192,1536]{1,0:T(8,128)(2,1)S(1)} %fusion.35.refs_0_), channel_id=1, source_target_pairs={{0,2},{4,0},{8,4},{12,8},{14,12},{10,14},{6,10},{2,6},{1,3},{5,1},... | collective-permute-start | bytes 1769480 | tf_op jit(solution)/shard_map/ppermute | solution.py:47
  80.6 24.1 %collective-permute-start.16 = (bf16[192,1536]{1,0:T(8,128)(2,1)S(1)}, bf16[192,1536]{1,0:T(8,128)(2,1)}, u32[]{:S(2)}, u32[]{:S(2)}) collective-permute-start(bf16[192,1536]{1,0:T(8,128)(2,1)S(1)} %fusion.35.refs_0_), channel_id=1, source_target_pairs={{0,4},{4,8},{8,12},{12,14},{14,10},{10,6},{6,2},{2,0},{1,5},{5,9},... | collective-permute-start | bytes 1769480 | tf_op jit(solution)/shard_map/ppermute | solution.py:47
  104.7 7.5 %collective-permute-start.18 = (bf16[2,8,256,128]{3,2,1,0:T(8,128)(2,1)}, bf16[2,8,256,128]{3,2,1,0:T(8,128)(2,1)}, u32[]{:S(2)}, u32[]{:S(2)}) collective-permute-start(bf16[2,8,256,128]{3,2,1,0:T(8,128)(2,1)} %get-tuple-element.140.own_ref), channel_id=1, source_target_pairs={{0,1},{1,0},{2,3},{3,2},{4,5},{5,4},{6,7},{7,6},{8,9},{9,8},{10,11... | collective-permute-start | bytes 3145736 | tf_op jit(solution)/shard_map/ppermute | solution.py:42
  108.7 20.0 %collective-permute-start.19 = (bf16[8,32,1024]{2,1,0:T(8,128)(2,1)S(1)}, bf16[8,32,1024]{2,1,0:T(8,128)(2,1)S(1)}, u32[]{:S(2)}, u32[]{:S(2)}) collective-permute-start(bf16[8,32,1024]{2,1,0:T(8,128)(2,1)S(1)} %bitcast_dynamic-update-slice_fusion.refs_0_), channel_id=1, source_target_pairs={{0,16},{16,0},{1,17},{17,1},{2,18},{18,2},{3,19},{19,3},{4,20},{20... | collective-permute-start | bytes 1572872 | tf_op jit(solution)/shard_map/ppermute | solution.py:42
  110.2 18.5 %collective-permute-start.20 = (bf16[192,1536]{1,0:T(8,128)(2,1)}, bf16[192,1536]{1,0:T(8,128)(2,1)}, u32[]{:S(2)}, u32[]{:S(2)}) collective-permute-start(bf16[192,1536]{1,0:T(8,128)(2,1)} %collective-permute-done.16.refs_1_), channel_id=1, source_target_pairs={{0,4},{4,8},{8,12},{12,14},{14,10},{10,6},{6,2},{2,0},{1,5},{5,9},... | collective-permute-start | bytes 1769480 | tf_op jit(solution)/shard_map/ppermute | solution.py:47
  111.2 17.5 %collective-permute-start.21 = (bf16[192,1536]{1,0:T(8,128)(2,1)S(1)}, bf16[192,1536]{1,0:T(8,128)(2,1)S(1)}, u32[]{:S(2)}, u32[]{:S(2)}) collective-permute-start(bf16[192,1536]{1,0:T(8,128)(2,1)S(1)} %collective-permute-done.17.refs_8_), channel_id=1, source_target_pairs={{0,2},{4,0},{8,4},{12,8},{14,12},{10,14},{6,10},{2,6},{1,3},{5,1},... | collective-permute-start | bytes 1769480 | tf_op jit(solution)/shard_map/ppermute | solution.py:47
  129.7 26.5 %all-to-all-start.1 = ((bf16[8,256,128]{2,1,0:T(8,128)(2,1)}), bf16[8,256,128]{2,1,0:T(8,128)(2,1)S(1)}, u32[]{:S(2)}, u32[]{:S(2)}) async-start(bf16[8,256,128]{2,1,0:T(8,128)(2,1)} %get-tuple-element.145), calls=%async_computation.1 | async-start | bytes 1048576 | tf_op jit(solution)/shard_map/all_to_all | solution.py:56
  133.9 20.2 %collective-permute-start.22 = (bf16[192,1536]{1,0:T(8,128)(2,1)}, bf16[192,1536]{1,0:T(8,128)(2,1)S(1)}, u32[]{:S(2)}, u32[]{:S(2)}) collective-permute-start(bf16[192,1536]{1,0:T(8,128)(2,1)} %collective-permute-done.20.refs_2_), channel_id=1, source_target_pairs={{0,4},{4,8},{8,12},{12,14},{14,10},{10,6},{6,2},{2,0},{1,5},{5,9},... | collective-permute-start | bytes 1769480 | tf_op jit(solution)/shard_map/ppermute | solution.py:47
  135.9 20.3 %collective-permute-start.23 = (bf16[192,1536]{1,0:T(8,128)(2,1)}, bf16[192,1536]{1,0:T(8,128)(2,1)S(1)}, u32[]{:S(2)}, u32[]{:S(2)}) collective-permute-start(bf16[192,1536]{1,0:T(8,128)(2,1)} %copy-done.26), channel_id=1, source_target_pairs={{0,2},{4,0},{8,4},{12,8},{14,12},{10,14},{6,10},{2,6},{1,3},{5,1},... | collective-permute-start | bytes 1769480 | tf_op jit(solution)/shard_map/ppermute | solution.py:47
  136.0 27.4 %collective-permute-start.24 = (bf16[8,32,1024]{2,1,0:T(8,128)(2,1)S(1)}, bf16[8,32,1024]{2,1,0:T(8,128)(2,1)S(1)}, u32[]{:S(2)}, u32[]{:S(2)}) collective-permute-start(bf16[8,32,1024]{2,1,0:T(8,128)(2,1)S(1)} %bitcast_dynamic-update-slice_fusion.refs_0_), channel_id=1, source_target_pairs={{0,1},{1,0},{2,3},{3,2},{4,5},{5,4},{6,7},{7,6},{8,9},{9,8},{10,11... | collective-permute-start | bytes 1572872 | tf_op jit(solution)/shard_map/ppermute | solution.py:42
  136.0 27.4 %collective-permute-start.25 = (bf16[8,32,1024]{2,1,0:T(8,128)(2,1)}, bf16[8,32,1024]{2,1,0:T(8,128)(2,1)}, u32[]{:S(2)}, u32[]{:S(2)}) collective-permute-start(bf16[8,32,1024]{2,1,0:T(8,128)(2,1)} %copy-done.30), channel_id=1, source_target_pairs={{0,1},{1,0},{2,3},{3,2},{4,5},{5,4},{6,7},{7,6},{8,9},{9,8},{10,11... | collective-permute-start | bytes 1572872 | tf_op jit(solution)/shard_map/ppermute | solution.py:42
  157.8 10.4 %collective-permute-start.27 = (bf16[96,1536]{1,0:T(8,128)(2,1)}, bf16[96,1536]{1,0:T(8,128)(2,1)S(1)}, u32[]{:S(2)}, u32[]{:S(2)}) collective-permute-start(bf16[96,1536]{1,0:T(8,128)(2,1)} %slice.359), channel_id=1, source_target_pairs={{0,2},{4,0},{8,4},{12,8},{14,12},{10,14},{6,10},{2,6},{1,3},{5,1},... | collective-permute-start | bytes 884744 | tf_op jit(solution)/shard_map/ppermute | solution.py:47
  159.2 9.8 %collective-permute-start.26 = (bf16[96,1536]{1,0:T(8,128)(2,1)}, bf16[96,1536]{1,0:T(8,128)(2,1)}, u32[]{:S(2)}, u32[]{:S(2)}) collective-permute-start(bf16[96,1536]{1,0:T(8,128)(2,1)} %slice.358), channel_id=1, source_target_pairs={{0,4},{4,8},{8,12},{12,14},{14,10},{10,6},{6,2},{2,0},{1,5},{5,9},... | collective-permute-start | bytes 884744 | tf_op jit(solution)/shard_map/ppermute | solution.py:47
  169.1 4.7 %collective-permute-start.28 = (bf16[256,1024]{1,0:T(8,128)(2,1)}, bf16[256,1024]{1,0:T(8,128)(2,1)S(1)}, u32[]{:S(2)}, u32[]{:S(2)}) collective-permute-start(bf16[256,1024]{1,0:T(8,128)(2,1)} %get-tuple-element.154.na.refs_0_), channel_id=1, source_target_pairs={{0,1},{1,0},{2,3},{3,2},{4,5},{5,4},{6,7},{7,6},{8,9},{9,8},{10,11... | collective-permute-start | bytes 1572872 | tf_op jit(solution)/shard_map/ppermute | solution.py:42
  169.1 15.8 %collective-permute-start.29 = (bf16[256,1024]{1,0:T(8,128)(2,1)}, bf16[256,1024]{1,0:T(8,128)(2,1)S(1)}, u32[]{:S(2)}, u32[]{:S(2)}) collective-permute-start(bf16[256,1024]{1,0:T(8,128)(2,1)} %get-tuple-element.154.na.refs_0_), channel_id=1, source_target_pairs={{0,16},{16,0},{1,17},{17,1},{2,18},{18,2},{3,19},{19,3},{4,20},{20... | collective-permute-start | bytes 1572872 | tf_op jit(solution)/shard_map/ppermute | solution.py:42
  184.9 2.1 collective-permute-start.30
  199.5 2.0 collective-permute-start.31
  201.2 14.7 %collective-permute-start.35 = (bf16[256,1024]{1,0:T(8,128)(2,1)S(1)}, bf16[256,1024]{1,0:T(8,128)(2,1)S(1)}, u32[]{:S(2)}, u32[]{:S(2)}) collective-permute-start(bf16[256,1024]{1,0:T(8,128)(2,1)S(1)} %get-tuple-element.245), channel_id=1, source_target_pairs={{0,1},{1,0},{2,3},{3,2},{4,5},{5,4},{6,7},{7,6},{8,9},{9,8},{10,11... | collective-permute-start | bytes 1572872 | tf_op jit(solution)/shard_map/ppermute | solution.py:42
  201.7 14.3 %collective-permute-start.36 = (bf16[256,1024]{1,0:T(8,128)(2,1)S(1)}, bf16[256,1024]{1,0:T(8,128)(2,1)S(1)}, u32[]{:S(2)}, u32[]{:S(2)}) collective-permute-start(bf16[256,1024]{1,0:T(8,128)(2,1)S(1)} %fusion.28), channel_id=1, source_target_pairs={{0,16},{16,0},{1,17},{17,1},{2,18},{18,2},{3,19},{19,3},{4,20},{20... | collective-permute-start | bytes 1572872 | tf_op jit(solution)/shard_map/ppermute | solution.py:42
  224.5 5.5 %collective-permute-start.37 = (bf16[1,2,8,32,1024]{4,3,2,1,0:T(8,128)(2,1)}, bf16[1,2,8,32,1024]{4,3,2,1,0:T(8,128)(2,1)}, u32[]{:S(2)}, u32[]{:S(2)}) collective-permute-start(bf16[1,2,8,32,1024]{4,3,2,1,0:T(8,128)(2,1)} %select_bitcast_fusion), channel_id=1, source_target_pairs={{0,1},{1,0},{2,3},{3,2},{4,5},{5,4},{6,7},{7,6},{8,9},{9,8},{10,11... | collective-permute-start | bytes 3145736 | tf_op jit(solution)/shard_map/ppermute | solution.py:42
  225.8 61.4 %collective-permute-start.33 = (bf16[256,1024]{1,0:T(8,128)(2,1)}, bf16[256,1024]{1,0:T(8,128)(2,1)}, u32[]{:S(2)}, u32[]{:S(2)}) collective-permute-start(bf16[256,1024]{1,0:T(8,128)(2,1)} %slice_bitcast_fusion.4), channel_id=1, source_target_pairs={{0,1},{1,0},{2,3},{3,2},{4,5},{5,4},{6,7},{7,6},{8,9},{9,8},{10,11... | collective-permute-start | bytes 1572872 | tf_op jit(solution)/shard_map/ppermute | solution.py:42
  225.8 29.0 %all-to-all-start.2 = ((bf16[8,256,128]{2,1,0:T(8,128)(2,1)}), bf16[8,256,128]{2,1,0:T(8,128)(2,1)}, u32[]{:S(2)}, u32[]{:S(2)}) async-start(bf16[8,256,128]{2,1,0:T(8,128)(2,1)} %get-tuple-element.187), calls=%async_computation.2 | async-start | bytes 1048576 | tf_op jit(solution)/shard_map/all_to_all | solution.py:56
  231.9 14.4 %collective-permute-start.38 = (bf16[1,8,32,1024]{3,2,1,0:T(8,128)(2,1)S(1)}, bf16[1,8,32,1024]{3,2,1,0:T(8,128)(2,1)S(1)}, u32[]{:S(2)}, u32[]{:S(2)}) collective-permute-start(bf16[1,8,32,1024]{3,2,1,0:T(8,128)(2,1)S(1)} %fusion.37), channel_id=1, source_target_pairs={{0,16},{16,0},{1,17},{17,1},{2,18},{18,2},{3,19},{19,3},{4,20},{20... | collective-permute-start | bytes 1572872 | tf_op jit(solution)/shard_map/ppermute | solution.py:42
  234.7 18.0 %collective-permute-start.40 = (bf16[88,1536]{1,0:T(8,128)(2,1)S(1)}, bf16[88,1536]{1,0:T(8,128)(2,1)S(1)}, u32[]{:S(2)}, u32[]{:S(2)}) collective-permute-start(bf16[88,1536]{1,0:T(8,128)(2,1)S(1)} %slice_bitcast_fusion.8), channel_id=1, source_target_pairs={{0,2},{4,0},{8,4},{12,8},{14,12},{10,14},{6,10},{2,6},{1,3},{5,1},... | collective-permute-start | bytes 811016 | tf_op jit(solution)/shard_map/ppermute | solution.py:47
  237.6 16.1 %collective-permute-start.39 = (bf16[128,1536]{1,0:T(8,128)(2,1)S(1)}, bf16[128,1536]{1,0:T(8,128)(2,1)S(1)}, u32[]{:S(2)}, u32[]{:S(2)}) collective-permute-start(bf16[128,1536]{1,0:T(8,128)(2,1)S(1)} %slice_bitcast_fusion.7), channel_id=1, source_target_pairs={{0,4},{4,8},{8,12},{12,14},{14,10},{10,6},{6,2},{2,0},{1,5},{5,9},... | collective-permute-start | bytes 1179656 | tf_op jit(solution)/shard_map/ppermute | solution.py:47
  254.8 25.5 %collective-permute-start.41 = (bf16[216,1536]{1,0:T(8,128)(2,1)}, bf16[216,1536]{1,0:T(8,128)(2,1)S(1)}, u32[]{:S(2)}, u32[]{:S(2)}) collective-permute-start(bf16[216,1536]{1,0:T(8,128)(2,1)} %pad_maximum_fusion.3), channel_id=1, source_target_pairs={{0,4},{4,8},{8,12},{12,14},{14,10},{10,6},{6,2},{2,0},{1,5},{5,9},... | collective-permute-start | bytes 1990664 | tf_op jit(solution)/shard_map/ppermute | solution.py:47
  256.4 23.9 %collective-permute-start.42 = (bf16[216,1536]{1,0:T(8,128)(2,1)}, bf16[216,1536]{1,0:T(8,128)(2,1)S(1)}, u32[]{:S(2)}, u32[]{:S(2)}) collective-permute-start(bf16[216,1536]{1,0:T(8,128)(2,1)} %pad_maximum_fusion.4), channel_id=1, source_target_pairs={{0,2},{4,0},{8,4},{12,8},{14,12},{10,14},{6,10},{2,6},{1,3},{5,1},... | collective-permute-start | bytes 1990664 | tf_op jit(solution)/shard_map/ppermute | solution.py:47
  280.2 10.7 %collective-permute-start.43 = (bf16[2,8,256,128]{3,2,1,0:T(8,128)(2,1)}, bf16[2,8,256,128]{3,2,1,0:T(8,128)(2,1)}, u32[]{:S(2)}, u32[]{:S(2)}) collective-permute-start(bf16[2,8,256,128]{3,2,1,0:T(8,128)(2,1)} %get-tuple-element.200), channel_id=1, source_target_pairs={{0,1},{1,0},{2,3},{3,2},{4,5},{5,4},{6,7},{7,6},{8,9},{9,8},{10,11... | collective-permute-start | bytes 3145736 | tf_op jit(solution)/shard_map/ppermute | solution.py:42
  284.1 19.6 %collective-permute-start.44 = (bf16[216,1536]{1,0:T(8,128)(2,1)}, bf16[216,1536]{1,0:T(8,128)(2,1)S(1)}, u32[]{:S(2)}, u32[]{:S(2)}) collective-permute-start(bf16[216,1536]{1,0:T(8,128)(2,1)} %get-tuple-element.203), channel_id=1, source_target_pairs={{0,4},{4,8},{8,12},{12,14},{14,10},{10,6},{6,2},{2,0},{1,5},{5,9},... | collective-permute-start | bytes 1990664 | tf_op jit(solution)/shard_map/ppermute | solution.py:47
  285.7 18.1 %collective-permute-start.45 = (bf16[216,1536]{1,0:T(8,128)(2,1)}, bf16[216,1536]{1,0:T(8,128)(2,1)}, u32[]{:S(2)}, u32[]{:S(2)}) collective-permute-start(bf16[216,1536]{1,0:T(8,128)(2,1)} %get-tuple-element.204), channel_id=1, source_target_pairs={{0,2},{4,0},{8,4},{12,8},{14,12},{10,14},{6,10},{2,6},{1,3},{5,1},... | collective-permute-start | bytes 1990664 | tf_op jit(solution)/shard_map/ppermute | solution.py:47
  287.2 20.1 %collective-permute-start.32 = (bf16[256,1024]{1,0:T(8,128)(2,1)}, bf16[256,1024]{1,0:T(8,128)(2,1)}, u32[]{:S(2)}, u32[]{:S(2)}) collective-permute-start(bf16[256,1024]{1,0:T(8,128)(2,1)} %slice_bitcast_fusion.5), channel_id=1, source_target_pairs={{0,1},{1,0},{2,3},{3,2},{4,5},{5,4},{6,7},{7,6},{8,9},{9,8},{10,11... | collective-permute-start | bytes 1572872 | tf_op jit(solution)/shard_map/ppermute | solution.py:42
  289.2 18.0 %collective-permute-start.34 = (bf16[256,1024]{1,0:T(8,128)(2,1)}, bf16[256,1024]{1,0:T(8,128)(2,1)S(1)}, u32[]{:S(2)}, u32[]{:S(2)}) collective-permute-start(bf16[256,1024]{1,0:T(8,128)(2,1)} %fusion.24), channel_id=1, source_target_pairs={{0,16},{16,0},{1,17},{17,1},{2,18},{18,2},{3,19},{19,3},{4,20},{20... | collective-permute-start | bytes 1572872 | tf_op jit(solution)/shard_map/ppermute | solution.py:42
  305.2 8.6 %collective-permute-start.47 = (bf16[128,1024]{1,0:T(8,128)(2,1)S(1)}, bf16[128,1024]{1,0:T(8,128)(2,1)S(1)}, u32[]{:S(2)}, u32[]{:S(2)}) collective-permute-start(bf16[128,1024]{1,0:T(8,128)(2,1)S(1)} %get-tuple-element.238), channel_id=1, source_target_pairs={{0,2},{4,0},{8,4},{12,8},{14,12},{10,14},{6,10},{2,6},{1,3},{5,1},... | collective-permute-start | bytes 786440 | tf_op jit(solution)/shard_map/ppermute | solution.py:47
  306.9 8.2 %collective-permute-start.46 = (bf16[128,1024]{1,0:T(8,128)(2,1)S(1)}, bf16[128,1024]{1,0:T(8,128)(2,1)S(1)}, u32[]{:S(2)}, u32[]{:S(2)}) collective-permute-start(bf16[128,1024]{1,0:T(8,128)(2,1)S(1)} %get-tuple-element.240), channel_id=1, source_target_pairs={{0,4},{4,8},{8,12},{12,14},{14,10},{10,6},{6,2},{2,0},{1,5},{5,9},... | collective-permute-start | bytes 786440 | tf_op jit(solution)/shard_map/ppermute | solution.py:47
  309.4 40.1 %collective-permute-start.58 = (bf16[64,512]{1,0:T(8,128)(2,1)S(1)}, bf16[64,512]{1,0:T(8,128)(2,1)}, u32[]{:S(2)}, u32[]{:S(2)}) collective-permute-start(bf16[64,512]{1,0:T(8,128)(2,1)S(1)} %copy-done.50), channel_id=1, source_target_pairs={{0,14},{4,10},{8,6},{12,2},{14,0},{10,4},{6,8},{2,12},{1,15},{5,11... | collective-permute-start | bytes 196616 | tf_op jit(solution)/shard_map/ppermute | solution.py:47
  317.5 5.5 %collective-permute-start.48 = (bf16[1,2,8,32,384]{4,3,2,1,0:T(8,128)(2,1)S(1)}, bf16[1,2,8,32,384]{4,3,2,1,0:T(8,128)(2,1)S(1)}, u32[]{:S(2)}, u32[]{:S(2)}) collective-permute-start(bf16[1,2,8,32,384]{4,3,2,1,0:T(8,128)(2,1)S(1)} %fusion.42), channel_id=1, source_target_pairs={{0,1},{1,0},{2,3},{3,2},{4,5},{5,4},{6,7},{7,6},{8,9},{9,8},{10,11... | collective-permute-start | bytes 1179656 | tf_op jit(solution)/shard_map/ppermute | solution.py:42
  317.6 14.8 %collective-permute-start.50 = (bf16[256,1024]{1,0:T(8,128)(2,1)S(1)}, bf16[256,1024]{1,0:T(8,128)(2,1)S(1)}, u32[]{:S(2)}, u32[]{:S(2)}) collective-permute-start(bf16[256,1024]{1,0:T(8,128)(2,1)S(1)} %pad_maximum_fusion.6), channel_id=1, source_target_pairs={{0,4},{4,8},{8,12},{12,14},{14,10},{10,6},{6,2},{2,0},{1,5},{5,9},... | collective-permute-start | bytes 1572872 | tf_op jit(solution)/shard_map/ppermute | solution.py:47
  319.0 14.8 %collective-permute-start.51 = (bf16[256,1024]{1,0:T(8,128)(2,1)S(1)}, bf16[256,1024]{1,0:T(8,128)(2,1)S(1)}, u32[]{:S(2)}, u32[]{:S(2)}) collective-permute-start(bf16[256,1024]{1,0:T(8,128)(2,1)S(1)} %pad_maximum_fusion.7), channel_id=1, source_target_pairs={{0,2},{4,0},{8,4},{12,8},{14,12},{10,14},{6,10},{2,6},{1,3},{5,1},... | collective-permute-start | bytes 1572872 | tf_op jit(solution)/shard_map/ppermute | solution.py:47
  321.5 25.2 %collective-permute-start.56 = (bf16[216,1536]{1,0:T(8,128)(2,1)S(1)}, bf16[216,1536]{1,0:T(8,128)(2,1)S(1)}, u32[]{:S(2)}, u32[]{:S(2)}) collective-permute-start(bf16[216,1536]{1,0:T(8,128)(2,1)S(1)} %get-tuple-element.227), channel_id=1, source_target_pairs={{0,4},{4,8},{8,12},{12,14},{14,10},{10,6},{6,2},{2,0},{1,5},{5,9},... | collective-permute-start | bytes 1990664 | tf_op jit(solution)/shard_map/ppermute | solution.py:47
  323.0 25.1 %collective-permute-start.57 = (bf16[216,1536]{1,0:T(8,128)(2,1)S(1)}, bf16[216,1536]{1,0:T(8,128)(2,1)S(1)}, u32[]{:S(2)}, u32[]{:S(2)}) collective-permute-start(bf16[216,1536]{1,0:T(8,128)(2,1)S(1)} %get-tuple-element.228), channel_id=1, source_target_pairs={{0,2},{4,0},{8,4},{12,8},{14,12},{10,14},{6,10},{2,6},{1,3},{5,1},... | collective-permute-start | bytes 1990664 | tf_op jit(solution)/shard_map/ppermute | solution.py:47
  332.4 5.9 %collective-permute-start.49 = (bf16[1,8,32,384]{3,2,1,0:T(8,128)(2,1)S(1)}, bf16[1,8,32,384]{3,2,1,0:T(8,128)(2,1)S(1)}, u32[]{:S(2)}, u32[]{:S(2)}) collective-permute-start(bf16[1,8,32,384]{3,2,1,0:T(8,128)(2,1)S(1)} %fusion.48), channel_id=1, source_target_pairs={{0,16},{16,0},{1,17},{17,1},{2,18},{18,2},{3,19},{19,3},{4,20},{20... | collective-permute-start | bytes 589832 | tf_op jit(solution)/shard_map/ppermute | solution.py:42
  339.1 14.6 %all-to-all-start.3 = ((bf16[8,32,384]{2,1,0:T(8,128)(2,1)}), bf16[8,32,384]{2,1,0:T(8,128)(2,1)S(1)}, u32[]{:S(2)}, u32[]{:S(2)}) async-start(bf16[8,32,384]{2,1,0:T(8,128)(2,1)} %fusion.49), calls=%async_computation.3 | async-start | bytes 393216 | tf_op jit(solution)/shard_map/all_to_all | solution.py:56
  344.4 17.3 %collective-permute-start.52 = (bf16[256,1024]{1,0:T(8,128)(2,1)}, bf16[256,1024]{1,0:T(8,128)(2,1)}, u32[]{:S(2)}, u32[]{:S(2)}) collective-permute-start(bf16[256,1024]{1,0:T(8,128)(2,1)} %get-tuple-element.212), channel_id=1, source_target_pairs={{0,4},{4,8},{8,12},{12,14},{14,10},{10,6},{6,2},{2,0},{1,5},{5,9},... | collective-permute-start | bytes 1572872 | tf_op jit(solution)/shard_map/ppermute | solution.py:47
  346.5 15.5 %collective-permute-start.54 = (bf16[256,1024]{1,0:T(8,128)(2,1)}, bf16[256,1024]{1,0:T(8,128)(2,1)}, u32[]{:S(2)}, u32[]{:S(2)}) collective-permute-start(bf16[256,1024]{1,0:T(8,128)(2,1)} %get-tuple-element.213), channel_id=1, source_target_pairs={{0,2},{4,0},{8,4},{12,8},{14,12},{10,14},{6,10},{2,6},{1,3},{5,1},... | collective-permute-start | bytes 1572872 | tf_op jit(solution)/shard_map/ppermute | solution.py:47
  352.6 7.0 %collective-permute-start.60 = (bf16[2,32,1536]{2,1,0:T(8,128)(2,1)S(1)}, bf16[2,32,1536]{2,1,0:T(8,128)(2,1)S(1)}, u32[]{:S(2)}, u32[]{:S(2)}) collective-permute-start(bf16[2,32,1536]{2,1,0:T(8,128)(2,1)S(1)} %fusion.47), channel_id=1, source_target_pairs={{0,16},{16,0},{1,17},{17,1},{2,18},{18,2},{3,19},{19,3},{4,20},{20... | collective-permute-start | bytes 589832 | tf_op jit(solution)/shard_map/ppermute | solution.py:42
  364.8 13.8 %collective-permute-start.53 = (bf16[256,1024]{1,0:T(8,128)(2,1)}, bf16[256,1024]{1,0:T(8,128)(2,1)S(1)}, u32[]{:S(2)}, u32[]{:S(2)}) collective-permute-start(bf16[256,1024]{1,0:T(8,128)(2,1)} %get-tuple-element.233), channel_id=1, source_target_pairs={{0,4},{4,8},{8,12},{12,14},{14,10},{10,6},{6,2},{2,0},{1,5},{5,9},... | collective-permute-start | bytes 1572872 | tf_op jit(solution)/shard_map/ppermute | solution.py:47
  367.6 13.1 %collective-permute-start.55 = (bf16[256,1024]{1,0:T(8,128)(2,1)}, bf16[256,1024]{1,0:T(8,128)(2,1)S(1)}, u32[]{:S(2)}, u32[]{:S(2)}) collective-permute-start(bf16[256,1024]{1,0:T(8,128)(2,1)} %get-tuple-element.234), channel_id=1, source_target_pairs={{0,2},{4,0},{8,4},{12,8},{14,12},{10,14},{6,10},{2,6},{1,3},{5,1},... | collective-permute-start | bytes 1572872 | tf_op jit(solution)/shard_map/ppermute | solution.py:47
  (67 other events, 580.9 us)
